TPU v7x, 128 devices: a whole 4x4x4 slice. The times are simulated.
128 devices in a mesh: row: 8 (over z, core), col: 16 (over y, x).
Axes of the slice: x: 4, y: 4, z: 4, core: 2. Of those that a mesh axis runs over, the one named last changes fastest.
Arguments:
- amp_tiles: float32 [16, 32, 256, 256], P('row', 'col'), may hold values from -6 to 6
- int_tiles: float32 [32, 32, 256, 256], P('col', 'row'), may hold values from -0.125 to 0.125
- resid_init: float32 [16, 32, 256, 256], P('row', 'col'), may hold values from -6 to 6
- triples: int32 [8, 16, 3, 32], P('row', 'col'), may hold values from 0 to 1023, as said below
Outputs:
- resid_out: float32 [16, 32, 256, 256], P('row', 'col')
Inputs may be any that keep to these rules, and one draw needn't show every extreme that they name: Each triple names tiles (i, j), (j, k), (i, k) with one i, j, k. The amplitude tile of every triple on device (r, c) is one that device holds. For every device and every column index q, exactly 2 distinct residual tiles held at (r, q) are named by that device's triples, each by exactly one of that device's triples. No triple is listed twice; the order of triples on a device is arbitrary.
All inputs are finite; a program needn't handle non-finite values.
Results may differ from a plain program's by a relative error of at most 0.0001.
Values sent between devices are 32-bit elements; how exact they have to be, the bound alone decides.
No kernel may reach another device: no remote copies, remote signals or barrier semaphores. Data moves between devices by JAX's collectives and lax.ppermute only.
A program may use at most 128 MiB of HBM per device.

v0:
```python
import jax
import jax.numpy as jnp
from jax import lax
from jax.sharding import PartitionSpec as P


def on_device(amp_tiles, int_tiles, resid_init, triples):
    occ_blocks = amp_tiles.shape[0]
    vir_blocks = amp_tiles.shape[1]
    width = amp_tiles.shape[2]
    own_k = resid_init.shape[1]
    col_count = lax.axis_size("col")
    all_k = own_k * col_count
    all_j = vir_blocks * col_count
    row_place = lax.axis_index("row")
    col_place = lax.axis_index("col")
    listing = triples[0, 0]
    amp_ids = listing[0]
    int_ids = listing[1]
    res_ids = listing[2]
    amp_occ = amp_ids // all_j - row_place * occ_blocks
    amp_vir = amp_ids % all_j - col_place * vir_blocks
    int_vir = int_ids // all_k - col_place * vir_blocks
    int_col = int_ids % all_k
    res_occ = res_ids // all_k - row_place * occ_blocks
    res_col = res_ids % all_k
    amp_index = amp_occ * vir_blocks + amp_vir
    int_index = int_vir * all_k + int_col
    gathered = lax.all_gather(int_tiles, "row", axis=1, tiled=True)
    amp_flat = amp_tiles.reshape(-1, width, width)
    int_flat = gathered.reshape(-1, width, width)
    target = res_occ * all_k + res_col
    slots_total = occ_blocks * all_k
    block = 8

    def add_block(partial_value, pieces):
        amp_pick, int_pick, target_pick = pieces
        products = jnp.einsum(
            "bxy,byz->bxz",
            amp_flat[amp_pick],
            int_flat[int_pick],
            precision=lax.Precision.HIGHEST,
            preferred_element_type=jnp.float32,
        )
        return (partial_value.at[target_pick].add(products), None)

    start = jnp.zeros((slots_total, width, width), jnp.float32)
    pieces = (amp_index.reshape(-1, block), int_index.reshape(-1, block), target.reshape(-1, block))
    partial_value, _ = lax.scan(add_block, start, pieces)
    summed = lax.psum_scatter(
        partial_value.reshape(occ_blocks, all_k, width, width),
        "col",
        scatter_dimension=1,
        tiled=True,
    )
    return resid_init + summed


def solution(mesh):
    return jax.shard_map(
        on_device,
        mesh=mesh,
        in_specs=(
            P("row", "col", None, None),
            P("col", "row", None, None),
            P("row", "col", None, None),
            P("row", "col", None, None),
        ),
        out_specs=P("row", "col", None, None),
        check_vma=False,
    )
```

profile of v0, /device:TPU:1, one launch (start us, length us, event | category | flops | bytes accessed | tf_op | source)
XLA Modules:
  0.0 409.3 jit_solution(13803242583573978467)
XLA Ops:
  6.5 0.0 copy-start.2
  6.5 0.0 all-gather.2.cloned.1.call-start
  6.5 0.7 all-gather.2.cloned.1.call-update
  7.3 0.0 all-reduce.3.cloned.1.call-start
  7.3 0.0 copy-done.2
  7.3 0.1 squeeze.20
  7.4 0.1 squeeze.21
  7.5 0.1 squeeze.22
  7.6 90.2 %all-gather.2.cloned.1.call-done = f32[2,32,256,256]{3,2,1,0:T(8,128)} async-done(((f32[2,4,256,256]{3,2,1,0:T(8,128)}), f32[2,32,256,256]{3,2,1,0:T(8,128)}) %all-gather.2.cloned.1.call-update) | async-done | bytes 16777232 | tf_op jit(solution)/shard_map/all_gather | solution.py:29
  97.9 0.0 copy-start
  97.9 7.8 %broadcast_in_dim.2 = f32[64,256,256]{2,1,0:T(8,128)} broadcast(f32[]{:T(128)} %constant.72.clone.1), dimensions={} | broadcast | bytes 16777220 | tf_op jit(solution)/shard_map/broadcast_in_dim | solution.py:47
  105.6 0.0 copy-done
  105.6 74.3 %while.10 = (s32[]{:T(128)}, f32[64,256,256]{2,1,0:T(8,128)}, s32[4,8]{1,0:T(4,128)S(1)}, s32[4,8]{1,0:T(4,128)S(1)}, f32[4,256,256]{2,1,0:T(8,128)S(1)}, /*inde...) while((s32[]{:T(128)}, f32[64,256,256]{2,1,0:T(8,128)}, s32[4,8]{1,0:T(4,128)S(1)}, ...), condition=%wide.region_2.3_spmd, body=%wide.region_0.2_spmd.sunk | while | flops 1611139200 | bytes 20980156 | solution.py:49
  105.7 2.0 gather_fusion
  107.7 7.8 %gather_fusion.1 = f32[8,256,256]{2,1,0:T(8,128)} fusion(f32[64,256,256]{2,1,0:T(8,128)} %get-tuple-element.133, s32[1024]{0:T(1024)S(1)} %pad_clamp_fusion.5), kind=kCustom, calls=%fused_computation.1.clone.1 | custom fusion | bytes 4194336 | tf_op jit(solution)/shard_map/while/body/eval_jaxpr/gather | solution.py:41
  115.5 4.3 %fusion.34 = f32[8,256,256]{2,1,0:T(8,128)S(1)} fusion(f32[8,256,256]{2,1,0:T(8,128)} %gather_fusion, f32[8,256,256]{2,1,0:T(8,128)} %gather_fusion.1), kind=kOutput, calls=%fused_computation.55.clone.1 | convolution fusion | flops 1610612736 | bytes 6291456 | tf_op jit(solution)/shard_map/while/body/eval_jaxpr/bxy,byz->bxz/dot_general | solution.py:38
  119.8 4.4 %scatter_fusion = f32[64,256,256]{2,1,0:T(8,128)} fusion(f32[64,256,256]{2,1,0:T(8,128)} %get-tuple-element.120, s32[8]{0:T(128)S(1)} %get-tuple-element.109, f32[8,256,256]{2,1,0:T(8,128)S(1)} %fusion.34), kind=kCustom, calls=%fused_computation.2.clone.1 | custom fusion | flops 524288 | bytes 6291488 | tf_op jit(solution)/shard_map/while/body/eval_jaxpr/scatter-add | solution.py:45
  124.2 2.0 gather_fusion
  126.2 7.8 %gather_fusion.1 = f32[8,256,256]{2,1,0:T(8,128)} fusion(f32[64,256,256]{2,1,0:T(8,128)} %get-tuple-element.133, s32[1024]{0:T(1024)S(1)} %pad_clamp_fusion.5), kind=kCustom, calls=%fused_computation.1.clone.1 | custom fusion | bytes 4194336 | tf_op jit(solution)/shard_map/while/body/eval_jaxpr/gather | solution.py:41
  134.0 4.3 %fusion.34 = f32[8,256,256]{2,1,0:T(8,128)S(1)} fusion(f32[8,256,256]{2,1,0:T(8,128)} %gather_fusion, f32[8,256,256]{2,1,0:T(8,128)} %gather_fusion.1), kind=kOutput, calls=%fused_computation.55.clone.1 | convolution fusion | flops 1610612736 | bytes 6291456 | tf_op jit(solution)/shard_map/while/body/eval_jaxpr/bxy,byz->bxz/dot_general | solution.py:38
  138.3 4.4 %scatter_fusion = f32[64,256,256]{2,1,0:T(8,128)} fusion(f32[64,256,256]{2,1,0:T(8,128)} %get-tuple-element.120, s32[8]{0:T(128)S(1)} %get-tuple-element.109, f32[8,256,256]{2,1,0:T(8,128)S(1)} %fusion.34), kind=kCustom, calls=%fused_computation.2.clone.1 | custom fusion | flops 524288 | bytes 6291488 | tf_op jit(solution)/shard_map/while/body/eval_jaxpr/scatter-add | solution.py:45
  142.8 2.0 gather_fusion
  144.8 7.8 %gather_fusion.1 = f32[8,256,256]{2,1,0:T(8,128)} fusion(f32[64,256,256]{2,1,0:T(8,128)} %get-tuple-element.133, s32[1024]{0:T(1024)S(1)} %pad_clamp_fusion.5), kind=kCustom, calls=%fused_computation.1.clone.1 | custom fusion | bytes 4194336 | tf_op jit(solution)/shard_map/while/body/eval_jaxpr/gather | solution.py:41
  152.6 4.3 %fusion.34 = f32[8,256,256]{2,1,0:T(8,128)S(1)} fusion(f32[8,256,256]{2,1,0:T(8,128)} %gather_fusion, f32[8,256,256]{2,1,0:T(8,128)} %gather_fusion.1), kind=kOutput, calls=%fused_computation.55.clone.1 | convolution fusion | flops 1610612736 | bytes 6291456 | tf_op jit(solution)/shard_map/while/body/eval_jaxpr/bxy,byz->bxz/dot_general | solution.py:38
  156.9 4.5 %scatter_fusion = f32[64,256,256]{2,1,0:T(8,128)} fusion(f32[64,256,256]{2,1,0:T(8,128)} %get-tuple-element.120, s32[8]{0:T(128)S(1)} %get-tuple-element.109, f32[8,256,256]{2,1,0:T(8,128)S(1)} %fusion.34), kind=kCustom, calls=%fused_computation.2.clone.1 | custom fusion | flops 524288 | bytes 6291488 | tf_op jit(solution)/shard_map/while/body/eval_jaxpr/scatter-add | solution.py:45
  161.4 2.0 gather_fusion
  163.4 7.8 %gather_fusion.1 = f32[8,256,256]{2,1,0:T(8,128)} fusion(f32[64,256,256]{2,1,0:T(8,128)} %get-tuple-element.133, s32[1024]{0:T(1024)S(1)} %pad_clamp_fusion.5), kind=kCustom, calls=%fused_computation.1.clone.1 | custom fusion | bytes 4194336 | tf_op jit(solution)/shard_map/while/body/eval_jaxpr/gather | solution.py:41
  171.2 4.3 %fusion.34 = f32[8,256,256]{2,1,0:T(8,128)S(1)} fusion(f32[8,256,256]{2,1,0:T(8,128)} %gather_fusion, f32[8,256,256]{2,1,0:T(8,128)} %gather_fusion.1), kind=kOutput, calls=%fused_computation.55.clone.1 | convolution fusion | flops 1610612736 | bytes 6291456 | tf_op jit(solution)/shard_map/while/body/eval_jaxpr/bxy,byz->bxz/dot_general | solution.py:38
  175.5 4.4 %scatter_fusion = f32[64,256,256]{2,1,0:T(8,128)} fusion(f32[64,256,256]{2,1,0:T(8,128)} %get-tuple-element.120, s32[8]{0:T(128)S(1)} %get-tuple-element.109, f32[8,256,256]{2,1,0:T(8,128)S(1)} %fusion.34), kind=kCustom, calls=%fused_computation.2.clone.1 | custom fusion | flops 524288 | bytes 6291488 | tf_op jit(solution)/shard_map/while/body/eval_jaxpr/scatter-add | solution.py:45
  179.9 0.0 copy-start.3
  179.9 0.0 copy-start.1
  179.9 0.0 all-reduce.3.cloned.1.call-update
  180.0 0.6 copy-done.3
  180.6 0.6 dynamic-slice
  181.8 218.3 %all-reduce.3.cloned.1.call-done = f32[2,32,256,256]{3,2,1,0:T(8,128)} async-done(((f32[2,32,256,256]{3,2,1,0:T(8,128)}), f32[2,32,256,256]{3,2,1,0:T(8,128)}) %all-reduce.3.cloned.1.call-update) | async-done | bytes 16777232
  400.2 0.0 copy-done.1
  400.2 2.3 dynamic-slice_add_fusion
  (19 shorter events, 0.2 us)
Async XLA Ops:
  6.5 0.8 copy-start.2
  6.5 91.3 %all-gather.2.cloned.1.call-start = ((), (), s32[]{:S(2)}) async-start(), calls=%async_computation | async-start | bytes 18874368 | tf_op jit(solution)/shard_map/all_gather | solution.py:29
  7.3 392.9 %all-reduce.3.cloned.1.call-start = ((), (), s32[]{:S(2)}) async-start(), calls=%async_computation.1 | async-start | bytes 33554432
  97.9 7.8 %copy-start = (f32[2,2,256,256]{3,2,1,0:T(8,128)S(1)}, f32[2,2,256,256]{3,2,1,0:T(8,128)}, u32[]{:S(2)}) copy-start(f32[2,2,256,256]{3,2,1,0:T(8,128)} %param.6) | copy-start | bytes 3145732
  179.9 0.7 copy-start.3
  179.9 220.2 %copy-start.1 = (f32[2,2,256,256]{3,2,1,0:T(8,128)S(1)}, f32[2,2,256,256]{3,2,1,0:T(8,128)}, u32[]{:S(2)}) copy-start(f32[2,2,256,256]{3,2,1,0:T(8,128)} %param.8) | copy-start | bytes 3145732
Sparse Core Ops, SparseCore 0:
  9.1 88.7 all-gather.1
  180.1 220.0 all-reduce.2
where the time goes:
time: 410 us; the launch traced here: 409 us
  waiting for transfers between devices  309 us (75%)
  local copies, waits for them, and re-layouts  48.5 us (12%)
  other arithmetic  20.1 us (5%)
  matrix products  17.2 us (4%)
  between operations  14.1 us (3%)
    unnamed x3, waiting for transfers between devices  219 us
    all_gather x1, waiting for transfers between devices, on_device(): gathered = lax.all_gather(int_tiles, 'row', axis=1, tiled=True)  90.2 us
    gather x4, local copies, waits for them, and re-layouts, add_block(): int_flat[int_pick]  31.3 us
    scatter-add x4, other arithmetic, add_block(): return (partial_value.at[target_pick].add(products), None)  17.6 us
    dot_general x4, matrix products, add_block(): jnp.einsum('bxy,byz->bxz', amp_flat[amp_pick], int_flat[int_pick], precis...  17.2 us
  transfers between devices with their start and end apart: 2, of which 2 were waited for; matrix products, arithmetic and copies ran while one was open for 0% of the time, Pallas kernels for 0%

commit v1 on v0

v1 whole, which is shorter than its diff:
```python
import functools

import jax
import jax.numpy as jnp
from jax import lax
from jax.experimental import pallas as pl
from jax.experimental.pallas import tpu as pltpu
from jax.sharding import Mesh, PartitionSpec as P

SIZE = {"z": 4, "c": 2, "y": 4, "x": 4}


def shift(t, axis, s):
    n = SIZE[axis]
    return lax.ppermute(t, axis, [(i, (i + s) % n) for i in range(n)])


def split_kernel(a_ref, o_ref):
    a = a_ref[0]
    w = a.shape[1]
    hi = a.astype(jnp.bfloat16)
    lo = (a - hi.astype(jnp.float32)).astype(jnp.bfloat16)
    o_ref[0, :, :w] = hi
    o_ref[0, :, w : 2 * w] = lo
    o_ref[0, :, 2 * w :] = hi


def split_amp(a):
    n, w, _ = a.shape
    return pl.pallas_call(
        split_kernel,
        grid=(n,),
        in_specs=[pl.BlockSpec((1, w, w), lambda g: (g, 0, 0))],
        out_specs=pl.BlockSpec((1, w, 3 * w), lambda g: (g, 0, 0)),
        out_shape=jax.ShapeDtypeStruct((n, w, 3 * w), jnp.bfloat16),
        cost_estimate=pl.CostEstimate(flops=0, bytes_accessed=n * w * w * 10, transcendentals=0),
        name="split_amp",
    )(a)


def contract_kernel(meta_ref, a_ref, p_ref, r_ref, l_ref, f_ref, g_ref, o_ref, b_ref):
    step = pl.program_id(0)
    w = p_ref.shape[1]
    ka = lax.rem(meta_ref[128] + jnp.where(step == 1, 3, jnp.where(step == 2, 1, jnp.where(step == 3, 2, 0))), 4)

    def load(jx, b):
        hi = b.astype(jnp.bfloat16)
        lo = (b - hi.astype(jnp.float32)).astype(jnp.bfloat16)
        b_ref[jx, :w] = hi
        b_ref[jx, w : 2 * w] = hi
        b_ref[jx, 2 * w :] = lo

    for s, piece in enumerate((p_ref, r_ref, l_ref)):
        @pl.when(step == s)
        def _():
            for jx in range(4):
                load(jx, piece[jx])

    @pl.when(step == 3)
    def _():
        for jx in range(2):
            load(jx, f_ref[jx])
            load(jx + 2, g_ref[jx])

    o_ref[...] = jnp.zeros_like(o_ref)
    for i in range(4):
        for jx in range(4):
            @pl.when(meta_ref[ka * 16 + jx * 4 + i] != 0)
            def _():
                o_ref[i] += jnp.dot(a_ref[jx * 4 + i], b_ref[jx], preferred_element_type=jnp.float32)


def contract(meta, a3, pieces):
    w = a3.shape[1]
    full = lambda t: pl.BlockSpec(t.shape, lambda g, m: (0,) * t.ndim)
    order = lambda g, m: lax.rem(m[128] + jnp.where(g == 1, 3, jnp.where(g == 2, 1, jnp.where(g == 3, 2, 0))), 4)
    return pl.pallas_call(
        contract_kernel,
        grid_spec=pltpu.PrefetchScalarGridSpec(
            num_scalar_prefetch=1,
            grid=(4,),
            in_specs=[full(a3)] + [full(t) for t in pieces],
            out_specs=pl.BlockSpec((4, w, w), lambda g, m: (order(g, m), 0, 0)),
            scratch_shapes=[pltpu.VMEM((4, 3 * w, w), jnp.bfloat16)],
        ),
        out_shape=jax.ShapeDtypeStruct((16, w, w), jnp.float32),
        compiler_params=pltpu.CompilerParams(vmem_limit_bytes=50 * 1024 * 1024),
        cost_estimate=pl.CostEstimate(flops=16 * 6 * w**3, bytes_accessed=14 * 2**20, transcendentals=0),
        name="contract",
    )(meta, a3, *pieces)


def on_device(amp, integ, resid, triples):
    w = amp.shape[-1]
    z = lax.axis_index("z")
    c = lax.axis_index("c")
    x = lax.axis_index("x")

    def joined(mine, other):
        return jnp.where(c == 0, jnp.concatenate([mine, other]), jnp.concatenate([other, mine]))

    mine = lax.dynamic_index_in_dim(integ, c, 0, keepdims=False)
    other = shift(lax.dynamic_index_in_dim(integ, 1 - c, 0, keepdims=False), "c", 1)
    a_mine = lax.dynamic_index_in_dim(amp, c, 1, keepdims=False)
    a_other = shift(lax.dynamic_index_in_dim(amp, 1 - c, 1, keepdims=False), "c", 1)
    a_all = lax.all_gather(joined(a_mine, a_other), "x", axis=0, tiled=True)
    a3 = split_amp(a_all)

    tri = triples[0, 0]
    both = jnp.stack([tri, shift(tri, "c", 1)])
    lists = jnp.stack([both, shift(both, "x", 1), shift(both, "x", 2), shift(both, "x", 3)])
    amp_ids = lists[:, :, 0].reshape(-1)
    int_ids = lists[:, :, 1].reshape(-1)
    i = amp_ids // 32 - 4 * z
    j = amp_ids % 32
    k = int_ids % 32
    listed = (j % 2 == c) & ((k // 2) % 4 == x)
    slot = ((k % 2 * 4 + k // 8) * 4 + (j // 2) % 4) * 4 + i
    place = lax.broadcasted_iota(jnp.int32, (128, amp_ids.shape[0]), 0)
    mask = jnp.sum(((place == slot[None]) & listed[None]).astype(jnp.int32), axis=1)

    mine = mine.reshape(2, 2, w, w)
    other = other.reshape(2, 2, w, w)
    held = [lax.all_to_all(joined(mine[:, kp], other[:, kp]), "x", 0, 0, tiled=True) for kp in range(2)]
    right = [None, None]
    left = [None, None]
    sums = []
    for kp in range(2):
        right[kp] = shift(held[kp], "z", 1)
        left[kp] = shift(held[kp], "z", -1)
        if kp == 0:
            right[0], left[0], held[1] = lax.optimization_barrier((right[0], left[0], held[1]))
        far_a = shift(right[kp][:2], "z", 1)
        far_b = shift(left[kp][2:], "z", -1)
        meta = jnp.concatenate([mask.reshape(2, 64)[kp], jnp.zeros((64,), jnp.int32), z[None]])
        part = contract(meta, a3, (held[kp], right[kp], left[kp], far_a, far_b))
        sums.append(lax.psum_scatter(part, ("y", "c"), scatter_dimension=0, tiled=True))
    return resid + jnp.stack(sums, axis=1)


def solution(mesh):
    fine = Mesh(mesh.devices.reshape(4, 2, 4, 4), ("z", "c", "y", "x"))
    row, col = ("z", "c"), ("y", "x")
    return jax.shard_map(
        on_device,
        mesh=fine,
        in_specs=(P(row, col), P(col, row), P(row, col), P(row, col)),
        out_specs=P(row, col),
        check_vma=False,
    )
```

time: 410 us -> 202 us (0.49)
  waiting for transfers between devices: 309 us -> 88.7 us
  local copies, waits for them, and re-layouts: 48.5 us -> 6.67 us
  Pallas kernels: 0 us -> 32.4 us
  starting transfers between devices: 0.04 us -> 31.1 us
  blocking collectives: 0 us -> 22.5 us
  matrix products: 17.2 us -> 0 us
  other arithmetic: 20.1 us -> 3.84 us
    unnamed x3, waiting for transfers between devices: 219 us -> 0.05 us
    all_gather x1, waiting for transfers between devices: 90.2 us -> 1.16 us  [on_device(): a_all = lax.all_gather(joined(a_mine, a_other), 'x', axis=0, tiled=True)]
    ppermute x0 -> x14, waiting for transfers between devices: none -> 47.9 us  [shift(): return lax.ppermute(t, axis, [(i, (i + s) % n) for i in range(n)])]
    reduce_scatter x0 -> x2, waiting for transfers between devices: none -> 39.6 us  [on_device(): lax.psum_scatter(part, ('y', 'c'), scatter_dimension=0, tiled=True)]
    gather x8 -> x0, local copies, waits for them, and re-layouts: 39.2 us -> none  [the longest x4 31.3 us: add_block(): int_flat[int_pick]]
    pallas_call x0 -> x3, Pallas kernels: none -> 32.4 us  [the longest x2 21.8 us: contract(): pl.pallas_call(contract_kernel, grid_spec=pltpu.PrefetchScalarGridSpec(nu...]
    ppermute x0 -> x14, starting transfers between devices: none -> 27.5 us  [shift(): return lax.ppermute(t, axis, [(i, (i + s) % n) for i in range(n)])]
    all_to_all x0 -> x1, blocking collectives: none -> 22.5 us  [on_device(): lax.all_to_all(joined(mine[:, kp], other[:, kp]), 'x', 0, 0, tiled=True)]
  transfers between devices with their start and end apart: 2 -> 18, of which waited for: 2 -> 10; matrix products, arithmetic and copies ran while one was open for 0% -> 2% of each run, Pallas kernels for 0% -> 11%
where the time goes in v1:
time: 202 us; the launch traced here: 199 us
  waiting for transfers between devices  88.7 us (44%)
  Pallas kernels  32.4 us (16%)
  starting transfers between devices  31.1 us (15%)
  blocking collectives  22.5 us (11%)
  between operations  13.3 us (7%)
  local copies, waits for them, and re-layouts  6.67 us (3%)
  other arithmetic  3.84 us (2%)
    ppermute x14, waiting for transfers between devices, shift(): return lax.ppermute(t, axis, [(i, (i + s) % n) for i in range(n)])  47.9 us
    reduce_scatter x2, waiting for transfers between devices, on_device(): lax.psum_scatter(part, ('y', 'c'), scatter_dimension=0, tiled=True)  39.6 us
    ppermute x14, starting transfers between devices, shift(): return lax.ppermute(t, axis, [(i, (i + s) % n) for i in range(n)])  27.5 us
    all_to_all x1, blocking collectives, on_device(): lax.all_to_all(joined(mine[:, kp], other[:, kp]), 'x', 0, 0, tiled=True)  22.5 us
    pallas_call x2, Pallas kernels, contract(): pl.pallas_call(contract_kernel, grid_spec=pltpu.PrefetchScalarGridSpec(nu...  21.8 us
    pallas_call x1, Pallas kernels, split_amp(): pl.pallas_call(split_kernel, grid=(n,), in_specs=[pl.BlockSpec((1, w, w),...  10.6 us
  transfers between devices with their start and end apart: 18, of which 10 were waited for; matrix products, arithmetic and copies ran while one was open for 2% of the time, Pallas kernels for 11%

profile of v1, /device:TPU:1, one launch (start us, length us, event | category | flops | bytes accessed | tf_op | source)
XLA Modules:
  0.0 198.5 jit_solution(10774896549364699568)
XLA Ops:
  6.5 0.0 all-gather.2.cloned.1.call-start
  6.5 2.2 %dynamic-slice_bitcast_fusion.2 = (f32[2,256,256]{2,1,0:T(8,128)S(1)}, f32[2,256,256]{2,1,0:T(8,128)}) fusion(f32[2,2,256,256]{3,2,1,0:T(8,128)} %param.4, s32[]{:T(128)S(6)} %select_n.124, s32[]{:T(128)S(6)} %select_n.125), kind=kLoop, calls=%fused_computation.10 | loop fusion | bytes 2097160 | tf_op jit(solution)/shard_map/jit(dynamic_index_in_dim)/squeeze | solution.py:104
  8.8 1.4 collective-permute-start.4
  10.2 1.7 collective-permute-done.4
  11.9 1.1 maximum_select_fusion
  13.0 0.0 all-gather.2.cloned.1.call-update
  13.0 0.0 copy-done.1
  13.1 0.1 constant_dynamic-slice_fusion
  13.2 0.5 collective-permute-start.5
  13.7 0.1 slice_bitcast_fusion.1
  13.8 2.2 %collective-permute-done.5 = f32[4,256,256]{2,1,0:T(8,128)S(1)} collective-permute-done((f32[4,256,256]{2,1,0:T(8,128)S(1)}, f32[4,256,256]{2,1,0:T(8,128)S(1)}, u32[]{:S(2)}, u32[]{:S(2)}) %collective-permute-start.5) | collective-permute-done | bytes 1048608 | tf_op jit(solution)/shard_map/ppermute | solution.py:15
  15.9 0.1 slice_bitcast_fusion
  16.0 0.0 copy-start.3
  16.0 0.1 maximum_select_fusion.1
  16.1 22.5 %all_to_all.10.p_ref = f32[4,256,256]{2,1,0:T(8,128)S(1)} all-to-all(f32[4,256,256]{2,1,0:T(8,128)S(1)} %maximum_select_fusion.1), channel_id=1, replica_groups=mesh['z'=4,'c'=2,'y'=4,'x'=4] {'x'}, dimensions={0} | all-to-all | bytes 2097152 | tf_op jit(solution)/shard_map/all_to_all | solution.py:124
  38.7 2.0 %collective-permute-start.6 = (f32[4,256,256]{2,1,0:T(8,128)S(1)}, f32[4,256,256]{2,1,0:T(8,128)S(1)}, u32[]{:S(2)}, u32[]{:S(2)}) collective-permute-start(f32[4,256,256]{2,1,0:T(8,128)S(1)} %all_to_all.10.p_ref), channel_id=1, source_target_pairs={{0,32},{32,64},{64,96},{96,0},{1,33},{33,65},{65,97},{97,1},{2,34}... | collective-permute-start | bytes 3145736 | tf_op jit(solution)/shard_map/ppermute | solution.py:15
  40.7 2.8 %collective-permute-start.7 = (f32[4,256,256]{2,1,0:T(8,128)S(1)}, f32[4,256,256]{2,1,0:T(8,128)}, u32[]{:S(2)}, u32[]{:S(2)}) collective-permute-start(f32[4,256,256]{2,1,0:T(8,128)S(1)} %all_to_all.10.p_ref), channel_id=1, source_target_pairs={{0,96},{32,0},{64,32},{96,64},{1,97},{33,1},{65,33},{97,65},{2,98}... | collective-permute-start | bytes 3145736 | tf_op jit(solution)/shard_map/ppermute | solution.py:15
  43.5 1.1 maximum_select_fusion.2
  44.6 3.5 %all-to-all-start.1 = ((f32[4,256,256]{2,1,0:T(8,128)}), f32[4,256,256]{2,1,0:T(8,128)S(1)}, u32[]{:S(2)}, u32[]{:S(2)}) async-start(f32[4,256,256]{2,1,0:T(8,128)} %maximum_select_fusion.2), calls=%async_computation.1 | async-start | bytes 2097152 | tf_op jit(solution)/shard_map/all_to_all | solution.py:124
  48.1 0.0 reduce-scatter.3.cloned.1.call-start
  48.2 0.0 copy-done.3
  48.2 4.4 %collective-permute-start = (s32[3,32]{1,0:T(4,128)S(1)}, s32[3,32]{1,0:T(4,128)S(1)}, u32[]{:S(2)}, u32[]{:S(2)}) collective-permute-start(s32[3,32]{1,0:T(4,128)S(1)} %bitcast.50), channel_id=1, source_target_pairs={{0,16},{16,0},{1,17},{17,1},{2,18},{18,2},{3,19},{19,3},{4,20},{20... | collective-permute-start | bytes 1160 | tf_op jit(solution)/shard_map/ppermute | solution.py:15
  52.6 0.8 collective-permute-done
  53.4 1.7 collective-permute-start.1
  55.2 2.4 %collective-permute-start.2 = (s32[2,3,32]{2,0,1:T(2,128)S(1)}, s32[2,3,32]{2,0,1:T(2,128)S(1)}, u32[]{:S(2)}, u32[]{:S(2)}) collective-permute-start(s32[2,3,32]{2,0,1:T(2,128)S(1)} %get-tuple-element.22), channel_id=1, source_target_pairs={{0,2},{1,3},{2,0},{3,1},{4,6},{5,7},{6,4},{7,5},{8,10},{9,11},{10,... | collective-permute-start | bytes 2312 | tf_op jit(solution)/shard_map/ppermute | solution.py:15
  57.6 1.2 collective-permute-start.3
  58.7 11.2 %collective-permute-done.1 = s32[2,3,32]{2,0,1:T(2,128)S(1)} collective-permute-done((s32[2,3,32]{2,0,1:T(2,128)S(1)}, s32[2,3,32]{2,0,1:T(2,128)S(1)}, u32[]{:S(2)}, u32[]{:S(2)}) %collective-permute-start.1) | collective-permute-done | bytes 800 | tf_op jit(solution)/shard_map/ppermute | solution.py:15
  69.9 3.7 %collective-permute-done.2 = s32[2,3,32]{2,0,1:T(2,128)S(1)} collective-permute-done((s32[2,3,32]{2,0,1:T(2,128)S(1)}, s32[2,3,32]{2,0,1:T(2,128)S(1)}, u32[]{:S(2)}, u32[]{:S(2)}) %collective-permute-start.2) | collective-permute-done | bytes 800 | tf_op jit(solution)/shard_map/ppermute | solution.py:15
  73.6 0.0 collective-permute-done.3
  73.6 0.1 reshape_squeeze.6
  73.7 0.1 reshape_squeeze.7
  73.8 0.0 all-to-all-done.1.p_ref
  73.8 0.0 collective-permute-done.6.r_ref
  73.9 0.0 collective-permute-done.7.l_ref
  73.9 0.9 slice.45
  74.8 0.0 collective-permute-start.8
  74.8 1.9 slice.46
  76.6 2.7 %collective-permute-start.9 = (f32[2,256,256]{2,1,0:T(8,128)}, f32[2,256,256]{2,1,0:T(8,128)}, u32[]{:S(2)}, u32[]{:S(2)}) collective-permute-start(f32[2,256,256]{2,1,0:T(8,128)} %slice.46), channel_id=1, source_target_pairs={{0,96},{32,0},{64,32},{96,64},{1,97},{33,1},{65,33},{97,65},{2,98}... | collective-permute-start | bytes 1572872 | tf_op jit(solution)/shard_map/ppermute | solution.py:15
  79.3 0.1 convert_reduce_fusion
  79.4 0.1 fusion.9
  79.5 0.1 pad_add_fusion.8
  79.6 1.2 all-gather.2.cloned.1.call-done.a_ref
  80.8 10.6 %split_amp.1.a_ref = bf16[16,256,768]{2,1,0:T(8,128)(2,1)} custom-call(f32[16,256,256]{2,1,0:T(8,128)} %all-gather.2.cloned.1.call-done.a_ref), custom_call_target="tpu_custom_call" | custom-call | bytes 10485760 | tf_op jit(solution)/shard_map/split_amp/pallas_call | solution.py:30
  91.4 0.0 collective-permute-done.8.f_ref
  91.4 0.0 collective-permute-done.9.g_ref
  91.4 10.3 %contract.2 = f32[16,256,256]{2,1,0:T(8,128)} custom-call(s32[129]{0:T(256)S(1)} %get-tuple-element.23.meta_ref, bf16[16,256,768]{2,1,0:T(8,128)(2,1)} %split_amp.1.a_ref, f32[4,256,256]{2,1,0:T(8,128)S(1)} %all_to_all.10.p_ref, f32[4,256,256]{2,1,0:T(8,128)S(1)} %collective-permute-done.6.r_ref, f32[4,256,256]{2,1,0:T(8,128)} %collective-permute-done.7.l_ref, ...), custom_call_target="tpu_custom_call" | custom-call | flops 1610612736 | bytes 14680064 | tf_op jit(solution)/shard_map/contract/pallas_call | solution.py:77
  101.7 0.0 reduce-scatter.3.cloned.1.call-update
  101.7 0.0 reduce-scatter.5.cloned.1.call-start
  101.8 3.2 %collective-permute-start.10 = (f32[4,256,256]{2,1,0:T(8,128)S(1)}, f32[4,256,256]{2,1,0:T(8,128)S(1)}, u32[]{:S(2)}, u32[]{:S(2)}) collective-permute-start(f32[4,256,256]{2,1,0:T(8,128)S(1)} %all-to-all-done.1.p_ref), channel_id=1, source_target_pairs={{0,32},{32,64},{64,96},{96,0},{1,33},{33,65},{65,97},{97,1},{2,34}... | collective-permute-start | bytes 3145736 | tf_op jit(solution)/shard_map/ppermute | solution.py:15
  104.9 1.5 collective-permute-start.11
  106.5 19.8 %collective-permute-done.10.r_ref = f32[4,256,256]{2,1,0:T(8,128)S(1)} collective-permute-done((f32[4,256,256]{2,1,0:T(8,128)S(1)}, f32[4,256,256]{2,1,0:T(8,128)S(1)}, u32[]{:S(2)}, u32[]{:S(2)}) %collective-permute-start.10) | collective-permute-done | bytes 1048608 | tf_op jit(solution)/shard_map/ppermute | solution.py:15
  126.3 1.6 collective-permute-start.12
  127.8 0.0 collective-permute-done.11.l_ref
  127.9 2.2 %collective-permute-start.13 = (f32[2,256,256]{2,1,0:T(8,128)S(1)}, f32[2,256,256]{2,1,0:T(8,128)S(1)}, u32[]{:S(2)}, u32[]{:S(2)}) collective-permute-start(f32[2,256,256]{2,1,0:T(8,128)S(1)} %slice.55), channel_id=1, source_target_pairs={{0,96},{32,0},{64,32},{96,64},{1,97},{33,1},{65,33},{97,65},{2,98}... | collective-permute-start | bytes 1572872 | tf_op jit(solution)/shard_map/ppermute | solution.py:15
  130.0 8.1 %collective-permute-done.12.f_ref = f32[2,256,256]{2,1,0:T(8,128)S(1)} collective-permute-done((f32[2,256,256]{2,1,0:T(8,128)S(1)}, f32[2,256,256]{2,1,0:T(8,128)S(1)}, u32[]{:S(2)}, u32[]{:S(2)}) %collective-permute-start.12) | collective-permute-done | bytes 524320 | tf_op jit(solution)/shard_map/ppermute | solution.py:15
  138.1 0.4 collective-permute-done.13.g_ref
  138.5 0.0 copy-done
  138.5 11.5 %contract.3 = f32[16,256,256]{2,1,0:T(8,128)} custom-call(s32[129]{0:T(256)S(1)} %get-tuple-element.24.meta_ref, bf16[16,256,768]{2,1,0:T(8,128)(2,1)} %split_amp.1.a_ref, f32[4,256,256]{2,1,0:T(8,128)S(1)} %all-to-all-done.1.p_ref, f32[4,256,256]{2,1,0:T(8,128)S(1)} %collective-permute-done.10.r_ref, f32[4,256,256]{2,1,0:T(8,128)} %copy-done, ...), custom_call_target="tpu_custom_call" | custom-call | flops 1610612736 | bytes 14680064 | tf_op jit(solution)/shard_map/contract/pallas_call | solution.py:77
  150.0 0.0 reduce-scatter.5.cloned.1.call-update
  150.0 0.0 reduce-scatter.3.cloned.1.call-done
  150.0 39.6 %reduce-scatter.5.cloned.1.call-done = f32[2,256,256]{2,1,0:T(8,128)} async-done(((f32[16,256,256]{2,1,0:T(8,128)}), f32[2,256,256]{2,1,0:T(8,128)}) %reduce-scatter.5.cloned.1.call-update) | async-done | bytes 524304 | tf_op jit(solution)/shard_map/reduce_scatter | solution.py:137
  189.6 0.0 copy-done.2
  189.6 1.3 maximum_add_fusion
  191.0 1.0 copy.28
  (12 shorter events, 0.2 us)
Async XLA Ops:
  6.5 6.5 %copy-start.1 = (f32[2,4,256,256]{3,2,1,0:T(8,128)S(1)}, f32[2,4,256,256]{3,2,1,0:T(8,128)}, u32[]{:S(2)}) copy-start(f32[2,4,256,256]{3,2,1,0:T(8,128)} %param.5) | copy-start | bytes 6291460
  6.5 74.2 %all-gather.2.cloned.1.call-start = ((), (), s32[]{:S(2)}) async-start(), calls=%async_computation.4 | async-start | bytes 5242880 | tf_op jit(solution)/shard_map/all_gather | solution.py:106
  8.8 3.2 %collective-permute-start.4 = (f32[2,256,256]{2,1,0:T(8,128)}, f32[2,256,256]{2,1,0:T(8,128)S(1)}, u32[]{:S(2)}, u32[]{:S(2)}) collective-permute-start(f32[2,256,256]{2,1,0:T(8,128)} %get-tuple-element.18), channel_id=1, source_target_pairs={{0,16},{16,0},{1,17},{17,1},{2,18},{18,2},{3,19},{19,3},{4,20},{20... | collective-permute-start | bytes 1572872 | tf_op jit(solution)/shard_map/ppermute | solution.py:15
  13.2 2.7 %collective-permute-start.5 = (f32[4,256,256]{2,1,0:T(8,128)S(1)}, f32[4,256,256]{2,1,0:T(8,128)S(1)}, u32[]{:S(2)}, u32[]{:S(2)}) collective-permute-start(f32[4,256,256]{2,1,0:T(8,128)S(1)} %get-tuple-element.12), channel_id=1, source_target_pairs={{0,16},{16,0},{1,17},{17,1},{2,18},{18,2},{3,19},{19,3},{4,20},{20... | collective-permute-start | bytes 3145736 | tf_op jit(solution)/shard_map/ppermute | solution.py:15
  16.0 32.2 %copy-start.3 = (s32[1,1,3,32]{3,1,2,0:T(1,128)S(1)}, s32[1,1,3,32]{3,1,2,0:T(1,128)}, u32[]{:S(2)}) copy-start(s32[1,1,3,32]{3,1,2,0:T(1,128)} %param.7) | copy-start | bytes 1156
  38.7 35.2 %collective-permute-start.6 = (f32[4,256,256]{2,1,0:T(8,128)S(1)}, f32[4,256,256]{2,1,0:T(8,128)S(1)}, u32[]{:S(2)}, u32[]{:S(2)}) collective-permute-start(f32[4,256,256]{2,1,0:T(8,128)S(1)} %all_to_all.10.p_ref), channel_id=1, source_target_pairs={{0,32},{32,64},{64,96},{96,0},{1,33},{33,65},{65,97},{97,1},{2,34}... | collective-permute-start | bytes 3145736 | tf_op jit(solution)/shard_map/ppermute | solution.py:15
  40.7 33.2 %collective-permute-start.7 = (f32[4,256,256]{2,1,0:T(8,128)S(1)}, f32[4,256,256]{2,1,0:T(8,128)}, u32[]{:S(2)}, u32[]{:S(2)}) collective-permute-start(f32[4,256,256]{2,1,0:T(8,128)S(1)} %all_to_all.10.p_ref), channel_id=1, source_target_pairs={{0,96},{32,0},{64,32},{96,64},{1,97},{33,1},{65,33},{97,65},{2,98}... | collective-permute-start | bytes 3145736 | tf_op jit(solution)/shard_map/ppermute | solution.py:15
  44.6 29.2 %all-to-all-start.1 = ((f32[4,256,256]{2,1,0:T(8,128)}), f32[4,256,256]{2,1,0:T(8,128)S(1)}, u32[]{:S(2)}, u32[]{:S(2)}) async-start(f32[4,256,256]{2,1,0:T(8,128)} %maximum_select_fusion.2), calls=%async_computation.1 | async-start | bytes 2097152 | tf_op jit(solution)/shard_map/all_to_all | solution.py:124
  48.1 101.9 %reduce-scatter.3.cloned.1.call-start = ((), (), s32[]{:S(2)}) async-start(), calls=%async_computation.5 | async-start | bytes 4718592 | tf_op jit(solution)/shard_map/reduce_scatter | solution.py:137
  48.2 5.2 %collective-permute-start = (s32[3,32]{1,0:T(4,128)S(1)}, s32[3,32]{1,0:T(4,128)S(1)}, u32[]{:S(2)}, u32[]{:S(2)}) collective-permute-start(s32[3,32]{1,0:T(4,128)S(1)} %bitcast.50), channel_id=1, source_target_pairs={{0,16},{16,0},{1,17},{17,1},{2,18},{18,2},{3,19},{19,3},{4,20},{20... | collective-permute-start | bytes 1160 | tf_op jit(solution)/shard_map/ppermute | solution.py:15
  53.4 16.5 %collective-permute-start.1 = (s32[2,3,32]{2,0,1:T(2,128)S(1)}, s32[2,3,32]{2,0,1:T(2,128)S(1)}, u32[]{:S(2)}, u32[]{:S(2)}) collective-permute-start(s32[2,3,32]{2,0,1:T(2,128)S(1)} %get-tuple-element.22), channel_id=1, source_target_pairs={{0,1},{1,2},{2,3},{3,0},{4,5},{5,6},{6,7},{7,4},{8,9},{9,10},{10,1... | collective-permute-start | bytes 2312 | tf_op jit(solution)/shard_map/ppermute | solution.py:15
  55.2 18.5 %collective-permute-start.2 = (s32[2,3,32]{2,0,1:T(2,128)S(1)}, s32[2,3,32]{2,0,1:T(2,128)S(1)}, u32[]{:S(2)}, u32[]{:S(2)}) collective-permute-start(s32[2,3,32]{2,0,1:T(2,128)S(1)} %get-tuple-element.22), channel_id=1, source_target_pairs={{0,2},{1,3},{2,0},{3,1},{4,6},{5,7},{6,4},{7,5},{8,10},{9,11},{10,... | collective-permute-start | bytes 2312 | tf_op jit(solution)/shard_map/ppermute | solution.py:15
  57.6 16.1 %collective-permute-start.3 = (s32[2,3,32]{2,0,1:T(2,128)S(1)}, s32[2,3,32]{2,0,1:T(2,128)S(1)}, u32[]{:S(2)}, u32[]{:S(2)}) collective-permute-start(s32[2,3,32]{2,0,1:T(2,128)S(1)} %get-tuple-element.22), channel_id=1, source_target_pairs={{0,3},{1,0},{2,1},{3,2},{4,7},{5,4},{6,5},{7,6},{8,11},{9,8},{10,9... | collective-permute-start | bytes 2312 | tf_op jit(solution)/shard_map/ppermute | solution.py:15
  74.8 16.6 %collective-permute-start.8 = (f32[2,256,256]{2,1,0:T(8,128)}, f32[2,256,256]{2,1,0:T(8,128)}, u32[]{:S(2)}, u32[]{:S(2)}) collective-permute-start(f32[2,256,256]{2,1,0:T(8,128)} %slice.45), channel_id=1, source_target_pairs={{0,32},{32,64},{64,96},{96,0},{1,33},{33,65},{65,97},{97,1},{2,34}... | collective-permute-start | bytes 1572872 | tf_op jit(solution)/shard_map/ppermute | solution.py:15
  76.6 14.7 %collective-permute-start.9 = (f32[2,256,256]{2,1,0:T(8,128)}, f32[2,256,256]{2,1,0:T(8,128)}, u32[]{:S(2)}, u32[]{:S(2)}) collective-permute-start(f32[2,256,256]{2,1,0:T(8,128)} %slice.46), channel_id=1, source_target_pairs={{0,96},{32,0},{64,32},{96,64},{1,97},{33,1},{65,33},{97,65},{2,98}... | collective-permute-start | bytes 1572872 | tf_op jit(solution)/shard_map/ppermute | solution.py:15
  101.7 87.9 %reduce-scatter.5.cloned.1.call-start = ((), (), s32[]{:S(2)}) async-start(), calls=%async_computation.6 | async-start | bytes 4718592 | tf_op jit(solution)/shard_map/reduce_scatter | solution.py:137
  101.8 24.5 %collective-permute-start.10 = (f32[4,256,256]{2,1,0:T(8,128)S(1)}, f32[4,256,256]{2,1,0:T(8,128)S(1)}, u32[]{:S(2)}, u32[]{:S(2)}) collective-permute-start(f32[4,256,256]{2,1,0:T(8,128)S(1)} %all-to-all-done.1.p_ref), channel_id=1, source_target_pairs={{0,32},{32,64},{64,96},{96,0},{1,33},{33,65},{65,97},{97,1},{2,34}... | collective-permute-start | bytes 3145736 | tf_op jit(solution)/shard_map/ppermute | solution.py:15
  104.9 22.9 %collective-permute-start.11 = (f32[4,256,256]{2,1,0:T(8,128)S(1)}, f32[4,256,256]{2,1,0:T(8,128)S(1)}, u32[]{:S(2)}, u32[]{:S(2)}) collective-permute-start(f32[4,256,256]{2,1,0:T(8,128)S(1)} %all-to-all-done.1.p_ref), channel_id=1, source_target_pairs={{0,96},{32,0},{64,32},{96,64},{1,97},{33,1},{65,33},{97,65},{2,98}... | collective-permute-start | bytes 3145736 | tf_op jit(solution)/shard_map/ppermute | solution.py:15
  126.3 11.9 %collective-permute-start.12 = (f32[2,256,256]{2,1,0:T(8,128)S(1)}, f32[2,256,256]{2,1,0:T(8,128)S(1)}, u32[]{:S(2)}, u32[]{:S(2)}) collective-permute-start(f32[2,256,256]{2,1,0:T(8,128)S(1)} %slice.54), channel_id=1, source_target_pairs={{0,32},{32,64},{64,96},{96,0},{1,33},{33,65},{65,97},{97,1},{2,34}... | collective-permute-start | bytes 1572872 | tf_op jit(solution)/shard_map/ppermute | solution.py:15
  127.9 10.7 %copy-start = (f32[4,256,256]{2,1,0:T(8,128)}, f32[4,256,256]{2,1,0:T(8,128)S(1)}, u32[]{:S(2)}) copy-start(f32[4,256,256]{2,1,0:T(8,128)S(1)} %collective-permute-done.11.l_ref) | copy-start | bytes 3145732
  127.9 10.6 %collective-permute-start.13 = (f32[2,256,256]{2,1,0:T(8,128)S(1)}, f32[2,256,256]{2,1,0:T(8,128)S(1)}, u32[]{:S(2)}, u32[]{:S(2)}) collective-permute-start(f32[2,256,256]{2,1,0:T(8,128)S(1)} %slice.55), channel_id=1, source_target_pairs={{0,96},{32,0},{64,32},{96,64},{1,97},{33,1},{65,33},{97,65},{2,98}... | collective-permute-start | bytes 1572872 | tf_op jit(solution)/shard_map/ppermute | solution.py:15
  150.0 39.7 %copy-start.2 = (f32[2,2,256,256]{3,2,1,0:T(8,128)S(1)}, f32[2,2,256,256]{3,2,1,0:T(8,128)}, u32[]{:S(2)}) copy-start(f32[2,2,256,256]{3,2,1,0:T(8,128)} %param.6) | copy-start | bytes 3145732
Sparse Core Ops, SparseCore 0:
  13.2 67.5 all-gather.1
  101.8 38.6 reduce-scatter.2
  150.1 39.4 reduce-scatter.4

commit v2 on v0

v2 whole, which is shorter than its diff:
```python
import jax
import jax.numpy as jnp
from jax import lax
from jax.experimental import pallas as pl
from jax.experimental.pallas import tpu as pltpu
from jax.sharding import Mesh, PartitionSpec as P

NAMES = ("z", "c", "y", "x")
MIB = 1024 * 1024


def device(z, c, y, x):
    return ((z * 2 + c) * 4 + y) * 4 + x


EVERY = [(z, c, y, x) for z in range(4) for c in range(2) for y in range(4) for x in range(4)]


def move(t, target, keep=lambda *d: True):
    return lax.ppermute(t, NAMES, [(device(*d), device(*target(*d))) for d in EVERY if keep(*d)])


def along_z(t, s):
    return move(t, lambda z, c, y, x: ((z + s) % 4, c, y, x))


def over_core(t):
    return move(t, lambda z, c, y, x: (z, 1 - c, y, x))


def exchange(t, s):
    return move(t, lambda z, c, y, x: (z, c, y, (x + s) % 4) if c == 0 else (z, c, (y + s) % 4, x))


def reduce_to(t, s):
    return move(t, lambda z, c, y, x: (z, c, (y + s) % 4, x) if c == 0 else (z, c, y, (x + s) % 4))


def halves(a):
    hi = a.astype(jnp.bfloat16)
    return hi, (a - hi.astype(jnp.float32)).astype(jnp.bfloat16)


def split_kernel(a_ref, r_ref, l_ref, fa_ref, fb_ref, o_ref):
    w = a_ref.shape[-1]

    def put(s, a):
        hi, lo = halves(a)
        o_ref[s, 0, :, :w] = hi
        o_ref[s, 0, :, w : 2 * w] = lo
        o_ref[s, 0, :, 2 * w :] = hi

    put(0, a_ref[0])
    put(1, r_ref[0])
    put(3, l_ref[0])

    @pl.when(pl.program_id(0) < 2)
    def _():
        put(2, fa_ref[0])

    @pl.when(pl.program_id(0) >= 2)
    def _():
        put(2, fb_ref[0])


def split_amp(a, r, l, fa, fb):
    w = a.shape[-1]
    tile = lambda f: pl.BlockSpec((1, w, w), lambda g: (f(g), 0, 0))
    same = tile(lambda g: g)
    return pl.pallas_call(
        split_kernel,
        grid=(4,),
        in_specs=[same, same, same, tile(lambda g: jnp.minimum(g, 1)), tile(lambda g: jnp.maximum(g - 2, 0))],
        out_specs=pl.BlockSpec((4, 1, w, 3 * w), lambda g: (0, g, 0, 0)),
        out_shape=jax.ShapeDtypeStruct((4, 4, w, 3 * w), jnp.bfloat16),
        compiler_params=pltpu.CompilerParams(vmem_limit_bytes=12 * MIB),
        cost_estimate=pl.CostEstimate(flops=0, bytes_accessed=10 * MIB, transcendentals=0),
        name="split_amp",
    )(a, r, l, fa, fb)


def source_of(step, z):
    return lax.rem(z + jnp.where(step == 1, 3, jnp.where(step == 2, 1, jnp.where(step == 3, 2, 0))), 4)


def make_contract_kernel(kp):
    def kernel(meta_ref, a_ref, own, own_r, own_l, own_fa, own_fb, rest, rest_r, rest_l, rest_fa, rest_fb, *outs):
        outs, (b_ref, acc_ref) = outs[:4], outs[4:]
        step = pl.program_id(0)
        w = b_ref.shape[2]
        h = w // 2
        ka = source_of(step, meta_ref[64])

        def load(s, b, at=0):
            n = b.shape[0]
            hi, lo = halves(b)
            b_ref[s, at : at + n] = hi
            b_ref[s, w + at : w + at + n] = hi
            b_ref[s, 2 * w + at : 2 * w + at + n] = lo

        for at, (mine, others) in enumerate(((own, rest), (own_r, rest_r), (own_l, rest_l))):
            @pl.when(step == at)
            def _():
                load(0, mine[kp])
                for s in range(3):
                    load(s + 1, others[s])

        @pl.when(step == 3)
        def _():
            for part, (mine, others) in enumerate(((own_fa, rest_fa), (own_fb, rest_fb))):
                load(0, mine[3, kp * h : kp * h + h], part * h)
                for s in range(3):
                    load(s + 1, others[s], part * h)

        acc_ref[...] = jnp.zeros_like(acc_ref)
        for i in range(4):
            for s in range(4):
                @pl.when(meta_ref[ka * 16 + s * 4 + i] != 0)
                def _():
                    acc_ref[i] += jnp.dot(a_ref[s, i], b_ref[s], preferred_element_type=jnp.float32)
        away = lax.rem(ka + 4 - meta_ref[65], 4)
        for s in range(4):
            @pl.when(away == s)
            def _():
                outs[s][...] = acc_ref[...]

    return kernel


def contract(kp, meta, a3, own, rest):
    w = a3.shape[2]
    full = lambda t: pl.BlockSpec(t.shape, lambda g, m: (0,) * t.ndim)
    out = jax.ShapeDtypeStruct((4, w, w), jnp.float32)
    return pl.pallas_call(
        make_contract_kernel(kp),
        grid_spec=pltpu.PrefetchScalarGridSpec(
            num_scalar_prefetch=1,
            grid=(4,),
            in_specs=[full(t) for t in (a3,) + own + rest],
            out_specs=[full(out)] * 4,
            scratch_shapes=[pltpu.VMEM((4, 3 * w, w), jnp.bfloat16), pltpu.VMEM((4, w, w), jnp.float32)],
        ),
        out_shape=[out] * 4,
        compiler_params=pltpu.CompilerParams(vmem_limit_bytes=40 * MIB),
        cost_estimate=pl.CostEstimate(flops=16 * 6 * w**3, bytes_accessed=14 * MIB, transcendentals=0),
        name="contract",
    )(meta, a3, *own, *rest)


def on_device(amp, integ, resid, triples):
    w = amp.shape[-1]
    h = w // 2
    z, c, y, x = (lax.axis_index(n) for n in NAMES)
    upos = jnp.where(c == 0, x, y)
    vpos = jnp.where(c == 0, y, x)

    def joined(mine, other):
        return jnp.where(c == 0, jnp.concatenate([mine, other]), jnp.concatenate([other, mine]))

    mine = lax.dynamic_index_in_dim(integ, c, 0, keepdims=False)
    other = over_core(lax.dynamic_index_in_dim(integ, 1 - c, 0, keepdims=False))
    pairs = joined(mine.reshape(2, 2, w, w), other.reshape(2, 2, w, w))
    tiles = [lax.dynamic_index_in_dim(pairs, lax.rem(upos + s, 4), 0, keepdims=False) for s in range(4)]
    own = tiles[0]
    own_r, own_l = along_z(own, 1), along_z(own, -1)
    came = [exchange(tiles[s], s) for s in (1, 2, 3)]
    rest = [jnp.stack([t[kp] for t in came]) for kp in range(2)]

    a_mine = lax.dynamic_index_in_dim(amp, c, 1, keepdims=False)
    a_other = over_core(lax.dynamic_index_in_dim(amp, 1 - c, 1, keepdims=False))
    a0 = joined(a_mine, a_other)
    a0, tri, rest[0], rest[1] = lax.optimization_barrier((a0, triples[0, 0], rest[0], rest[1]))
    a_r, a_l = exchange(a0, 1), exchange(a0, -1)
    a3 = split_amp(a0, a_r, a_l, exchange(a_r[:2], 1), exchange(a_l[2:], -1))

    two_r = along_z(jnp.concatenate([rest[0], own_r[:, :h].reshape(1, w, w)]), 1)
    two_l = along_z(jnp.concatenate([rest[0], own_l[:, h:].reshape(1, w, w)]), -1)
    two_r, two_l, rest[1] = lax.optimization_barrier((two_r, two_l, rest[1]))
    far0 = along_z(two_r[:3, :h], 1), along_z(two_l[:3, h:], -1)
    rest1_r, rest1_l = along_z(rest[1], 1), along_z(rest[1], -1)
    far1 = along_z(rest1_r[:, :h], 1), along_z(rest1_l[:, h:], -1)

    both = jnp.stack([tri, over_core(tri)])
    lists = jnp.stack([both, exchange(both, 1), exchange(both, 2), exchange(both, 3)])
    amp_ids = lists[:, :, 0].reshape(-1)
    int_ids = lists[:, :, 1].reshape(-1)
    i = amp_ids // 32 - 4 * z
    j = amp_ids % 32
    k = int_ids % 32
    listed = (j % 2 == c) & ((k // 2) % 4 == upos)
    s = (upos - jnp.where(c == 0, (j // 2) % 4, j // 8)) % 4
    slot = ((k % 2 * 4 + k // 8) * 4 + s) * 4 + i
    place = lax.broadcasted_iota(jnp.int32, (128, amp_ids.shape[0]), 0)
    mask = jnp.sum(((place == slot[None]) & listed[None]).astype(jnp.int32), axis=1)
    where = jnp.stack([z, vpos])

    outs = []
    pieces = ((rest[0], two_r, two_l) + far0, (rest[1], rest1_r, rest1_l) + far1)
    for kp in range(2):
        meta = jnp.concatenate([mask[64 * kp : 64 * kp + 64], where])
        parts = contract(kp, meta, a3, (own, own_r, own_l, two_r, two_l), pieces[kp])
        total = parts[0]
        for s in (1, 2, 3):
            total = total + reduce_to(parts[s], s)
        lower, upper = total[:2], total[2:]
        swapped = move(
            jnp.where(c == 0, upper, lower), lambda z, c, y, x: (z, 1, y, x) if c == 0 else (z, 0, x, y)
        )
        turned = move(upper, lambda z, c, y, x: (z, 1, x, y), lambda z, c, y, x: c == 1)
        outs.append(resid[:, kp] + swapped + jnp.where(c == 0, lower, turned))
    return jnp.stack(outs, axis=1)


def solution(mesh):
    fine = Mesh(mesh.devices.reshape(4, 2, 4, 4), NAMES)
    row, col = ("z", "c"), ("y", "x")
    return jax.shard_map(
        on_device,
        mesh=fine,
        in_specs=(P(row, col), P(col, row), P(row, col), P(row, col)),
        out_specs=P(row, col),
        check_vma=False,
    )
```

time: 410 us -> 186 us (0.45)
  the two profiles are of different devices: /device:TPU:1 before, /device:TPU:3 now
where the time goes in v2:
time: 186 us; the launch traced here: 187 us
  starting transfers between devices  85.1 us (46%)
  waiting for transfers between devices  61.7 us (33%)
  Pallas kernels  21.1 us (11%)
  local copies, waits for them, and re-layouts  11.8 us (6%)
  other arithmetic  6.48 us (3%)
    ppermute x33, starting transfers between devices, move(): lax.ppermute(t, NAMES, [(device(*d), device(*target(*d))) for d in EVERY...  85.1 us
    ppermute x33, waiting for transfers between devices, move(): lax.ppermute(t, NAMES, [(device(*d), device(*target(*d))) for d in EVERY...  61.7 us
    pallas_call x2, Pallas kernels, contract(): pl.pallas_call(make_contract_kernel(kp), grid_spec=pltpu.PrefetchScalarGr...  17.8 us
    unnamed x19, local copies, waits for them, and re-layouts  4.23 us
  transfers between devices with their start and end apart: 33, of which 13 were waited for; matrix products, arithmetic and copies ran while one was open for 5% of the time, Pallas kernels for 11%

profile of v2, /device:TPU:3, one launch (start us, length us, event | category | flops | bytes accessed | tf_op | source)
XLA Modules:
  0.0 186.5 jit_solution(5650739628085054236)
XLA Ops:
  0.0 2.8 %constant_dynamic-slice_fusion = (f32[1,4,256,256]{3,2,1,0:T(8,128)S(1)}, f32[4,256,256]{2,1,0:T(8,128)}) fusion(f32[2,4,256,256]{3,2,1,0:T(8,128)} %param.5, s32[]{:T(128)S(6)} %select_n.181, s32[]{:T(128)S(6)} %select_n.182), kind=kLoop, calls=%fused_computation.42 | loop fusion | bytes 4194312 | tf_op jit(solution)/shard_map/jit(dynamic_index_in_dim)/dynamic_slice | solution.py:160
  2.8 0.7 collective-permute-start.1
  3.5 0.9 dynamic-slice_bitcast_fusion.6
  4.4 1.6 collective-permute-done.1
  6.0 0.2 maximum_select_fusion
  6.2 0.1 dynamic-slice_bitcast_fusion.1
  6.4 1.4 collective-permute-start.2
  7.7 2.6 %collective-permute-start.3 = (f32[2,256,256]{2,1,0:T(8,128)S(1)}, f32[2,256,256]{2,1,0:T(8,128)S(1)}, u32[]{:S(2)}, u32[]{:S(2)}) collective-permute-start(f32[2,256,256]{2,1,0:T(8,128)S(1)} %get-tuple-element.39), channel_id=1, source_target_pairs={{0,2},{1,3},{2,0},{3,1},{4,6},{5,7},{6,4},{7,5},{8,10},{9,11},{10,... | collective-permute-start | bytes 1572872 | tf_op jit(solution)/shard_map/ppermute | solution.py:20
  10.4 1.1 collective-permute-start.4
  11.4 2.3 %maximum_select_fusion.1.a_ref = f32[4,256,256]{2,1,0:T(8,128)} fusion(f32[2,256,256]{2,1,0:T(8,128)} %collective-permute-done, f32[2,256,256]{2,1,0:T(8,128)S(1)} %get-tuple-element.49, pred[]{:T(512)S(6)} %eq.45), kind=kLoop, calls=%fused_computation.3 | loop fusion | flops 786432 | bytes 2097153 | tf_op jit(solution)/shard_map/jit(_where)/select_n | solution.py:158
  13.7 1.6 collective-permute-start.13
  15.4 2.1 %collective-permute-start.14 = (f32[2,256,256]{2,1,0:T(8,128)S(1)}, f32[2,256,256]{2,1,0:T(8,128)S(1)}, u32[]{:S(2)}, u32[]{:S(2)}) collective-permute-start(f32[2,256,256]{2,1,0:T(8,128)S(1)} %get-tuple-element.37.own), channel_id=1, source_target_pairs={{0,96},{1,97},{2,98},{3,99},{4,100},{5,101},{6,102},{7,103},{8,104... | collective-permute-start | bytes 1572872 | tf_op jit(solution)/shard_map/ppermute | solution.py:20
  17.5 5.0 %collective-permute-done.3 = f32[2,256,256]{2,1,0:T(8,128)S(1)} collective-permute-done((f32[2,256,256]{2,1,0:T(8,128)S(1)}, f32[2,256,256]{2,1,0:T(8,128)S(1)}, u32[]{:S(2)}, u32[]{:S(2)}) %collective-permute-start.3) | collective-permute-done | bytes 524320 | tf_op jit(solution)/shard_map/ppermute | solution.py:20
  22.6 1.0 pad_maximum_fusion.3
  23.6 1.2 collective-permute-start.9
  24.8 1.5 collective-permute-start.10
  26.3 3.3 %collective-permute-done.13.own_r = f32[2,256,256]{2,1,0:T(8,128)S(1)} collective-permute-done((f32[2,256,256]{2,1,0:T(8,128)S(1)}, f32[2,256,256]{2,1,0:T(8,128)S(1)}, u32[]{:S(2)}, u32[]{:S(2)}) %collective-permute-start.13) | collective-permute-done | bytes 524320 | tf_op jit(solution)/shard_map/ppermute | solution.py:20
  29.7 0.7 copy-done.1
  30.5 0.8 copy-done.3
  31.2 1.5 pad_maximum_fusion
  32.8 2.7 %collective-permute-start.16 = (f32[4,256,256]{2,1,0:T(8,128)}, f32[4,256,256]{2,1,0:T(8,128)S(1)}, u32[]{:S(2)}, u32[]{:S(2)}) collective-permute-start(f32[4,256,256]{2,1,0:T(8,128)} %get-tuple-element.51), channel_id=1, source_target_pairs={{0,96},{1,97},{2,98},{3,99},{4,100},{5,101},{6,102},{7,103},{8,104... | collective-permute-start | bytes 3145736 | tf_op jit(solution)/shard_map/ppermute | solution.py:20
  35.4 1.3 collective-permute-start.5
  36.7 0.8 collective-permute-done.5
  37.5 0.4 collective-permute-start.6
  37.9 3.6 %collective-permute-done.6 = s32[2,3,32]{2,1,0:T(4,128)S(1)} collective-permute-done((s32[2,3,32]{2,1,0:T(4,128)S(1)}, s32[2,3,32]{2,1,0:T(4,128)S(1)}, u32[]{:S(2)}, u32[]{:S(2)}) %collective-permute-start.6) | collective-permute-done | bytes 800 | tf_op jit(solution)/shard_map/ppermute | solution.py:20
  41.5 4.0 %collective-permute-done.7 = s32[2,3,32]{2,1,0:T(4,128)S(1)} collective-permute-done((s32[2,3,32]{2,1,0:T(4,128)S(1)}, s32[2,3,32]{2,1,0:T(4,128)S(1)}, u32[]{:S(2)}, u32[]{:S(2)}) %collective-permute-start.7) | collective-permute-done | bytes 800 | tf_op jit(solution)/shard_map/ppermute | solution.py:20
  45.5 2.7 %collective-permute-done.8 = s32[2,3,32]{2,1,0:T(4,128)S(1)} collective-permute-done((s32[2,3,32]{2,1,0:T(4,128)S(1)}, s32[2,3,32]{2,1,0:T(4,128)S(1)}, u32[]{:S(2)}, u32[]{:S(2)}) %collective-permute-start.8) | collective-permute-done | bytes 800 | tf_op jit(solution)/shard_map/ppermute | solution.py:20
  48.3 0.1 reshape_squeeze.6
  48.3 0.1 reshape_squeeze.7
  48.4 1.2 slice.102
  49.7 1.1 slice.103
  50.8 2.7 %collective-permute-start.12 = (f32[2,256,256]{2,1,0:T(8,128)S(1)}, f32[2,256,256]{2,1,0:T(8,128)S(1)}, u32[]{:S(2)}, u32[]{:S(2)}) collective-permute-start(f32[2,256,256]{2,1,0:T(8,128)S(1)} %slice.103), channel_id=1, source_target_pairs={{0,3},{1,0},{2,1},{3,2},{4,7},{5,4},{6,5},{7,6},{8,11},{9,8},{10,9... | collective-permute-start | bytes 1572872 | tf_op jit(solution)/shard_map/ppermute | solution.py:20
  53.6 4.6 %collective-permute-done.15.own_fa.rest_r = f32[4,256,256]{2,1,0:T(8,128)S(1)} collective-permute-done((f32[4,256,256]{2,1,0:T(8,128)}, f32[4,256,256]{2,1,0:T(8,128)S(1)}, u32[]{:S(2)}, u32[]{:S(2)}) %collective-permute-start.15) | collective-permute-done | bytes 1048608 | tf_op jit(solution)/shard_map/ppermute | solution.py:20
  58.2 0.1 collective-permute-start.17
  58.3 2.7 %collective-permute-start.18 = (f32[3,128,256]{2,1,0:T(8,128)S(1)}, f32[3,128,256]{2,1,0:T(8,128)S(1)}, u32[]{:S(2)}, u32[]{:S(2)}) collective-permute-start(f32[3,128,256]{2,1,0:T(8,128)S(1)} %slice.87), channel_id=1, source_target_pairs={{0,96},{1,97},{2,98},{3,99},{4,100},{5,101},{6,102},{7,103},{8,104... | collective-permute-start | bytes 1179656 | tf_op jit(solution)/shard_map/ppermute | solution.py:20
  61.0 0.1 convert_reduce_fusion
  61.1 0.1 collective-permute-start.24
  61.2 2.7 %collective-permute-start.25 = (f32[3,256,256]{2,1,0:T(8,128)S(1)}, f32[3,256,256]{2,1,0:T(8,128)S(1)}, u32[]{:S(2)}, u32[]{:S(2)}) collective-permute-start(f32[3,256,256]{2,1,0:T(8,128)S(1)} %copy-done.5), channel_id=1, source_target_pairs={{0,96},{1,97},{2,98},{3,99},{4,100},{5,101},{6,102},{7,103},{8,104... | collective-permute-start | bytes 2359304 | tf_op jit(solution)/shard_map/ppermute | solution.py:20
  64.0 0.1 add_add_fusion.2.meta_ref
  64.1 3.3 %split_amp.1.a_ref = bf16[4,4,256,768]{3,2,1,0:T(8,128)(2,1)S(1)} custom-call(f32[4,256,256]{2,1,0:T(8,128)} %maximum_select_fusion.1.a_ref, f32[4,256,256]{2,1,0:T(8,128)} %collective-permute-done.9.r_ref, f32[4,256,256]{2,1,0:T(8,128)} %collective-permute-done.10.l_ref, f32[2,256,256]{2,1,0:T(8,128)S(1)} %collective-permute-done.11.fa_ref, ...), custom_call_target="tpu_custom_call" | custom-call | bytes 10485760 | tf_op jit(solution)/shard_map/split_amp/pallas_call | solution.py:70
  67.4 2.7 %copy-done = bf16[4,4,256,768]{3,2,1,0:T(8,128)(2,1)} copy-done((bf16[4,4,256,768]{3,2,1,0:T(8,128)(2,1)}, bf16[4,4,256,768]{3,2,1,0:T(8,128)(2,1)S(1)}, u32[]{:S(2)}) %copy-start) | copy-done | bytes 6291480
  70.1 9.7 %contract.2 = (f32[4,256,256]{2,1,0:T(8,128)S(1)}, f32[4,256,256]{2,1,0:T(8,128)S(1)}, f32[4,256,256]{2,1,0:T(8,128)S(1)}, f32[4,256,256]{2,1,0:T(8,128)S(1)}) custom-call(s32[66]{0:T(128)S(1)} %add_add_fusion.2.meta_ref, bf16[4,4,256,768]{3,2,1,0:T(8,128)(2,1)} %copy-done, f32[2,256,256]{2,1,0:T(8,128)S(1)} %get-tuple-element.37.own, ...), custom_call_target="tpu_custom_call" | custom-call | flops 1610612736 | bytes 14680064 | tf_op jit(solution)/shard_map/contract/pallas_call | solution.py:134
  79.9 2.0 %collective-permute-start.20 = (f32[4,256,256]{2,1,0:T(8,128)S(1)}, f32[4,256,256]{2,1,0:T(8,128)S(1)}, u32[]{:S(2)}, u32[]{:S(2)}) collective-permute-start(f32[4,256,256]{2,1,0:T(8,128)S(1)} %get-tuple-element.28), channel_id=1, source_target_pairs={{0,8},{1,9},{2,10},{3,11},{4,12},{5,13},{6,14},{7,15},{8,0},{9,1},... | collective-permute-start | bytes 3145736 | tf_op jit(solution)/shard_map/ppermute | solution.py:20
  81.9 2.0 %collective-permute-start.21 = (f32[4,256,256]{2,1,0:T(8,128)S(1)}, f32[4,256,256]{2,1,0:T(8,128)S(1)}, u32[]{:S(2)}, u32[]{:S(2)}) collective-permute-start(f32[4,256,256]{2,1,0:T(8,128)S(1)} %get-tuple-element.29), channel_id=1, source_target_pairs={{0,12},{1,13},{2,14},{3,15},{4,0},{5,1},{6,2},{7,3},{8,4},{9,5},{1... | collective-permute-start | bytes 3145736 | tf_op jit(solution)/shard_map/ppermute | solution.py:20
  83.9 1.4 collective-permute-done.24.rest_r
  85.3 0.1 collective-permute-start.26
  85.5 2.7 %collective-permute-start.27 = (f32[3,128,256]{2,1,0:T(8,128)S(1)}, f32[3,128,256]{2,1,0:T(8,128)S(1)}, u32[]{:S(2)}, u32[]{:S(2)}) collective-permute-start(f32[3,128,256]{2,1,0:T(8,128)S(1)} %slice.109), channel_id=1, source_target_pairs={{0,96},{1,97},{2,98},{3,99},{4,100},{5,101},{6,102},{7,103},{8,104... | collective-permute-start | bytes 1179656 | tf_op jit(solution)/shard_map/ppermute | solution.py:20
  88.3 6.4 %collective-permute-done.26.rest_fa = f32[3,128,256]{2,1,0:T(8,128)S(1)} collective-permute-done((f32[3,128,256]{2,1,0:T(8,128)S(1)}, f32[3,128,256]{2,1,0:T(8,128)S(1)}, u32[]{:S(2)}, u32[]{:S(2)}) %collective-permute-start.26) | collective-permute-done | bytes 393248 | tf_op jit(solution)/shard_map/ppermute | solution.py:20
  94.7 8.1 %contract.3 = (f32[4,256,256]{2,1,0:T(8,128)S(1)}, f32[4,256,256]{2,1,0:T(8,128)S(1)}, f32[4,256,256]{2,1,0:T(8,128)S(1)}, f32[4,256,256]{2,1,0:T(8,128)S(1)}) custom-call(s32[66]{0:T(128)S(1)} %add_add_fusion.3.meta_ref, bf16[4,4,256,768]{3,2,1,0:T(8,128)(2,1)} %copy-done, f32[2,256,256]{2,1,0:T(8,128)S(1)} %get-tuple-element.37.own, ...), custom_call_target="tpu_custom_call" | custom-call | flops 1610612736 | bytes 14680064 | tf_op jit(solution)/shard_map/contract/pallas_call | solution.py:134
  102.8 6.2 %collective-permute-start.28 = (f32[4,256,256]{2,1,0:T(8,128)S(1)}, f32[4,256,256]{2,1,0:T(8,128)S(1)}, u32[]{:S(2)}, u32[]{:S(2)}) collective-permute-start(f32[4,256,256]{2,1,0:T(8,128)S(1)} %get-tuple-element.32), channel_id=1, source_target_pairs={{0,4},{1,5},{2,6},{3,7},{4,8},{5,9},{6,10},{7,11},{8,12},{9,13},{1... | collective-permute-start | bytes 3145736 | tf_op jit(solution)/shard_map/ppermute | solution.py:20
  109.1 1.9 %collective-permute-start.30 = (f32[4,256,256]{2,1,0:T(8,128)S(1)}, f32[4,256,256]{2,1,0:T(8,128)S(1)}, u32[]{:S(2)}, u32[]{:S(2)}) collective-permute-start(f32[4,256,256]{2,1,0:T(8,128)S(1)} %get-tuple-element.34), channel_id=1, source_target_pairs={{0,12},{1,13},{2,14},{3,15},{4,0},{5,1},{6,2},{7,3},{8,4},{9,5},{1... | collective-permute-start | bytes 3145736 | tf_op jit(solution)/shard_map/ppermute | solution.py:20
  110.9 0.3 add_add_fusion.1
  111.2 0.1 fusion.16
  111.4 4.9 %collective-permute-start.23 = (f32[2,256,256]{2,1,0:T(8,128)S(1)}, f32[2,256,256]{2,1,0:T(8,128)S(1)}, u32[]{:S(2)}, u32[]{:S(2)}) collective-permute-start(f32[2,256,256]{2,1,0:T(8,128)S(1)} %get-tuple-element.45), channel_id=1, source_target_pairs={{16,16},{17,20},{18,24},{19,28},{20,17},{21,21},{22,25},{23,29},{2... | collective-permute-start | bytes 1572872 | tf_op jit(solution)/shard_map/ppermute | solution.py:20
  116.3 15.7 %collective-permute-done.28 = f32[4,256,256]{2,1,0:T(8,128)S(1)} collective-permute-done((f32[4,256,256]{2,1,0:T(8,128)S(1)}, f32[4,256,256]{2,1,0:T(8,128)S(1)}, u32[]{:S(2)}, u32[]{:S(2)}) %collective-permute-start.28) | collective-permute-done | bytes 1048608 | tf_op jit(solution)/shard_map/ppermute | solution.py:20
  132.0 2.2 %collective-permute-done.30 = f32[4,256,256]{2,1,0:T(8,128)S(1)} collective-permute-done((f32[4,256,256]{2,1,0:T(8,128)S(1)}, f32[4,256,256]{2,1,0:T(8,128)S(1)}, u32[]{:S(2)}, u32[]{:S(2)}) %collective-permute-start.30) | collective-permute-done | bytes 1048608 | tf_op jit(solution)/shard_map/ppermute | solution.py:20
  134.2 0.3 add_add_fusion
  134.5 0.1 fusion.17
  134.6 2.5 %collective-permute-start.31 = (f32[2,256,256]{2,1,0:T(8,128)S(1)}, f32[2,256,256]{2,1,0:T(8,128)S(1)}, u32[]{:S(2)}, u32[]{:S(2)}) collective-permute-start(f32[2,256,256]{2,1,0:T(8,128)S(1)} %get-tuple-element.48), channel_id=1, source_target_pairs={{0,16},{1,17},{2,18},{3,19},{4,20},{5,21},{6,22},{7,23},{8,24},{9,... | collective-permute-start | bytes 1572872 | tf_op jit(solution)/shard_map/ppermute | solution.py:20
  137.1 37.8 %collective-permute-start.32 = (f32[2,256,256]{2,1,0:T(8,128)S(1)}, f32[2,256,256]{2,1,0:T(8,128)S(1)}, u32[]{:S(2)}, u32[]{:S(2)}) collective-permute-start(f32[2,256,256]{2,1,0:T(8,128)S(1)} %get-tuple-element.47), channel_id=1, source_target_pairs={{16,16},{17,20},{18,24},{19,28},{20,17},{21,21},{22,25},{23,29},{2... | collective-permute-start | bytes 1572872 | tf_op jit(solution)/shard_map/ppermute | solution.py:20
  174.9 10.2 %collective-permute-done.32 = f32[2,256,256]{2,1,0:T(8,128)S(1)} collective-permute-done((f32[2,256,256]{2,1,0:T(8,128)S(1)}, f32[2,256,256]{2,1,0:T(8,128)S(1)}, u32[]{:S(2)}, u32[]{:S(2)}) %collective-permute-start.32) | collective-permute-done | bytes 524320 | tf_op jit(solution)/shard_map/ppermute | solution.py:20
  185.1 0.3 fusion.3
  185.4 0.1 pad_maximum_fusion.2
  185.5 1.0 copy.10
  (59 shorter events, 0.8 us)
Async XLA Ops:
  0.0 3.5 %copy-start.6 = (f32[2,2,256,256]{3,2,1,0:T(8,128)S(1)}, f32[2,2,256,256]{3,2,1,0:T(8,128)}, u32[]{:S(2)}) copy-start(f32[2,2,256,256]{3,2,1,0:T(8,128)} %param.4) | copy-start | bytes 3145732
  2.8 3.2 %collective-permute-start.1 = (f32[4,256,256]{2,1,0:T(8,128)}, f32[4,256,256]{2,1,0:T(8,128)S(1)}, u32[]{:S(2)}, u32[]{:S(2)}) collective-permute-start(f32[4,256,256]{2,1,0:T(8,128)} %get-tuple-element.42), channel_id=1, source_target_pairs={{0,16},{1,17},{2,18},{3,19},{4,20},{5,21},{6,22},{7,23},{8,24},{9,... | collective-permute-start | bytes 3145736 | tf_op jit(solution)/shard_map/ppermute | solution.py:20
  4.4 7.1 %collective-permute-start = (f32[2,256,256]{2,1,0:T(8,128)}, f32[2,256,256]{2,1,0:T(8,128)}, u32[]{:S(2)}, u32[]{:S(2)}) collective-permute-start(f32[2,256,256]{2,1,0:T(8,128)} %get-tuple-element.50), channel_id=1, source_target_pairs={{0,16},{1,17},{2,18},{3,19},{4,20},{5,21},{6,22},{7,23},{8,24},{9,... | collective-permute-start | bytes 1572872 | tf_op jit(solution)/shard_map/ppermute | solution.py:20
  6.2 4.2 %copy-start.8 = (s32[1,1,3,32]{3,1,2,0:T(1,128)S(1)}, s32[1,1,3,32]{3,1,2,0:T(1,128)}, u32[]{:S(2)}) copy-start(s32[1,1,3,32]{3,1,2,0:T(1,128)} %param.7) | copy-start | bytes 1156
  6.4 11.1 %collective-permute-start.2 = (f32[2,256,256]{2,1,0:T(8,128)S(1)}, f32[2,256,256]{2,1,0:T(8,128)S(1)}, u32[]{:S(2)}, u32[]{:S(2)}) collective-permute-start(f32[2,256,256]{2,1,0:T(8,128)S(1)} %get-tuple-element.40), channel_id=1, source_target_pairs={{0,1},{1,2},{2,3},{3,0},{4,5},{5,6},{6,7},{7,4},{8,9},{9,10},{10,1... | collective-permute-start | bytes 1572872 | tf_op jit(solution)/shard_map/ppermute | solution.py:20
  7.7 14.8 %collective-permute-start.3 = (f32[2,256,256]{2,1,0:T(8,128)S(1)}, f32[2,256,256]{2,1,0:T(8,128)S(1)}, u32[]{:S(2)}, u32[]{:S(2)}) collective-permute-start(f32[2,256,256]{2,1,0:T(8,128)S(1)} %get-tuple-element.39), channel_id=1, source_target_pairs={{0,2},{1,3},{2,0},{3,1},{4,6},{5,7},{6,4},{7,5},{8,10},{9,11},{10,... | collective-permute-start | bytes 1572872 | tf_op jit(solution)/shard_map/ppermute | solution.py:20
  10.4 12.2 %collective-permute-start.4 = (f32[2,256,256]{2,1,0:T(8,128)S(1)}, f32[2,256,256]{2,1,0:T(8,128)S(1)}, u32[]{:S(2)}, u32[]{:S(2)}) collective-permute-start(f32[2,256,256]{2,1,0:T(8,128)S(1)} %get-tuple-element.38), channel_id=1, source_target_pairs={{0,3},{1,0},{2,1},{3,2},{4,7},{5,4},{6,5},{7,6},{8,11},{9,8},{10,9... | collective-permute-start | bytes 1572872 | tf_op jit(solution)/shard_map/ppermute | solution.py:20
  13.7 15.9 %collective-permute-start.13 = (f32[2,256,256]{2,1,0:T(8,128)S(1)}, f32[2,256,256]{2,1,0:T(8,128)S(1)}, u32[]{:S(2)}, u32[]{:S(2)}) collective-permute-start(f32[2,256,256]{2,1,0:T(8,128)S(1)} %get-tuple-element.37.own), channel_id=1, source_target_pairs={{0,32},{1,33},{2,34},{3,35},{4,36},{5,37},{6,38},{7,39},{8,40},{9,... | collective-permute-start | bytes 1572872 | tf_op jit(solution)/shard_map/ppermute | solution.py:20
  15.4 14.3 %collective-permute-start.14 = (f32[2,256,256]{2,1,0:T(8,128)S(1)}, f32[2,256,256]{2,1,0:T(8,128)S(1)}, u32[]{:S(2)}, u32[]{:S(2)}) collective-permute-start(f32[2,256,256]{2,1,0:T(8,128)S(1)} %get-tuple-element.37.own), channel_id=1, source_target_pairs={{0,96},{1,97},{2,98},{3,99},{4,100},{5,101},{6,102},{7,103},{8,104... | collective-permute-start | bytes 1572872 | tf_op jit(solution)/shard_map/ppermute | solution.py:20
  23.6 24.8 %collective-permute-start.9 = (f32[4,256,256]{2,1,0:T(8,128)}, f32[4,256,256]{2,1,0:T(8,128)}, u32[]{:S(2)}, u32[]{:S(2)}) collective-permute-start(f32[4,256,256]{2,1,0:T(8,128)} %maximum_select_fusion.1.a_ref), channel_id=1, source_target_pairs={{0,1},{1,2},{2,3},{3,0},{4,5},{5,6},{6,7},{7,4},{8,9},{9,10},{10,1... | collective-permute-start | bytes 3145736 | tf_op jit(solution)/shard_map/ppermute | solution.py:20
  24.8 24.9 %collective-permute-start.10 = (f32[4,256,256]{2,1,0:T(8,128)}, f32[4,256,256]{2,1,0:T(8,128)}, u32[]{:S(2)}, u32[]{:S(2)}) collective-permute-start(f32[4,256,256]{2,1,0:T(8,128)} %maximum_select_fusion.1.a_ref), channel_id=1, source_target_pairs={{0,3},{1,0},{2,1},{3,2},{4,7},{5,4},{6,5},{7,6},{8,11},{9,8},{10,9... | collective-permute-start | bytes 3145736 | tf_op jit(solution)/shard_map/ppermute | solution.py:20
  29.7 0.8 copy-start.1
  30.4 0.8 copy-start.3
  32.8 25.4 %collective-permute-start.15 = (f32[4,256,256]{2,1,0:T(8,128)}, f32[4,256,256]{2,1,0:T(8,128)S(1)}, u32[]{:S(2)}, u32[]{:S(2)}) collective-permute-start(f32[4,256,256]{2,1,0:T(8,128)} %get-tuple-element.52), channel_id=1, source_target_pairs={{0,32},{1,33},{2,34},{3,35},{4,36},{5,37},{6,38},{7,39},{8,40},{9,... | collective-permute-start | bytes 3145736 | tf_op jit(solution)/shard_map/ppermute | solution.py:20
  32.8 25.4 %collective-permute-start.16 = (f32[4,256,256]{2,1,0:T(8,128)}, f32[4,256,256]{2,1,0:T(8,128)S(1)}, u32[]{:S(2)}, u32[]{:S(2)}) collective-permute-start(f32[4,256,256]{2,1,0:T(8,128)} %get-tuple-element.51), channel_id=1, source_target_pairs={{0,96},{1,97},{2,98},{3,99},{4,100},{5,101},{6,102},{7,103},{8,104... | collective-permute-start | bytes 3145736 | tf_op jit(solution)/shard_map/ppermute | solution.py:20
  35.4 2.1 %collective-permute-start.5 = (s32[3,32]{1,0:T(4,128)S(1)}, s32[3,32]{1,0:T(4,128)S(1)}, u32[]{:S(2)}, u32[]{:S(2)}) collective-permute-start(s32[3,32]{1,0:T(4,128)S(1)} %bitcast.54), channel_id=1, source_target_pairs={{0,16},{1,17},{2,18},{3,19},{4,20},{5,21},{6,22},{7,23},{8,24},{9,... | collective-permute-start | bytes 1160 | tf_op jit(solution)/shard_map/ppermute | solution.py:20
  37.5 4.0 %collective-permute-start.6 = (s32[2,3,32]{2,1,0:T(4,128)S(1)}, s32[2,3,32]{2,1,0:T(4,128)S(1)}, u32[]{:S(2)}, u32[]{:S(2)}) collective-permute-start(s32[2,3,32]{2,1,0:T(4,128)S(1)} %get-tuple-element.60), channel_id=1, source_target_pairs={{0,1},{1,2},{2,3},{3,0},{4,5},{5,6},{6,7},{7,4},{8,9},{9,10},{10,1... | collective-permute-start | bytes 2312 | tf_op jit(solution)/shard_map/ppermute | solution.py:20
  41.5 4.0 %collective-permute-start.7 = (s32[2,3,32]{2,1,0:T(4,128)S(1)}, s32[2,3,32]{2,1,0:T(4,128)S(1)}, u32[]{:S(2)}, u32[]{:S(2)}) collective-permute-start(s32[2,3,32]{2,1,0:T(4,128)S(1)} %get-tuple-element.60), channel_id=1, source_target_pairs={{0,2},{1,3},{2,0},{3,1},{4,6},{5,7},{6,4},{7,5},{8,10},{9,11},{10,... | collective-permute-start | bytes 2312 | tf_op jit(solution)/shard_map/ppermute | solution.py:20
  45.5 2.8 %collective-permute-start.8 = (s32[2,3,32]{2,1,0:T(4,128)S(1)}, s32[2,3,32]{2,1,0:T(4,128)S(1)}, u32[]{:S(2)}, u32[]{:S(2)}) collective-permute-start(s32[2,3,32]{2,1,0:T(4,128)S(1)} %get-tuple-element.60), channel_id=1, source_target_pairs={{0,3},{1,0},{2,1},{3,2},{4,7},{5,4},{6,5},{7,6},{8,11},{9,8},{10,9... | collective-permute-start | bytes 2312 | tf_op jit(solution)/shard_map/ppermute | solution.py:20
  48.4 12.7 %copy-start.5 = (f32[3,256,256]{2,1,0:T(8,128)S(1)}, f32[3,256,256]{2,1,0:T(8,128)}, u32[]{:S(2)}) copy-start(f32[3,256,256]{2,1,0:T(8,128)} %get-tuple-element.30.rest) | copy-start | bytes 2359300
  49.6 11.6 %collective-permute-start.11 = (f32[2,256,256]{2,1,0:T(8,128)S(1)}, f32[2,256,256]{2,1,0:T(8,128)S(1)}, u32[]{:S(2)}, u32[]{:S(2)}) collective-permute-start(f32[2,256,256]{2,1,0:T(8,128)S(1)} %slice.102), channel_id=1, source_target_pairs={{0,1},{1,2},{2,3},{3,0},{4,5},{5,6},{6,7},{7,4},{8,9},{9,10},{10,1... | collective-permute-start | bytes 1572872 | tf_op jit(solution)/shard_map/ppermute | solution.py:20
  50.8 13.3 %collective-permute-start.12 = (f32[2,256,256]{2,1,0:T(8,128)S(1)}, f32[2,256,256]{2,1,0:T(8,128)S(1)}, u32[]{:S(2)}, u32[]{:S(2)}) collective-permute-start(f32[2,256,256]{2,1,0:T(8,128)S(1)} %slice.103), channel_id=1, source_target_pairs={{0,3},{1,0},{2,1},{3,2},{4,7},{5,4},{6,5},{7,6},{8,11},{9,8},{10,9... | collective-permute-start | bytes 1572872 | tf_op jit(solution)/shard_map/ppermute | solution.py:20
  58.2 11.9 %collective-permute-start.17 = (f32[3,128,256]{2,1,0:T(8,128)S(1)}, f32[3,128,256]{2,1,0:T(8,128)S(1)}, u32[]{:S(2)}, u32[]{:S(2)}) collective-permute-start(f32[3,128,256]{2,1,0:T(8,128)S(1)} %slice.86), channel_id=1, source_target_pairs={{0,32},{1,33},{2,34},{3,35},{4,36},{5,37},{6,38},{7,39},{8,40},{9,... | collective-permute-start | bytes 1179656 | tf_op jit(solution)/shard_map/ppermute | solution.py:20
  58.3 11.7 %collective-permute-start.18 = (f32[3,128,256]{2,1,0:T(8,128)S(1)}, f32[3,128,256]{2,1,0:T(8,128)S(1)}, u32[]{:S(2)}, u32[]{:S(2)}) collective-permute-start(f32[3,128,256]{2,1,0:T(8,128)S(1)} %slice.87), channel_id=1, source_target_pairs={{0,96},{1,97},{2,98},{3,99},{4,100},{5,101},{6,102},{7,103},{8,104... | collective-permute-start | bytes 1179656 | tf_op jit(solution)/shard_map/ppermute | solution.py:20
  61.1 24.2 %collective-permute-start.24 = (f32[3,256,256]{2,1,0:T(8,128)S(1)}, f32[3,256,256]{2,1,0:T(8,128)S(1)}, u32[]{:S(2)}, u32[]{:S(2)}) collective-permute-start(f32[3,256,256]{2,1,0:T(8,128)S(1)} %copy-done.5), channel_id=1, source_target_pairs={{0,32},{1,33},{2,34},{3,35},{4,36},{5,37},{6,38},{7,39},{8,40},{9,... | collective-permute-start | bytes 2359304 | tf_op jit(solution)/shard_map/ppermute | solution.py:20
  61.2 24.2 %collective-permute-start.25 = (f32[3,256,256]{2,1,0:T(8,128)S(1)}, f32[3,256,256]{2,1,0:T(8,128)S(1)}, u32[]{:S(2)}, u32[]{:S(2)}) collective-permute-start(f32[3,256,256]{2,1,0:T(8,128)S(1)} %copy-done.5), channel_id=1, source_target_pairs={{0,96},{1,97},{2,98},{3,99},{4,100},{5,101},{6,102},{7,103},{8,104... | collective-permute-start | bytes 2359304 | tf_op jit(solution)/shard_map/ppermute | solution.py:20
  64.0 6.0 %copy-start.2 = (f32[2,256,256]{2,1,0:T(8,128)S(1)}, f32[2,256,256]{2,1,0:T(8,128)}, u32[]{:S(2)}) copy-start(f32[2,256,256]{2,1,0:T(8,128)} %copy-done.1) | copy-start | bytes 1572868
  64.0 6.0 %copy-start.4 = (f32[2,256,256]{2,1,0:T(8,128)S(1)}, f32[2,256,256]{2,1,0:T(8,128)}, u32[]{:S(2)}) copy-start(f32[2,256,256]{2,1,0:T(8,128)} %copy-done.3) | copy-start | bytes 1572868
  67.3 2.7 %copy-start = (bf16[4,4,256,768]{3,2,1,0:T(8,128)(2,1)}, bf16[4,4,256,768]{3,2,1,0:T(8,128)(2,1)S(1)}, u32[]{:S(2)}) copy-start(bf16[4,4,256,768]{3,2,1,0:T(8,128)(2,1)S(1)} %split_amp.1.a_ref) | copy-start | bytes 18874372
  79.8 29.3 %collective-permute-start.19 = (f32[4,256,256]{2,1,0:T(8,128)S(1)}, f32[4,256,256]{2,1,0:T(8,128)S(1)}, u32[]{:S(2)}, u32[]{:S(2)}) collective-permute-start(f32[4,256,256]{2,1,0:T(8,128)S(1)} %get-tuple-element.27), channel_id=1, source_target_pairs={{0,4},{1,5},{2,6},{3,7},{4,8},{5,9},{6,10},{7,11},{8,12},{9,13},{1... | collective-permute-start | bytes 3145736 | tf_op jit(solution)/shard_map/ppermute | solution.py:20
  79.9 31.1 %collective-permute-start.20 = (f32[4,256,256]{2,1,0:T(8,128)S(1)}, f32[4,256,256]{2,1,0:T(8,128)S(1)}, u32[]{:S(2)}, u32[]{:S(2)}) collective-permute-start(f32[4,256,256]{2,1,0:T(8,128)S(1)} %get-tuple-element.28), channel_id=1, source_target_pairs={{0,8},{1,9},{2,10},{3,11},{4,12},{5,13},{6,14},{7,15},{8,0},{9,1},... | collective-permute-start | bytes 3145736 | tf_op jit(solution)/shard_map/ppermute | solution.py:20
  81.9 29.0 %collective-permute-start.21 = (f32[4,256,256]{2,1,0:T(8,128)S(1)}, f32[4,256,256]{2,1,0:T(8,128)S(1)}, u32[]{:S(2)}, u32[]{:S(2)}) collective-permute-start(f32[4,256,256]{2,1,0:T(8,128)S(1)} %get-tuple-element.29), channel_id=1, source_target_pairs={{0,12},{1,13},{2,14},{3,15},{4,0},{5,1},{6,2},{7,3},{8,4},{9,5},{1... | collective-permute-start | bytes 3145736 | tf_op jit(solution)/shard_map/ppermute | solution.py:20
  85.3 9.4 %collective-permute-start.26 = (f32[3,128,256]{2,1,0:T(8,128)S(1)}, f32[3,128,256]{2,1,0:T(8,128)S(1)}, u32[]{:S(2)}, u32[]{:S(2)}) collective-permute-start(f32[3,128,256]{2,1,0:T(8,128)S(1)} %slice.108), channel_id=1, source_target_pairs={{0,32},{1,33},{2,34},{3,35},{4,36},{5,37},{6,38},{7,39},{8,40},{9,... | collective-permute-start | bytes 1179656 | tf_op jit(solution)/shard_map/ppermute | solution.py:20
  85.5 9.2 %collective-permute-start.27 = (f32[3,128,256]{2,1,0:T(8,128)S(1)}, f32[3,128,256]{2,1,0:T(8,128)S(1)}, u32[]{:S(2)}, u32[]{:S(2)}) collective-permute-start(f32[3,128,256]{2,1,0:T(8,128)S(1)} %slice.109), channel_id=1, source_target_pairs={{0,96},{1,97},{2,98},{3,99},{4,100},{5,101},{6,102},{7,103},{8,104... | collective-permute-start | bytes 1179656 | tf_op jit(solution)/shard_map/ppermute | solution.py:20
  102.8 29.2 %collective-permute-start.28 = (f32[4,256,256]{2,1,0:T(8,128)S(1)}, f32[4,256,256]{2,1,0:T(8,128)S(1)}, u32[]{:S(2)}, u32[]{:S(2)}) collective-permute-start(f32[4,256,256]{2,1,0:T(8,128)S(1)} %get-tuple-element.32), channel_id=1, source_target_pairs={{0,4},{1,5},{2,6},{3,7},{4,8},{5,9},{6,10},{7,11},{8,12},{9,13},{1... | collective-permute-start | bytes 3145736 | tf_op jit(solution)/shard_map/ppermute | solution.py:20
  109.0 23.0 %collective-permute-start.29 = (f32[4,256,256]{2,1,0:T(8,128)S(1)}, f32[4,256,256]{2,1,0:T(8,128)S(1)}, u32[]{:S(2)}, u32[]{:S(2)}) collective-permute-start(f32[4,256,256]{2,1,0:T(8,128)S(1)} %get-tuple-element.33), channel_id=1, source_target_pairs={{0,8},{1,9},{2,10},{3,11},{4,12},{5,13},{6,14},{7,15},{8,0},{9,1},... | collective-permute-start | bytes 3145736 | tf_op jit(solution)/shard_map/ppermute | solution.py:20
  109.1 25.2 %collective-permute-start.30 = (f32[4,256,256]{2,1,0:T(8,128)S(1)}, f32[4,256,256]{2,1,0:T(8,128)S(1)}, u32[]{:S(2)}, u32[]{:S(2)}) collective-permute-start(f32[4,256,256]{2,1,0:T(8,128)S(1)} %get-tuple-element.34), channel_id=1, source_target_pairs={{0,12},{1,13},{2,14},{3,15},{4,0},{5,1},{6,2},{7,3},{8,4},{9,5},{1... | collective-permute-start | bytes 3145736 | tf_op jit(solution)/shard_map/ppermute | solution.py:20
  111.3 63.5 %collective-permute-start.22 = (f32[2,256,256]{2,1,0:T(8,128)S(1)}, f32[2,256,256]{2,1,0:T(8,128)S(1)}, u32[]{:S(2)}, u32[]{:S(2)}) collective-permute-start(f32[2,256,256]{2,1,0:T(8,128)S(1)} %get-tuple-element.46), channel_id=1, source_target_pairs={{0,16},{1,17},{2,18},{3,19},{4,20},{5,21},{6,22},{7,23},{8,24},{9,... | collective-permute-start | bytes 1572872 | tf_op jit(solution)/shard_map/ppermute | solution.py:20
  111.4 63.5 %collective-permute-start.23 = (f32[2,256,256]{2,1,0:T(8,128)S(1)}, f32[2,256,256]{2,1,0:T(8,128)S(1)}, u32[]{:S(2)}, u32[]{:S(2)}) collective-permute-start(f32[2,256,256]{2,1,0:T(8,128)S(1)} %get-tuple-element.45), channel_id=1, source_target_pairs={{16,16},{17,20},{18,24},{19,28},{20,17},{21,21},{22,25},{23,29},{2... | collective-permute-start | bytes 1572872 | tf_op jit(solution)/shard_map/ppermute | solution.py:20
  134.5 50.6 %copy-start.7 = (f32[2,2,256,256]{3,2,1,0:T(8,128)S(1)}, f32[2,2,256,256]{3,2,1,0:T(8,128)}, u32[]{:S(2)}) copy-start(f32[2,2,256,256]{3,2,1,0:T(8,128)} %param.6) | copy-start | bytes 3145732
  134.6 40.3 %collective-permute-start.31 = (f32[2,256,256]{2,1,0:T(8,128)S(1)}, f32[2,256,256]{2,1,0:T(8,128)S(1)}, u32[]{:S(2)}, u32[]{:S(2)}) collective-permute-start(f32[2,256,256]{2,1,0:T(8,128)S(1)} %get-tuple-element.48), channel_id=1, source_target_pairs={{0,16},{1,17},{2,18},{3,19},{4,20},{5,21},{6,22},{7,23},{8,24},{9,... | collective-permute-start | bytes 1572872 | tf_op jit(solution)/shard_map/ppermute | solution.py:20
  137.1 48.0 %collective-permute-start.32 = (f32[2,256,256]{2,1,0:T(8,128)S(1)}, f32[2,256,256]{2,1,0:T(8,128)S(1)}, u32[]{:S(2)}, u32[]{:S(2)}) collective-permute-start(f32[2,256,256]{2,1,0:T(8,128)S(1)} %get-tuple-element.47), channel_id=1, source_target_pairs={{16,16},{17,20},{18,24},{19,28},{20,17},{21,21},{22,25},{23,29},{2... | collective-permute-start | bytes 1572872 | tf_op jit(solution)/shard_map/ppermute | solution.py:20

commit v3 on v0

v3 whole, which is shorter than its diff:
```python
import jax
import jax.numpy as jnp
from jax import lax
from jax.experimental import pallas as pl
from jax.experimental.pallas import tpu as pltpu
from jax.sharding import Mesh, PartitionSpec as P

NAMES = ("z", "c", "y", "x")
SIZE = {"z": 4, "c": 2, "y": 4, "x": 4}
MIB = 1024 * 1024
CHUNKS = ((0, 0, 256), (1, 0, 128), (1, 128, 128))


def shift(t, axis, s):
    n = SIZE[axis]
    return lax.ppermute(t, axis, [(i, (i + s) % n) for i in range(n)])


def halves(a):
    hi = a.astype(jnp.bfloat16)
    return hi, (a - hi.astype(jnp.float32)).astype(jnp.bfloat16)


def split_kernel(a_ref, r_ref, l_ref, fa_ref, fb_ref, o_ref):
    w = a_ref.shape[-1]

    def put(s, ref):
        for il in range(2):
            hi, lo = halves(ref[0, il * w : il * w + w])
            o_ref[s, il, :, :w] = hi
            o_ref[s, il, :, w : 2 * w] = lo
            o_ref[s, il, :, 2 * w :] = hi

    put(0, a_ref)
    put(1, r_ref)
    put(3, l_ref)

    @pl.when(pl.program_id(0) == 0)
    def _():
        put(2, fa_ref)

    @pl.when(pl.program_id(0) == 1)
    def _():
        put(2, fb_ref)


def split_amp(a, r, l, fa, fb):
    rows, w = a.shape[1:]
    each = pl.BlockSpec((1, rows, w), lambda g: (g, 0, 0))
    only = pl.BlockSpec((1, rows, w), lambda g: (0, 0, 0))
    return pl.pallas_call(
        split_kernel,
        grid=(2,),
        in_specs=[each, each, each, only, only],
        out_specs=pl.BlockSpec((4, 2, w, 3 * w), lambda g: (0, g, 0, 0)),
        out_shape=jax.ShapeDtypeStruct((4, 4, w, 3 * w), jnp.bfloat16),
        compiler_params=pltpu.CompilerParams(vmem_limit_bytes=18 * MIB),
        cost_estimate=pl.CostEstimate(flops=0, bytes_accessed=10 * MIB, transcendentals=0),
        name="split_amp",
    )(a, r, l, fa, fb)


def make_contract_kernel(kp, first, width):
    def kernel(flag_ref, a_ref, own, own_r, own_l, own_fa, own_fb, rest, rest_r, rest_l, rest_fa, rest_fb,
               mine_ref, other_ref, b_ref):
        w = a_ref.shape[2]
        h = w // 2
        columns = slice(first, first + width)

        def load(s, b, at=0):
            n = b.shape[0]
            hi, lo = halves(b)
            b_ref[s, at : at + n] = hi
            b_ref[s, w + at : w + at + n] = hi
            b_ref[s, 2 * w + at : 2 * w + at + n] = lo

        z, c, y = flag_ref[128], flag_ref[129], flag_ref[130]

        @pl.loop(0, 4)
        def _(step):
            ka = lax.rem(z + jnp.where(step == 1, 3, jnp.where(step == 2, 1, jnp.where(step == 3, 2, 0))), 4)
            for at, (mine, others) in enumerate(((own, rest), (own_r, rest_r), (own_l, rest_l))):
                @pl.when(step == at)
                def _():
                    load(0, mine[kp, :, columns])
                    for s in range(3):
                        load(s + 1, others[s])

            @pl.when(step == 3)
            def _():
                for part, (mine, others) in enumerate(((own_fa, rest_fa), (own_fb, rest_fb))):
                    load(0, mine[kp, :, columns], part * h)
                    for s in range(3):
                        load(s + 1, others[s], part * h)

            away = lax.rem(ka + 4 - y, 4)
            for out, core in ((mine_ref, c), (other_ref, 1 - c)):
                for il in range(2):
                    out[away, il] = jnp.zeros((w, width), jnp.float32)
                    for s in range(4):
                        @pl.when(flag_ref[(s * 2 + core) * 16 + kp * 8 + ka * 2 + il] != 0)
                        def _():
                            out[away, il] += jnp.dot(
                                a_ref[s, 2 * core + il], b_ref[s], preferred_element_type=jnp.float32
                            )

    return kernel


def contract(chunk, flags, a3, own, rest):
    w = a3.shape[2]
    width = chunk[2]
    inside = pl.BlockSpec(memory_space=pltpu.VMEM)
    out = jax.ShapeDtypeStruct((4, 2, w, width), jnp.float32)
    return pl.pallas_call(
        make_contract_kernel(*chunk),
        in_specs=[pl.BlockSpec(memory_space=pltpu.SMEM)] + [inside] * 11,
        out_specs=[inside, inside],
        scratch_shapes=[pltpu.VMEM((4, 3 * w, width), jnp.bfloat16)],
        out_shape=[out, out],
        compiler_params=pltpu.CompilerParams(vmem_limit_bytes=28 * MIB),
        cost_estimate=pl.CostEstimate(flops=16 * 6 * w * w * width, bytes_accessed=8 * MIB, transcendentals=0),
        name="contract",
    )(flags, a3, *own, *rest)


def on_device(amp, integ, resid, triples):
    w = amp.shape[-1]
    h = w // 2
    z, c, y, x = (lax.axis_index(n) for n in NAMES)

    def joined(mine, other):
        return jnp.where(c == 0, jnp.stack([mine, other]), jnp.stack([other, mine]))

    mine = lax.dynamic_index_in_dim(integ, c, 0, keepdims=False)
    other = shift(lax.dynamic_index_in_dim(integ, 1 - c, 0, keepdims=False), "c", 1)
    pairs = joined(mine, other).reshape(4, 2, w, w)
    tiles = [lax.dynamic_index_in_dim(pairs, lax.rem(x + s, 4), 0, keepdims=False) for s in range(4)]
    own = tiles[0]
    own_r, own_l = shift(own, "z", 1), shift(own, "z", -1)
    came = [[shift(tiles[s][kp], "x", s) for s in (1, 2, 3)] for kp in range(2)]
    rest = [jnp.stack([t[:, f : f + n] for t in came[kp]]) for kp, f, n in CHUNKS]

    tri = triples[0, 0]
    i = tri[0] // 32
    j = tri[0] % 32
    k = tri[1] % 32
    slot = (((j % 2 * 4 + (k // 2) % 4) * 2 + k % 2) * 4 + k // 8) * 2 + i % 2
    place = lax.broadcasted_iota(jnp.int32, (32, w), 1)
    listed = jnp.sum((place == slot[:, None]).astype(jnp.float32), axis=0, keepdims=True)
    listed = jnp.broadcast_to(listed, (8, w))

    def with_flags(parity):
        tile = lax.dynamic_index_in_dim(amp, parity, 1, keepdims=False)
        return jnp.concatenate([tile.reshape(2 * w, w), listed])

    a0 = joined(with_flags(c), shift(with_flags(1 - c), "c", 1))
    a0, rest[0] = lax.optimization_barrier((a0, rest[0]))
    a_r, a_l = shift(a0, "x", 1), shift(a0, "x", -1)
    a_fa, a_fb = shift(a_r[:1], "x", 1), shift(a_l[1:], "x", -1)
    a3 = split_amp(a0, a_r, a_l, a_fa, a_fb)
    rows = jnp.stack([a0[:, 2 * w, :128], a_r[:, 2 * w, :128],
                      jnp.concatenate([a_fa[:, 2 * w, :128], a_fb[:, 2 * w, :128]]), a_l[:, 2 * w, :128]])
    flags = lax.dynamic_index_in_dim(rows.reshape(4, 2, 8, 16), c * 4 + x, 2, keepdims=False)
    flags = jnp.concatenate([flags.reshape(-1).astype(jnp.int32), jnp.stack([z, c, y])])

    own_fa, own_fb = shift(own_r[:, :h], "z", 1), shift(own_l[:, h:], "z", -1)
    right, left, far = [], [], []
    for n in range(len(CHUNKS)):
        if n:
            right[-1], left[-1], rest[n] = lax.optimization_barrier((right[-1], left[-1], rest[n]))
            far.append((shift(right[-1][:, :h], "z", 1), shift(left[-1][:, h:], "z", -1)))
        right.append(shift(rest[n], "z", 1))
        left.append(shift(rest[n], "z", -1))
    far.append((shift(right[-1][:, :h], "z", 1), shift(left[-1][:, h:], "z", -1)))

    outs = []
    for n, chunk in enumerate(CHUNKS):
        kp, first, width = chunk
        held, away = contract(
            chunk, flags, a3, (own, own_r, own_l, own_fa, own_fb), (rest[n], right[n], left[n]) + far[n]
        )
        part = held + shift(away, "c", 1)
        total = resid[:, kp, :, first : first + width] + part[0]
        for s in (1, 2, 3):
            total = total + shift(part[s], "y", s)
        outs.append(total)
    return jnp.stack([outs[0], jnp.concatenate(outs[1:], axis=-1)], axis=1)


def solution(mesh):
    fine = Mesh(mesh.devices.reshape(4, 2, 4, 4), NAMES)
    row, col = ("z", "c"), ("y", "x")
    return jax.shard_map(
        on_device,
        mesh=fine,
        in_specs=(P(row, col), P(col, row), P(row, col), P(row, col)),
        out_specs=P(row, col),
        check_vma=False,
    )
```

time: 410 us -> 217 us (0.53)
  waiting for transfers between devices: 309 us -> 88.1 us
  starting transfers between devices: 0.04 us -> 62.8 us
  Pallas kernels: 0 us -> 22.5 us
  matrix products: 17.2 us -> 0 us
  other arithmetic: 20.1 us -> 5.69 us
  between operations: 14.1 us -> 0.37 us
  local copies, waits for them, and re-layouts: 48.5 us -> 35.5 us
    unnamed x3 -> x0, waiting for transfers between devices: 219 us -> none
    all_gather x1 -> x0, waiting for transfers between devices: 90.2 us -> none  [on_device(): gathered = lax.all_gather(int_tiles, 'row', axis=1, tiled=True)]
    ppermute x0 -> x40, waiting for transfers between devices: none -> 88.1 us  [shift(): return lax.ppermute(t, axis, [(i, (i + s) % n) for i in range(n)])]
    ppermute x0 -> x40, starting transfers between devices: none -> 62.8 us  [shift(): return lax.ppermute(t, axis, [(i, (i + s) % n) for i in range(n)])]
    gather x8 -> x0, local copies, waits for them, and re-layouts: 39.2 us -> none  [the longest x4 31.3 us: add_block(): int_flat[int_pick]]
    pallas_call x0 -> x4, Pallas kernels: none -> 22.5 us  [the longest x3 19.7 us: contract(): pl.pallas_call(make_contract_kernel(*chunk), in_specs=[pl.BlockSpec(memor...]
    scatter-add x4 -> x0, other arithmetic: 17.6 us -> none  [add_block(): return (partial_value.at[target_pick].add(products), None)]
    dot_general x4 -> x0, matrix products: 17.2 us -> none  [add_block(): jnp.einsum('bxy,byz->bxz', amp_flat[amp_pick], int_flat[int_pick], precis...]
  transfers between devices with their start and end apart: 2 -> 40, of which waited for: 2 -> 15; matrix products, arithmetic and copies ran while one was open for 0% -> 17% of each run, Pallas kernels for 0% -> 10%
where the time goes in v3:
time: 217 us; the launch traced here: 215 us
  waiting for transfers between devices  88.1 us (41%)
  starting transfers between devices  62.8 us (29%)
  local copies, waits for them, and re-layouts  35.5 us (16%)
  Pallas kernels  22.5 us (10%)
  other arithmetic  5.69 us (3%)
    ppermute x40, waiting for transfers between devices, shift(): return lax.ppermute(t, axis, [(i, (i + s) % n) for i in range(n)])  88.1 us
    ppermute x40, starting transfers between devices, shift(): return lax.ppermute(t, axis, [(i, (i + s) % n) for i in range(n)])  62.8 us
    pallas_call x3, Pallas kernels, contract(): pl.pallas_call(make_contract_kernel(*chunk), in_specs=[pl.BlockSpec(memor...  19.7 us
    another operation x3, local copies, waits for them, and re-layouts, on_device(): rest = [jnp.stack([t[:, f:f + n] for t in came[kp]]) for kp, f, n in CHUNKS]  5.03 us
  transfers between devices with their start and end apart: 40, of which 15 were waited for; matrix products, arithmetic and copies ran while one was open for 17% of the time, Pallas kernels for 10%

profile of v3, /device:TPU:1, one launch (start us, length us, event | category | flops | bytes accessed | tf_op | source)
XLA Modules:
  0.0 214.9 jit_solution(6845589394557022200)
XLA Ops:
  0.0 2.8 %constant_dynamic-slice_fusion = (f32[1,4,256,256]{3,2,1,0:T(8,128)S(1)}, f32[4,256,256]{2,1,0:T(8,128)}) fusion(f32[2,4,256,256]{3,2,1,0:T(8,128)} %param.5, s32[]{:T(128)S(6)} %select_n.122, s32[]{:T(128)S(6)} %select_n.132), kind=kLoop, calls=%fused_computation.61 | loop fusion | bytes 4194312 | tf_op jit(solution)/shard_map/jit(dynamic_index_in_dim)/dynamic_slice | solution.py:135
  2.8 1.4 collective-permute-start.1
  5.4 1.3 collective-permute-done.1
  6.9 1.1 dynamic-slice_bitcast_fusion.4
  8.0 2.6 %collective-permute-start.4 = (f32[256,256]{1,0:T(8,128)S(1)}, f32[256,256]{1,0:T(8,128)S(1)}, u32[]{:S(2)}, u32[]{:S(2)}) collective-permute-start(f32[256,256]{1,0:T(8,128)S(1)} %get-tuple-element.37), channel_id=1, source_target_pairs={{0,3},{1,0},{2,1},{3,2},{4,7},{5,4},{6,5},{7,6},{8,11},{9,8},{10,9... | collective-permute-start | bytes 786440 | tf_op jit(solution)/shard_map/ppermute | solution.py:16
  11.8 9.6 %collective-permute-done.4 = f32[256,256]{1,0:T(8,128)S(1)} collective-permute-done((f32[256,256]{1,0:T(8,128)S(1)}, f32[256,256]{1,0:T(8,128)S(1)}, u32[]{:S(2)}, u32[]{:S(2)}) %collective-permute-start.4) | collective-permute-done | bytes 262176 | tf_op jit(solution)/shard_map/ppermute | solution.py:16
  21.3 4.6 %collective-permute-done.2 = f32[256,256]{1,0:T(8,128)S(1)} collective-permute-done((f32[256,256]{1,0:T(8,128)S(1)}, f32[256,256]{1,0:T(8,128)S(1)}, u32[]{:S(2)}, u32[]{:S(2)}) %collective-permute-start.2) | collective-permute-done | bytes 262176 | tf_op jit(solution)/shard_map/ppermute | solution.py:16
  26.0 1.5 collective-permute-start.5
  27.5 1.3 collective-permute-start.17
  29.4 1.1 dynamic-slice_bitcast_fusion.1.own
  30.4 25.9 %collective-permute-done.17 = f32[256,256]{1,0:T(8,128)} collective-permute-done((f32[256,256]{1,0:T(8,128)S(1)}, f32[256,256]{1,0:T(8,128)}, u32[]{:S(2)}, u32[]{:S(2)}) %collective-permute-start.17) | collective-permute-done | bytes 262176 | tf_op jit(solution)/shard_map/ppermute | solution.py:16
  56.3 1.6 collective-permute-start.9
  58.0 1.6 collective-permute-start.13
  59.6 2.9 %collective-permute-done.15 = f32[256,256]{1,0:T(8,128)S(1)} collective-permute-done((f32[256,256]{1,0:T(8,128)}, f32[256,256]{1,0:T(8,128)S(1)}, u32[]{:S(2)}, u32[]{:S(2)}) %collective-permute-start.15) | collective-permute-done | bytes 262176 | tf_op jit(solution)/shard_map/ppermute | solution.py:16
  62.5 3.8 %collective-permute-start.14 = (f32[3,256,256]{2,1,0:T(8,128)S(1)}, f32[3,256,256]{2,1,0:T(8,128)}, u32[]{:S(2)}, u32[]{:S(2)}) collective-permute-start(f32[3,256,256]{2,1,0:T(8,128)S(1)} %pad_maximum_fusion.1.rest), channel_id=1, source_target_pairs={{0,96},{32,0},{64,32},{96,64},{1,97},{33,1},{65,33},{97,65},{2,98}... | collective-permute-start | bytes 2359304 | tf_op jit(solution)/shard_map/ppermute | solution.py:16
  66.3 1.6 slice_bitcast_fusion.12
  68.2 1.7 slice_bitcast_fusion.13
  69.9 1.9 slice.188
  71.7 3.0 %collective-permute-start.8 = (f32[1,520,256]{2,1,0:T(8,128)}, f32[1,520,256]{2,1,0:T(8,128)}, u32[]{:S(2)}, u32[]{:S(2)}) collective-permute-start(f32[1,520,256]{2,1,0:T(8,128)} %slice.188), channel_id=1, source_target_pairs={{0,3},{1,0},{2,1},{3,2},{4,7},{5,4},{6,5},{7,6},{8,11},{9,8},{10,9... | collective-permute-start | bytes 1597448 | tf_op jit(solution)/shard_map/ppermute | solution.py:16
  74.8 1.7 slice_bitcast_fusion.14
  76.5 1.9 slice.186
  79.0 1.3 stack.101
  80.3 1.8 pad_maximum_fusion.4.rest
  82.8 9.6 %collective-permute-done.10.own_l = f32[2,256,256]{2,1,0:T(8,128)S(1)} collective-permute-done((f32[2,256,256]{2,1,0:T(8,128)S(1)}, f32[2,256,256]{2,1,0:T(8,128)S(1)}, u32[]{:S(2)}, u32[]{:S(2)}) %collective-permute-start.10) | collective-permute-done | bytes 524320 | tf_op jit(solution)/shard_map/ppermute | solution.py:16
  93.7 1.8 slice.162
  95.5 1.2 collective-permute-start.18
  96.6 1.8 slice.163
  98.4 1.7 collective-permute-start.19
  100.1 1.2 slice_reduce_fusion
  101.4 1.2 slice_reduce_fusion.1
  102.6 1.3 stack.103
  103.9 1.3 stack.102
  105.2 1.5 collective-permute-start.12
  106.7 1.3 slice_reduce_fusion.3
  108.0 2.7 %collective-permute-start.25 = (f32[3,256,128]{2,1,0:T(8,128)}, f32[3,256,128]{2,1,0:T(8,128)}, u32[]{:S(2)}, u32[]{:S(2)}) collective-permute-start(f32[3,256,128]{2,1,0:T(8,128)} %pad_maximum_fusion.4.rest), channel_id=1, source_target_pairs={{0,96},{32,0},{64,32},{96,64},{1,97},{33,1},{65,33},{97,65},{2,98}... | collective-permute-start | bytes 1179656 | tf_op jit(solution)/shard_map/ppermute | solution.py:16
  110.6 1.2 slice_reduce_fusion.4
  111.8 1.3 concatenate.24
  113.2 1.3 concatenate.23
  114.5 1.4 convert_reduce_fusion.1
  115.8 1.3 convert_element_type.11
  117.1 2.7 %split_amp.1.a_ref = bf16[4,4,256,768]{3,2,1,0:T(8,128)(2,1)S(1)} custom-call(f32[2,520,256]{2,1,0:T(8,128)S(1)} %maximum_select_fusion.1.a_ref, f32[2,520,256]{2,1,0:T(8,128)} %collective-permute-done.5.r_ref, f32[2,520,256]{2,1,0:T(8,128)} %collective-permute-done.7.l_ref, f32[1,520,256]{2,1,0:T(8,128)} %collective-permute-done.6.fa_ref, ...), custom_call_target="tpu_custom_call" | custom-call | bytes 10485760 | tf_op jit(solution)/shard_map/split_amp/pallas_call | solution.py:51
  120.0 6.4 %contract.3 = (f32[4,2,256,256]{3,2,1,0:T(8,128)S(1)}, f32[4,2,256,256]{3,2,1,0:T(8,128)S(1)}) custom-call(s32[131]{0:T(256)S(1)} %pad_add_fusion.flag_ref, bf16[4,4,256,768]{3,2,1,0:T(8,128)(2,1)S(1)} %split_amp.1.a_ref, f32[2,256,256]{2,1,0:T(8,128)S(1)} %dynamic-slice_bitcast_fusion.1.own, f32[2,256,256]{2,1,0:T(8,128)S(1)} %collective-permute-done.9.own_r, ...), custom_call_target="tpu_custom_call" | custom-call | flops 1610612736 | bytes 8388608 | tf_op jit(solution)/shard_map/contract/pallas_call | solution.py:115
  126.4 7.0 %collective-permute-start.20 = (f32[4,2,256,256]{3,2,1,0:T(8,128)S(1)}, f32[4,2,256,256]{3,2,1,0:T(8,128)S(1)}, u32[]{:S(2)}, u32[]{:S(2)}) collective-permute-start(f32[4,2,256,256]{3,2,1,0:T(8,128)S(1)} %get-tuple-element.24), channel_id=1, source_target_pairs={{0,16},{16,0},{1,17},{17,1},{2,18},{18,2},{3,19},{19,3},{4,20},{20... | collective-permute-start | bytes 6291464 | tf_op jit(solution)/shard_map/ppermute | solution.py:16
  133.5 2.7 %collective-permute-start.33 = (f32[3,256,128]{2,1,0:T(8,128)S(1)}, f32[3,256,128]{2,1,0:T(8,128)S(1)}, u32[]{:S(2)}, u32[]{:S(2)}) collective-permute-start(f32[3,256,128]{2,1,0:T(8,128)S(1)} %pad_maximum_fusion.5.rest), channel_id=1, source_target_pairs={{0,96},{32,0},{64,32},{96,64},{1,97},{33,1},{65,33},{97,65},{2,98}... | collective-permute-start | bytes 1179656 | tf_op jit(solution)/shard_map/ppermute | solution.py:16
  136.1 0.9 slice.172
  137.2 0.9 slice.173
  138.1 2.7 %collective-permute-start.27 = (f32[3,128,128]{2,1,0:T(8,128)S(1)}, f32[3,128,128]{2,1,0:T(8,128)S(1)}, u32[]{:S(2)}, u32[]{:S(2)}) collective-permute-start(f32[3,128,128]{2,1,0:T(8,128)S(1)} %slice.173), channel_id=1, source_target_pairs={{0,96},{32,0},{64,32},{96,64},{1,97},{33,1},{65,33},{97,65},{2,98}... | collective-permute-start | bytes 589832 | tf_op jit(solution)/shard_map/ppermute | solution.py:16
  140.8 4.5 %collective-permute-done.32.rest_r = f32[3,256,128]{2,1,0:T(8,128)S(1)} collective-permute-done((f32[3,256,128]{2,1,0:T(8,128)S(1)}, f32[3,256,128]{2,1,0:T(8,128)S(1)}, u32[]{:S(2)}, u32[]{:S(2)}) %collective-permute-start.32) | collective-permute-done | bytes 393248 | tf_op jit(solution)/shard_map/ppermute | solution.py:16
  145.5 2.7 %collective-permute-start.35 = (f32[3,128,128]{2,1,0:T(8,128)S(1)}, f32[3,128,128]{2,1,0:T(8,128)S(1)}, u32[]{:S(2)}, u32[]{:S(2)}) collective-permute-start(f32[3,128,128]{2,1,0:T(8,128)S(1)} %slice.208), channel_id=1, source_target_pairs={{0,96},{32,0},{64,32},{96,64},{1,97},{33,1},{65,33},{97,65},{2,98}... | collective-permute-start | bytes 589832 | tf_op jit(solution)/shard_map/ppermute | solution.py:16
  148.2 1.4 collective-permute-done.26.rest_fa
  149.6 6.8 %contract.4 = (f32[4,2,256,128]{3,2,1,0:T(8,128)S(1)}, f32[4,2,256,128]{3,2,1,0:T(8,128)S(1)}) custom-call(s32[131]{0:T(256)S(1)} %pad_add_fusion.flag_ref, bf16[4,4,256,768]{3,2,1,0:T(8,128)(2,1)S(1)} %split_amp.1.a_ref, f32[2,256,256]{2,1,0:T(8,128)S(1)} %dynamic-slice_bitcast_fusion.1.own, f32[2,256,256]{2,1,0:T(8,128)S(1)} %collective-permute-done.9.own_r, ...), custom_call_target="tpu_custom_call" | custom-call | flops 805306368 | bytes 8388608 | tf_op jit(solution)/shard_map/contract/pallas_call | solution.py:115
  156.7 6.5 %contract.5 = (f32[4,2,256,128]{3,2,1,0:T(8,128)S(1)}, f32[4,2,256,128]{3,2,1,0:T(8,128)S(1)}) custom-call(s32[131]{0:T(256)S(1)} %pad_add_fusion.flag_ref, bf16[4,4,256,768]{3,2,1,0:T(8,128)(2,1)S(1)} %split_amp.1.a_ref, f32[2,256,256]{2,1,0:T(8,128)S(1)} %dynamic-slice_bitcast_fusion.1.own, f32[2,256,256]{2,1,0:T(8,128)S(1)} %collective-permute-done.9.own_r, ...), custom_call_target="tpu_custom_call" | custom-call | flops 805306368 | bytes 8388608 | tf_op jit(solution)/shard_map/contract/pallas_call | solution.py:115
  163.6 1.0 collective-permute-start.31
  164.6 2.2 %collective-permute-start.30 = (f32[2,256,128]{2,1,0:T(8,128)S(1)}, f32[2,256,128]{2,1,0:T(8,128)S(1)}, u32[]{:S(2)}, u32[]{:S(2)}) collective-permute-start(f32[2,256,128]{2,1,0:T(8,128)S(1)} %get-tuple-element.48), channel_id=1, source_target_pairs={{0,8},{4,12},{8,0},{12,4},{1,9},{5,13},{9,1},{13,5},{2,10},{6,14},... | collective-permute-start | bytes 786440 | tf_op jit(solution)/shard_map/ppermute | solution.py:16
  167.0 2.7 %collective-permute-start.39 = (f32[2,256,128]{2,1,0:T(8,128)S(1)}, f32[2,256,128]{2,1,0:T(8,128)S(1)}, u32[]{:S(2)}, u32[]{:S(2)}) collective-permute-start(f32[2,256,128]{2,1,0:T(8,128)S(1)} %get-tuple-element.50), channel_id=1, source_target_pairs={{0,12},{4,0},{8,4},{12,8},{1,13},{5,1},{9,5},{13,9},{2,14},{6,2},{... | collective-permute-start | bytes 786440 | tf_op jit(solution)/shard_map/ppermute | solution.py:16
  171.0 7.0 %collective-permute-start.37 = (f32[2,256,128]{2,1,0:T(8,128)S(1)}, f32[2,256,128]{2,1,0:T(8,128)S(1)}, u32[]{:S(2)}, u32[]{:S(2)}) collective-permute-start(f32[2,256,128]{2,1,0:T(8,128)S(1)} %get-tuple-element.49), channel_id=1, source_target_pairs={{0,4},{4,8},{8,12},{12,0},{1,5},{5,9},{9,13},{13,1},{2,6},{6,10},{... | collective-permute-start | bytes 786440 | tf_op jit(solution)/shard_map/ppermute | solution.py:16
  179.1 1.9 collective-permute-done.29
  181.0 1.3 collective-permute-done.39
  182.3 7.0 %collective-permute-start.21 = (f32[2,256,256]{2,1,0:T(8,128)S(1)}, f32[2,256,256]{2,1,0:T(8,128)S(1)}, u32[]{:S(2)}, u32[]{:S(2)}) collective-permute-start(f32[2,256,256]{2,1,0:T(8,128)S(1)} %get-tuple-element.33), channel_id=1, source_target_pairs={{0,4},{4,8},{8,12},{12,0},{1,5},{5,9},{9,13},{13,1},{2,6},{6,10},{... | collective-permute-start | bytes 1572872 | tf_op jit(solution)/shard_map/ppermute | solution.py:16
  189.3 2.9 %collective-permute-done.37 = f32[2,256,128]{2,1,0:T(8,128)S(1)} collective-permute-done((f32[2,256,128]{2,1,0:T(8,128)S(1)}, f32[2,256,128]{2,1,0:T(8,128)S(1)}, u32[]{:S(2)}, u32[]{:S(2)}) %collective-permute-start.37) | collective-permute-done | bytes 262176 | tf_op jit(solution)/shard_map/ppermute | solution.py:16
  192.4 6.8 %collective-permute-done.23 = f32[2,256,256]{2,1,0:T(8,128)S(1)} collective-permute-done((f32[2,256,256]{2,1,0:T(8,128)S(1)}, f32[2,256,256]{2,1,0:T(8,128)S(1)}, u32[]{:S(2)}, u32[]{:S(2)}) %collective-permute-start.23) | collective-permute-done | bytes 524320 | tf_op jit(solution)/shard_map/ppermute | solution.py:16
  199.2 2.1 collective-permute-done.22
  201.3 12.3 %collective-permute-done.21 = f32[2,256,256]{2,1,0:T(8,128)S(1)} collective-permute-done((f32[2,256,256]{2,1,0:T(8,128)S(1)}, f32[2,256,256]{2,1,0:T(8,128)S(1)}, u32[]{:S(2)}, u32[]{:S(2)}) %collective-permute-start.21) | collective-permute-done | bytes 524320 | tf_op jit(solution)/shard_map/ppermute | solution.py:16
  213.9 1.0 copy.12
  (90 shorter events, 10.0 us)
Async XLA Ops:
  0.0 4.2 %copy-start.9 = (s32[1,1,3,32]{3,1,2,0:T(1,128)S(1)}, s32[1,1,3,32]{3,1,2,0:T(1,128)}, u32[]{:S(2)}) copy-start(s32[1,1,3,32]{3,1,2,0:T(1,128)} %param.7) | copy-start | bytes 1156
  0.0 4.4 %copy-start.2 = (f32[2,2,256,256]{3,2,1,0:T(8,128)S(1)}, f32[2,2,256,256]{3,2,1,0:T(8,128)}, u32[]{:S(2)}) copy-start(f32[2,2,256,256]{3,2,1,0:T(8,128)} %param.4) | copy-start | bytes 3145732
  2.8 3.9 %collective-permute-start.1 = (f32[4,256,256]{2,1,0:T(8,128)}, f32[4,256,256]{2,1,0:T(8,128)S(1)}, u32[]{:S(2)}, u32[]{:S(2)}) collective-permute-start(f32[4,256,256]{2,1,0:T(8,128)} %get-tuple-element.43), channel_id=1, source_target_pairs={{0,16},{16,0},{1,17},{17,1},{2,18},{18,2},{3,19},{19,3},{4,20},{20... | collective-permute-start | bytes 3145736 | tf_op jit(solution)/shard_map/ppermute | solution.py:16
  5.4 6.3 %collective-permute-start = (f32[520,256]{1,0:T(8,128)}, f32[520,256]{1,0:T(8,128)S(1)}, u32[]{:S(2)}, u32[]{:S(2)}) collective-permute-start(f32[520,256]{1,0:T(8,128)} %get-tuple-element.61), channel_id=1, source_target_pairs={{0,16},{16,0},{1,17},{17,1},{2,18},{18,2},{3,19},{19,3},{4,20},{20... | collective-permute-start | bytes 1597448 | tf_op jit(solution)/shard_map/ppermute | solution.py:16
  6.9 4.8 %copy-start.1 = (f32[2,4,256,256]{3,2,1,0:T(8,128)}, f32[2,4,256,256]{3,2,1,0:T(8,128)S(1)}, u32[]{:S(2)}) copy-start(f32[2,4,256,256]{3,2,1,0:T(8,128)S(1)} %maximum_select_fusion) | copy-start | bytes 6291460
  8.0 13.4 %collective-permute-start.4 = (f32[256,256]{1,0:T(8,128)S(1)}, f32[256,256]{1,0:T(8,128)S(1)}, u32[]{:S(2)}, u32[]{:S(2)}) collective-permute-start(f32[256,256]{1,0:T(8,128)S(1)} %get-tuple-element.37), channel_id=1, source_target_pairs={{0,3},{1,0},{2,1},{3,2},{4,7},{5,4},{6,5},{7,6},{8,11},{9,8},{10,9... | collective-permute-start | bytes 786440 | tf_op jit(solution)/shard_map/ppermute | solution.py:16
  10.5 10.8 %collective-permute-start.3 = (f32[256,256]{1,0:T(8,128)S(1)}, f32[256,256]{1,0:T(8,128)S(1)}, u32[]{:S(2)}, u32[]{:S(2)}) collective-permute-start(f32[256,256]{1,0:T(8,128)S(1)} %get-tuple-element.38), channel_id=1, source_target_pairs={{0,2},{1,3},{2,0},{3,1},{4,6},{5,7},{6,4},{7,5},{8,10},{9,11},{10,... | collective-permute-start | bytes 786440 | tf_op jit(solution)/shard_map/ppermute | solution.py:16
  11.1 14.8 %collective-permute-start.2 = (f32[256,256]{1,0:T(8,128)S(1)}, f32[256,256]{1,0:T(8,128)S(1)}, u32[]{:S(2)}, u32[]{:S(2)}) collective-permute-start(f32[256,256]{1,0:T(8,128)S(1)} %get-tuple-element.39), channel_id=1, source_target_pairs={{0,1},{1,2},{2,3},{3,0},{4,5},{5,6},{6,7},{7,4},{8,9},{9,10},{10,1... | collective-permute-start | bytes 786440 | tf_op jit(solution)/shard_map/ppermute | solution.py:16
  26.0 42.0 %collective-permute-start.7 = (f32[2,520,256]{2,1,0:T(8,128)S(1)}, f32[2,520,256]{2,1,0:T(8,128)}, u32[]{:S(2)}, u32[]{:S(2)}) collective-permute-start(f32[2,520,256]{2,1,0:T(8,128)S(1)} %maximum_select_fusion.1.a_ref), channel_id=1, source_target_pairs={{0,3},{1,0},{2,1},{3,2},{4,7},{5,4},{6,5},{7,6},{8,11},{9,8},{10,9... | collective-permute-start | bytes 3194888 | tf_op jit(solution)/shard_map/ppermute | solution.py:16
  26.0 45.7 %collective-permute-start.5 = (f32[2,520,256]{2,1,0:T(8,128)S(1)}, f32[2,520,256]{2,1,0:T(8,128)}, u32[]{:S(2)}, u32[]{:S(2)}) collective-permute-start(f32[2,520,256]{2,1,0:T(8,128)S(1)} %maximum_select_fusion.1.a_ref), channel_id=1, source_target_pairs={{0,1},{1,2},{2,3},{3,0},{4,5},{5,6},{6,7},{7,4},{8,9},{9,10},{10,1... | collective-permute-start | bytes 3194888 | tf_op jit(solution)/shard_map/ppermute | solution.py:16
  27.5 28.8 %collective-permute-start.17 = (f32[256,256]{1,0:T(8,128)S(1)}, f32[256,256]{1,0:T(8,128)}, u32[]{:S(2)}, u32[]{:S(2)}) collective-permute-start(f32[256,256]{1,0:T(8,128)S(1)} %get-tuple-element.40), channel_id=1, source_target_pairs={{0,3},{1,0},{2,1},{3,2},{4,7},{5,4},{6,5},{7,6},{8,11},{9,8},{10,9... | collective-permute-start | bytes 786440 | tf_op jit(solution)/shard_map/ppermute | solution.py:16
  28.8 29.2 %collective-permute-start.16 = (f32[256,256]{1,0:T(8,128)}, f32[256,256]{1,0:T(8,128)S(1)}, u32[]{:S(2)}, u32[]{:S(2)}) collective-permute-start(f32[256,256]{1,0:T(8,128)} %get-tuple-element.41), channel_id=1, source_target_pairs={{0,2},{1,3},{2,0},{3,1},{4,6},{5,7},{6,4},{7,5},{8,10},{9,11},{10,... | collective-permute-start | bytes 786440 | tf_op jit(solution)/shard_map/ppermute | solution.py:16
  29.3 33.3 %collective-permute-start.15 = (f32[256,256]{1,0:T(8,128)}, f32[256,256]{1,0:T(8,128)S(1)}, u32[]{:S(2)}, u32[]{:S(2)}) collective-permute-start(f32[256,256]{1,0:T(8,128)} %get-tuple-element.36), channel_id=1, source_target_pairs={{0,1},{1,2},{2,3},{3,0},{4,5},{5,6},{6,7},{7,4},{8,9},{9,10},{10,1... | collective-permute-start | bytes 786440 | tf_op jit(solution)/shard_map/ppermute | solution.py:16
  56.3 22.0 %collective-permute-start.9 = (f32[2,256,256]{2,1,0:T(8,128)S(1)}, f32[2,256,256]{2,1,0:T(8,128)S(1)}, u32[]{:S(2)}, u32[]{:S(2)}) collective-permute-start(f32[2,256,256]{2,1,0:T(8,128)S(1)} %dynamic-slice_bitcast_fusion.1.own), channel_id=1, source_target_pairs={{0,32},{32,64},{64,96},{96,0},{1,33},{33,65},{65,97},{97,1},{2,34}... | collective-permute-start | bytes 1572872 | tf_op jit(solution)/shard_map/ppermute | solution.py:16
  58.0 10.0 %copy-start.7 = (f32[256,256]{1,0:T(8,128)}, f32[256,256]{1,0:T(8,128)S(1)}, u32[]{:S(2)}) copy-start(f32[256,256]{1,0:T(8,128)S(1)} %collective-permute-done.16) | copy-start | bytes 786436
  58.0 35.7 %collective-permute-start.13 = (f32[3,256,256]{2,1,0:T(8,128)S(1)}, f32[3,256,256]{2,1,0:T(8,128)}, u32[]{:S(2)}, u32[]{:S(2)}) collective-permute-start(f32[3,256,256]{2,1,0:T(8,128)S(1)} %pad_maximum_fusion.1.rest), channel_id=1, source_target_pairs={{0,32},{32,64},{64,96},{96,0},{1,33},{33,65},{65,97},{97,1},{2,34}... | collective-permute-start | bytes 2359304 | tf_op jit(solution)/shard_map/ppermute | solution.py:16
  62.5 5.4 %copy-start.6 = (f32[256,256]{1,0:T(8,128)}, f32[256,256]{1,0:T(8,128)S(1)}, u32[]{:S(2)}) copy-start(f32[256,256]{1,0:T(8,128)S(1)} %collective-permute-done.15) | copy-start | bytes 786436
  62.5 31.2 %collective-permute-start.14 = (f32[3,256,256]{2,1,0:T(8,128)S(1)}, f32[3,256,256]{2,1,0:T(8,128)}, u32[]{:S(2)}, u32[]{:S(2)}) collective-permute-start(f32[3,256,256]{2,1,0:T(8,128)S(1)} %pad_maximum_fusion.1.rest), channel_id=1, source_target_pairs={{0,96},{32,0},{64,32},{96,64},{1,97},{33,1},{65,33},{97,65},{2,98}... | collective-permute-start | bytes 2359304 | tf_op jit(solution)/shard_map/ppermute | solution.py:16
  67.9 24.5 %collective-permute-start.10 = (f32[2,256,256]{2,1,0:T(8,128)S(1)}, f32[2,256,256]{2,1,0:T(8,128)S(1)}, u32[]{:S(2)}, u32[]{:S(2)}) collective-permute-start(f32[2,256,256]{2,1,0:T(8,128)S(1)} %dynamic-slice_bitcast_fusion.1.own), channel_id=1, source_target_pairs={{0,96},{32,0},{64,32},{96,64},{1,97},{33,1},{65,33},{97,65},{2,98}... | collective-permute-start | bytes 1572872 | tf_op jit(solution)/shard_map/ppermute | solution.py:16
  71.7 33.5 %collective-permute-start.8 = (f32[1,520,256]{2,1,0:T(8,128)}, f32[1,520,256]{2,1,0:T(8,128)}, u32[]{:S(2)}, u32[]{:S(2)}) collective-permute-start(f32[1,520,256]{2,1,0:T(8,128)} %slice.188), channel_id=1, source_target_pairs={{0,3},{1,0},{2,1},{3,2},{4,7},{5,4},{6,5},{7,6},{8,11},{9,8},{10,9... | collective-permute-start | bytes 1597448 | tf_op jit(solution)/shard_map/ppermute | solution.py:16
  78.4 29.6 %collective-permute-start.6 = (f32[1,520,256]{2,1,0:T(8,128)}, f32[1,520,256]{2,1,0:T(8,128)}, u32[]{:S(2)}, u32[]{:S(2)}) collective-permute-start(f32[1,520,256]{2,1,0:T(8,128)} %slice.186), channel_id=1, source_target_pairs={{0,1},{1,2},{2,3},{3,0},{4,5},{5,6},{6,7},{7,4},{8,9},{9,10},{10,1... | collective-permute-start | bytes 1597448 | tf_op jit(solution)/shard_map/ppermute | solution.py:16
  92.4 15.5 %collective-permute-start.11 = (f32[2,128,256]{2,1,0:T(8,128)}, f32[2,128,256]{2,1,0:T(8,128)}, u32[]{:S(2)}, u32[]{:S(2)}) collective-permute-start(f32[2,128,256]{2,1,0:T(8,128)} %slice.191), channel_id=1, source_target_pairs={{0,32},{32,64},{64,96},{96,0},{1,33},{33,65},{65,97},{97,1},{2,34}... | collective-permute-start | bytes 786440 | tf_op jit(solution)/shard_map/ppermute | solution.py:16
  95.5 24.5 %collective-permute-start.18 = (f32[3,128,256]{2,1,0:T(8,128)}, f32[3,128,256]{2,1,0:T(8,128)}, u32[]{:S(2)}, u32[]{:S(2)}) collective-permute-start(f32[3,128,256]{2,1,0:T(8,128)} %slice.162), channel_id=1, source_target_pairs={{0,32},{32,64},{64,96},{96,0},{1,33},{33,65},{65,97},{97,1},{2,34}... | collective-permute-start | bytes 1179656 | tf_op jit(solution)/shard_map/ppermute | solution.py:16
  98.4 21.5 %collective-permute-start.19 = (f32[3,128,256]{2,1,0:T(8,128)}, f32[3,128,256]{2,1,0:T(8,128)}, u32[]{:S(2)}, u32[]{:S(2)}) collective-permute-start(f32[3,128,256]{2,1,0:T(8,128)} %slice.163), channel_id=1, source_target_pairs={{0,96},{32,0},{64,32},{96,64},{1,97},{33,1},{65,33},{97,65},{2,98}... | collective-permute-start | bytes 1179656 | tf_op jit(solution)/shard_map/ppermute | solution.py:16
  105.2 14.7 %collective-permute-start.12 = (f32[2,128,256]{2,1,0:T(8,128)}, f32[2,128,256]{2,1,0:T(8,128)}, u32[]{:S(2)}, u32[]{:S(2)}) collective-permute-start(f32[2,128,256]{2,1,0:T(8,128)} %slice.192), channel_id=1, source_target_pairs={{0,96},{32,0},{64,32},{96,64},{1,97},{33,1},{65,33},{97,65},{2,98}... | collective-permute-start | bytes 786440 | tf_op jit(solution)/shard_map/ppermute | solution.py:16
  107.9 25.4 %collective-permute-start.24 = (f32[3,256,128]{2,1,0:T(8,128)}, f32[3,256,128]{2,1,0:T(8,128)}, u32[]{:S(2)}, u32[]{:S(2)}) collective-permute-start(f32[3,256,128]{2,1,0:T(8,128)} %pad_maximum_fusion.4.rest), channel_id=1, source_target_pairs={{0,32},{32,64},{64,96},{96,0},{1,33},{33,65},{65,97},{97,1},{2,34}... | collective-permute-start | bytes 1179656 | tf_op jit(solution)/shard_map/ppermute | solution.py:16
  108.0 25.4 %collective-permute-start.25 = (f32[3,256,128]{2,1,0:T(8,128)}, f32[3,256,128]{2,1,0:T(8,128)}, u32[]{:S(2)}, u32[]{:S(2)}) collective-permute-start(f32[3,256,128]{2,1,0:T(8,128)} %pad_maximum_fusion.4.rest), channel_id=1, source_target_pairs={{0,96},{32,0},{64,32},{96,64},{1,97},{33,1},{65,33},{97,65},{2,98}... | collective-permute-start | bytes 1179656 | tf_op jit(solution)/shard_map/ppermute | solution.py:16
  117.1 2.7 %copy-start.8 = (s32[128]{0:T(128)S(1)}, s32[128]{0:T(128)}, u32[]{:S(2)}) copy-start(s32[128]{0:T(128)} %convert_element_type.11) | copy-start | bytes 1540
  119.9 13.4 %copy-start.4 = (f32[1,256,128]{2,1,0:T(8,128)S(1)}, f32[1,256,128]{2,1,0:T(8,128)}, u32[]{:S(2)}) copy-start(f32[1,256,128]{2,1,0:T(8,128)} %get-tuple-element.56) | copy-start | bytes 393220
  119.9 13.4 %copy-start.5 = (f32[1,256,128]{2,1,0:T(8,128)S(1)}, f32[1,256,128]{2,1,0:T(8,128)}, u32[]{:S(2)}) copy-start(f32[1,256,128]{2,1,0:T(8,128)} %get-tuple-element.54) | copy-start | bytes 393220
  126.4 23.2 %copy-start = (f32[3,256,128]{2,1,0:T(8,128)S(1)}, f32[3,256,128]{2,1,0:T(8,128)}, u32[]{:S(2)}) copy-start(f32[3,256,128]{2,1,0:T(8,128)} %pad_maximum_fusion.4.rest) | copy-start | bytes 1179652
  126.4 43.4 %collective-permute-start.20 = (f32[4,2,256,256]{3,2,1,0:T(8,128)S(1)}, f32[4,2,256,256]{3,2,1,0:T(8,128)S(1)}, u32[]{:S(2)}, u32[]{:S(2)}) collective-permute-start(f32[4,2,256,256]{3,2,1,0:T(8,128)S(1)} %get-tuple-element.24), channel_id=1, source_target_pairs={{0,16},{16,0},{1,17},{17,1},{2,18},{18,2},{3,19},{19,3},{4,20},{20... | collective-permute-start | bytes 6291464 | tf_op jit(solution)/shard_map/ppermute | solution.py:16
  133.4 12.0 %collective-permute-start.32 = (f32[3,256,128]{2,1,0:T(8,128)S(1)}, f32[3,256,128]{2,1,0:T(8,128)S(1)}, u32[]{:S(2)}, u32[]{:S(2)}) collective-permute-start(f32[3,256,128]{2,1,0:T(8,128)S(1)} %pad_maximum_fusion.5.rest), channel_id=1, source_target_pairs={{0,32},{32,64},{64,96},{96,0},{1,33},{33,65},{65,97},{97,1},{2,34}... | collective-permute-start | bytes 1179656 | tf_op jit(solution)/shard_map/ppermute | solution.py:16
  133.5 12.0 %collective-permute-start.33 = (f32[3,256,128]{2,1,0:T(8,128)S(1)}, f32[3,256,128]{2,1,0:T(8,128)S(1)}, u32[]{:S(2)}, u32[]{:S(2)}) collective-permute-start(f32[3,256,128]{2,1,0:T(8,128)S(1)} %pad_maximum_fusion.5.rest), channel_id=1, source_target_pairs={{0,96},{32,0},{64,32},{96,64},{1,97},{33,1},{65,33},{97,65},{2,98}... | collective-permute-start | bytes 1179656 | tf_op jit(solution)/shard_map/ppermute | solution.py:16
  137.1 12.5 %collective-permute-start.26 = (f32[3,128,128]{2,1,0:T(8,128)S(1)}, f32[3,128,128]{2,1,0:T(8,128)S(1)}, u32[]{:S(2)}, u32[]{:S(2)}) collective-permute-start(f32[3,128,128]{2,1,0:T(8,128)S(1)} %slice.172), channel_id=1, source_target_pairs={{0,32},{32,64},{64,96},{96,0},{1,33},{33,65},{65,97},{97,1},{2,34}... | collective-permute-start | bytes 589832 | tf_op jit(solution)/shard_map/ppermute | solution.py:16
  138.1 11.5 %collective-permute-start.27 = (f32[3,128,128]{2,1,0:T(8,128)S(1)}, f32[3,128,128]{2,1,0:T(8,128)S(1)}, u32[]{:S(2)}, u32[]{:S(2)}) collective-permute-start(f32[3,128,128]{2,1,0:T(8,128)S(1)} %slice.173), channel_id=1, source_target_pairs={{0,96},{32,0},{64,32},{96,64},{1,97},{33,1},{65,33},{97,65},{2,98}... | collective-permute-start | bytes 589832 | tf_op jit(solution)/shard_map/ppermute | solution.py:16
  145.4 11.3 %collective-permute-start.34 = (f32[3,128,128]{2,1,0:T(8,128)S(1)}, f32[3,128,128]{2,1,0:T(8,128)S(1)}, u32[]{:S(2)}, u32[]{:S(2)}) collective-permute-start(f32[3,128,128]{2,1,0:T(8,128)S(1)} %slice.207), channel_id=1, source_target_pairs={{0,32},{32,64},{64,96},{96,0},{1,33},{33,65},{65,97},{97,1},{2,34}... | collective-permute-start | bytes 589832 | tf_op jit(solution)/shard_map/ppermute | solution.py:16
  145.5 11.2 %collective-permute-start.35 = (f32[3,128,128]{2,1,0:T(8,128)S(1)}, f32[3,128,128]{2,1,0:T(8,128)S(1)}, u32[]{:S(2)}, u32[]{:S(2)}) collective-permute-start(f32[3,128,128]{2,1,0:T(8,128)S(1)} %slice.208), channel_id=1, source_target_pairs={{0,96},{32,0},{64,32},{96,64},{1,97},{33,1},{65,33},{97,65},{2,98}... | collective-permute-start | bytes 589832 | tf_op jit(solution)/shard_map/ppermute | solution.py:16
  156.4 7.0 %collective-permute-start.28 = (f32[4,2,256,128]{3,2,1,0:T(8,128)S(1)}, f32[4,2,256,128]{3,2,1,0:T(8,128)S(1)}, u32[]{:S(2)}, u32[]{:S(2)}) collective-permute-start(f32[4,2,256,128]{3,2,1,0:T(8,128)S(1)} %get-tuple-element.29), channel_id=1, source_target_pairs={{0,16},{16,0},{1,17},{17,1},{2,18},{18,2},{3,19},{19,3},{4,20},{20... | collective-permute-start | bytes 3145736 | tf_op jit(solution)/shard_map/ppermute | solution.py:16
  163.3 3.5 %collective-permute-start.36 = (f32[4,2,256,128]{3,2,1,0:T(8,128)S(1)}, f32[4,2,256,128]{3,2,1,0:T(8,128)S(1)}, u32[]{:S(2)}, u32[]{:S(2)}) collective-permute-start(f32[4,2,256,128]{3,2,1,0:T(8,128)S(1)} %get-tuple-element.32), channel_id=1, source_target_pairs={{0,16},{16,0},{1,17},{17,1},{2,18},{18,2},{3,19},{19,3},{4,20},{20... | collective-permute-start | bytes 3145736 | tf_op jit(solution)/shard_map/ppermute | solution.py:16
  163.6 7.5 %collective-permute-start.31 = (f32[2,256,128]{2,1,0:T(8,128)S(1)}, f32[2,256,128]{2,1,0:T(8,128)S(1)}, u32[]{:S(2)}, u32[]{:S(2)}) collective-permute-start(f32[2,256,128]{2,1,0:T(8,128)S(1)} %get-tuple-element.47), channel_id=1, source_target_pairs={{0,12},{4,0},{8,4},{12,8},{1,13},{5,1},{9,5},{13,9},{2,14},{6,2},{... | collective-permute-start | bytes 786440 | tf_op jit(solution)/shard_map/ppermute | solution.py:16
  164.6 13.7 %collective-permute-start.30 = (f32[2,256,128]{2,1,0:T(8,128)S(1)}, f32[2,256,128]{2,1,0:T(8,128)S(1)}, u32[]{:S(2)}, u32[]{:S(2)}) collective-permute-start(f32[2,256,128]{2,1,0:T(8,128)S(1)} %get-tuple-element.48), channel_id=1, source_target_pairs={{0,8},{4,12},{8,0},{12,4},{1,9},{5,13},{9,1},{13,5},{2,10},{6,14},... | collective-permute-start | bytes 786440 | tf_op jit(solution)/shard_map/ppermute | solution.py:16
  166.8 14.2 %collective-permute-start.29 = (f32[2,256,128]{2,1,0:T(8,128)S(1)}, f32[2,256,128]{2,1,0:T(8,128)S(1)}, u32[]{:S(2)}, u32[]{:S(2)}) collective-permute-start(f32[2,256,128]{2,1,0:T(8,128)S(1)} %get-tuple-element.46), channel_id=1, source_target_pairs={{0,4},{4,8},{8,12},{12,0},{1,5},{5,9},{9,13},{13,1},{2,6},{6,10},{... | collective-permute-start | bytes 786440 | tf_op jit(solution)/shard_map/ppermute | solution.py:16
  167.0 15.3 %collective-permute-start.39 = (f32[2,256,128]{2,1,0:T(8,128)S(1)}, f32[2,256,128]{2,1,0:T(8,128)S(1)}, u32[]{:S(2)}, u32[]{:S(2)}) collective-permute-start(f32[2,256,128]{2,1,0:T(8,128)S(1)} %get-tuple-element.50), channel_id=1, source_target_pairs={{0,12},{4,0},{8,4},{12,8},{1,13},{5,1},{9,5},{13,9},{2,14},{6,2},{... | collective-permute-start | bytes 786440 | tf_op jit(solution)/shard_map/ppermute | solution.py:16
  169.7 19.5 %collective-permute-start.38 = (f32[2,256,128]{2,1,0:T(8,128)S(1)}, f32[2,256,128]{2,1,0:T(8,128)S(1)}, u32[]{:S(2)}, u32[]{:S(2)}) collective-permute-start(f32[2,256,128]{2,1,0:T(8,128)S(1)} %get-tuple-element.51), channel_id=1, source_target_pairs={{0,8},{4,12},{8,0},{12,4},{1,9},{5,13},{9,1},{13,5},{2,10},{6,14},... | collective-permute-start | bytes 786440 | tf_op jit(solution)/shard_map/ppermute | solution.py:16
  170.1 22.1 %copy-start.3 = (f32[2,2,256,256]{3,2,1,0:T(8,128)S(1)}, f32[2,2,256,256]{3,2,1,0:T(8,128)}, u32[]{:S(2)}) copy-start(f32[2,2,256,256]{3,2,1,0:T(8,128)} %param.6) | copy-start | bytes 3145732
  171.0 21.2 %collective-permute-start.37 = (f32[2,256,128]{2,1,0:T(8,128)S(1)}, f32[2,256,128]{2,1,0:T(8,128)S(1)}, u32[]{:S(2)}, u32[]{:S(2)}) collective-permute-start(f32[2,256,128]{2,1,0:T(8,128)S(1)} %get-tuple-element.49), channel_id=1, source_target_pairs={{0,4},{4,8},{8,12},{12,0},{1,5},{5,9},{9,13},{13,1},{2,6},{6,10},{... | collective-permute-start | bytes 786440 | tf_op jit(solution)/shard_map/ppermute | solution.py:16
  178.3 20.9 %collective-permute-start.23 = (f32[2,256,256]{2,1,0:T(8,128)S(1)}, f32[2,256,256]{2,1,0:T(8,128)S(1)}, u32[]{:S(2)}, u32[]{:S(2)}) collective-permute-start(f32[2,256,256]{2,1,0:T(8,128)S(1)} %get-tuple-element.34), channel_id=1, source_target_pairs={{0,12},{4,0},{8,4},{12,8},{1,13},{5,1},{9,5},{13,9},{2,14},{6,2},{... | collective-permute-start | bytes 1572872 | tf_op jit(solution)/shard_map/ppermute | solution.py:16
  181.0 20.3 %collective-permute-start.22 = (f32[2,256,256]{2,1,0:T(8,128)S(1)}, f32[2,256,256]{2,1,0:T(8,128)S(1)}, u32[]{:S(2)}, u32[]{:S(2)}) collective-permute-start(f32[2,256,256]{2,1,0:T(8,128)S(1)} %get-tuple-element.35), channel_id=1, source_target_pairs={{0,8},{4,12},{8,0},{12,4},{1,9},{5,13},{9,1},{13,5},{2,10},{6,14},... | collective-permute-start | bytes 1572872 | tf_op jit(solution)/shard_map/ppermute | solution.py:16
  182.3 31.3 %collective-permute-start.21 = (f32[2,256,256]{2,1,0:T(8,128)S(1)}, f32[2,256,256]{2,1,0:T(8,128)S(1)}, u32[]{:S(2)}, u32[]{:S(2)}) collective-permute-start(f32[2,256,256]{2,1,0:T(8,128)S(1)} %get-tuple-element.33), channel_id=1, source_target_pairs={{0,4},{4,8},{8,12},{12,0},{1,5},{5,9},{9,13},{13,1},{2,6},{6,10},{... | collective-permute-start | bytes 1572872 | tf_op jit(solution)/shard_map/ppermute | solution.py:16

commit v4 on v3

v4 whole, which is shorter than its diff:
```python
import jax
import jax.numpy as jnp
from jax import lax
from jax.experimental import pallas as pl
from jax.experimental.pallas import tpu as pltpu
from jax.sharding import Mesh, PartitionSpec as P

NAMES = ("z", "c", "y", "x")
SIZE = {"z": 4, "c": 2, "y": 4, "x": 4}
MIB = 1024 * 1024
CHUNKS = ((0, (0,)), (0, (1,)), (1, (0, 1)))


def shift(t, axis, s):
    n = SIZE[axis]
    return lax.ppermute(t, axis, [(i, (i + s) % n) for i in range(n)])


def halves(a):
    hi = a.astype(jnp.bfloat16)
    return hi, (a - hi.astype(jnp.float32)).astype(jnp.bfloat16)


def split_kernel(a_ref, o_ref):
    w = a_ref.shape[-1]
    for c in range(2):
        hi, lo = halves(a_ref[0, c, :w])
        o_ref[0, c, :, :w] = hi
        o_ref[0, c, :, w : 2 * w] = lo
        o_ref[0, c, :, 2 * w :] = hi


def split_amp(a):
    rows, w = a.shape[2:]
    return pl.pallas_call(
        split_kernel,
        grid=(4,),
        in_specs=[pl.BlockSpec((1, 2, rows, w), lambda g: (g, 0, 0, 0))],
        out_specs=pl.BlockSpec((1, 2, w, 3 * w), lambda g: (g, 0, 0, 0)),
        out_shape=jax.ShapeDtypeStruct((4, 2, w, 3 * w), jnp.bfloat16),
        compiler_params=pltpu.CompilerParams(vmem_limit_bytes=8 * MIB),
        cost_estimate=pl.CostEstimate(flops=0, bytes_accessed=5 * MIB, transcendentals=0),
        name="split_amp",
    )(a)


def make_contract_kernel(kp, rows):
    def kernel(flag_ref, *refs):
        amps, refs = refs[: len(rows)], refs[len(rows) :]
        own, own_r, own_l, rest, two_r, two_l, fa, fb, mine_ref, other_ref, b_ref = refs
        w = amps[0].shape[2]
        h = w // 2

        def load(s, b, at=0):
            n = b.shape[0]
            hi, lo = halves(b)
            b_ref[s, at : at + n] = hi
            b_ref[s, w + at : w + at + n] = hi
            b_ref[s, 2 * w + at : 2 * w + at + n] = lo

        z, c, x = flag_ref[128], flag_ref[129], flag_ref[130]

        @pl.loop(0, 4)
        def _(step):
            ka = lax.rem(z + jnp.where(step == 1, 3, jnp.where(step == 2, 1, jnp.where(step == 3, 2, 0))), 4)
            for at, (mine, others) in enumerate(((own, rest), (own_r, two_r), (own_l, two_l))):
                @pl.when(step == at)
                def _():
                    load(0, mine[kp])
                    for s in range(3):
                        load(s + 1, others[s])

            @pl.when(step == 3)
            def _():
                for part, ref in enumerate((fa, fb)):
                    for s in range(4):
                        load(s, ref[s], part * h)

            for out, core in ((mine_ref, c), (other_ref, 1 - c)):
                for n, il in enumerate(rows):
                    out[ka, n] = jnp.zeros((w, w), jnp.float32)
                    for s in range(4):
                        jx = lax.rem(x + s, 4)

                        @pl.when(flag_ref[(jx * 2 + core) * 16 + kp * 8 + ka * 2 + il] != 0)
                        def _():
                            out[ka, n] += jnp.dot(amps[n][jx, core], b_ref[s], preferred_element_type=jnp.float32)

    return kernel


def contract(chunk, flags, amps, pieces):
    kp, rows = chunk
    w = amps[0].shape[2]
    inside = pl.BlockSpec(memory_space=pltpu.VMEM)
    out = jax.ShapeDtypeStruct((4, len(rows), w, w), jnp.float32)
    return pl.pallas_call(
        make_contract_kernel(kp, rows),
        in_specs=[pl.BlockSpec(memory_space=pltpu.SMEM)] + [inside] * (len(amps) + len(pieces)),
        out_specs=[inside, inside],
        scratch_shapes=[pltpu.VMEM((4, 3 * w, w), jnp.bfloat16)],
        out_shape=[out, out],
        compiler_params=pltpu.CompilerParams(vmem_limit_bytes=28 * MIB),
        cost_estimate=pl.CostEstimate(flops=16 * 6 * w**3, bytes_accessed=8 * MIB, transcendentals=0),
        name="contract",
    )(flags, *amps, *pieces)


def on_device(amp, integ, resid, triples):
    w = amp.shape[-1]
    h = w // 2
    z, c, y, x = (lax.axis_index(n) for n in NAMES)

    def joined(mine, other):
        return jnp.where(c == 0, jnp.stack([mine, other]), jnp.stack([other, mine]))

    mine = lax.dynamic_index_in_dim(integ, c, 0, keepdims=False)
    other = shift(lax.dynamic_index_in_dim(integ, 1 - c, 0, keepdims=False), "c", 1)
    pairs = joined(mine, other).reshape(4, 2, w, w)
    own = lax.dynamic_index_in_dim(pairs, x, 0, keepdims=False)
    own_r, own_l = shift(own, "z", 1), shift(own, "z", -1)

    def others(kp):
        held = lax.all_to_all(pairs[:, kp], "x", 0, 0, tiled=True)
        return lax.dynamic_slice_in_dim(jnp.concatenate([held, held]), x + 1, 3, 0)

    rest = [others(0), others(1)]

    tri = triples[0, 0]
    i = tri[0] // 32
    j = tri[0] % 32
    k = tri[1] % 32
    slot = (((j % 2 * 4 + (k // 2) % 4) * 2 + k % 2) * 4 + k // 8) * 2 + i % 2
    place = lax.broadcasted_iota(jnp.int32, (32, w), 1)
    listed = jnp.sum((place == slot[:, None]).astype(jnp.float32), axis=0, keepdims=True)
    listed = jnp.broadcast_to(listed, (8, w))

    def with_flags(parity):
        tile = lax.dynamic_index_in_dim(amp, parity, 1, keepdims=False)
        return jnp.concatenate([tile, jnp.broadcast_to(listed[None], (2, 8, w))], axis=1)

    a0 = joined(with_flags(c), shift(with_flags(1 - c), "c", 1))
    gathered = [lax.all_gather(a0[:, il], "x") for il in range(2)]
    amps = [split_amp(g) for g in gathered]
    flags = gathered[0][:, :, w, :128].reshape(4, 2, 8, 16)
    flags = lax.dynamic_index_in_dim(flags, c * 4 + x, 2, keepdims=False)
    flags = jnp.concatenate([flags.reshape(-1).astype(jnp.int32), jnp.stack([z, c, x])])

    two_r = shift(jnp.concatenate([rest[0], own_r[:, :h].reshape(1, w, w)]), "z", 1)
    two_l = shift(jnp.concatenate([rest[0], own_l[:, h:].reshape(1, w, w)]), "z", -1)
    two_r, two_l, rest[1] = lax.optimization_barrier((two_r, two_l, rest[1]))
    far0 = shift(two_r[:3, :h], "z", 1), shift(two_l[:3, h:], "z", -1)
    rest1_r, rest1_l = shift(rest[1], "z", 1), shift(rest[1], "z", -1)
    far1 = shift(rest1_r[:, :h], "z", 1), shift(rest1_l[:, h:], "z", -1)
    own_fa, own_fb = two_r[3].reshape(2, h, w), two_l[3].reshape(2, h, w)

    def far(kp, fa, fb):
        return jnp.concatenate([own_fa[kp : kp + 1], fa]), jnp.concatenate([own_fb[kp : kp + 1], fb])

    pieces = ((rest[0], two_r, two_l) + far(0, *far0), (rest[1], rest1_r, rest1_l) + far(1, *far1))
    sums = []
    for kp, rows in CHUNKS:
        held, away = contract((kp, rows), flags, [amps[il] for il in rows], (own, own_r, own_l) + pieces[kp])
        part = held + shift(away, "c", 1)
        part, flags = lax.optimization_barrier((part, flags))
        part = lax.all_to_all(part, "y", 0, 0, tiled=True)
        sums.append(part[0] + part[1] + part[2] + part[3])
    return resid + jnp.stack([jnp.concatenate(sums[:2]), sums[2]], axis=1)


def solution(mesh):
    fine = Mesh(mesh.devices.reshape(4, 2, 4, 4), NAMES)
    row, col = ("z", "c"), ("y", "x")
    return jax.shard_map(
        on_device,
        mesh=fine,
        in_specs=(P(row, col), P(col, row), P(row, col), P(row, col)),
        out_specs=P(row, col),
        check_vma=False,
    )
```

time: 217 us -> 235 us (1.083)
  blocking collectives: 0 us -> 34.9 us
  starting transfers between devices: 62.8 us -> 40.6 us
  between operations: 0.37 us -> 13.9 us
  local copies, waits for them, and re-layouts: 35.5 us -> 25.3 us
  other arithmetic: 5.69 us -> 15.3 us
  Pallas kernels: 22.5 us -> 17.1 us
  waiting for transfers between devices: 88.1 us -> 85.3 us
    ppermute x40 -> x15, waiting for transfers between devices: 88.1 us -> 45.6 us  [shift(): return lax.ppermute(t, axis, [(i, (i + s) % n) for i in range(n)])]
    all_to_all x0 -> x3, waiting for transfers between devices: none -> 39.6 us  [the longest x2 33.4 us: on_device(): part = lax.all_to_all(part, 'y', 0, 0, tiled=True)]
    all_to_all x0 -> x2, blocking collectives: none -> 34.9 us  [the longest x1 21 us: on_device(): part = lax.all_to_all(part, 'y', 0, 0, tiled=True)]
    ppermute x40 -> x15, starting transfers between devices: 62.8 us -> 28.4 us  [shift(): return lax.ppermute(t, axis, [(i, (i + s) % n) for i in range(n)])]
    unnamed x20 -> x62, local copies, waits for them, and re-layouts: 0.04 us -> 17 us
    slice x15 -> x9, local copies, waits for them, and re-layouts: 16.3 us -> 4.09 us  [the longest x2 2.04 us: on_device(): far1 = (shift(rest1_r[:, :h], 'z', 1), shift(rest1_l[:, h:], 'z', -1))]
    all_to_all x0 -> x3, starting transfers between devices: none -> 12.1 us  [the longest x2 7.87 us: on_device(): part = lax.all_to_all(part, 'y', 0, 0, tiled=True)]
    another operation x7 -> x2, local copies, waits for them, and re-layouts: 9.98 us -> 0.08 us  [the longest x1 0.08 us: on_device(): flags = gathered[0][:, :, w, :128].reshape(4, 2, 8, 16)]
  transfers between devices with their start and end apart: 40 -> 20, of which waited for: 15 -> 12; matrix products, arithmetic and copies ran while one was open for 17% -> 8% of each run, Pallas kernels for 10% -> 4%
where the time goes in v4:
time: 235 us; the launch traced here: 232 us
  waiting for transfers between devices  85.3 us (36%)
  starting transfers between devices  40.6 us (17%)
  blocking collectives  34.9 us (15%)
  local copies, waits for them, and re-layouts  25.3 us (11%)
  Pallas kernels  17.1 us (7%)
  other arithmetic  15.3 us (7%)
  between operations  13.9 us (6%)
    ppermute x15, waiting for transfers between devices, shift(): return lax.ppermute(t, axis, [(i, (i + s) % n) for i in range(n)])  45.6 us
    all_to_all x2, waiting for transfers between devices, on_device(): part = lax.all_to_all(part, 'y', 0, 0, tiled=True)  33.4 us
    ppermute x15, starting transfers between devices, shift(): return lax.ppermute(t, axis, [(i, (i + s) % n) for i in range(n)])  28.4 us
    all_to_all x1, blocking collectives, on_device(): part = lax.all_to_all(part, 'y', 0, 0, tiled=True)  21 us
    unnamed x62, local copies, waits for them, and re-layouts  17 us
    pallas_call x3, Pallas kernels, contract(): pl.pallas_call(make_contract_kernel(kp, rows), in_specs=[pl.BlockSpec(mem...  16.2 us
    all_to_all x1, blocking collectives, others(): held = lax.all_to_all(pairs[:, kp], 'x', 0, 0, tiled=True)  13.9 us
    all_to_all x2, starting transfers between devices, on_device(): part = lax.all_to_all(part, 'y', 0, 0, tiled=True)  7.87 us
  transfers between devices with their start and end apart: 20, of which 12 were waited for; matrix products, arithmetic and copies ran while one was open for 8% of the time, Pallas kernels for 4%

profile of v4, /device:TPU:1, one launch (start us, length us, event | category | flops | bytes accessed | tf_op | source)
XLA Modules:
  0.0 232.4 jit_solution(2667270529966887740)
XLA Ops:
  6.5 0.7 fusion.8
  7.3 1.3 dynamic-slice_bitcast_fusion.3
  8.7 1.5 collective-permute-start
  10.2 1.6 collective-permute-done
  11.9 1.1 fusion.14
  13.1 0.7 copy-done.29
  13.9 0.5 collective-permute-start.1
  14.4 2.3 collective-permute-done.1
  16.9 1.6 slice_bitcast_fusion
  18.4 4.3 %all-to-all-start = ((f32[4,256,256]{2,1,0:T(8,128)}), f32[4,256,256]{2,1,0:T(8,128)}, u32[]{:S(2)}, u32[]{:S(2)}) async-start(f32[4,256,256]{2,1,0:T(8,128)} %get-tuple-element.34), calls=%async_computation | async-start | bytes 2097152 | tf_op jit(solution)/shard_map/all_to_all | solution.py:124
  22.8 1.8 collective-permute-start.2
  24.6 2.2 collective-permute-start.3
  26.8 12.0 %collective-permute-done.2.refs_2_.refs_3_ = f32[2,256,256]{2,1,0:T(8,128)S(1)} collective-permute-done((f32[2,256,256]{2,1,0:T(8,128)S(1)}, f32[2,256,256]{2,1,0:T(8,128)S(1)}, u32[]{:S(2)}, u32[]{:S(2)}) %collective-permute-start.2) | collective-permute-done | bytes 524320 | tf_op jit(solution)/shard_map/ppermute | solution.py:16
  38.9 6.2 %all-to-all-done = f32[4,256,256]{2,1,0:T(8,128)} async-done(((f32[4,256,256]{2,1,0:T(8,128)}), f32[4,256,256]{2,1,0:T(8,128)}, u32[]{:S(2)}, u32[]{:S(2)}) %all-to-all-start) | async-done | bytes 1048608 | tf_op jit(solution)/shard_map/all_to_all | solution.py:124
  45.1 1.2 fusion.1.refs_4_
  46.6 2.5 %collective-permute-start.4 = (f32[4,256,256]{2,1,0:T(8,128)S(1)}, f32[4,256,256]{2,1,0:T(8,128)S(1)}, u32[]{:S(2)}, u32[]{:S(2)}) collective-permute-start(f32[4,256,256]{2,1,0:T(8,128)S(1)} %get-tuple-element.46), channel_id=1, source_target_pairs={{0,32},{32,64},{64,96},{96,0},{1,33},{33,65},{65,97},{97,1},{2,34}... | collective-permute-start | bytes 3145736 | tf_op jit(solution)/shard_map/ppermute | solution.py:16
  49.1 2.9 %collective-permute-start.5 = (f32[4,256,256]{2,1,0:T(8,128)S(1)}, f32[4,256,256]{2,1,0:T(8,128)S(1)}, u32[]{:S(2)}, u32[]{:S(2)}) collective-permute-start(f32[4,256,256]{2,1,0:T(8,128)S(1)} %get-tuple-element.45), channel_id=1, source_target_pairs={{0,96},{32,0},{64,32},{96,64},{1,97},{33,1},{65,33},{97,65},{2,98}... | collective-permute-start | bytes 3145736 | tf_op jit(solution)/shard_map/ppermute | solution.py:16
  52.0 13.9 %all_to_all.25 = f32[4,256,256]{2,1,0:T(8,128)S(1)} all-to-all(f32[4,256,256]{2,1,0:T(8,128)S(1)} %copy-done.28), channel_id=1, replica_groups=mesh['z'=4,'c'=2,'y'=4,'x'=4] {'x'}, dimensions={0} | all-to-all | bytes 2097152 | tf_op jit(solution)/shard_map/all_to_all | solution.py:124
  65.9 1.0 fusion.refs_5_
  66.9 5.4 %collective-permute-done.4.refs_5_ = f32[4,256,256]{2,1,0:T(8,128)S(1)} collective-permute-done((f32[4,256,256]{2,1,0:T(8,128)S(1)}, f32[4,256,256]{2,1,0:T(8,128)S(1)}, u32[]{:S(2)}, u32[]{:S(2)}) %collective-permute-start.4) | collective-permute-done | bytes 1048608 | tf_op jit(solution)/shard_map/ppermute | solution.py:16
  72.4 2.5 %collective-permute-start.7 = (f32[3,128,256]{2,1,0:T(8,128)S(1)}, f32[3,128,256]{2,1,0:T(8,128)}, u32[]{:S(2)}, u32[]{:S(2)}) collective-permute-start(f32[3,128,256]{2,1,0:T(8,128)S(1)} %slice.111), channel_id=1, source_target_pairs={{0,96},{32,0},{64,32},{96,64},{1,97},{33,1},{65,33},{97,65},{2,98}... | collective-permute-start | bytes 1179656 | tf_op jit(solution)/shard_map/ppermute | solution.py:16
  75.1 4.6 %collective-permute-done.7 = f32[3,128,256]{2,1,0:T(8,128)} collective-permute-done((f32[3,128,256]{2,1,0:T(8,128)S(1)}, f32[3,128,256]{2,1,0:T(8,128)}, u32[]{:S(2)}, u32[]{:S(2)}) %collective-permute-start.7) | collective-permute-done | bytes 393248 | tf_op jit(solution)/shard_map/ppermute | solution.py:16
  79.6 1.9 pad_maximum_fusion.5.refs_8_
  81.5 1.7 collective-permute-done.6
  83.3 1.9 pad_maximum_fusion.4.refs_7_
  85.1 1.6 copy-done.22
  87.2 0.8 slice_reduce_fusion
  88.2 1.1 copy-done.1
  89.3 1.0 copy-done.4
  90.4 1.2 copy-done.7
  91.6 1.2 copy-done.10
  92.8 1.0 copy-done.13
  93.9 1.0 copy-done.16
  94.9 1.0 copy-done.18
  96.0 1.0 copy-done.20
  97.0 4.3 %contract.3 = (f32[4,1,256,256]{3,2,1,0:T(8,128)S(1)}, f32[4,1,256,256]{3,2,1,0:T(8,128)}) custom-call(s32[131]{0:T(256)S(1)} %pad_add_fusion.flag_ref, bf16[4,2,256,768]{3,2,1,0:T(8,128)(2,1)S(1)} %split_amp.2.refs_0_, f32[2,256,256]{2,1,0:T(8,128)S(1)} %copy-done.4, f32[2,256,256]{2,1,0:T(8,128)S(1)} %copy-done.13, f32[2,256,256]{2,1,0:T(8,128)S(1)} %copy-done.16, ...), custom_call_target="tpu_custom_call" | custom-call | flops 1610612736 | bytes 8388608 | tf_op jit(solution)/shard_map/contract/pallas_call | solution.py:97
  101.3 1.0 copy-done.26
  102.2 5.9 %collective-permute-start.8 = (f32[4,1,256,256]{3,2,1,0:T(8,128)}, f32[4,1,256,256]{3,2,1,0:T(8,128)}, u32[]{:S(2)}, u32[]{:S(2)}) collective-permute-start(f32[4,1,256,256]{3,2,1,0:T(8,128)} %get-tuple-element.22), channel_id=1, source_target_pairs={{0,16},{16,0},{1,17},{17,1},{2,18},{18,2},{3,19},{19,3},{4,20},{20... | collective-permute-start | bytes 3145736 | tf_op jit(solution)/shard_map/ppermute | solution.py:16
  108.2 1.5 collective-permute-start.11
  109.7 1.6 copy-done.23
  111.3 0.4 split_amp.3.refs_0_.refs_1_
  111.8 0.7 copy-done.27
  112.5 1.9 add.265
  114.6 3.0 %contract.4 = (f32[4,1,256,256]{3,2,1,0:T(8,128)S(1)}, f32[4,1,256,256]{3,2,1,0:T(8,128)S(1)}) custom-call(s32[131]{0:T(256)S(1)} %pad_add_fusion.flag_ref, bf16[4,2,256,768]{3,2,1,0:T(8,128)(2,1)S(1)} %split_amp.3.refs_0_.refs_1_, f32[2,256,256]{2,1,0:T(8,128)S(1)} %copy-done.5, f32[2,256,256]{2,1,0:T(8,128)S(1)} %copy-done.14, ...), custom_call_target="tpu_custom_call" | custom-call | flops 1610612736 | bytes 8388608 | tf_op jit(solution)/shard_map/contract/pallas_call | solution.py:97
  117.6 2.7 %collective-permute-start.9 = (f32[4,1,256,256]{3,2,1,0:T(8,128)S(1)}, f32[4,1,256,256]{3,2,1,0:T(8,128)S(1)}, u32[]{:S(2)}, u32[]{:S(2)}) collective-permute-start(f32[4,1,256,256]{3,2,1,0:T(8,128)S(1)} %get-tuple-element.26), channel_id=1, source_target_pairs={{0,16},{16,0},{1,17},{17,1},{2,18},{18,2},{3,19},{19,3},{4,20},{20... | collective-permute-start | bytes 3145736 | tf_op jit(solution)/shard_map/ppermute | solution.py:16
  120.3 7.3 %collective-permute-done.11.refs_7_ = f32[3,256,256]{2,1,0:T(8,128)} collective-permute-done((f32[3,256,256]{2,1,0:T(8,128)}, f32[3,256,256]{2,1,0:T(8,128)}, u32[]{:S(2)}, u32[]{:S(2)}) %collective-permute-start.11) | collective-permute-done | bytes 786464 | tf_op jit(solution)/shard_map/ppermute | solution.py:16
  127.7 1.0 slice.145
  128.7 2.8 %collective-permute-start.13 = (f32[3,128,256]{2,1,0:T(8,128)S(1)}, f32[3,128,256]{2,1,0:T(8,128)S(1)}, u32[]{:S(2)}, u32[]{:S(2)}) collective-permute-start(f32[3,128,256]{2,1,0:T(8,128)S(1)} %slice.145), channel_id=1, source_target_pairs={{0,96},{32,0},{64,32},{96,64},{1,97},{33,1},{65,33},{97,65},{2,98}... | collective-permute-start | bytes 1179656 | tf_op jit(solution)/shard_map/ppermute | solution.py:16
  131.5 1.0 slice.144
  132.8 6.4 %collective-permute-done.13 = f32[3,128,256]{2,1,0:T(8,128)S(1)} collective-permute-done((f32[3,128,256]{2,1,0:T(8,128)S(1)}, f32[3,128,256]{2,1,0:T(8,128)S(1)}, u32[]{:S(2)}, u32[]{:S(2)}) %collective-permute-start.13) | collective-permute-done | bytes 393248 | tf_op jit(solution)/shard_map/ppermute | solution.py:16
  139.2 4.3 %collective-permute-done.12 = f32[3,128,256]{2,1,0:T(8,128)S(1)} collective-permute-done((f32[3,128,256]{2,1,0:T(8,128)S(1)}, f32[3,128,256]{2,1,0:T(8,128)S(1)}, u32[]{:S(2)}, u32[]{:S(2)}) %collective-permute-start.12) | collective-permute-done | bytes 393248 | tf_op jit(solution)/shard_map/ppermute | solution.py:16
  143.5 1.1 add.270
  144.7 8.9 %contract.5 = (f32[4,2,256,256]{3,2,1,0:T(8,128)S(1)}, f32[4,2,256,256]{3,2,1,0:T(8,128)}) custom-call(s32[131]{0:T(256)S(1)} %pad_add_fusion.flag_ref, bf16[4,2,256,768]{3,2,1,0:T(8,128)(2,1)S(1)} %split_amp.2.refs_0_, bf16[4,2,256,768]{3,2,1,0:T(8,128)(2,1)S(1)} %split_amp.3.refs_0_.refs_1_, f32[2,256,256]{2,1,0:T(8,128)S(1)} %copy-done.5, ...), custom_call_target="tpu_custom_call" | custom-call | flops 1610612736 | bytes 8388608 | tf_op jit(solution)/shard_map/contract/pallas_call | solution.py:97
  153.6 1.4 copy-done.24
  155.0 1.2 collective-permute-start.14
  156.2 21.0 %all_to_all.26 = f32[4,1,256,256]{3,2,1,0:T(8,128)S(1)} all-to-all(f32[4,1,256,256]{3,2,1,0:T(8,128)S(1)} %add.265), channel_id=1, replica_groups=mesh['z'=4,'c'=2,'y'=4,'x'=4] {'y'}, dimensions={0} | all-to-all | bytes 2097152 | tf_op jit(solution)/shard_map/all_to_all | solution.py:166
  177.2 4.3 %all-to-all-start.3 = ((f32[4,1,256,256]{3,2,1,0:T(8,128)}), f32[4,1,256,256]{3,2,1,0:T(8,128)}, u32[]{:S(2)}, u32[]{:S(2)}) async-start(f32[4,1,256,256]{3,2,1,0:T(8,128)} %add.270), calls=%async_computation.3 | async-start | bytes 2097152 | tf_op jit(solution)/shard_map/all_to_all | solution.py:166
  181.5 3.2 %add.275 = f32[4,2,256,256]{3,2,1,0:T(8,128)} add(f32[4,2,256,256]{3,2,1,0:T(8,128)S(1)} %copy-done.25, f32[4,2,256,256]{3,2,1,0:T(8,128)} %collective-permute-done.14) | non-fusion elementwise | flops 524288 | bytes 6291456 | tf_op jit(solution)/shard_map/add | solution.py:164
  184.7 10.7 %all-to-all-done.3 = f32[4,1,256,256]{3,2,1,0:T(8,128)} async-done(((f32[4,1,256,256]{3,2,1,0:T(8,128)}), f32[4,1,256,256]{3,2,1,0:T(8,128)}, u32[]{:S(2)}, u32[]{:S(2)}) %all-to-all-start.3) | async-done | bytes 1048608 | tf_op jit(solution)/shard_map/all_to_all | solution.py:166
  195.4 3.6 %all-to-all-start.4 = ((f32[4,2,256,256]{3,2,1,0:T(8,128)}), f32[4,2,256,256]{3,2,1,0:T(8,128)S(1)}, u32[]{:S(2)}, u32[]{:S(2)}) async-start(f32[4,2,256,256]{3,2,1,0:T(8,128)} %add.275), calls=%async_computation.4 | async-start | bytes 4194304 | tf_op jit(solution)/shard_map/all_to_all | solution.py:166
  199.1 1.3 fusion.4
  200.4 22.8 %all-to-all-done.4 = f32[4,2,256,256]{3,2,1,0:T(8,128)S(1)} async-done(((f32[4,2,256,256]{3,2,1,0:T(8,128)}), f32[4,2,256,256]{3,2,1,0:T(8,128)S(1)}, u32[]{:S(2)}, u32[]{:S(2)}) %all-to-all-start.4) | async-done | bytes 2097184 | tf_op jit(solution)/shard_map/all_to_all | solution.py:166
  223.3 1.1 copy-done.30
  224.5 1.0 copy.22
  (87 shorter events, 2.6 us)
Async XLA Ops:
  6.5 78.6 %all-gather.5.cloned.1.call-start = ((), (), s32[]{:S(2)}) async-start(), calls=%async_computation.5 | async-start | bytes 2703360 | tf_op jit(solution)/shard_map/all_gather | solution.py:143
  8.7 3.1 %collective-permute-start = (f32[2,264,256]{2,1,0:T(8,128)S(1)}, f32[2,264,256]{2,1,0:T(8,128)S(1)}, u32[]{:S(2)}, u32[]{:S(2)}) collective-permute-start(f32[2,264,256]{2,1,0:T(8,128)S(1)} %get-tuple-element.48), channel_id=1, source_target_pairs={{0,16},{16,0},{1,17},{17,1},{2,18},{18,2},{3,19},{19,3},{4,20},{20... | collective-permute-start | bytes 1622024 | tf_op jit(solution)/shard_map/ppermute | solution.py:16
  11.8 2.0 copy-start.29
  13.9 2.7 %collective-permute-start.1 = (f32[4,256,256]{2,1,0:T(8,128)S(1)}, f32[4,256,256]{2,1,0:T(8,128)S(1)}, u32[]{:S(2)}, u32[]{:S(2)}) collective-permute-start(f32[4,256,256]{2,1,0:T(8,128)S(1)} %get-tuple-element.36), channel_id=1, source_target_pairs={{0,16},{16,0},{1,17},{17,1},{2,18},{18,2},{3,19},{19,3},{4,20},{20... | collective-permute-start | bytes 3145736 | tf_op jit(solution)/shard_map/ppermute | solution.py:16
  18.4 26.7 %all-to-all-start = ((f32[4,256,256]{2,1,0:T(8,128)}), f32[4,256,256]{2,1,0:T(8,128)}, u32[]{:S(2)}, u32[]{:S(2)}) async-start(f32[4,256,256]{2,1,0:T(8,128)} %get-tuple-element.34), calls=%async_computation | async-start | bytes 2097152 | tf_op jit(solution)/shard_map/all_to_all | solution.py:124
  22.7 87.0 %all-gather.7.cloned.1.call-start = ((), (), s32[]{:S(2)}) async-start(), calls=%async_computation.6 | async-start | bytes 2703360 | tf_op jit(solution)/shard_map/all_gather | solution.py:143
  22.8 23.7 %copy-start.3 = (f32[2,256,256]{2,1,0:T(8,128)}, f32[2,256,256]{2,1,0:T(8,128)S(1)}, u32[]{:S(2)}) copy-start(f32[2,256,256]{2,1,0:T(8,128)S(1)} %dynamic-slice_bitcast_fusion.1.refs_1_.refs_2_) | copy-start | bytes 1572868
  22.8 16.0 %collective-permute-start.2 = (f32[2,256,256]{2,1,0:T(8,128)S(1)}, f32[2,256,256]{2,1,0:T(8,128)S(1)}, u32[]{:S(2)}, u32[]{:S(2)}) collective-permute-start(f32[2,256,256]{2,1,0:T(8,128)S(1)} %dynamic-slice_bitcast_fusion.1.refs_1_.refs_2_), channel_id=1, source_target_pairs={{0,32},{32,64},{64,96},{96,0},{1,33},{33,65},{65,97},{97,1},{2,34}... | collective-permute-start | bytes 1572872 | tf_op jit(solution)/shard_map/ppermute | solution.py:16
  24.6 14.2 %collective-permute-start.3 = (f32[2,256,256]{2,1,0:T(8,128)S(1)}, f32[2,256,256]{2,1,0:T(8,128)S(1)}, u32[]{:S(2)}, u32[]{:S(2)}) collective-permute-start(f32[2,256,256]{2,1,0:T(8,128)S(1)} %dynamic-slice_bitcast_fusion.1.refs_1_.refs_2_), channel_id=1, source_target_pairs={{0,96},{32,0},{64,32},{96,64},{1,97},{33,1},{65,33},{97,65},{2,98}... | collective-permute-start | bytes 1572872 | tf_op jit(solution)/shard_map/ppermute | solution.py:16
  38.8 7.7 %copy-start.12 = (f32[2,256,256]{2,1,0:T(8,128)}, f32[2,256,256]{2,1,0:T(8,128)S(1)}, u32[]{:S(2)}) copy-start(f32[2,256,256]{2,1,0:T(8,128)S(1)} %collective-permute-done.2.refs_2_.refs_3_) | copy-start | bytes 1572868
  38.9 7.7 %copy-start.15 = (f32[2,256,256]{2,1,0:T(8,128)}, f32[2,256,256]{2,1,0:T(8,128)S(1)}, u32[]{:S(2)}) copy-start(f32[2,256,256]{2,1,0:T(8,128)S(1)} %collective-permute-done.3.refs_3_.refs_4_) | copy-start | bytes 1572868
  46.3 19.6 %copy-start = (f32[3,256,256]{2,1,0:T(8,128)}, f32[3,256,256]{2,1,0:T(8,128)S(1)}, u32[]{:S(2)}) copy-start(f32[3,256,256]{2,1,0:T(8,128)S(1)} %fusion.1.refs_4_) | copy-start | bytes 2359300
  46.3 5.7 %copy-start.28 = (f32[4,256,256]{2,1,0:T(8,128)S(1)}, f32[4,256,256]{2,1,0:T(8,128)}, u32[]{:S(2)}) copy-start(f32[4,256,256]{2,1,0:T(8,128)} %get-tuple-element.33) | copy-start | bytes 3145732
  46.6 25.8 %collective-permute-start.4 = (f32[4,256,256]{2,1,0:T(8,128)S(1)}, f32[4,256,256]{2,1,0:T(8,128)S(1)}, u32[]{:S(2)}, u32[]{:S(2)}) collective-permute-start(f32[4,256,256]{2,1,0:T(8,128)S(1)} %get-tuple-element.46), channel_id=1, source_target_pairs={{0,32},{32,64},{64,96},{96,0},{1,33},{33,65},{65,97},{97,1},{2,34}... | collective-permute-start | bytes 3145736 | tf_op jit(solution)/shard_map/ppermute | solution.py:16
  49.1 23.2 %collective-permute-start.5 = (f32[4,256,256]{2,1,0:T(8,128)S(1)}, f32[4,256,256]{2,1,0:T(8,128)S(1)}, u32[]{:S(2)}, u32[]{:S(2)}) collective-permute-start(f32[4,256,256]{2,1,0:T(8,128)S(1)} %get-tuple-element.45), channel_id=1, source_target_pairs={{0,96},{32,0},{64,32},{96,64},{1,97},{33,1},{65,33},{97,65},{2,98}... | collective-permute-start | bytes 3145736 | tf_op jit(solution)/shard_map/ppermute | solution.py:16
  72.3 12.8 %copy-start.6 = (f32[4,256,256]{2,1,0:T(8,128)}, f32[4,256,256]{2,1,0:T(8,128)S(1)}, u32[]{:S(2)}) copy-start(f32[4,256,256]{2,1,0:T(8,128)S(1)} %collective-permute-done.4.refs_5_) | copy-start | bytes 3145732
  72.3 12.8 %copy-start.9 = (f32[4,256,256]{2,1,0:T(8,128)}, f32[4,256,256]{2,1,0:T(8,128)S(1)}, u32[]{:S(2)}) copy-start(f32[4,256,256]{2,1,0:T(8,128)S(1)} %collective-permute-done.5.refs_6_) | copy-start | bytes 3145732
  72.4 7.3 %collective-permute-start.7 = (f32[3,128,256]{2,1,0:T(8,128)S(1)}, f32[3,128,256]{2,1,0:T(8,128)}, u32[]{:S(2)}, u32[]{:S(2)}) collective-permute-start(f32[3,128,256]{2,1,0:T(8,128)S(1)} %slice.111), channel_id=1, source_target_pairs={{0,96},{32,0},{64,32},{96,64},{1,97},{33,1},{65,33},{97,65},{2,98}... | collective-permute-start | bytes 1179656 | tf_op jit(solution)/shard_map/ppermute | solution.py:16
  74.9 8.3 %collective-permute-start.6 = (f32[3,128,256]{2,1,0:T(8,128)S(1)}, f32[3,128,256]{2,1,0:T(8,128)}, u32[]{:S(2)}, u32[]{:S(2)}) collective-permute-start(f32[3,128,256]{2,1,0:T(8,128)S(1)} %slice.109), channel_id=1, source_target_pairs={{0,32},{32,64},{64,96},{96,0},{1,33},{33,65},{65,97},{97,1},{2,34}... | collective-permute-start | bytes 1179656 | tf_op jit(solution)/shard_map/ppermute | solution.py:16
  85.1 1.6 copy-start.22
  88.2 1.1 copy-start.1
  89.3 1.0 copy-start.4
  90.4 1.2 copy-start.7
  91.6 1.2 copy-start.10
  92.8 1.0 copy-start.13
  93.9 1.0 copy-start.16
  94.9 1.0 copy-start.18
  96.0 1.0 copy-start.20
  101.3 1.0 copy-start.26
  102.2 9.6 %collective-permute-start.8 = (f32[4,1,256,256]{3,2,1,0:T(8,128)}, f32[4,1,256,256]{3,2,1,0:T(8,128)}, u32[]{:S(2)}, u32[]{:S(2)}) collective-permute-start(f32[4,1,256,256]{3,2,1,0:T(8,128)} %get-tuple-element.22), channel_id=1, source_target_pairs={{0,16},{16,0},{1,17},{17,1},{2,18},{18,2},{3,19},{19,3},{4,20},{20... | collective-permute-start | bytes 3145736 | tf_op jit(solution)/shard_map/ppermute | solution.py:16
  108.2 19.5 %collective-permute-start.11 = (f32[3,256,256]{2,1,0:T(8,128)}, f32[3,256,256]{2,1,0:T(8,128)}, u32[]{:S(2)}, u32[]{:S(2)}) collective-permute-start(f32[3,256,256]{2,1,0:T(8,128)} %fusion.refs_5_), channel_id=1, source_target_pairs={{0,96},{32,0},{64,32},{96,64},{1,97},{33,1},{65,33},{97,65},{2,98}... | collective-permute-start | bytes 2359304 | tf_op jit(solution)/shard_map/ppermute | solution.py:16
  109.7 21.8 %collective-permute-start.10 = (f32[3,256,256]{2,1,0:T(8,128)}, f32[3,256,256]{2,1,0:T(8,128)}, u32[]{:S(2)}, u32[]{:S(2)}) collective-permute-start(f32[3,256,256]{2,1,0:T(8,128)} %fusion.refs_5_), channel_id=1, source_target_pairs={{0,32},{32,64},{64,96},{96,0},{1,33},{33,65},{65,97},{97,1},{2,34}... | collective-permute-start | bytes 2359304 | tf_op jit(solution)/shard_map/ppermute | solution.py:16
  109.7 1.6 copy-start.23
  111.3 1.2 copy-start.27
  111.3 3.2 %copy-start.11 = (f32[4,256,256]{2,1,0:T(8,128)S(1)}, f32[4,256,256]{2,1,0:T(8,128)}, u32[]{:S(2)}) copy-start(f32[4,256,256]{2,1,0:T(8,128)} %copy-done.9) | copy-start | bytes 3145732
  111.3 3.2 %copy-start.17 = (f32[2,256,256]{2,1,0:T(8,128)S(1)}, f32[2,256,256]{2,1,0:T(8,128)}, u32[]{:S(2)}) copy-start(f32[2,256,256]{2,1,0:T(8,128)} %copy-done.15) | copy-start | bytes 1572868
  111.3 3.2 %copy-start.19 = (f32[4,128,256]{2,1,0:T(8,128)S(1)}, f32[4,128,256]{2,1,0:T(8,128)}, u32[]{:S(2)}) copy-start(f32[4,128,256]{2,1,0:T(8,128)} %pad_maximum_fusion.5.refs_8_) | copy-start | bytes 1572868
  111.3 3.2 %copy-start.21 = (f32[4,128,256]{2,1,0:T(8,128)S(1)}, f32[4,128,256]{2,1,0:T(8,128)}, u32[]{:S(2)}) copy-start(f32[4,128,256]{2,1,0:T(8,128)} %pad_maximum_fusion.4.refs_7_) | copy-start | bytes 1572868
  111.8 2.7 %copy-start.2 = (f32[3,256,256]{2,1,0:T(8,128)S(1)}, f32[3,256,256]{2,1,0:T(8,128)}, u32[]{:S(2)}) copy-start(f32[3,256,256]{2,1,0:T(8,128)} %copy-done) | copy-start | bytes 2359300
  111.8 2.7 %copy-start.5 = (f32[2,256,256]{2,1,0:T(8,128)S(1)}, f32[2,256,256]{2,1,0:T(8,128)}, u32[]{:S(2)}) copy-start(f32[2,256,256]{2,1,0:T(8,128)} %copy-done.3) | copy-start | bytes 1572868
  111.8 2.7 %copy-start.8 = (f32[4,256,256]{2,1,0:T(8,128)S(1)}, f32[4,256,256]{2,1,0:T(8,128)}, u32[]{:S(2)}) copy-start(f32[4,256,256]{2,1,0:T(8,128)} %copy-done.6) | copy-start | bytes 3145732
  111.8 2.8 %copy-start.14 = (f32[2,256,256]{2,1,0:T(8,128)S(1)}, f32[2,256,256]{2,1,0:T(8,128)}, u32[]{:S(2)}) copy-start(f32[2,256,256]{2,1,0:T(8,128)} %copy-done.12) | copy-start | bytes 1572868
  117.6 25.9 %collective-permute-start.9 = (f32[4,1,256,256]{3,2,1,0:T(8,128)S(1)}, f32[4,1,256,256]{3,2,1,0:T(8,128)S(1)}, u32[]{:S(2)}, u32[]{:S(2)}) collective-permute-start(f32[4,1,256,256]{3,2,1,0:T(8,128)S(1)} %get-tuple-element.26), channel_id=1, source_target_pairs={{0,16},{16,0},{1,17},{17,1},{2,18},{18,2},{3,19},{19,3},{4,20},{20... | collective-permute-start | bytes 3145736 | tf_op jit(solution)/shard_map/ppermute | solution.py:16
  128.7 10.4 %collective-permute-start.13 = (f32[3,128,256]{2,1,0:T(8,128)S(1)}, f32[3,128,256]{2,1,0:T(8,128)S(1)}, u32[]{:S(2)}, u32[]{:S(2)}) collective-permute-start(f32[3,128,256]{2,1,0:T(8,128)S(1)} %slice.145), channel_id=1, source_target_pairs={{0,96},{32,0},{64,32},{96,64},{1,97},{33,1},{65,33},{97,65},{2,98}... | collective-permute-start | bytes 1179656 | tf_op jit(solution)/shard_map/ppermute | solution.py:16
  132.5 11.0 %collective-permute-start.12 = (f32[3,128,256]{2,1,0:T(8,128)S(1)}, f32[3,128,256]{2,1,0:T(8,128)S(1)}, u32[]{:S(2)}, u32[]{:S(2)}) collective-permute-start(f32[3,128,256]{2,1,0:T(8,128)S(1)} %slice.144), channel_id=1, source_target_pairs={{0,32},{32,64},{64,96},{96,0},{1,33},{33,65},{65,97},{97,1},{2,34}... | collective-permute-start | bytes 1179656 | tf_op jit(solution)/shard_map/ppermute | solution.py:16
  153.6 1.4 copy-start.24
  155.0 26.5 %copy-start.25 = (f32[4,2,256,256]{3,2,1,0:T(8,128)S(1)}, f32[4,2,256,256]{3,2,1,0:T(8,128)}, u32[]{:S(2)}) copy-start(f32[4,2,256,256]{3,2,1,0:T(8,128)} %copy-done.24) | copy-start | bytes 6291460
  155.0 26.5 %collective-permute-start.14 = (f32[4,2,256,256]{3,2,1,0:T(8,128)}, f32[4,2,256,256]{3,2,1,0:T(8,128)}, u32[]{:S(2)}, u32[]{:S(2)}) collective-permute-start(f32[4,2,256,256]{3,2,1,0:T(8,128)} %get-tuple-element.31), channel_id=1, source_target_pairs={{0,16},{16,0},{1,17},{17,1},{2,18},{18,2},{3,19},{19,3},{4,20},{20... | collective-permute-start | bytes 6291464 | tf_op jit(solution)/shard_map/ppermute | solution.py:16
  177.2 18.2 %all-to-all-start.3 = ((f32[4,1,256,256]{3,2,1,0:T(8,128)}), f32[4,1,256,256]{3,2,1,0:T(8,128)}, u32[]{:S(2)}, u32[]{:S(2)}) async-start(f32[4,1,256,256]{3,2,1,0:T(8,128)} %add.270), calls=%async_computation.3 | async-start | bytes 2097152 | tf_op jit(solution)/shard_map/all_to_all | solution.py:166
  195.4 27.7 %all-to-all-start.4 = ((f32[4,2,256,256]{3,2,1,0:T(8,128)}), f32[4,2,256,256]{3,2,1,0:T(8,128)S(1)}, u32[]{:S(2)}, u32[]{:S(2)}) async-start(f32[4,2,256,256]{3,2,1,0:T(8,128)} %add.275), calls=%async_computation.4 | async-start | bytes 4194304 | tf_op jit(solution)/shard_map/all_to_all | solution.py:166
  223.1 1.2 copy-start.30
Sparse Core Ops, SparseCore 0:
  13.2 42.5 all-gather.4
  57.4 31.9 all-gather.6

commit v5 on v4

v5 whole, which is shorter than its diff:
```python
import jax
import jax.numpy as jnp
from jax import lax
from jax.experimental import pallas as pl
from jax.experimental.pallas import tpu as pltpu
from jax.sharding import Mesh, PartitionSpec as P

NAMES = ("z", "c", "y", "x")
SIZE = {"z": 4, "c": 2, "y": 4, "x": 4}
MIB = 1024 * 1024
CHUNKS = ((0, 0, 1), (0, 1, 1), (1, 0, 2))
BLOCK = 128


def shift(t, axis, s):
    n = SIZE[axis]
    return lax.ppermute(t, axis, [(i, (i + s) % n) for i in range(n)])


def halves(a):
    hi = a.astype(jnp.bfloat16)
    return hi, (a - hi.astype(jnp.float32)).astype(jnp.bfloat16)


def split_kernel(c_ref, a_ref, b_ref, o_ref):
    w = a_ref.shape[-1]
    for il, ref in enumerate((a_ref, b_ref)):
        for core in range(2):
            hi, lo = halves(ref[core])
            o_ref[0, 2 * core + il, :, :w] = hi
            o_ref[0, 2 * core + il, :, w : 2 * w] = lo
            o_ref[0, 2 * core + il, :, 2 * w :] = hi


def split_amp(c, a):
    w = a.shape[-1]
    tile = lambda il: pl.BlockSpec((2, w, w), lambda g, m: (g, 2 * il + m[0], 0))
    return pl.pallas_call(
        split_kernel,
        grid_spec=pltpu.PrefetchScalarGridSpec(
            num_scalar_prefetch=1,
            grid=(4,),
            in_specs=[tile(0), tile(1)],
            out_specs=pl.BlockSpec((1, 4, w, 3 * w), lambda g, m: (g, 0, 0, 0)),
        ),
        out_shape=jax.ShapeDtypeStruct((4, 4, w, 3 * w), jnp.bfloat16),
        compiler_params=pltpu.CompilerParams(vmem_limit_bytes=12 * MIB),
        cost_estimate=pl.CostEstimate(flops=0, bytes_accessed=10 * MIB, transcendentals=0),
        name="split_amp",
    )(c, a, a)


def make_contract_kernel(wide, places):
    def kernel(flag_ref, *refs):
        count = 1 + max(p[0] for step in places for p in step)
        pieces, refs = refs[:count], refs[count:]
        amp_ref, mine_ref, other_ref, a_ref, raw_ref, b_ref, sems = refs
        w = a_ref.shape[2]
        copies = []
        number = 0
        for step, wanted in enumerate(places):
            row = []
            for operand, first, rows, to in wanted:
                source = pieces[operand].at[pl.ds(first, rows)]
                row.append(pltpu.make_async_copy(source, raw_ref.at[step, pl.ds(to, rows)], sems.at[number]))
                number += 1
            copies.append(row)
        whole = pltpu.make_async_copy(amp_ref, a_ref, sems.at[number])
        for copy in copies[0]:
            copy.start()
        whole.start()
        for row in copies[1:]:
            for copy in row:
                copy.start()
        whole.wait()
        z, c, x = flag_ref[128], flag_ref[129], flag_ref[130]
        kp = flag_ref[131]
        for step, turn in enumerate((0, 3, 1, 2)):
            for copy in copies[step]:
                copy.wait()
            for s in range(4):
                for block in range(wide):
                    hi, lo = halves(raw_ref[step, (s * wide + block) * w : (s * wide + block + 1) * w])
                    columns = slice(block * BLOCK, block * BLOCK + BLOCK)
                    b_ref[s, :w, columns] = hi
                    b_ref[s, w : 2 * w, columns] = hi
                    b_ref[s, 2 * w :, columns] = lo
            ka = lax.rem(z + turn, 4)
            for out, core in ((mine_ref, c), (other_ref, 1 - c)):
                for il in range(2):
                    out[ka, il] = jnp.zeros(out.shape[2:], jnp.float32)

                    @pl.loop(0, 4)
                    def _(s):
                        jx = lax.rem(x + s, 4)

                        @pl.when(flag_ref[(jx * 2 + core) * 16 + kp * 8 + ka * 2 + il] != 0)
                        def _():
                            out[ka, il] += jnp.dot(
                                a_ref[jx, 2 * core + il], b_ref[s], preferred_element_type=jnp.float32
                            )

    return kernel


def contract(wide, flags, a3, pieces, places):
    w = a3.shape[2]
    inside = pl.BlockSpec(memory_space=pltpu.VMEM)
    outside = pl.BlockSpec(memory_space=pltpu.HBM)
    out = jax.ShapeDtypeStruct((4, 2, w, wide * BLOCK), jnp.float32)
    return pl.pallas_call(
        make_contract_kernel(wide, places),
        in_specs=[pl.BlockSpec(memory_space=pltpu.SMEM)] + [outside] * (len(pieces) + 1),
        out_specs=[inside, inside],
        scratch_shapes=[
            pltpu.VMEM(a3.shape, jnp.bfloat16),
            pltpu.VMEM((4, 4 * wide * w, BLOCK), jnp.float32),
            pltpu.VMEM((4, 3 * w, wide * BLOCK), jnp.bfloat16),
            pltpu.SemaphoreType.DMA((sum(len(p) for p in places) + 1,)),
        ],
        out_shape=[out, out],
        compiler_params=pltpu.CompilerParams(vmem_limit_bytes=24 * MIB),
        cost_estimate=pl.CostEstimate(flops=6 * wide * 10**9, bytes_accessed=4 * MIB, transcendentals=0),
        name="contract",
    )(flags, *pieces, a3)


def on_device(amp, integ, resid, triples):
    w = amp.shape[-1]
    h = w // 2
    z, c, y, x = (lax.axis_index(n) for n in NAMES)

    tri = triples[0, 0]
    i = tri[0] // 32
    j = tri[0] % 32
    k = tri[1] % 32
    slot = (((j % 2 * 4 + (k // 2) % 4) * 2 + k % 2) * 4 + k // 8) * 2 + i % 2
    place = lax.broadcasted_iota(jnp.int32, (32, w), 1)
    listed = jnp.sum((place == slot[:, None]).astype(jnp.float32), axis=0, keepdims=True)

    gathered = lax.all_gather(
        jnp.concatenate([amp.reshape(4 * w, w), jnp.broadcast_to(listed, (8, w))]), ("x", "c")
    )
    a3 = split_amp(c[None], gathered)
    flags = lax.dynamic_index_in_dim(gathered[:, 4 * w, :128].reshape(4, 2, 8, 16), c * 4 + x, 2, keepdims=False)
    flags = flags.reshape(-1).astype(jnp.int32)

    def blocked(t):
        return t.reshape(-1, w, 2, BLOCK).transpose(0, 2, 1, 3)

    mine = lax.dynamic_index_in_dim(integ, c, 0, keepdims=False)
    other = shift(lax.dynamic_index_in_dim(integ, 1 - c, 0, keepdims=False), "c", 1)
    pairs = jnp.where(c == 0, jnp.stack([mine, other]), jnp.stack([other, mine])).reshape(4, 2, w, w)
    own = blocked(lax.dynamic_index_in_dim(pairs, x, 0, keepdims=False)).reshape(-1, BLOCK)
    own, pairs = lax.optimization_barrier((own, pairs))
    own_r, own_l = shift(own, "z", 1), shift(own, "z", -1)
    rest = []
    for kp, first, blocks in CHUNKS:
        sent = pairs[:, kp, :, first * BLOCK : (first + blocks) * BLOCK]
        if not rest:
            held = jnp.stack([
                shift(lax.dynamic_index_in_dim(sent, lax.rem(x + 4 - s, 4), 0, keepdims=False), "x", -s)
                for s in (1, 2, 3)
            ])
        else:
            held = lax.all_to_all(sent, "x", 0, 0, tiled=True)
            held = lax.dynamic_slice_in_dim(jnp.concatenate([held, held]), x + 1, 3, 0)
        rest.append((blocked(held) if blocks == 2 else held).reshape(-1, BLOCK))

    def halved(right, left):
        right, left = right.reshape(-1, 2, h, BLOCK), left.reshape(-1, 2, h, BLOCK)
        return right[:, 0].reshape(-1, BLOCK), left[:, 1].reshape(-1, BLOCK)

    near = [(own_r, own_l)]
    pending = halved(own_r, own_l)
    for n in range(3):
        right, left = jnp.concatenate([rest[n], pending[0]]), jnp.concatenate([rest[n], pending[1]])
        if n == 2:
            right, left, flags = lax.optimization_barrier((right, left, flags))
        right, left = shift(right, "z", 1), shift(left, "z", -1)
        if n < 2:
            right, left, rest[n + 1] = lax.optimization_barrier((right, left, rest[n + 1]))
        near.append((right, left))
        body = rest[n].shape[0]
        pending = halved(right[:body], left[:body])
    near.append((shift(pending[0], "z", 1), shift(pending[1], "z", -1)))

    outs = []
    for n, (kp, first, blocks) in enumerate(CHUNKS):
        at = kp * 2 + first
        before = 0 if n == 2 else rest[n + 1].shape[0]
        pieces = [own, rest[n], own_r, near[n + 1][0], own_l, near[n + 1][1], *near[1], *near[n + 2]]
        places = [[(o, at * w, blocks * w, 0), (o + 1, 0, 3 * blocks * w, blocks * w)] for o in (0, 2, 4)]
        last = []
        for side in range(2):
            for t in range(4 * blocks):
                source = (6 + side, rest[0].shape[0] + (at + t) * h) if t < blocks else (
                    8 + side, before + (t - blocks) * h)
                last.append((*source, h, t * w + side * h))
        places.append(last)
        meta = jnp.concatenate([flags, jnp.stack([z, c, x, jnp.full_like(z, kp)])])
        held, away = contract(blocks, meta, a3, pieces, places)
        part = held + shift(away, "c", 1)
        part, flags = lax.optimization_barrier((part, flags))
        part = lax.all_to_all(part, "y", 0, 0, tiled=True)
        outs.append(part[0] + part[1] + part[2] + part[3])
        if n == 1:
            flags, outs[0] = lax.optimization_barrier((flags, outs[0]))
    return resid + jnp.stack([jnp.concatenate(outs[:2], axis=-1), outs[2]], axis=1)


def solution(mesh):
    fine = Mesh(mesh.devices.reshape(4, 2, 4, 4), NAMES)
    row, col = ("z", "c"), ("y", "x")
    return jax.shard_map(
        on_device,
        mesh=fine,
        in_specs=(P(row, col), P(col, row), P(row, col), P(row, col)),
        out_specs=P(row, col),
        check_vma=False,
    )
```

time: 235 us -> 277 us (1.18)
  blocking collectives: 34.9 us -> 0 us
  local copies, waits for them, and re-layouts: 25.3 us -> 58.1 us
  waiting for transfers between devices: 85.3 us -> 101 us
  Pallas kernels: 17.1 us -> 29.2 us
  starting transfers between devices: 40.6 us -> 48.5 us
  other arithmetic: 15.3 us -> 21.9 us
    all_to_all x2 -> x0, blocking collectives: 34.9 us -> none  [the longest x1 21 us: on_device(): part = lax.all_to_all(part, 'y', 0, 0, tiled=True)]
    unnamed x62 -> x84, local copies, waits for them, and re-layouts: 17 us -> 43 us
    all_to_all x1 -> x2, waiting for transfers between devices: 6.2 us -> 19.6 us  [on_device(): held = lax.all_to_all(sent, 'x', 0, 0, tiled=True)]
    all_to_all x2 -> x3, waiting for transfers between devices: 33.4 us -> 46.1 us  [on_device(): part = lax.all_to_all(part, 'y', 0, 0, tiled=True)]
    pallas_call x5 -> x4, Pallas kernels: 17.1 us -> 29.2 us  [the longest x3 28 us: contract(): pl.pallas_call(make_contract_kernel(wide, places), in_specs=[pl.BlockSpec...]
    ppermute x15 -> x17, waiting for transfers between devices: 45.6 us -> 35.4 us  [shift(): return lax.ppermute(t, axis, [(i, (i + s) % n) for i in range(n)])]
    all_to_all x2 -> x3, starting transfers between devices: 7.87 us -> 12.1 us  [on_device(): part = lax.all_to_all(part, 'y', 0, 0, tiled=True)]
    all_to_all x1 -> x2, starting transfers between devices: 4.25 us -> 7.77 us  [on_device(): held = lax.all_to_all(sent, 'x', 0, 0, tiled=True)]
  transfers between devices with their start and end apart: 20 -> 23, of which waited for: 12 -> 11; matrix products, arithmetic and copies ran while one was open for 8% -> 11% of each run, Pallas kernels for 4% -> 0%
where the time goes in v5:
time: 277 us; the launch traced here: 273 us
  waiting for transfers between devices  101 us (36%)
  local copies, waits for them, and re-layouts  58.1 us (21%)
  starting transfers between devices  48.5 us (18%)
  Pallas kernels  29.2 us (11%)
  other arithmetic  21.9 us (8%)
  between operations  13.9 us (5%)
    all_to_all x3, waiting for transfers between devices, on_device(): part = lax.all_to_all(part, 'y', 0, 0, tiled=True)  46.1 us
    unnamed x84, local copies, waits for them, and re-layouts  43 us
    ppermute x17, waiting for transfers between devices, shift(): return lax.ppermute(t, axis, [(i, (i + s) % n) for i in range(n)])  35.4 us
    ppermute x17, starting transfers between devices, shift(): return lax.ppermute(t, axis, [(i, (i + s) % n) for i in range(n)])  28.6 us
    pallas_call x3, Pallas kernels, contract(): pl.pallas_call(make_contract_kernel(wide, places), in_specs=[pl.BlockSpec...  28 us
    all_to_all x2, waiting for transfers between devices, on_device(): held = lax.all_to_all(sent, 'x', 0, 0, tiled=True)  19.6 us
    all_to_all x3, starting transfers between devices, on_device(): part = lax.all_to_all(part, 'y', 0, 0, tiled=True)  12.1 us
    all_to_all x2, starting transfers between devices, on_device(): held = lax.all_to_all(sent, 'x', 0, 0, tiled=True)  7.77 us
  transfers between devices with their start and end apart: 23, of which 11 were waited for; matrix products, arithmetic and copies ran while one was open for 11% of the time, Pallas kernels for 0%

profile of v5, /device:TPU:1, one launch (start us, length us, event | category | flops | bytes accessed | tf_op | source)
XLA Modules:
  0.0 272.8 jit_solution(3964816612083925342)
XLA Ops:
  7.5 2.3 pad_maximum_fusion
  9.8 1.2 constant_dynamic-slice_fusion.5
  11.0 1.4 collective-permute-start
  12.4 2.5 collective-permute-done
  14.9 1.5 maximum_select_fusion
  16.4 1.9 copy.44
  18.4 1.2 copy-done.38
  19.9 3.9 %collective-permute-start.6 = (f32[1024,128]{1,0:T(8,128)S(1)}, f32[1024,128]{1,0:T(8,128)S(1)}, u32[]{:S(2)}, u32[]{:S(2)}) collective-permute-start(f32[1024,128]{1,0:T(8,128)S(1)} %bitcast.96), channel_id=1, source_target_pairs={{0,96},{32,0},{64,32},{96,64},{1,97},{33,1},{65,33},{97,65},{2,98}... | collective-permute-start | bytes 1572872 | tf_op jit(solution)/shard_map/ppermute | solution.py:17
  23.8 2.2 slice_bitcast_fusion.1
  26.3 2.8 %collective-permute-start.2 = (f32[256,128]{1,0:T(8,128)S(1)}, f32[256,128]{1,0:T(8,128)S(1)}, u32[]{:S(2)}, u32[]{:S(2)}) collective-permute-start(f32[256,128]{1,0:T(8,128)S(1)} %bitcast.122), channel_id=1, source_target_pairs={{0,2},{1,3},{2,0},{3,1},{4,6},{5,7},{6,4},{7,5},{8,10},{9,11},{10,... | collective-permute-start | bytes 393224 | tf_op jit(solution)/shard_map/ppermute | solution.py:17
  29.4 2.4 collective-permute-start.1
  31.8 4.0 %collective-permute-done.2 = f32[256,128]{1,0:T(8,128)S(1)} collective-permute-done((f32[256,128]{1,0:T(8,128)S(1)}, f32[256,128]{1,0:T(8,128)S(1)}, u32[]{:S(2)}, u32[]{:S(2)}) %collective-permute-start.2) | collective-permute-done | bytes 131104 | tf_op jit(solution)/shard_map/ppermute | solution.py:17
  35.8 4.6 %collective-permute-done.3 = f32[256,128]{1,0:T(8,128)S(1)} collective-permute-done((f32[256,128]{1,0:T(8,128)S(1)}, f32[256,128]{1,0:T(8,128)S(1)}, u32[]{:S(2)}, u32[]{:S(2)}) %collective-permute-start.3) | collective-permute-done | bytes 131104 | tf_op jit(solution)/shard_map/ppermute | solution.py:17
  40.5 1.2 collective-permute-done.1
  41.8 1.3 pad_maximum_fusion.3
  43.1 2.5 collective-permute-start.7
  45.6 3.5 %all-to-all-start = ((f32[4,256,128]{1,2,0:T(8,128)}), f32[4,256,128]{1,2,0:T(8,128)S(1)}, u32[]{:S(2)}, u32[]{:S(2)}) async-start(f32[4,256,128]{1,2,0:T(8,128)} %get-tuple-element.53), calls=%async_computation | async-start | bytes 1048576 | tf_op jit(solution)/shard_map/all_to_all | solution.py:166
  49.2 2.3 slice_bitcast_fusion
  51.5 12.5 %all-to-all-done = f32[4,256,128]{1,2,0:T(8,128)S(1)} async-done(((f32[4,256,128]{1,2,0:T(8,128)}), f32[4,256,128]{1,2,0:T(8,128)S(1)}, u32[]{:S(2)}, u32[]{:S(2)}) %all-to-all-start) | async-done | bytes 524320 | tf_op jit(solution)/shard_map/all_to_all | solution.py:166
  64.0 4.2 %all-to-all-start.1 = ((f32[4,256,256]{1,2,0:T(8,128)}), f32[4,256,256]{1,2,0:T(8,128)}, u32[]{:S(2)}, u32[]{:S(2)}) async-start(f32[4,256,256]{1,2,0:T(8,128)} %slice_bitcast_fusion), calls=%async_computation.1 | async-start | bytes 2097152 | tf_op jit(solution)/shard_map/all_to_all | solution.py:166
  69.0 1.1 copy.51
  70.3 1.3 pad_maximum_fusion.5
  71.6 2.6 collective-permute-start.9
  74.2 7.1 %all-to-all-done.1 = f32[4,256,256]{1,2,0:T(8,128)} async-done(((f32[4,256,256]{1,2,0:T(8,128)}), f32[4,256,256]{1,2,0:T(8,128)}, u32[]{:S(2)}, u32[]{:S(2)}) %all-to-all-start.1) | async-done | bytes 1048608 | tf_op jit(solution)/shard_map/all_to_all | solution.py:166
  81.3 2.1 fusion
  83.4 1.4 copy.52
  84.8 2.2 collective-permute-done.8.refs_8_.refs_3_
  87.2 1.4 pad_maximum_fusion.1
  89.4 3.4 %copy-done = f32[8256,256]{1,0:T(8,128)S(1)} copy-done((f32[8256,256]{1,0:T(8,128)S(1)}, f32[8256,256]{1,0:T(8,128)}, u32[]{:S(2)}) %copy-start) | copy-done | bytes 8454168
  92.8 1.3 split_amp.1.refs_10_
  94.1 2.6 copy-done.1
  97.0 2.8 %copy-done.2 = bf16[4,4,256,768]{3,2,1,0:T(8,128)(2,1)S(1)} copy-done((bf16[4,4,256,768]{3,2,1,0:T(8,128)(2,1)S(1)}, bf16[4,4,256,768]{3,2,1,0:T(8,128)(2,1)}, u32[]{:S(2)}) %copy-start.2) | copy-done | bytes 6291480
  99.8 1.1 copy-done.19
  100.8 1.1 copy-done.23
  104.0 8.0 %contract.3 = (f32[4,2,256,128]{3,2,1,0:T(8,128)S(1)}, f32[4,2,256,128]{3,2,1,0:T(8,128)S(1)}) custom-call(s32[132]{0:T(256)S(1)} %concatenate.48.flag_ref, f32[1024,128]{1,0:T(8,128)S(1)} %bitcast.98, f32[768,128]{1,0:T(8,128)S(1)} %bitcast.91, f32[1024,128]{1,0:T(8,128)S(1)} %copy-done.31, f32[1280,128]{1,0:T(8,128)S(1)} %copy-done.23, ...), custom_call_target="tpu_custom_call" | custom-call | flops 6000000000 | bytes 4194304 | tf_op jit(solution)/shard_map/contract/pallas_call | solution.py:111
  112.1 4.9 %collective-permute-start.10 = (f32[4,2,256,128]{3,2,1,0:T(8,128)S(1)}, f32[4,2,256,128]{3,2,1,0:T(8,128)S(1)}, u32[]{:S(2)}, u32[]{:S(2)}) collective-permute-start(f32[4,2,256,128]{3,2,1,0:T(8,128)S(1)} %get-tuple-element.39), channel_id=1, source_target_pairs={{0,16},{16,0},{1,17},{17,1},{2,18},{18,2},{3,19},{19,3},{4,20},{20... | collective-permute-start | bytes 3145736 | tf_op jit(solution)/shard_map/ppermute | solution.py:17
  116.9 2.7 collective-permute-start.12
  119.6 1.1 add.236
  120.8 20.8 %collective-permute-done.11.refs_8_.refs_3_ = f32[1920,128]{1,0:T(8,128)S(1)} collective-permute-done((f32[1920,128]{1,0:T(8,128)}, f32[1920,128]{1,0:T(8,128)S(1)}, u32[]{:S(2)}, u32[]{:S(2)}) %collective-permute-start.11) | collective-permute-done | bytes 983072 | tf_op jit(solution)/shard_map/ppermute | solution.py:17
  143.6 2.8 %copy-done.3 = bf16[4,4,256,768]{3,2,1,0:T(8,128)(2,1)S(1)} copy-done((bf16[4,4,256,768]{3,2,1,0:T(8,128)(2,1)S(1)}, bf16[4,4,256,768]{3,2,1,0:T(8,128)(2,1)}, u32[]{:S(2)}) %copy-start.3) | copy-done | bytes 6291480
  146.4 1.2 copy-done.6
  147.6 1.2 copy-done.9
  152.0 1.1 copy-done.20
  153.1 1.1 copy-done.24
  156.2 9.0 %contract.4 = (f32[4,2,256,128]{3,2,1,0:T(8,128)S(1)}, f32[4,2,256,128]{3,2,1,0:T(8,128)}) custom-call(s32[132]{0:T(256)S(1)} %concatenate.49.flag_ref, f32[1024,128]{1,0:T(8,128)S(1)} %bitcast.99, f32[768,128]{1,0:T(8,128)S(1)} %bitcast.93, f32[1024,128]{1,0:T(8,128)S(1)} %copy-done.32, f32[1152,128]{1,0:T(8,128)S(1)} %copy-done.17, ...), custom_call_target="tpu_custom_call" | custom-call | flops 6000000000 | bytes 4194304 | tf_op jit(solution)/shard_map/contract/pallas_call | solution.py:111
  165.2 1.4 collective-permute-start.13
  166.7 4.3 %all-to-all-start.2 = ((f32[4,2,256,128]{3,2,1,0:T(8,128)}), f32[4,2,256,128]{3,2,1,0:T(8,128)}, u32[]{:S(2)}, u32[]{:S(2)}) async-start(f32[4,2,256,128]{3,2,1,0:T(8,128)} %add.236), calls=%async_computation.2 | async-start | bytes 2097152 | tf_op jit(solution)/shard_map/all_to_all | solution.py:205
  173.0 3.2 %collective-permute-start.15 = (f32[768,128]{1,0:T(8,128)}, f32[768,128]{1,0:T(8,128)S(1)}, u32[]{:S(2)}, u32[]{:S(2)}) collective-permute-start(f32[768,128]{1,0:T(8,128)} %bitcast.44), channel_id=1, source_target_pairs={{0,96},{32,0},{64,32},{96,64},{1,97},{33,1},{65,33},{97,65},{2,98}... | collective-permute-start | bytes 1179656 | tf_op jit(solution)/shard_map/ppermute | solution.py:17
  176.2 9.9 %all-to-all-done.2 = f32[4,2,256,128]{3,2,1,0:T(8,128)} async-done(((f32[4,2,256,128]{3,2,1,0:T(8,128)}), f32[4,2,256,128]{3,2,1,0:T(8,128)}, u32[]{:S(2)}, u32[]{:S(2)}) %all-to-all-start.2) | async-done | bytes 1048608 | tf_op jit(solution)/shard_map/all_to_all | solution.py:205
  186.1 1.9 fusion.4
  188.0 2.3 add.237
  191.9 2.8 %copy-done.4 = bf16[4,4,256,768]{3,2,1,0:T(8,128)(2,1)S(1)} copy-done((bf16[4,4,256,768]{3,2,1,0:T(8,128)(2,1)S(1)}, bf16[4,4,256,768]{3,2,1,0:T(8,128)(2,1)}, u32[]{:S(2)}) %copy-start.4) | copy-done | bytes 6291480
  194.7 1.2 copy-done.7
  195.9 1.2 copy-done.10
  197.1 1.1 copy-done.21
  198.2 1.1 copy-done.25
  203.4 11.0 %contract.5 = (f32[4,2,256,256]{3,2,1,0:T(8,128)S(1)}, f32[4,2,256,256]{3,2,1,0:T(8,128)}) custom-call(s32[132]{0:T(256)S(1)} %concatenate.51.flag_ref, f32[1024,128]{1,0:T(8,128)S(1)} %bitcast.100, f32[1536,128]{1,0:T(8,128)S(1)} %bitcast.89, f32[1024,128]{1,0:T(8,128)S(1)} %copy-done.33, f32[1920,128]{1,0:T(8,128)S(1)} %copy-done.7, ...), custom_call_target="tpu_custom_call" | custom-call | flops 12000000000 | bytes 4194304 | tf_op jit(solution)/shard_map/contract/pallas_call | solution.py:111
  214.9 4.3 %all-to-all-start.3 = ((f32[4,2,256,128]{3,2,1,0:T(8,128)}), f32[4,2,256,128]{3,2,1,0:T(8,128)}, u32[]{:S(2)}, u32[]{:S(2)}) async-start(f32[4,2,256,128]{3,2,1,0:T(8,128)} %add.237), calls=%async_computation.3 | async-start | bytes 2097152 | tf_op jit(solution)/shard_map/all_to_all | solution.py:205
  219.1 3.2 %add.246 = f32[4,2,256,256]{3,2,1,0:T(8,128)} add(f32[4,2,256,256]{3,2,1,0:T(8,128)S(1)} %get-tuple-element.50, f32[4,2,256,256]{3,2,1,0:T(8,128)} %collective-permute-done.16) | non-fusion elementwise | flops 524288 | bytes 6291456 | tf_op jit(solution)/shard_map/add | solution.py:203
  222.4 12.0 %all-to-all-done.3 = f32[4,2,256,128]{3,2,1,0:T(8,128)} async-done(((f32[4,2,256,128]{3,2,1,0:T(8,128)}), f32[4,2,256,128]{3,2,1,0:T(8,128)}, u32[]{:S(2)}, u32[]{:S(2)}) %all-to-all-start.3) | async-done | bytes 1048608 | tf_op jit(solution)/shard_map/all_to_all | solution.py:205
  234.4 3.6 %all-to-all-start.4 = ((f32[4,2,256,256]{3,2,1,0:T(8,128)}), f32[4,2,256,256]{3,2,1,0:T(8,128)S(1)}, u32[]{:S(2)}, u32[]{:S(2)}) async-start(f32[4,2,256,256]{3,2,1,0:T(8,128)} %add.246), calls=%async_computation.4 | async-start | bytes 4194304 | tf_op jit(solution)/shard_map/all_to_all | solution.py:205
  238.0 1.2 fusion.3
  239.3 24.2 %all-to-all-done.4 = f32[4,2,256,256]{3,2,1,0:T(8,128)S(1)} async-done(((f32[4,2,256,256]{3,2,1,0:T(8,128)}), f32[4,2,256,256]{3,2,1,0:T(8,128)S(1)}, u32[]{:S(2)}, u32[]{:S(2)}) %all-to-all-start.4) | async-done | bytes 2097184 | tf_op jit(solution)/shard_map/all_to_all | solution.py:205
  263.6 1.1 copy-done.40
  (127 shorter events, 23.0 us)
Async XLA Ops:
  6.5 3.3 %copy-start.39 = (f32[2,4,256,256]{3,2,1,0:T(8,128)S(1)}, f32[2,4,256,256]{3,2,1,0:T(8,128)}, u32[]{:S(2)}) copy-start(f32[2,4,256,256]{3,2,1,0:T(8,128)} %param.5) | copy-start | bytes 6291460
  6.5 82.1 %all-gather.3.cloned.1.call-start = ((), (), s32[]{:S(2)}) async-start(), calls=%async_computation.5 | async-start | bytes 9510912 | tf_op jit(solution)/shard_map/all_gather | solution.py:141
  11.0 3.9 %collective-permute-start = (f32[4,256,256]{2,1,0:T(8,128)}, f32[4,256,256]{2,1,0:T(8,128)S(1)}, u32[]{:S(2)}, u32[]{:S(2)}) collective-permute-start(f32[4,256,256]{2,1,0:T(8,128)} %get-tuple-element.56), channel_id=1, source_target_pairs={{0,16},{16,0},{1,17},{17,1},{2,18},{18,2},{3,19},{19,3},{4,20},{20... | collective-permute-start | bytes 3145736 | tf_op jit(solution)/shard_map/ppermute | solution.py:17
  18.4 1.3 copy-start.38
  19.9 77.1 %copy-start.11 = (f32[2,2,256,128]{3,2,1,0:T(8,128)}, f32[2,2,256,128]{3,2,1,0:T(8,128)S(1)}, u32[]{:S(2)}) copy-start(f32[2,2,256,128]{3,2,1,0:T(8,128)S(1)} %copy.45) | copy-start | bytes 1572868
  19.9 21.8 %collective-permute-start.6 = (f32[1024,128]{1,0:T(8,128)S(1)}, f32[1024,128]{1,0:T(8,128)S(1)}, u32[]{:S(2)}, u32[]{:S(2)}) collective-permute-start(f32[1024,128]{1,0:T(8,128)S(1)} %bitcast.96), channel_id=1, source_target_pairs={{0,96},{32,0},{64,32},{96,64},{1,97},{33,1},{65,33},{97,65},{2,98}... | collective-permute-start | bytes 1572872 | tf_op jit(solution)/shard_map/ppermute | solution.py:17
  23.8 17.9 %collective-permute-start.4 = (f32[1024,128]{1,0:T(8,128)S(1)}, f32[1024,128]{1,0:T(8,128)S(1)}, u32[]{:S(2)}, u32[]{:S(2)}) collective-permute-start(f32[1024,128]{1,0:T(8,128)S(1)} %bitcast.97), channel_id=1, source_target_pairs={{0,32},{32,64},{64,96},{96,0},{1,33},{33,65},{65,97},{97,1},{2,34}... | collective-permute-start | bytes 1572872 | tf_op jit(solution)/shard_map/ppermute | solution.py:17
  26.3 9.5 %collective-permute-start.2 = (f32[256,128]{1,0:T(8,128)S(1)}, f32[256,128]{1,0:T(8,128)S(1)}, u32[]{:S(2)}, u32[]{:S(2)}) collective-permute-start(f32[256,128]{1,0:T(8,128)S(1)} %bitcast.122), channel_id=1, source_target_pairs={{0,2},{1,3},{2,0},{3,1},{4,6},{5,7},{6,4},{7,5},{8,10},{9,11},{10,... | collective-permute-start | bytes 393224 | tf_op jit(solution)/shard_map/ppermute | solution.py:17
  29.1 11.4 %collective-permute-start.3 = (f32[256,128]{1,0:T(8,128)S(1)}, f32[256,128]{1,0:T(8,128)S(1)}, u32[]{:S(2)}, u32[]{:S(2)}) collective-permute-start(f32[256,128]{1,0:T(8,128)S(1)} %bitcast.121), channel_id=1, source_target_pairs={{0,1},{1,2},{2,3},{3,0},{4,5},{5,6},{6,7},{7,4},{8,9},{9,10},{10,1... | collective-permute-start | bytes 393224 | tf_op jit(solution)/shard_map/ppermute | solution.py:17
  29.4 12.2 %collective-permute-start.1 = (f32[256,128]{1,0:T(8,128)S(1)}, f32[256,128]{1,0:T(8,128)S(1)}, u32[]{:S(2)}, u32[]{:S(2)}) collective-permute-start(f32[256,128]{1,0:T(8,128)S(1)} %bitcast.120), channel_id=1, source_target_pairs={{0,3},{1,0},{2,1},{3,2},{4,7},{5,4},{6,5},{7,6},{8,11},{9,8},{10,9... | collective-permute-start | bytes 393224 | tf_op jit(solution)/shard_map/ppermute | solution.py:17
  41.7 1.4 copy-start.26
  41.7 3.9 %copy-start.30 = (f32[1024,128]{1,0:T(8,128)}, f32[1024,128]{1,0:T(8,128)S(1)}, u32[]{:S(2)}) copy-start(f32[1024,128]{1,0:T(8,128)S(1)} %collective-permute-done.4.refs_2_) | copy-start | bytes 1572868
  43.1 27.1 %collective-permute-start.7 = (f32[1280,128]{1,0:T(8,128)}, f32[1280,128]{1,0:T(8,128)S(1)}, u32[]{:S(2)}, u32[]{:S(2)}) collective-permute-start(f32[1280,128]{1,0:T(8,128)} %get-tuple-element.64), channel_id=1, source_target_pairs={{0,96},{32,0},{64,32},{96,64},{1,97},{33,1},{65,33},{97,65},{2,98}... | collective-permute-start | bytes 1966088 | tf_op jit(solution)/shard_map/ppermute | solution.py:17
  45.6 24.6 %collective-permute-start.5 = (f32[1280,128]{1,0:T(8,128)}, f32[1280,128]{1,0:T(8,128)S(1)}, u32[]{:S(2)}, u32[]{:S(2)}) collective-permute-start(f32[1280,128]{1,0:T(8,128)} %get-tuple-element.65), channel_id=1, source_target_pairs={{0,32},{32,64},{64,96},{96,0},{1,33},{33,65},{65,97},{97,1},{2,34}... | collective-permute-start | bytes 1966088 | tf_op jit(solution)/shard_map/ppermute | solution.py:17
  45.6 18.3 %all-to-all-start = ((f32[4,256,128]{1,2,0:T(8,128)}), f32[4,256,128]{1,2,0:T(8,128)S(1)}, u32[]{:S(2)}, u32[]{:S(2)}) async-start(f32[4,256,128]{1,2,0:T(8,128)} %get-tuple-element.53), calls=%async_computation | async-start | bytes 1048576 | tf_op jit(solution)/shard_map/all_to_all | solution.py:166
  64.0 17.4 %all-to-all-start.1 = ((f32[4,256,256]{1,2,0:T(8,128)}), f32[4,256,256]{1,2,0:T(8,128)}, u32[]{:S(2)}, u32[]{:S(2)}) async-start(f32[4,256,256]{1,2,0:T(8,128)} %slice_bitcast_fusion), calls=%async_computation.1 | async-start | bytes 2097152 | tf_op jit(solution)/shard_map/all_to_all | solution.py:166
  70.2 1.4 copy-start.18
  70.2 1.4 copy-start.22
  71.6 13.2 %collective-permute-start.9 = (f32[1152,128]{1,0:T(8,128)}, f32[1152,128]{1,0:T(8,128)S(1)}, u32[]{:S(2)}, u32[]{:S(2)}) collective-permute-start(f32[1152,128]{1,0:T(8,128)} %get-tuple-element.62), channel_id=1, source_target_pairs={{0,96},{32,0},{64,32},{96,64},{1,97},{33,1},{65,33},{97,65},{2,98}... | collective-permute-start | bytes 1769480 | tf_op jit(solution)/shard_map/ppermute | solution.py:17
  74.2 12.9 %collective-permute-start.8 = (f32[1152,128]{1,0:T(8,128)}, f32[1152,128]{1,0:T(8,128)S(1)}, u32[]{:S(2)}, u32[]{:S(2)}) collective-permute-start(f32[1152,128]{1,0:T(8,128)} %get-tuple-element.63), channel_id=1, source_target_pairs={{0,32},{32,64},{64,96},{96,0},{1,33},{33,65},{65,97},{97,1},{2,34}... | collective-permute-start | bytes 1769480 | tf_op jit(solution)/shard_map/ppermute | solution.py:17
  84.8 12.1 %copy-start.14 = (f32[1152,128]{1,0:T(8,128)}, f32[1152,128]{1,0:T(8,128)S(1)}, u32[]{:S(2)}) copy-start(f32[1152,128]{1,0:T(8,128)S(1)} %collective-permute-done.9.refs_9_.refs_5_) | copy-start | bytes 1769476
  87.1 9.9 %copy-start.16 = (f32[1152,128]{1,0:T(8,128)}, f32[1152,128]{1,0:T(8,128)S(1)}, u32[]{:S(2)}) copy-start(f32[1152,128]{1,0:T(8,128)S(1)} %collective-permute-done.8.refs_8_.refs_3_) | copy-start | bytes 1769476
  89.4 3.4 %copy-start = (f32[8256,256]{1,0:T(8,128)S(1)}, f32[8256,256]{1,0:T(8,128)}, u32[]{:S(2)}) copy-start(f32[8256,256]{1,0:T(8,128)} %all-gather.3.cloned.1.call-done) | copy-start | bytes 25362436
  94.1 2.6 copy-start.1
  97.0 2.8 %copy-start.2 = (bf16[4,4,256,768]{3,2,1,0:T(8,128)(2,1)S(1)}, bf16[4,4,256,768]{3,2,1,0:T(8,128)(2,1)}, u32[]{:S(2)}) copy-start(bf16[4,4,256,768]{3,2,1,0:T(8,128)(2,1)} %copy-done.1) | copy-start | bytes 18874372
  99.8 1.1 copy-start.19
  100.8 1.1 copy-start.23
  101.9 1.0 copy-start.27
  103.0 1.0 copy-start.31
  112.1 7.6 %collective-permute-start.10 = (f32[4,2,256,128]{3,2,1,0:T(8,128)S(1)}, f32[4,2,256,128]{3,2,1,0:T(8,128)S(1)}, u32[]{:S(2)}, u32[]{:S(2)}) collective-permute-start(f32[4,2,256,128]{3,2,1,0:T(8,128)S(1)} %get-tuple-element.39), channel_id=1, source_target_pairs={{0,16},{16,0},{1,17},{17,1},{2,18},{18,2},{3,19},{19,3},{4,20},{20... | collective-permute-start | bytes 3145736 | tf_op jit(solution)/shard_map/ppermute | solution.py:17
  116.9 24.7 %collective-permute-start.11 = (f32[1920,128]{1,0:T(8,128)}, f32[1920,128]{1,0:T(8,128)S(1)}, u32[]{:S(2)}, u32[]{:S(2)}) collective-permute-start(f32[1920,128]{1,0:T(8,128)} %get-tuple-element.41), channel_id=1, source_target_pairs={{0,32},{32,64},{64,96},{96,0},{1,33},{33,65},{65,97},{97,1},{2,34}... | collective-permute-start | bytes 2949128 | tf_op jit(solution)/shard_map/ppermute | solution.py:17
  116.9 25.7 %collective-permute-start.12 = (f32[1920,128]{1,0:T(8,128)}, f32[1920,128]{1,0:T(8,128)S(1)}, u32[]{:S(2)}, u32[]{:S(2)}) collective-permute-start(f32[1920,128]{1,0:T(8,128)} %get-tuple-element.42), channel_id=1, source_target_pairs={{0,96},{32,0},{64,32},{96,64},{1,97},{33,1},{65,33},{97,65},{2,98}... | collective-permute-start | bytes 2949128 | tf_op jit(solution)/shard_map/ppermute | solution.py:17
  142.6 1.0 copy-start.8
  143.6 2.8 %copy-start.3 = (bf16[4,4,256,768]{3,2,1,0:T(8,128)(2,1)S(1)}, bf16[4,4,256,768]{3,2,1,0:T(8,128)(2,1)}, u32[]{:S(2)}) copy-start(bf16[4,4,256,768]{3,2,1,0:T(8,128)(2,1)} %copy-done.1) | copy-start | bytes 18874372
  146.4 1.2 copy-start.6
  147.6 1.2 copy-start.9
  148.8 1.0 copy-start.12
  149.8 1.1 copy-start.15
  150.9 1.1 copy-start.17
  152.0 1.1 copy-start.20
  153.1 1.1 copy-start.24
  154.1 1.0 copy-start.28
  155.2 1.0 copy-start.32
  165.2 5.7 %slice-start = ((f32[1920,128]{1,0:T(8,128)}), f32[1536,128]{1,0:T(8,128)S(1)}, s32[]{:S(2)}) async-start(f32[1920,128]{1,0:T(8,128)} %copy-done.5), calls=%async_computation.6 | async-start | bytes 1572864 | tf_op jit(solution)/shard_map/slice | solution.py:185
  165.2 22.8 %collective-permute-start.13 = (f32[4,2,256,128]{3,2,1,0:T(8,128)}, f32[4,2,256,128]{3,2,1,0:T(8,128)}, u32[]{:S(2)}, u32[]{:S(2)}) collective-permute-start(f32[4,2,256,128]{3,2,1,0:T(8,128)} %get-tuple-element.44), channel_id=1, source_target_pairs={{0,16},{16,0},{1,17},{17,1},{2,18},{18,2},{3,19},{19,3},{4,20},{20... | collective-permute-start | bytes 3145736 | tf_op jit(solution)/shard_map/ppermute | solution.py:17
  166.7 19.4 %all-to-all-start.2 = ((f32[4,2,256,128]{3,2,1,0:T(8,128)}), f32[4,2,256,128]{3,2,1,0:T(8,128)}, u32[]{:S(2)}, u32[]{:S(2)}) async-start(f32[4,2,256,128]{3,2,1,0:T(8,128)} %add.236), calls=%async_computation.2 | async-start | bytes 2097152 | tf_op jit(solution)/shard_map/all_to_all | solution.py:205
  170.9 1.3 slice-start.1
  171.7 18.7 %collective-permute-start.14 = (f32[768,128]{1,0:T(8,128)}, f32[768,128]{1,0:T(8,128)S(1)}, u32[]{:S(2)}, u32[]{:S(2)}) collective-permute-start(f32[768,128]{1,0:T(8,128)} %bitcast.42), channel_id=1, source_target_pairs={{0,32},{32,64},{64,96},{96,0},{1,33},{33,65},{65,97},{97,1},{2,34}... | collective-permute-start | bytes 1179656 | tf_op jit(solution)/shard_map/ppermute | solution.py:17
  173.0 18.9 %copy-start.13 = (f32[2,2,256,128]{3,2,1,0:T(8,128)S(1)}, f32[2,2,256,128]{3,2,1,0:T(8,128)}, u32[]{:S(2)}) copy-start(f32[2,2,256,128]{3,2,1,0:T(8,128)} %copy-done.11) | copy-start | bytes 1572868
  173.0 18.2 %collective-permute-start.15 = (f32[768,128]{1,0:T(8,128)}, f32[768,128]{1,0:T(8,128)S(1)}, u32[]{:S(2)}, u32[]{:S(2)}) collective-permute-start(f32[768,128]{1,0:T(8,128)} %bitcast.44), channel_id=1, source_target_pairs={{0,96},{32,0},{64,32},{96,64},{1,97},{33,1},{65,33},{97,65},{2,98}... | collective-permute-start | bytes 1179656 | tf_op jit(solution)/shard_map/ppermute | solution.py:17
  191.9 2.8 %copy-start.4 = (bf16[4,4,256,768]{3,2,1,0:T(8,128)(2,1)S(1)}, bf16[4,4,256,768]{3,2,1,0:T(8,128)(2,1)}, u32[]{:S(2)}) copy-start(bf16[4,4,256,768]{3,2,1,0:T(8,128)(2,1)} %copy-done.1) | copy-start | bytes 18874372
  194.7 1.2 copy-start.7
  195.9 1.2 copy-start.10
  197.1 1.1 copy-start.21
  198.2 1.1 copy-start.25
  199.3 1.0 copy-start.29
  200.4 1.0 copy-start.33
  201.4 1.0 copy-start.35
  202.4 1.0 copy-start.37
  214.4 4.8 %collective-permute-start.16 = (f32[4,2,256,256]{3,2,1,0:T(8,128)}, f32[4,2,256,256]{3,2,1,0:T(8,128)}, u32[]{:S(2)}, u32[]{:S(2)}) collective-permute-start(f32[4,2,256,256]{3,2,1,0:T(8,128)} %get-tuple-element.51), channel_id=1, source_target_pairs={{0,16},{16,0},{1,17},{17,1},{2,18},{18,2},{3,19},{19,3},{4,20},{20... | collective-permute-start | bytes 6291464 | tf_op jit(solution)/shard_map/ppermute | solution.py:17
  214.9 19.5 %all-to-all-start.3 = ((f32[4,2,256,128]{3,2,1,0:T(8,128)}), f32[4,2,256,128]{3,2,1,0:T(8,128)}, u32[]{:S(2)}, u32[]{:S(2)}) async-start(f32[4,2,256,128]{3,2,1,0:T(8,128)} %add.237), calls=%async_computation.3 | async-start | bytes 2097152 | tf_op jit(solution)/shard_map/all_to_all | solution.py:205
  222.4 16.9 %copy-start.41 = (f32[2,256,128]{2,1,0:T(8,128)S(1)}, f32[2,256,128]{2,1,0:T(8,128)}, u32[]{:S(2)}) copy-start(f32[2,256,128]{2,1,0:T(8,128)} %fusion.4) | copy-start | bytes 786436
  234.4 29.1 %all-to-all-start.4 = ((f32[4,2,256,256]{3,2,1,0:T(8,128)}), f32[4,2,256,256]{3,2,1,0:T(8,128)S(1)}, u32[]{:S(2)}, u32[]{:S(2)}) async-start(f32[4,2,256,256]{3,2,1,0:T(8,128)} %add.246), calls=%async_computation.4 | async-start | bytes 4194304 | tf_op jit(solution)/shard_map/all_to_all | solution.py:205
  263.5 1.2 copy-start.40
  (3 other events, 2.5 us)
Sparse Core Ops, SparseCore 0:
  9.9 65.1 all-gather.2

commit v6 on v4

v6 whole, which is shorter than its diff:
```python
import jax
import jax.numpy as jnp
from jax import lax
from jax.experimental import pallas as pl
from jax.experimental.pallas import tpu as pltpu
from jax.sharding import Mesh, PartitionSpec as P

NAMES = ("z", "c", "y", "x")
SIZE = {"z": 4, "c": 2, "y": 4, "x": 4}
MIB = 1024 * 1024

def shift(t, axis, s):
    n = SIZE[axis]
    return lax.ppermute(t, axis, [(i, (i + s) % n) for i in range(n)])


def halves(a):
    hi = a.astype(jnp.bfloat16)
    return hi, (a - hi.astype(jnp.float32)).astype(jnp.bfloat16)


def split_kernel(c_ref, a_ref, b_ref, o_ref):
    w = a_ref.shape[-1]
    for il, ref in enumerate((a_ref, b_ref)):
        for core in range(2):
            hi, lo = halves(ref[core])
            o_ref[0, 2 * core + il, :, :w] = hi
            o_ref[0, 2 * core + il, :, w : 2 * w] = lo
            o_ref[0, 2 * core + il, :, 2 * w :] = hi


def split_amp(c, a):
    w = a.shape[-1]
    tile = lambda il: pl.BlockSpec((2, w, w), lambda g, m: (g, 2 * il + m[0], 0))
    return pl.pallas_call(
        split_kernel,
        grid_spec=pltpu.PrefetchScalarGridSpec(
            num_scalar_prefetch=1,
            grid=(4,),
            in_specs=[tile(0), tile(1)],
            out_specs=pl.BlockSpec((1, 4, w, 3 * w), lambda g, m: (g, 0, 0, 0)),
        ),
        out_shape=jax.ShapeDtypeStruct((4, 4, w, 3 * w), jnp.bfloat16),
        compiler_params=pltpu.CompilerParams(vmem_limit_bytes=12 * MIB),
        cost_estimate=pl.CostEstimate(flops=0, bytes_accessed=10 * MIB, transcendentals=0),
        name="split_amp",
    )(c, a, a)


def make_contract_kernel(kp, split):
    def kernel(flag_ref, a_ref, own, own_r, own_l, rest, two_r, two_l, own_fa, own_fb, fa, fb, *refs):
        outs, b_ref = refs[:-1], refs[-1]
        w = b_ref.shape[2]
        h = w // 2

        def load(s, b, at=0):
            n = b.shape[0]
            hi, lo = halves(b)
            b_ref[s, at : at + n] = hi
            b_ref[s, w + at : w + at + n] = hi
            b_ref[s, 2 * w + at : 2 * w + at + n] = lo

        z, c, x = flag_ref[128], flag_ref[129], flag_ref[130]

        @pl.loop(0, 4)
        def _(step):
            ka = lax.rem(z + jnp.where(step == 1, 3, jnp.where(step == 2, 1, jnp.where(step == 3, 2, 0))), 4)
            for at, (mine, others) in enumerate(((own, rest), (own_r, two_r), (own_l, two_l))):
                @pl.when(step == at)
                def _():
                    load(0, mine[kp])
                    for s in range(3):
                        load(s + 1, others[s])

            @pl.when(step == 3)
            def _():
                for part, (mine, others) in enumerate(((own_fa, fa), (own_fb, fb))):
                    load(0, mine[3, kp * h : kp * h + h], part * h)
                    for s in range(3):
                        load(s + 1, others[s], part * h)

            for turn in range(2):
                core = lax.rem(c + turn, 2) if split else turn
                for il in range(2):
                    out, at = (outs[turn], (ka, il)) if split else (outs[0], (ka, 2 * turn + il))
                    out[at] = jnp.zeros((w, w), jnp.float32)
                    for s in range(4):
                        jx = lax.rem(x + s, 4)

                        @pl.when(flag_ref[(jx * 2 + core) * 16 + kp * 8 + ka * 2 + il] != 0)
                        def _():
                            out[at] += jnp.dot(
                                a_ref[jx, 2 * core + il], b_ref[s], preferred_element_type=jnp.float32
                            )

    return kernel


def contract(kp, split, flags, a3, pieces):
    w = a3.shape[2]
    inside = pl.BlockSpec(memory_space=pltpu.VMEM)
    out = [jax.ShapeDtypeStruct((4, 2, w, w), jnp.float32)] * 2 if split else [
        jax.ShapeDtypeStruct((4, 4, w, w), jnp.float32)]
    return pl.pallas_call(
        make_contract_kernel(kp, split),
        in_specs=[pl.BlockSpec(memory_space=pltpu.SMEM)] + [inside] * (len(pieces) + 1),
        out_specs=[inside] * len(out),
        scratch_shapes=[pltpu.VMEM((4, 3 * w, w), jnp.bfloat16)],
        out_shape=out,
        compiler_params=pltpu.CompilerParams(vmem_limit_bytes=28 * MIB),
        cost_estimate=pl.CostEstimate(flops=40 * 10**9, bytes_accessed=8 * MIB, transcendentals=0),
        name="contract",
    )(flags, a3, *pieces)


def on_device(amp, integ, resid, triples):
    w = amp.shape[-1]
    h = w // 2
    z, c, y, x = (lax.axis_index(n) for n in NAMES)

    tri = triples[0, 0]
    i = tri[0] // 32
    j = tri[0] % 32
    k = tri[1] % 32
    slot = (((j % 2 * 4 + (k // 2) % 4) * 2 + k % 2) * 4 + k // 8) * 2 + i % 2
    place = lax.broadcasted_iota(jnp.int32, (32, w), 1)
    listed = jnp.sum((place == slot[:, None]).astype(jnp.float32), axis=0, keepdims=True)

    gathered = lax.all_gather(
        jnp.concatenate([amp.reshape(4 * w, w), jnp.broadcast_to(listed, (8, w))]), ("x", "c")
    )
    a3 = split_amp(c[None], gathered)
    flags = lax.dynamic_index_in_dim(gathered[:, 4 * w, :128].reshape(4, 2, 8, 16), c * 4 + x, 2, keepdims=False)
    flags = jnp.concatenate([flags.reshape(-1).astype(jnp.int32), jnp.stack([z, c, x])])

    mine = lax.dynamic_index_in_dim(integ, c, 0, keepdims=False)
    other = shift(lax.dynamic_index_in_dim(integ, 1 - c, 0, keepdims=False), "c", 1)
    pairs = jnp.where(c == 0, jnp.stack([mine, other]), jnp.stack([other, mine])).reshape(4, 2, w, w)
    own = lax.dynamic_index_in_dim(pairs, x, 0, keepdims=False)
    own_r, own_l = shift(own, "z", 1), shift(own, "z", -1)

    def others(kp):
        held = lax.all_to_all(pairs[:, kp], "x", 0, 0, tiled=True)
        return lax.dynamic_slice_in_dim(jnp.concatenate([held, held]), x + 1, 3, 0)

    rest = [others(0), others(1)]

    two_r = shift(jnp.concatenate([rest[0], own_r[:, :h].reshape(1, w, w)]), "z", 1)
    two_l = shift(jnp.concatenate([rest[0], own_l[:, h:].reshape(1, w, w)]), "z", -1)
    two_r, two_l, rest[1] = lax.optimization_barrier((two_r, two_l, rest[1]))
    far0 = shift(two_r[:3, :h], "z", 1), shift(two_l[:3, h:], "z", -1)
    rest1_r, rest1_l = shift(rest[1], "z", 1), shift(rest[1], "z", -1)
    far1 = shift(rest1_r[:, :h], "z", 1), shift(rest1_l[:, h:], "z", -1)

    pieces = own, own_r, own_l
    (part,) = contract(0, False, flags, a3, pieces + (rest[0], two_r, two_l, two_r, two_l) + far0)
    even = lax.psum_scatter(part.reshape(16, w, w), ("y", "c"), scatter_dimension=0, tiled=True)
    held, away = contract(1, True, flags, a3, pieces + (rest[1], rest1_r, rest1_l, two_r, two_l) + far1)
    part = lax.all_to_all(held + shift(away, "c", 1), "y", 0, 0, tiled=True)
    return resid + jnp.stack([even, part[0] + part[1] + part[2] + part[3]], axis=1)


def solution(mesh):
    fine = Mesh(mesh.devices.reshape(4, 2, 4, 4), NAMES)
    row, col = ("z", "c"), ("y", "x")
    return jax.shard_map(
        on_device,
        mesh=fine,
        in_specs=(P(row, col), P(col, row), P(row, col), P(row, col)),
        out_specs=P(row, col),
        check_vma=False,
    )
```

time: 235 us -> 187 us (0.80)
  waiting for transfers between devices: 85.3 us -> 42.3 us
  blocking collectives: 34.9 us -> 56 us
  starting transfers between devices: 40.6 us -> 24.8 us
  other arithmetic: 15.3 us -> 9.28 us
    all_to_all x2 -> x0, waiting for transfers between devices: 33.4 us -> none  [on_device(): part = lax.all_to_all(part, 'y', 0, 0, tiled=True)]
    all_to_all x1, blocking collectives: 13.9 us -> 26.7 us  [others(): held = lax.all_to_all(pairs[:, kp], 'x', 0, 0, tiled=True)]
    ppermute x15 -> x12, waiting for transfers between devices: 45.6 us -> 34.1 us  [shift(): return lax.ppermute(t, axis, [(i, (i + s) % n) for i in range(n)])]
    all_to_all x1, blocking collectives: 21 us -> 29.3 us  [on_device(): part = lax.all_to_all(held + shift(away, 'c', 1), 'y', 0, 0, tiled=True)]
    ppermute x15 -> x12, starting transfers between devices: 28.4 us -> 20.5 us  [shift(): return lax.ppermute(t, axis, [(i, (i + s) % n) for i in range(n)])]
    all_to_all x2 -> x0, starting transfers between devices: 7.87 us -> none  [on_device(): part = lax.all_to_all(part, 'y', 0, 0, tiled=True)]
    add x7 -> x3, other arithmetic: 7.86 us -> 1.71 us  [the longest x1 1.18 us: on_device(): resid + jnp.stack([even, part[0] + part[1] + part[2] + part[3]], axis=1)]
    select_n x2 -> x1, other arithmetic: 0.27 us -> 2.68 us  [on_device(): jnp.where(c == 0, jnp.stack([mine, other]), jnp.stack([other, mine]))]
  transfers between devices with their start and end apart: 20 -> 15, of which waited for: 12 -> 9; matrix products, arithmetic and copies ran while one was open for 8% -> 6% of each run, Pallas kernels for 4% -> 8%
where the time goes in v6:
time: 187 us; the launch traced here: 184 us
  blocking collectives  56 us (30%)
  waiting for transfers between devices  42.3 us (23%)
  starting transfers between devices  24.8 us (13%)
  local copies, waits for them, and re-layouts  23 us (12%)
  Pallas kernels  15.2 us (8%)
  between operations  13.6 us (7%)
  other arithmetic  9.28 us (5%)
    ppermute x12, waiting for transfers between devices, shift(): return lax.ppermute(t, axis, [(i, (i + s) % n) for i in range(n)])  34.1 us
    all_to_all x1, blocking collectives, on_device(): part = lax.all_to_all(held + shift(away, 'c', 1), 'y', 0, 0, tiled=True)  29.3 us
    all_to_all x1, blocking collectives, others(): held = lax.all_to_all(pairs[:, kp], 'x', 0, 0, tiled=True)  26.7 us
    ppermute x12, starting transfers between devices, shift(): return lax.ppermute(t, axis, [(i, (i + s) % n) for i in range(n)])  20.5 us
    unnamed x34, local copies, waits for them, and re-layouts  15.2 us
    pallas_call x2, Pallas kernels, contract(): pl.pallas_call(make_contract_kernel(kp, split), in_specs=[pl.BlockSpec(me...  13.9 us
    all_to_all x1, waiting for transfers between devices, others(): held = lax.all_to_all(pairs[:, kp], 'x', 0, 0, tiled=True)  8.14 us
    all_to_all x1, starting transfers between devices, others(): held = lax.all_to_all(pairs[:, kp], 'x', 0, 0, tiled=True)  4.26 us
  transfers between devices with their start and end apart: 15, of which 9 were waited for; matrix products, arithmetic and copies ran while one was open for 6% of the time, Pallas kernels for 8%

profile of v6, /device:TPU:1, one launch (start us, length us, event | category | flops | bytes accessed | tf_op | source)
XLA Modules:
  0.0 184.2 jit_solution(15528328924848967877)
XLA Ops:
  6.5 0.9 fusion.5
  7.4 0.1 convert_reduce_fusion
  7.5 2.3 %pad_maximum_fusion.2 = f32[1032,256]{1,0:T(8,128)} fusion(f32[8,256]{1,0:T(8,128)S(1)} %broadcast_in_dim.2, f32[1024,256]{1,0:T(8,128)} %bitcast.52), kind=kLoop, calls=%fused_computation.7 | loop fusion | flops 264192 | bytes 2113536 | tf_op jit(solution)/shard_map/concatenate | solution.py:130
  9.8 0.0 all-gather.3.cloned.1.call-update
  9.8 1.6 constant_dynamic-slice_fusion
  11.4 1.4 collective-permute-start
  12.8 2.5 %collective-permute-done = f32[4,256,256]{2,1,0:T(8,128)S(1)} collective-permute-done((f32[4,256,256]{2,1,0:T(8,128)}, f32[4,256,256]{2,1,0:T(8,128)S(1)}, u32[]{:S(2)}, u32[]{:S(2)}) %collective-permute-start) | collective-permute-done | bytes 1048608 | tf_op jit(solution)/shard_map/ppermute | solution.py:14
  15.3 1.0 copy-done.16
  16.3 2.7 %maximum_select_fusion = f32[2,4,256,256]{3,2,1,0:T(8,128)S(1)} fusion(f32[1,4,256,256]{3,2,1,0:T(8,128)} %bitcast.51, f32[1,4,256,256]{3,2,1,0:T(8,128)} %get-tuple-element.17, pred[]{:T(512)S(6)} %eq.20), kind=kLoop, calls=%fused_computation | loop fusion | flops 1572864 | bytes 4194305 | tf_op jit(solution)/shard_map/jit(_where)/select_n | solution.py:138
  19.0 1.6 slice_bitcast_fusion
  20.6 4.3 %all-to-all-start = ((f32[4,256,256]{2,1,0:T(8,128)}), f32[4,256,256]{2,1,0:T(8,128)}, u32[]{:S(2)}, u32[]{:S(2)}) async-start(f32[4,256,256]{2,1,0:T(8,128)} %get-tuple-element.16), calls=%async_computation | async-start | bytes 2097152 | tf_op jit(solution)/shard_map/all_to_all | solution.py:143
  24.8 0.0 reduce-scatter.2.cloned.1.call-start
  24.9 3.9 %collective-permute-start.2 = (f32[2,256,256]{2,1,0:T(8,128)S(1)}, f32[2,256,256]{2,1,0:T(8,128)S(1)}, u32[]{:S(2)}, u32[]{:S(2)}) collective-permute-start(f32[2,256,256]{2,1,0:T(8,128)S(1)} %dynamic-slice_bitcast_fusion.1.own), channel_id=1, source_target_pairs={{0,96},{32,0},{64,32},{96,64},{1,97},{33,1},{65,33},{97,65},{2,98}... | collective-permute-start | bytes 1572872 | tf_op jit(solution)/shard_map/ppermute | solution.py:14
  28.8 0.0 collective-permute-start.1
  28.8 10.9 %collective-permute-done.2.own_l = f32[2,256,256]{2,1,0:T(8,128)S(1)} collective-permute-done((f32[2,256,256]{2,1,0:T(8,128)S(1)}, f32[2,256,256]{2,1,0:T(8,128)S(1)}, u32[]{:S(2)}, u32[]{:S(2)}) %collective-permute-start.2) | collective-permute-done | bytes 524320 | tf_op jit(solution)/shard_map/ppermute | solution.py:14
  39.8 3.2 %collective-permute-done.1.own_r = f32[2,256,256]{2,1,0:T(8,128)S(1)} collective-permute-done((f32[2,256,256]{2,1,0:T(8,128)S(1)}, f32[2,256,256]{2,1,0:T(8,128)S(1)}, u32[]{:S(2)}, u32[]{:S(2)}) %collective-permute-start.1) | collective-permute-done | bytes 524320 | tf_op jit(solution)/shard_map/ppermute | solution.py:14
  43.0 8.1 %all-to-all-done = f32[4,256,256]{2,1,0:T(8,128)} async-done(((f32[4,256,256]{2,1,0:T(8,128)}), f32[4,256,256]{2,1,0:T(8,128)}, u32[]{:S(2)}, u32[]{:S(2)}) %all-to-all-start) | async-done | bytes 1048608 | tf_op jit(solution)/shard_map/all_to_all | solution.py:143
  51.1 1.2 fusion.1.rest
  52.4 0.0 copy-start.13
  52.4 0.2 pad_maximum_fusion
  52.6 2.0 %collective-permute-start.3 = (f32[4,256,256]{2,1,0:T(8,128)S(1)}, f32[4,256,256]{2,1,0:T(8,128)S(1)}, u32[]{:S(2)}, u32[]{:S(2)}) collective-permute-start(f32[4,256,256]{2,1,0:T(8,128)S(1)} %get-tuple-element.20), channel_id=1, source_target_pairs={{0,32},{32,64},{64,96},{96,0},{1,33},{33,65},{65,97},{97,1},{2,34}... | collective-permute-start | bytes 3145736 | tf_op jit(solution)/shard_map/ppermute | solution.py:14
  54.6 2.4 %collective-permute-start.4 = (f32[4,256,256]{2,1,0:T(8,128)S(1)}, f32[4,256,256]{2,1,0:T(8,128)S(1)}, u32[]{:S(2)}, u32[]{:S(2)}) collective-permute-start(f32[4,256,256]{2,1,0:T(8,128)S(1)} %get-tuple-element.19), channel_id=1, source_target_pairs={{0,96},{32,0},{64,32},{96,64},{1,97},{33,1},{65,33},{97,65},{2,98}... | collective-permute-start | bytes 3145736 | tf_op jit(solution)/shard_map/ppermute | solution.py:14
  56.9 26.7 %all_to_all.15 = f32[4,256,256]{2,1,0:T(8,128)S(1)} all-to-all(f32[4,256,256]{2,1,0:T(8,128)S(1)} %copy-done.13), channel_id=1, replica_groups=mesh['z'=4,'c'=2,'y'=4,'x'=4] {'x'}, dimensions={0} | all-to-all | bytes 2097152 | tf_op jit(solution)/shard_map/all_to_all | solution.py:143
  83.6 0.1 fusion.rest
  83.8 0.0 collective-permute-done.3.two_r.own_fa
  83.8 0.8 slice.55
  84.6 1.0 copy-done.4
  85.6 1.2 collective-permute-start.5
  86.7 0.8 slice.56
  87.5 1.0 copy-done.7
  88.5 1.5 collective-permute-start.6
  90.0 0.0 collective-permute-start.7
  90.0 2.7 %collective-permute-start.8 = (f32[3,256,256]{2,1,0:T(8,128)S(1)}, f32[3,256,256]{2,1,0:T(8,128)}, u32[]{:S(2)}, u32[]{:S(2)}) collective-permute-start(f32[3,256,256]{2,1,0:T(8,128)S(1)} %fusion.rest), channel_id=1, source_target_pairs={{0,96},{32,0},{64,32},{96,64},{1,97},{33,1},{65,33},{97,65},{2,98}... | collective-permute-start | bytes 2359304 | tf_op jit(solution)/shard_map/ppermute | solution.py:14
  92.7 0.8 slice_reduce_fusion
  93.5 0.1 reshape_squeeze.3
  93.6 0.1 convert_element_type.11
  93.7 3.4 %copy-done = f32[8256,256]{1,0:T(8,128)S(1)} copy-done((f32[8256,256]{1,0:T(8,128)S(1)}, f32[8256,256]{1,0:T(8,128)}, u32[]{:S(2)}) %copy-start) | copy-done | bytes 8454168
  97.1 1.3 split_amp.1.a_ref
  98.4 0.1 pad_add_fusion.flag_ref
  98.4 0.2 copy-done.8
  98.6 0.1 copy-done.11
  98.7 6.3 %contract.2 = f32[4,4,256,256]{3,2,1,0:T(8,128)S(1)} custom-call(s32[131]{0:T(256)S(1)} %pad_add_fusion.flag_ref, bf16[4,4,256,768]{3,2,1,0:T(8,128)(2,1)S(1)} %split_amp.1.a_ref, f32[2,256,256]{2,1,0:T(8,128)S(1)} %dynamic-slice_bitcast_fusion.1.own, f32[2,256,256]{2,1,0:T(8,128)S(1)} %copy-done.11, f32[2,256,256]{2,1,0:T(8,128)S(1)} %collective-permute-done.2.own_l, ...), custom_call_target="tpu_custom_call" | custom-call | flops 40000000000 | bytes 8388608 | tf_op jit(solution)/shard_map/contract/pallas_call | solution.py:104
  105.1 2.0 %copy-done.3 = f32[4,4,256,256]{3,2,1,0:T(8,128)} copy-done((f32[4,4,256,256]{3,2,1,0:T(8,128)}, f32[4,4,256,256]{3,2,1,0:T(8,128)S(1)}, u32[]{:S(2)}) %copy-start.3) | copy-done | bytes 4194328
  107.1 0.0 reduce-scatter.2.cloned.1.call-update
  107.2 6.2 %collective-permute-done.7.two_r = f32[3,256,256]{2,1,0:T(8,128)S(1)} collective-permute-done((f32[3,256,256]{2,1,0:T(8,128)S(1)}, f32[3,256,256]{2,1,0:T(8,128)S(1)}, u32[]{:S(2)}, u32[]{:S(2)}) %collective-permute-start.7) | collective-permute-done | bytes 786464 | tf_op jit(solution)/shard_map/ppermute | solution.py:14
  113.4 0.1 collective-permute-start.9
  113.5 1.3 collective-permute-done.8.two_l
  114.8 1.0 slice.69
  115.8 3.1 %collective-permute-start.10 = (f32[3,128,256]{2,1,0:T(8,128)S(1)}, f32[3,128,256]{2,1,0:T(8,128)S(1)}, u32[]{:S(2)}, u32[]{:S(2)}) collective-permute-start(f32[3,128,256]{2,1,0:T(8,128)S(1)} %slice.69), channel_id=1, source_target_pairs={{0,96},{32,0},{64,32},{96,64},{1,97},{33,1},{65,33},{97,65},{2,98}... | collective-permute-start | bytes 1179656 | tf_op jit(solution)/shard_map/ppermute | solution.py:14
  118.9 4.3 %collective-permute-done.9.fa = f32[3,128,256]{2,1,0:T(8,128)S(1)} collective-permute-done((f32[3,128,256]{2,1,0:T(8,128)S(1)}, f32[3,128,256]{2,1,0:T(8,128)S(1)}, u32[]{:S(2)}, u32[]{:S(2)}) %collective-permute-start.9) | collective-permute-done | bytes 393248 | tf_op jit(solution)/shard_map/ppermute | solution.py:14
  123.2 1.8 collective-permute-done.10.fb
  125.0 2.9 %copy-done.2 = bf16[4,4,256,768]{3,2,1,0:T(8,128)(2,1)S(1)} copy-done((bf16[4,4,256,768]{3,2,1,0:T(8,128)(2,1)S(1)}, bf16[4,4,256,768]{3,2,1,0:T(8,128)(2,1)}, u32[]{:S(2)}) %copy-start.2) | copy-done | bytes 6291480
  127.9 1.2 copy-done.6
  129.2 1.2 copy-done.9
  130.4 7.6 %contract.3 = (f32[4,2,256,256]{3,2,1,0:T(8,128)S(1)}, f32[4,2,256,256]{3,2,1,0:T(8,128)S(1)}) custom-call(s32[131]{0:T(256)S(1)} %pad_add_fusion.flag_ref, bf16[4,4,256,768]{3,2,1,0:T(8,128)(2,1)S(1)} %copy-done.2, f32[2,256,256]{2,1,0:T(8,128)S(1)} %dynamic-slice_bitcast_fusion.1.own, f32[2,256,256]{2,1,0:T(8,128)S(1)} %copy-done.12, ...), custom_call_target="tpu_custom_call" | custom-call | flops 40000000000 | bytes 8388608 | tf_op jit(solution)/shard_map/contract/pallas_call | solution.py:104
  138.1 2.3 %collective-permute-start.11 = (f32[4,2,256,256]{3,2,1,0:T(8,128)S(1)}, f32[4,2,256,256]{3,2,1,0:T(8,128)S(1)}, u32[]{:S(2)}, u32[]{:S(2)}) collective-permute-start(f32[4,2,256,256]{3,2,1,0:T(8,128)S(1)} %get-tuple-element.14), channel_id=1, source_target_pairs={{0,16},{16,0},{1,17},{17,1},{2,18},{18,2},{3,19},{19,3},{4,20},{20... | collective-permute-start | bytes 6291464 | tf_op jit(solution)/shard_map/ppermute | solution.py:14
  140.3 3.8 %collective-permute-done.11 = f32[4,2,256,256]{3,2,1,0:T(8,128)S(1)} collective-permute-done((f32[4,2,256,256]{3,2,1,0:T(8,128)S(1)}, f32[4,2,256,256]{3,2,1,0:T(8,128)S(1)}, u32[]{:S(2)}, u32[]{:S(2)}) %collective-permute-start.11) | collective-permute-done | bytes 2097184 | tf_op jit(solution)/shard_map/ppermute | solution.py:14
  144.2 0.4 add.182
  144.6 29.3 %all_to_all.16 = f32[4,2,256,256]{3,2,1,0:T(8,128)S(1)} all-to-all(f32[4,2,256,256]{3,2,1,0:T(8,128)S(1)} %add.182), channel_id=1, replica_groups=mesh['z'=4,'c'=2,'y'=4,'x'=4] {'y'}, dimensions={0} | all-to-all | bytes 4194304 | tf_op jit(solution)/shard_map/all_to_all | solution.py:159
  173.9 0.1 fusion.2
  174.0 0.0 reduce-scatter.2.cloned.1.call-done
  174.0 1.1 copy-done.15
  175.1 1.2 maximum_add_fusion
  176.3 1.0 copy.17
  (34 shorter events, 0.2 us)
Async XLA Ops:
  6.5 3.3 %copy-start.14 = (f32[2,4,256,256]{3,2,1,0:T(8,128)S(1)}, f32[2,4,256,256]{3,2,1,0:T(8,128)}, u32[]{:S(2)}) copy-start(f32[2,4,256,256]{3,2,1,0:T(8,128)} %param.5) | copy-start | bytes 6291460
  6.5 86.2 %all-gather.3.cloned.1.call-start = ((), (), s32[]{:S(2)}) async-start(), calls=%async_computation.5 | async-start | bytes 9510912 | tf_op jit(solution)/shard_map/all_gather | solution.py:129
  11.4 3.9 %collective-permute-start = (f32[4,256,256]{2,1,0:T(8,128)}, f32[4,256,256]{2,1,0:T(8,128)S(1)}, u32[]{:S(2)}, u32[]{:S(2)}) collective-permute-start(f32[4,256,256]{2,1,0:T(8,128)} %get-tuple-element.18), channel_id=1, source_target_pairs={{0,16},{16,0},{1,17},{17,1},{2,18},{18,2},{3,19},{19,3},{4,20},{20... | collective-permute-start | bytes 3145736 | tf_op jit(solution)/shard_map/ppermute | solution.py:14
  15.3 1.0 copy-start.16
  20.6 30.6 %all-to-all-start = ((f32[4,256,256]{2,1,0:T(8,128)}), f32[4,256,256]{2,1,0:T(8,128)}, u32[]{:S(2)}, u32[]{:S(2)}) async-start(f32[4,256,256]{2,1,0:T(8,128)} %get-tuple-element.16), calls=%async_computation | async-start | bytes 2097152 | tf_op jit(solution)/shard_map/all_to_all | solution.py:143
  24.8 149.2 %reduce-scatter.2.cloned.1.call-start = ((), (), s32[]{:S(2)}) async-start(), calls=%async_computation.4 | async-start | bytes 4718592 | tf_op jit(solution)/shard_map/reduce_scatter | solution.py:157
  24.9 14.8 %collective-permute-start.2 = (f32[2,256,256]{2,1,0:T(8,128)S(1)}, f32[2,256,256]{2,1,0:T(8,128)S(1)}, u32[]{:S(2)}, u32[]{:S(2)}) collective-permute-start(f32[2,256,256]{2,1,0:T(8,128)S(1)} %dynamic-slice_bitcast_fusion.1.own), channel_id=1, source_target_pairs={{0,96},{32,0},{64,32},{96,64},{1,97},{33,1},{65,33},{97,65},{2,98}... | collective-permute-start | bytes 1572872 | tf_op jit(solution)/shard_map/ppermute | solution.py:14
  28.8 14.1 %collective-permute-start.1 = (f32[2,256,256]{2,1,0:T(8,128)S(1)}, f32[2,256,256]{2,1,0:T(8,128)S(1)}, u32[]{:S(2)}, u32[]{:S(2)}) collective-permute-start(f32[2,256,256]{2,1,0:T(8,128)S(1)} %dynamic-slice_bitcast_fusion.1.own), channel_id=1, source_target_pairs={{0,32},{32,64},{64,96},{96,0},{1,33},{33,65},{65,97},{97,1},{2,34}... | collective-permute-start | bytes 1572872 | tf_op jit(solution)/shard_map/ppermute | solution.py:14
  43.0 9.6 %copy-start.10 = (f32[2,256,256]{2,1,0:T(8,128)}, f32[2,256,256]{2,1,0:T(8,128)S(1)}, u32[]{:S(2)}) copy-start(f32[2,256,256]{2,1,0:T(8,128)S(1)} %collective-permute-done.1.own_r) | copy-start | bytes 1572868
  52.4 4.6 %copy-start.13 = (f32[4,256,256]{2,1,0:T(8,128)S(1)}, f32[4,256,256]{2,1,0:T(8,128)}, u32[]{:S(2)}) copy-start(f32[4,256,256]{2,1,0:T(8,128)} %get-tuple-element.15) | copy-start | bytes 3145732
  52.6 31.2 %collective-permute-start.3 = (f32[4,256,256]{2,1,0:T(8,128)S(1)}, f32[4,256,256]{2,1,0:T(8,128)S(1)}, u32[]{:S(2)}, u32[]{:S(2)}) collective-permute-start(f32[4,256,256]{2,1,0:T(8,128)S(1)} %get-tuple-element.20), channel_id=1, source_target_pairs={{0,32},{32,64},{64,96},{96,0},{1,33},{33,65},{65,97},{97,1},{2,34}... | collective-permute-start | bytes 3145736 | tf_op jit(solution)/shard_map/ppermute | solution.py:14
  54.6 29.2 %collective-permute-start.4 = (f32[4,256,256]{2,1,0:T(8,128)S(1)}, f32[4,256,256]{2,1,0:T(8,128)S(1)}, u32[]{:S(2)}, u32[]{:S(2)}) collective-permute-start(f32[4,256,256]{2,1,0:T(8,128)S(1)} %get-tuple-element.19), channel_id=1, source_target_pairs={{0,96},{32,0},{64,32},{96,64},{1,97},{33,1},{65,33},{97,65},{2,98}... | collective-permute-start | bytes 3145736 | tf_op jit(solution)/shard_map/ppermute | solution.py:14
  84.6 1.0 copy-start.4
  85.6 12.9 %collective-permute-start.5 = (f32[3,128,256]{2,1,0:T(8,128)}, f32[3,128,256]{2,1,0:T(8,128)}, u32[]{:S(2)}, u32[]{:S(2)}) collective-permute-start(f32[3,128,256]{2,1,0:T(8,128)} %slice.55), channel_id=1, source_target_pairs={{0,32},{32,64},{64,96},{96,0},{1,33},{33,65},{65,97},{97,1},{2,34}... | collective-permute-start | bytes 1179656 | tf_op jit(solution)/shard_map/ppermute | solution.py:14
  87.5 1.0 copy-start.7
  88.5 9.9 %collective-permute-start.6 = (f32[3,128,256]{2,1,0:T(8,128)}, f32[3,128,256]{2,1,0:T(8,128)}, u32[]{:S(2)}, u32[]{:S(2)}) collective-permute-start(f32[3,128,256]{2,1,0:T(8,128)} %slice.56), channel_id=1, source_target_pairs={{0,96},{32,0},{64,32},{96,64},{1,97},{33,1},{65,33},{97,65},{2,98}... | collective-permute-start | bytes 1179656 | tf_op jit(solution)/shard_map/ppermute | solution.py:14
  90.0 23.3 %collective-permute-start.7 = (f32[3,256,256]{2,1,0:T(8,128)S(1)}, f32[3,256,256]{2,1,0:T(8,128)S(1)}, u32[]{:S(2)}, u32[]{:S(2)}) collective-permute-start(f32[3,256,256]{2,1,0:T(8,128)S(1)} %fusion.rest), channel_id=1, source_target_pairs={{0,32},{32,64},{64,96},{96,0},{1,33},{33,65},{65,97},{97,1},{2,34}... | collective-permute-start | bytes 2359304 | tf_op jit(solution)/shard_map/ppermute | solution.py:14
  90.0 24.7 %collective-permute-start.8 = (f32[3,256,256]{2,1,0:T(8,128)S(1)}, f32[3,256,256]{2,1,0:T(8,128)}, u32[]{:S(2)}, u32[]{:S(2)}) collective-permute-start(f32[3,256,256]{2,1,0:T(8,128)S(1)} %fusion.rest), channel_id=1, source_target_pairs={{0,96},{32,0},{64,32},{96,64},{1,97},{33,1},{65,33},{97,65},{2,98}... | collective-permute-start | bytes 2359304 | tf_op jit(solution)/shard_map/ppermute | solution.py:14
  93.7 3.4 %copy-start = (f32[8256,256]{1,0:T(8,128)S(1)}, f32[8256,256]{1,0:T(8,128)}, u32[]{:S(2)}) copy-start(f32[8256,256]{1,0:T(8,128)} %all-gather.3.cloned.1.call-done) | copy-start | bytes 25362436
  97.1 1.4 copy-start.5
  97.1 1.5 copy-start.8
  97.1 1.7 copy-start.11
  98.3 6.7 %copy-start.1 = (bf16[4,4,256,768]{3,2,1,0:T(8,128)(2,1)}, bf16[4,4,256,768]{3,2,1,0:T(8,128)(2,1)S(1)}, u32[]{:S(2)}) copy-start(bf16[4,4,256,768]{3,2,1,0:T(8,128)(2,1)S(1)} %split_amp.1.a_ref) | copy-start | bytes 18874372
  105.1 2.1 %copy-start.3 = (f32[4,4,256,256]{3,2,1,0:T(8,128)}, f32[4,4,256,256]{3,2,1,0:T(8,128)S(1)}, u32[]{:S(2)}) copy-start(f32[4,4,256,256]{3,2,1,0:T(8,128)S(1)} %contract.2) | copy-start | bytes 12582916
  107.1 17.9 %copy-start.12 = (f32[2,256,256]{2,1,0:T(8,128)S(1)}, f32[2,256,256]{2,1,0:T(8,128)}, u32[]{:S(2)}) copy-start(f32[2,256,256]{2,1,0:T(8,128)} %copy-done.10) | copy-start | bytes 1572868
  113.4 9.9 %collective-permute-start.9 = (f32[3,128,256]{2,1,0:T(8,128)S(1)}, f32[3,128,256]{2,1,0:T(8,128)S(1)}, u32[]{:S(2)}, u32[]{:S(2)}) collective-permute-start(f32[3,128,256]{2,1,0:T(8,128)S(1)} %slice.68), channel_id=1, source_target_pairs={{0,32},{32,64},{64,96},{96,0},{1,33},{33,65},{65,97},{97,1},{2,34}... | collective-permute-start | bytes 1179656 | tf_op jit(solution)/shard_map/ppermute | solution.py:14
  115.8 9.2 %collective-permute-start.10 = (f32[3,128,256]{2,1,0:T(8,128)S(1)}, f32[3,128,256]{2,1,0:T(8,128)S(1)}, u32[]{:S(2)}, u32[]{:S(2)}) collective-permute-start(f32[3,128,256]{2,1,0:T(8,128)S(1)} %slice.69), channel_id=1, source_target_pairs={{0,96},{32,0},{64,32},{96,64},{1,97},{33,1},{65,33},{97,65},{2,98}... | collective-permute-start | bytes 1179656 | tf_op jit(solution)/shard_map/ppermute | solution.py:14
  125.0 2.9 %copy-start.2 = (bf16[4,4,256,768]{3,2,1,0:T(8,128)(2,1)S(1)}, bf16[4,4,256,768]{3,2,1,0:T(8,128)(2,1)}, u32[]{:S(2)}) copy-start(bf16[4,4,256,768]{3,2,1,0:T(8,128)(2,1)} %copy-done.1) | copy-start | bytes 18874372
  127.9 1.2 copy-start.6
  129.2 1.2 copy-start.9
  138.1 6.1 %collective-permute-start.11 = (f32[4,2,256,256]{3,2,1,0:T(8,128)S(1)}, f32[4,2,256,256]{3,2,1,0:T(8,128)S(1)}, u32[]{:S(2)}, u32[]{:S(2)}) collective-permute-start(f32[4,2,256,256]{3,2,1,0:T(8,128)S(1)} %get-tuple-element.14), channel_id=1, source_target_pairs={{0,16},{16,0},{1,17},{17,1},{2,18},{18,2},{3,19},{19,3},{4,20},{20... | collective-permute-start | bytes 6291464 | tf_op jit(solution)/shard_map/ppermute | solution.py:14
  173.9 1.2 copy-start.15
Sparse Core Ops, SparseCore 0:
  9.9 75.6 all-gather.2
  107.3 40.2 reduce-scatter.1

commit v7 on v6

v7 whole, which is shorter than its diff:
```python
import jax
import jax.numpy as jnp
from jax import lax
from jax.experimental import pallas as pl
from jax.experimental.pallas import tpu as pltpu
from jax.sharding import Mesh, PartitionSpec as P

NAMES = ("z", "c", "y", "x")
SIZE = {"z": 4, "c": 2, "y": 4, "x": 4}
MIB = 1024 * 1024
COST = (40, 40)

def shift(t, axis, s):
    n = SIZE[axis]
    return lax.ppermute(t, axis, [(i, (i + s) % n) for i in range(n)])


def halves(a):
    hi = a.astype(jnp.bfloat16)
    return hi, (a - hi.astype(jnp.float32)).astype(jnp.bfloat16)


def split_kernel(a_ref, r_ref, l_ref, fa_ref, fb_ref, o_ref):
    w = a_ref.shape[-1]

    def put(s, ref):
        for il in range(2):
            hi, lo = halves(ref[0, il * w : il * w + w])
            o_ref[s, il, :, :w] = hi
            o_ref[s, il, :, w : 2 * w] = lo
            o_ref[s, il, :, 2 * w :] = hi

    put(0, a_ref)
    put(1, r_ref)
    put(3, l_ref)

    @pl.when(pl.program_id(0) == 0)
    def _():
        put(2, fa_ref)

    @pl.when(pl.program_id(0) == 1)
    def _():
        put(2, fb_ref)


def split_amp(a, r, l, fa, fb):
    rows, w = a.shape[1:]
    each = pl.BlockSpec((1, rows, w), lambda g: (g, 0, 0))
    only = pl.BlockSpec((1, rows, w), lambda g: (0, 0, 0))
    return pl.pallas_call(
        split_kernel,
        grid=(2,),
        in_specs=[each, each, each, only, only],
        out_specs=pl.BlockSpec((4, 2, w, 3 * w), lambda g: (0, g, 0, 0)),
        out_shape=jax.ShapeDtypeStruct((4, 4, w, 3 * w), jnp.bfloat16),
        compiler_params=pltpu.CompilerParams(vmem_limit_bytes=18 * MIB),
        cost_estimate=pl.CostEstimate(flops=0, bytes_accessed=10 * MIB, transcendentals=0),
        name="split_amp",
    )(a, r, l, fa, fb)


def make_contract_kernel(kp):
    def kernel(flag_ref, a_ref, own, own_r, own_l, rest, two_r, two_l, own_fa, own_fb, fa, fb, *refs):
        outs, b_ref = refs[:-1], refs[-1]
        w = b_ref.shape[2]
        h = w // 2

        def load(s, b, at=0):
            n = b.shape[0]
            hi, lo = halves(b)
            b_ref[s, at : at + n] = hi
            b_ref[s, w + at : w + at + n] = hi
            b_ref[s, 2 * w + at : 2 * w + at + n] = lo

        z, c = flag_ref[128], flag_ref[129]

        @pl.loop(0, 4)
        def _(step):
            ka = lax.rem(z + jnp.where(step == 1, 3, jnp.where(step == 2, 1, jnp.where(step == 3, 2, 0))), 4)
            for at, (mine, others) in enumerate(((own, rest), (own_r, two_r), (own_l, two_l))):
                @pl.when(step == at)
                def _():
                    load(0, mine[kp])
                    for s in range(3):
                        load(s + 1, others[s])

            @pl.when(step == 3)
            def _():
                for part, (mine, others) in enumerate(((own_fa, fa), (own_fb, fb))):
                    load(0, mine[3, kp * h : kp * h + h], part * h)
                    for s in range(3):
                        load(s + 1, others[s], part * h)

            for turn in range(2):
                core = lax.rem(c + turn, 2)
                for il in range(2):
                    out, at = outs[turn], (ka, il)
                    out[at] = jnp.zeros((w, w), jnp.float32)
                    for s in range(4):
                        @pl.when(flag_ref[(s * 2 + core) * 16 + kp * 8 + ka * 2 + il] != 0)
                        def _():
                            out[at] += jnp.dot(
                                a_ref[s, 2 * core + il], b_ref[s], preferred_element_type=jnp.float32
                            )

    return kernel


def contract(kp, flags, a3, pieces):
    w = a3.shape[2]
    inside = pl.BlockSpec(memory_space=pltpu.VMEM)
    out = [jax.ShapeDtypeStruct((4, 2, w, w), jnp.float32)] * 2
    return pl.pallas_call(
        make_contract_kernel(kp),
        in_specs=[pl.BlockSpec(memory_space=pltpu.SMEM)] + [inside] * (len(pieces) + 1),
        out_specs=[inside] * len(out),
        scratch_shapes=[pltpu.VMEM((4, 3 * w, w), jnp.bfloat16)],
        out_shape=out,
        compiler_params=pltpu.CompilerParams(vmem_limit_bytes=28 * MIB),
        cost_estimate=pl.CostEstimate(flops=COST[kp] * 10**9, bytes_accessed=8 * MIB, transcendentals=0),
        name="contract",
    )(flags, a3, *pieces)


def on_device(amp, integ, resid, triples):
    w = amp.shape[-1]
    h = w // 2
    z, c, y, x = (lax.axis_index(n) for n in NAMES)

    tri = triples[0, 0]
    i = tri[0] // 32
    j = tri[0] % 32
    k = tri[1] % 32
    slot = (((j % 2 * 4 + (k // 2) % 4) * 2 + k % 2) * 4 + k // 8) * 2 + i % 2
    place = lax.broadcasted_iota(jnp.int32, (32, w), 1)
    listed = jnp.sum((place == slot[:, None]).astype(jnp.float32), axis=0, keepdims=True)

    mine = lax.dynamic_index_in_dim(integ, c, 0, keepdims=False)
    other = shift(lax.dynamic_index_in_dim(integ, 1 - c, 0, keepdims=False), "c", 1)
    pairs = jnp.where(c == 0, jnp.stack([mine, other]), jnp.stack([other, mine])).reshape(4, 2, w, w)
    own = lax.dynamic_index_in_dim(pairs, x, 0, keepdims=False)
    own_r, own_l = shift(own, "z", 1), shift(own, "z", -1)

    def others(kp):
        held = lax.all_to_all(pairs[:, kp], "x", 0, 0, tiled=True)
        return lax.dynamic_slice_in_dim(jnp.concatenate([held, held]), x + 1, 3, 0)

    rest = [others(0), others(1)]

    def with_flags(parity):
        tile = lax.dynamic_index_in_dim(amp, parity, 1, keepdims=False)
        return jnp.concatenate([tile.reshape(2 * w, w), jnp.broadcast_to(listed, (8, w))])

    a_mine, a_other = with_flags(c), shift(with_flags(1 - c), "c", 1)
    a0 = jnp.where(c == 0, jnp.stack([a_mine, a_other]), jnp.stack([a_other, a_mine]))
    a0, rest[0] = lax.optimization_barrier((a0, rest[0]))
    a_r, a_l = shift(a0, "x", -1), shift(a0, "x", 1)
    a_fa, a_fb = shift(a_r[:1], "x", -1), shift(a_l[1:], "x", 1)
    a3 = split_amp(a0, a_r, a_l, a_fa, a_fb)
    rows = jnp.stack([a0[:, 2 * w, :128], a_r[:, 2 * w, :128],
                      jnp.concatenate([a_fa[:, 2 * w, :128], a_fb[:, 2 * w, :128]]), a_l[:, 2 * w, :128]])
    flags = lax.dynamic_index_in_dim(rows.reshape(4, 2, 8, 16), c * 4 + x, 2, keepdims=False)
    flags = jnp.concatenate([flags.reshape(-1).astype(jnp.int32), jnp.stack([z, c])])

    two_r = shift(jnp.concatenate([rest[0], own_r[:, :h].reshape(1, w, w)]), "z", 1)
    two_l = shift(jnp.concatenate([rest[0], own_l[:, h:].reshape(1, w, w)]), "z", -1)
    two_r, two_l, rest[1] = lax.optimization_barrier((two_r, two_l, rest[1]))
    far0 = shift(two_r[:3, :h], "z", 1), shift(two_l[:3, h:], "z", -1)
    rest1_r, rest1_l = shift(rest[1], "z", 1), shift(rest[1], "z", -1)
    a3, rest1_r, rest1_l = lax.optimization_barrier((a3, rest1_r, rest1_l))
    far1 = shift(rest1_r[:, :h], "z", 1), shift(rest1_l[:, h:], "z", -1)

    pieces = own, own_r, own_l
    held, away = contract(0, flags, a3, pieces + (rest[0], two_r, two_l, two_r, two_l) + far0)
    part = held + shift(away, "c", 1)
    part = lax.all_to_all(part, "y", 0, 0, tiled=True)
    gate = part
    even = part[0] + part[1] + part[2] + part[3]
    held, away = contract(1, flags, a3, pieces + (rest[1], rest1_r, rest1_l, two_r, two_l) + far1)
    away, gate = lax.optimization_barrier((away, gate))
    part = lax.all_to_all(held + shift(away, "c", 1), "y", 0, 0, tiled=True)
    return resid + jnp.stack([even, part[0] + part[1] + part[2] + part[3]], axis=1)


def solution(mesh):
    fine = Mesh(mesh.devices.reshape(4, 2, 4, 4), NAMES)
    row, col = ("z", "c"), ("y", "x")
    return jax.shard_map(
        on_device,
        mesh=fine,
        in_specs=(P(row, col), P(col, row), P(row, col), P(row, col)),
        out_specs=P(row, col),
        check_vma=False,
    )
```

time: 187 us -> 196 us (1.048)
  blocking collectives: 56 us -> 0 us
  waiting for transfers between devices: 42.3 us -> 88.1 us
  starting transfers between devices: 24.8 us -> 45.1 us
  between operations: 13.6 us -> 0.23 us
  other arithmetic: 9.28 us -> 15.3 us
  Pallas kernels: 15.2 us -> 19.2 us
  local copies, waits for them, and re-layouts: 23 us -> 26.8 us
    all_to_all x2 -> x0, blocking collectives: 56 us -> none  [the longest x1 29.3 us: on_device(): part = lax.all_to_all(held + shift(away, 'c', 1), 'y', 0, 0, tiled=True)]
    all_to_all x0 -> x2, waiting for transfers between devices: none -> 33 us  [the longest x1 24.4 us: on_device(): part = lax.all_to_all(held + shift(away, 'c', 1), 'y', 0, 0, tiled=True)]
    all_to_all x1 -> x2, waiting for transfers between devices: 8.14 us -> 26.9 us  [others(): held = lax.all_to_all(pairs[:, kp], 'x', 0, 0, tiled=True)]
    all_to_all x0 -> x2, starting transfers between devices: none -> 8.2 us  [the longest x1 4.59 us: on_device(): part = lax.all_to_all(part, 'y', 0, 0, tiled=True)]
    ppermute x12 -> x18, starting transfers between devices: 20.5 us -> 28.3 us  [shift(): return lax.ppermute(t, axis, [(i, (i + s) % n) for i in range(n)])]
    unnamed x34 -> x24, local copies, waits for them, and re-layouts: 15.2 us -> 7.95 us
    ppermute x12 -> x18, waiting for transfers between devices: 34.1 us -> 28.2 us  [shift(): return lax.ppermute(t, axis, [(i, (i + s) % n) for i in range(n)])]
    all_to_all x1 -> x2, starting transfers between devices: 4.26 us -> 8.62 us  [others(): held = lax.all_to_all(pairs[:, kp], 'x', 0, 0, tiled=True)]
  transfers between devices with their start and end apart: 15 -> 22, of which waited for: 9 -> 10; matrix products, arithmetic and copies ran while one was open for 6% -> 13% of each run, Pallas kernels for 8% -> 6%
where the time goes in v7:
time: 196 us; the launch traced here: 195 us
  waiting for transfers between devices  88.1 us (45%)
  starting transfers between devices  45.1 us (23%)
  local copies, waits for them, and re-layouts  26.8 us (14%)
  Pallas kernels  19.2 us (10%)
  other arithmetic  15.3 us (8%)
    ppermute x18, starting transfers between devices, shift(): return lax.ppermute(t, axis, [(i, (i + s) % n) for i in range(n)])  28.3 us
    ppermute x18, waiting for transfers between devices, shift(): return lax.ppermute(t, axis, [(i, (i + s) % n) for i in range(n)])  28.2 us
    all_to_all x2, waiting for transfers between devices, others(): held = lax.all_to_all(pairs[:, kp], 'x', 0, 0, tiled=True)  26.9 us
    all_to_all x1, waiting for transfers between devices, on_device(): part = lax.all_to_all(held + shift(away, 'c', 1), 'y', 0, 0, tiled=True)  24.4 us
    pallas_call x2, Pallas kernels, contract(): pl.pallas_call(make_contract_kernel(kp), in_specs=[pl.BlockSpec(memory_sp...  16.7 us
    all_to_all x2, starting transfers between devices, others(): held = lax.all_to_all(pairs[:, kp], 'x', 0, 0, tiled=True)  8.62 us
    all_to_all x1, waiting for transfers between devices, on_device(): part = lax.all_to_all(part, 'y', 0, 0, tiled=True)  8.6 us
    unnamed x24, local copies, waits for them, and re-layouts  7.95 us
  transfers between devices with their start and end apart: 22, of which 10 were waited for; matrix products, arithmetic and copies ran while one was open for 13% of the time, Pallas kernels for 6%

profile of v7, /device:TPU:1, one launch (start us, length us, event | category | flops | bytes accessed | tf_op | source)
XLA Modules:
  0.0 194.7 jit_solution(3569315198240299945)
XLA Ops:
  0.0 1.8 constant_dynamic-slice_fusion
  1.8 1.5 collective-permute-start.1
  3.3 0.1 convert_reduce_fusion
  3.4 2.3 %constant_dynamic-slice_fusion.2 = (f32[2,1,256,256]{3,2,1,0:T(8,128)}, f32[2,1,256,256]{3,2,1,0:T(8,128)}) fusion(f32[2,2,256,256]{3,2,1,0:T(8,128)} %param.4, s32[]{:T(128)S(6)} %select_n.117, s32[]{:T(128)S(6)} %select_n.127), kind=kLoop, calls=%fused_computation.40 | loop fusion | bytes 2097160 | tf_op jit(solution)/shard_map/jit(dynamic_index_in_dim)/dynamic_slice | solution.py:151
  5.7 1.0 copy-done.10
  6.7 1.8 maximum_select_fusion
  8.5 1.5 slice_bitcast_fusion
  10.0 4.4 %all-to-all-start = ((f32[4,256,256]{2,1,0:T(8,128)}), f32[4,256,256]{2,1,0:T(8,128)}, u32[]{:S(2)}, u32[]{:S(2)}) async-start(f32[4,256,256]{2,1,0:T(8,128)} %get-tuple-element.32), calls=%async_computation | async-start | bytes 2097152 | tf_op jit(solution)/shard_map/all_to_all | solution.py:145
  14.4 2.0 %fusion.2 = (f32[1,520,256]{2,1,0:T(8,128)S(1)}, f32[520,256]{1,0:T(8,128)}) fusion(f32[8,256]{1,0:T(8,128)S(1)} %broadcast_in_dim.2, f32[512,256]{1,0:T(8,128)S(1)} %bitcast.46, f32[512,256]{1,0:T(8,128)} %bitcast.47), kind=kLoop, calls=%fused_computation.16 | loop fusion | flops 266240 | bytes 2121728 | tf_op jit(solution)/shard_map/stack | solution.py:155
  16.4 0.4 collective-permute-start
  16.8 1.7 collective-permute-start.6
  18.5 2.2 %collective-permute-start.8 = (f32[2,256,256]{2,1,0:T(8,128)S(1)}, f32[2,256,256]{2,1,0:T(8,128)}, u32[]{:S(2)}, u32[]{:S(2)}) collective-permute-start(f32[2,256,256]{2,1,0:T(8,128)S(1)} %dynamic-slice_bitcast_fusion.1.own), channel_id=1, source_target_pairs={{0,96},{32,0},{64,32},{96,64},{1,97},{33,1},{65,33},{97,65},{2,98}... | collective-permute-start | bytes 1572872 | tf_op jit(solution)/shard_map/ppermute | solution.py:15
  20.7 1.3 maximum_select_fusion.1.a_ref
  22.0 7.3 %all-to-all-done = f32[4,256,256]{2,1,0:T(8,128)} async-done(((f32[4,256,256]{2,1,0:T(8,128)}), f32[4,256,256]{2,1,0:T(8,128)}, u32[]{:S(2)}, u32[]{:S(2)}) %all-to-all-start) | async-done | bytes 1048608 | tf_op jit(solution)/shard_map/all_to_all | solution.py:145
  29.3 1.2 fusion.1.rest
  30.5 0.9 collective-permute-start.2
  31.5 1.4 collective-permute-done.6.own_r
  32.9 1.0 slice.110
  33.8 1.0 slice.111
  34.8 1.5 pad_maximum_fusion
  36.3 0.4 collective-permute-start.7
  36.7 2.3 %collective-permute-start.9 = (f32[4,256,256]{2,1,0:T(8,128)}, f32[4,256,256]{2,1,0:T(8,128)}, u32[]{:S(2)}, u32[]{:S(2)}) collective-permute-start(f32[4,256,256]{2,1,0:T(8,128)} %get-tuple-element.37), channel_id=1, source_target_pairs={{0,96},{32,0},{64,32},{96,64},{1,97},{33,1},{65,33},{97,65},{2,98}... | collective-permute-start | bytes 3145736 | tf_op jit(solution)/shard_map/ppermute | solution.py:15
  39.0 1.9 collective-permute-start.4
  40.9 4.2 %all-to-all-start.1 = ((f32[4,256,256]{2,1,0:T(8,128)}), f32[4,256,256]{2,1,0:T(8,128)}, u32[]{:S(2)}, u32[]{:S(2)}) async-start(f32[4,256,256]{2,1,0:T(8,128)} %get-tuple-element.31), calls=%async_computation.1 | async-start | bytes 2097152 | tf_op jit(solution)/shard_map/all_to_all | solution.py:145
  45.1 9.3 %collective-permute-done.2.r_ref = f32[2,520,256]{2,1,0:T(8,128)S(1)} collective-permute-done((f32[2,520,256]{2,1,0:T(8,128)S(1)}, f32[2,520,256]{2,1,0:T(8,128)S(1)}, u32[]{:S(2)}, u32[]{:S(2)}) %collective-permute-start.2) | collective-permute-done | bytes 1064992 | tf_op jit(solution)/shard_map/ppermute | solution.py:15
  54.4 0.8 slice.105
  55.3 2.1 %collective-permute-start.3 = (f32[1,520,256]{2,1,0:T(8,128)}, f32[1,520,256]{2,1,0:T(8,128)S(1)}, u32[]{:S(2)}, u32[]{:S(2)}) collective-permute-start(f32[1,520,256]{2,1,0:T(8,128)} %slice.105), channel_id=1, source_target_pairs={{0,3},{1,0},{2,1},{3,2},{4,7},{5,4},{6,5},{7,6},{8,11},{9,8},{10,9... | collective-permute-start | bytes 1597448 | tf_op jit(solution)/shard_map/ppermute | solution.py:15
  57.4 19.7 %all-to-all-done.1 = f32[4,256,256]{2,1,0:T(8,128)} async-done(((f32[4,256,256]{2,1,0:T(8,128)}), f32[4,256,256]{2,1,0:T(8,128)}, u32[]{:S(2)}, u32[]{:S(2)}) %all-to-all-start.1) | async-done | bytes 1048608 | tf_op jit(solution)/shard_map/all_to_all | solution.py:145
  77.0 2.1 %fusion.rest = f32[3,256,256]{2,1,0:T(8,128)} fusion(s32[]{:T(128)S(6)} %select_n.132, f32[4,256,256]{2,1,0:T(8,128)} %all-to-all-done.1), kind=kLoop, calls=%fused_computation.12 | loop fusion | flops 196608 | bytes 1835012 | tf_op jit(solution)/shard_map/concatenate | solution.py:146
  79.2 2.7 %collective-permute-start.11 = (f32[3,256,256]{2,1,0:T(8,128)}, f32[3,256,256]{2,1,0:T(8,128)}, u32[]{:S(2)}, u32[]{:S(2)}) collective-permute-start(f32[3,256,256]{2,1,0:T(8,128)} %fusion.rest), channel_id=1, source_target_pairs={{0,96},{32,0},{64,32},{96,64},{1,97},{33,1},{65,33},{97,65},{2,98}... | collective-permute-start | bytes 2359304 | tf_op jit(solution)/shard_map/ppermute | solution.py:15
  81.8 1.9 slice.107
  83.8 1.8 slice.91
  85.6 1.8 slice.92
  87.4 2.7 %collective-permute-start.13 = (f32[3,128,256]{2,1,0:T(8,128)}, f32[3,128,256]{2,1,0:T(8,128)}, u32[]{:S(2)}, u32[]{:S(2)}) collective-permute-start(f32[3,128,256]{2,1,0:T(8,128)} %slice.92), channel_id=1, source_target_pairs={{0,96},{32,0},{64,32},{96,64},{1,97},{33,1},{65,33},{97,65},{2,98}... | collective-permute-start | bytes 1179656 | tf_op jit(solution)/shard_map/ppermute | solution.py:15
  90.1 0.7 slice_reduce_fusion
  91.1 5.1 %collective-permute-done.5.fb_ref = f32[1,520,256]{2,1,0:T(8,128)} collective-permute-done((f32[1,520,256]{2,1,0:T(8,128)}, f32[1,520,256]{2,1,0:T(8,128)}, u32[]{:S(2)}, u32[]{:S(2)}) %collective-permute-start.5) | collective-permute-done | bytes 532512 | tf_op jit(solution)/shard_map/ppermute | solution.py:15
  96.2 0.7 slice_reduce_fusion.3
  97.0 0.1 convert_element_type.11
  97.1 2.5 %split_amp.1.a_ref = bf16[4,4,256,768]{3,2,1,0:T(8,128)(2,1)S(1)} custom-call(f32[2,520,256]{2,1,0:T(8,128)S(1)} %maximum_select_fusion.1.a_ref, f32[2,520,256]{2,1,0:T(8,128)S(1)} %collective-permute-done.2.r_ref, f32[2,520,256]{2,1,0:T(8,128)} %collective-permute-done.4.l_ref, f32[1,520,256]{2,1,0:T(8,128)S(1)} %collective-permute-done.3.fa_ref, ...), custom_call_target="tpu_custom_call" | custom-call | bytes 10485760 | tf_op jit(solution)/shard_map/split_amp/pallas_call | solution.py:50
  99.7 6.4 %collective-permute-done.12.fa = f32[3,128,256]{2,1,0:T(8,128)} collective-permute-done((f32[3,128,256]{2,1,0:T(8,128)}, f32[3,128,256]{2,1,0:T(8,128)}, u32[]{:S(2)}, u32[]{:S(2)}) %collective-permute-start.12) | collective-permute-done | bytes 393248 | tf_op jit(solution)/shard_map/ppermute | solution.py:15
  106.1 6.9 %contract.2 = (f32[4,2,256,256]{3,2,1,0:T(8,128)S(1)}, f32[4,2,256,256]{3,2,1,0:T(8,128)S(1)}) custom-call(s32[130]{0:T(256)S(1)} %pad_add_fusion.flag_ref, bf16[4,4,256,768]{3,2,1,0:T(8,128)(2,1)S(1)} %split_amp.1.a_ref, f32[2,256,256]{2,1,0:T(8,128)S(1)} %copy-done.3, f32[2,256,256]{2,1,0:T(8,128)} %collective-permute-done.6.own_r, ...), custom_call_target="tpu_custom_call" | custom-call | flops 40000000000 | bytes 8388608 | tf_op jit(solution)/shard_map/contract/pallas_call | solution.py:113
  113.0 5.3 %collective-permute-start.14 = (f32[4,2,256,256]{3,2,1,0:T(8,128)S(1)}, f32[4,2,256,256]{3,2,1,0:T(8,128)S(1)}, u32[]{:S(2)}, u32[]{:S(2)}) collective-permute-start(f32[4,2,256,256]{3,2,1,0:T(8,128)S(1)} %get-tuple-element.25), channel_id=1, source_target_pairs={{0,16},{16,0},{1,17},{17,1},{2,18},{18,2},{3,19},{19,3},{4,20},{20... | collective-permute-start | bytes 6291464 | tf_op jit(solution)/shard_map/ppermute | solution.py:15
  118.4 1.0 slice.97
  119.5 1.0 slice.98
  120.5 2.7 %collective-permute-start.16 = (f32[3,128,256]{2,1,0:T(8,128)S(1)}, f32[3,128,256]{2,1,0:T(8,128)S(1)}, u32[]{:S(2)}, u32[]{:S(2)}) collective-permute-start(f32[3,128,256]{2,1,0:T(8,128)S(1)} %slice.98), channel_id=1, source_target_pairs={{0,96},{32,0},{64,32},{96,64},{1,97},{33,1},{65,33},{97,65},{2,98}... | collective-permute-start | bytes 1179656 | tf_op jit(solution)/shard_map/ppermute | solution.py:15
  123.2 1.7 add.221
  124.9 4.6 %all-to-all-start.2 = ((f32[4,2,256,256]{3,2,1,0:T(8,128)}), f32[4,2,256,256]{3,2,1,0:T(8,128)}, u32[]{:S(2)}, u32[]{:S(2)}) async-start(f32[4,2,256,256]{3,2,1,0:T(8,128)} %add.221), calls=%async_computation.2 | async-start | bytes 4194304 | tf_op jit(solution)/shard_map/all_to_all | solution.py:176
  129.5 1.9 collective-permute-done.15.fa
  131.4 0.8 copy-done.6
  132.2 2.8 %copy-done.1 = bf16[4,4,256,768]{3,2,1,0:T(8,128)(2,1)S(1)} copy-done((bf16[4,4,256,768]{3,2,1,0:T(8,128)(2,1)S(1)}, bf16[4,4,256,768]{3,2,1,0:T(8,128)(2,1)}, u32[]{:S(2)}) %copy-start.1) | copy-done | bytes 6291480
  135.0 1.0 copy-done.7
  136.0 9.8 %contract.3 = (f32[4,2,256,256]{3,2,1,0:T(8,128)S(1)}, f32[4,2,256,256]{3,2,1,0:T(8,128)S(1)}) custom-call(s32[130]{0:T(256)S(1)} %pad_add_fusion.flag_ref, bf16[4,4,256,768]{3,2,1,0:T(8,128)(2,1)S(1)} %copy-done.1, f32[2,256,256]{2,1,0:T(8,128)S(1)} %copy-done.4, f32[2,256,256]{2,1,0:T(8,128)} %collective-permute-done.6.own_r, ...), custom_call_target="tpu_custom_call" | custom-call | flops 40000000000 | bytes 8388608 | tf_op jit(solution)/shard_map/contract/pallas_call | solution.py:113
  145.8 1.3 copy-done.5
  147.1 8.6 %all-to-all-done.2 = f32[4,2,256,256]{3,2,1,0:T(8,128)} async-done(((f32[4,2,256,256]{3,2,1,0:T(8,128)}), f32[4,2,256,256]{3,2,1,0:T(8,128)}, u32[]{:S(2)}, u32[]{:S(2)}) %all-to-all-start.2) | async-done | bytes 2097184 | tf_op jit(solution)/shard_map/all_to_all | solution.py:176
  155.7 1.3 collective-permute-start.17
  157.1 4.0 %collective-permute-done.17 = f32[4,2,256,256]{3,2,1,0:T(8,128)S(1)} collective-permute-done((f32[4,2,256,256]{3,2,1,0:T(8,128)}, f32[4,2,256,256]{3,2,1,0:T(8,128)S(1)}, u32[]{:S(2)}, u32[]{:S(2)}) %collective-permute-start.17) | collective-permute-done | bytes 2097184 | tf_op jit(solution)/shard_map/ppermute | solution.py:15
  161.0 1.6 add.226
  162.7 3.6 %all-to-all-start.3 = ((f32[4,2,256,256]{3,2,1,0:T(8,128)}), f32[4,2,256,256]{3,2,1,0:T(8,128)S(1)}, u32[]{:S(2)}, u32[]{:S(2)}) async-start(f32[4,2,256,256]{3,2,1,0:T(8,128)} %add.226), calls=%async_computation.3 | async-start | bytes 4194304 | tf_op jit(solution)/shard_map/all_to_all | solution.py:181
  166.3 1.7 fusion.4
  167.9 24.4 %all-to-all-done.3 = f32[4,2,256,256]{3,2,1,0:T(8,128)S(1)} async-done(((f32[4,2,256,256]{3,2,1,0:T(8,128)}), f32[4,2,256,256]{3,2,1,0:T(8,128)S(1)}, u32[]{:S(2)}, u32[]{:S(2)}) %all-to-all-start.3) | async-done | bytes 2097184 | tf_op jit(solution)/shard_map/all_to_all | solution.py:181
  192.3 0.1 fusion.3
  192.5 1.1 copy-done.9
  193.6 0.1 maximum_add_fusion
  193.7 1.0 copy.14
  (47 shorter events, 0.8 us)
Async XLA Ops:
  0.0 3.3 %copy-start.11 = (s32[1,1,3,32]{3,1,2,0:T(1,128)S(1)}, s32[1,1,3,32]{3,1,2,0:T(1,128)}, u32[]{:S(2)}) copy-start(s32[1,1,3,32]{3,1,2,0:T(1,128)} %param.7) | copy-start | bytes 1156
  1.8 3.9 %collective-permute-start.1 = (f32[4,256,256]{2,1,0:T(8,128)S(1)}, f32[4,256,256]{2,1,0:T(8,128)S(1)}, u32[]{:S(2)}, u32[]{:S(2)}) collective-permute-start(f32[4,256,256]{2,1,0:T(8,128)S(1)} %get-tuple-element.34), channel_id=1, source_target_pairs={{0,16},{16,0},{1,17},{17,1},{2,18},{18,2},{3,19},{19,3},{4,20},{20... | collective-permute-start | bytes 3145736 | tf_op jit(solution)/shard_map/ppermute | solution.py:15
  5.7 1.0 copy-start.10
  10.0 4.4 %copy-start.8 = (f32[2,1,256,256]{3,2,1,0:T(8,128)S(1)}, f32[2,1,256,256]{3,2,1,0:T(8,128)}, u32[]{:S(2)}) copy-start(f32[2,1,256,256]{3,2,1,0:T(8,128)} %get-tuple-element.35) | copy-start | bytes 1572868
  10.0 19.3 %all-to-all-start = ((f32[4,256,256]{2,1,0:T(8,128)}), f32[4,256,256]{2,1,0:T(8,128)}, u32[]{:S(2)}, u32[]{:S(2)}) async-start(f32[4,256,256]{2,1,0:T(8,128)} %get-tuple-element.32), calls=%async_computation | async-start | bytes 2097152 | tf_op jit(solution)/shard_map/all_to_all | solution.py:145
  16.4 4.3 %collective-permute-start = (f32[520,256]{1,0:T(8,128)}, f32[520,256]{1,0:T(8,128)}, u32[]{:S(2)}, u32[]{:S(2)}) collective-permute-start(f32[520,256]{1,0:T(8,128)} %get-tuple-element.40), channel_id=1, source_target_pairs={{0,16},{16,0},{1,17},{17,1},{2,18},{18,2},{3,19},{19,3},{4,20},{20... | collective-permute-start | bytes 1597448 | tf_op jit(solution)/shard_map/ppermute | solution.py:15
  16.8 17.1 %copy-start.2 = (f32[2,256,256]{2,1,0:T(8,128)}, f32[2,256,256]{2,1,0:T(8,128)S(1)}, u32[]{:S(2)}) copy-start(f32[2,256,256]{2,1,0:T(8,128)S(1)} %dynamic-slice_bitcast_fusion.1.own) | copy-start | bytes 1572868
  16.8 16.1 %collective-permute-start.6 = (f32[2,256,256]{2,1,0:T(8,128)S(1)}, f32[2,256,256]{2,1,0:T(8,128)}, u32[]{:S(2)}, u32[]{:S(2)}) collective-permute-start(f32[2,256,256]{2,1,0:T(8,128)S(1)} %dynamic-slice_bitcast_fusion.1.own), channel_id=1, source_target_pairs={{0,32},{32,64},{64,96},{96,0},{1,33},{33,65},{65,97},{97,1},{2,34}... | collective-permute-start | bytes 1572872 | tf_op jit(solution)/shard_map/ppermute | solution.py:15
  18.5 15.4 %collective-permute-start.8 = (f32[2,256,256]{2,1,0:T(8,128)S(1)}, f32[2,256,256]{2,1,0:T(8,128)}, u32[]{:S(2)}, u32[]{:S(2)}) collective-permute-start(f32[2,256,256]{2,1,0:T(8,128)S(1)} %dynamic-slice_bitcast_fusion.1.own), channel_id=1, source_target_pairs={{0,96},{32,0},{64,32},{96,64},{1,97},{33,1},{65,33},{97,65},{2,98}... | collective-permute-start | bytes 1572872 | tf_op jit(solution)/shard_map/ppermute | solution.py:15
  30.5 23.9 %collective-permute-start.2 = (f32[2,520,256]{2,1,0:T(8,128)S(1)}, f32[2,520,256]{2,1,0:T(8,128)S(1)}, u32[]{:S(2)}, u32[]{:S(2)}) collective-permute-start(f32[2,520,256]{2,1,0:T(8,128)S(1)} %maximum_select_fusion.1.a_ref), channel_id=1, source_target_pairs={{0,3},{1,0},{2,1},{3,2},{4,7},{5,4},{6,5},{7,6},{8,11},{9,8},{10,9... | collective-permute-start | bytes 3194888 | tf_op jit(solution)/shard_map/ppermute | solution.py:15
  36.3 42.8 %collective-permute-start.7 = (f32[4,256,256]{2,1,0:T(8,128)}, f32[4,256,256]{2,1,0:T(8,128)}, u32[]{:S(2)}, u32[]{:S(2)}) collective-permute-start(f32[4,256,256]{2,1,0:T(8,128)} %get-tuple-element.38), channel_id=1, source_target_pairs={{0,32},{32,64},{64,96},{96,0},{1,33},{33,65},{65,97},{97,1},{2,34}... | collective-permute-start | bytes 3145736 | tf_op jit(solution)/shard_map/ppermute | solution.py:15
  36.7 42.4 %collective-permute-start.9 = (f32[4,256,256]{2,1,0:T(8,128)}, f32[4,256,256]{2,1,0:T(8,128)}, u32[]{:S(2)}, u32[]{:S(2)}) collective-permute-start(f32[4,256,256]{2,1,0:T(8,128)} %get-tuple-element.37), channel_id=1, source_target_pairs={{0,96},{32,0},{64,32},{96,64},{1,97},{33,1},{65,33},{97,65},{2,98}... | collective-permute-start | bytes 3145736 | tf_op jit(solution)/shard_map/ppermute | solution.py:15
  39.0 42.8 %collective-permute-start.4 = (f32[2,520,256]{2,1,0:T(8,128)S(1)}, f32[2,520,256]{2,1,0:T(8,128)}, u32[]{:S(2)}, u32[]{:S(2)}) collective-permute-start(f32[2,520,256]{2,1,0:T(8,128)S(1)} %maximum_select_fusion.1.a_ref), channel_id=1, source_target_pairs={{0,1},{1,2},{2,3},{3,0},{4,5},{5,6},{6,7},{7,4},{8,9},{9,10},{10,1... | collective-permute-start | bytes 3194888 | tf_op jit(solution)/shard_map/ppermute | solution.py:15
  40.9 36.1 %all-to-all-start.1 = ((f32[4,256,256]{2,1,0:T(8,128)}), f32[4,256,256]{2,1,0:T(8,128)}, u32[]{:S(2)}, u32[]{:S(2)}) async-start(f32[4,256,256]{2,1,0:T(8,128)} %get-tuple-element.31), calls=%async_computation.1 | async-start | bytes 2097152 | tf_op jit(solution)/shard_map/all_to_all | solution.py:145
  55.3 32.1 %collective-permute-start.3 = (f32[1,520,256]{2,1,0:T(8,128)}, f32[1,520,256]{2,1,0:T(8,128)S(1)}, u32[]{:S(2)}, u32[]{:S(2)}) collective-permute-start(f32[1,520,256]{2,1,0:T(8,128)} %slice.105), channel_id=1, source_target_pairs={{0,3},{1,0},{2,1},{3,2},{4,7},{5,4},{6,5},{7,6},{8,11},{9,8},{10,9... | collective-permute-start | bytes 1597448 | tf_op jit(solution)/shard_map/ppermute | solution.py:15
  79.2 20.5 %collective-permute-start.10 = (f32[3,256,256]{2,1,0:T(8,128)}, f32[3,256,256]{2,1,0:T(8,128)}, u32[]{:S(2)}, u32[]{:S(2)}) collective-permute-start(f32[3,256,256]{2,1,0:T(8,128)} %fusion.rest), channel_id=1, source_target_pairs={{0,32},{32,64},{64,96},{96,0},{1,33},{33,65},{65,97},{97,1},{2,34}... | collective-permute-start | bytes 2359304 | tf_op jit(solution)/shard_map/ppermute | solution.py:15
  79.2 20.5 %collective-permute-start.11 = (f32[3,256,256]{2,1,0:T(8,128)}, f32[3,256,256]{2,1,0:T(8,128)}, u32[]{:S(2)}, u32[]{:S(2)}) collective-permute-start(f32[3,256,256]{2,1,0:T(8,128)} %fusion.rest), channel_id=1, source_target_pairs={{0,96},{32,0},{64,32},{96,64},{1,97},{33,1},{65,33},{97,65},{2,98}... | collective-permute-start | bytes 2359304 | tf_op jit(solution)/shard_map/ppermute | solution.py:15
  83.7 12.5 %collective-permute-start.5 = (f32[1,520,256]{2,1,0:T(8,128)}, f32[1,520,256]{2,1,0:T(8,128)}, u32[]{:S(2)}, u32[]{:S(2)}) collective-permute-start(f32[1,520,256]{2,1,0:T(8,128)} %slice.107), channel_id=1, source_target_pairs={{0,1},{1,2},{2,3},{3,0},{4,5},{5,6},{6,7},{7,4},{8,9},{9,10},{10,1... | collective-permute-start | bytes 1597448 | tf_op jit(solution)/shard_map/ppermute | solution.py:15
  85.6 20.5 %collective-permute-start.12 = (f32[3,128,256]{2,1,0:T(8,128)}, f32[3,128,256]{2,1,0:T(8,128)}, u32[]{:S(2)}, u32[]{:S(2)}) collective-permute-start(f32[3,128,256]{2,1,0:T(8,128)} %slice.91), channel_id=1, source_target_pairs={{0,32},{32,64},{64,96},{96,0},{1,33},{33,65},{65,97},{97,1},{2,34}... | collective-permute-start | bytes 1179656 | tf_op jit(solution)/shard_map/ppermute | solution.py:15
  87.4 18.7 %collective-permute-start.13 = (f32[3,128,256]{2,1,0:T(8,128)}, f32[3,128,256]{2,1,0:T(8,128)}, u32[]{:S(2)}, u32[]{:S(2)}) collective-permute-start(f32[3,128,256]{2,1,0:T(8,128)} %slice.92), channel_id=1, source_target_pairs={{0,96},{32,0},{64,32},{96,64},{1,97},{33,1},{65,33},{97,65},{2,98}... | collective-permute-start | bytes 1179656 | tf_op jit(solution)/shard_map/ppermute | solution.py:15
  97.1 9.0 %copy-start.3 = (f32[2,256,256]{2,1,0:T(8,128)S(1)}, f32[2,256,256]{2,1,0:T(8,128)}, u32[]{:S(2)}) copy-start(f32[2,256,256]{2,1,0:T(8,128)} %copy-done.2) | copy-start | bytes 1572868
  99.6 13.4 %copy-start = (bf16[4,4,256,768]{3,2,1,0:T(8,128)(2,1)}, bf16[4,4,256,768]{3,2,1,0:T(8,128)(2,1)S(1)}, u32[]{:S(2)}) copy-start(bf16[4,4,256,768]{3,2,1,0:T(8,128)(2,1)S(1)} %split_amp.1.a_ref) | copy-start | bytes 18874372
  113.0 10.2 %collective-permute-start.14 = (f32[4,2,256,256]{3,2,1,0:T(8,128)S(1)}, f32[4,2,256,256]{3,2,1,0:T(8,128)S(1)}, u32[]{:S(2)}, u32[]{:S(2)}) collective-permute-start(f32[4,2,256,256]{3,2,1,0:T(8,128)S(1)} %get-tuple-element.25), channel_id=1, source_target_pairs={{0,16},{16,0},{1,17},{17,1},{2,18},{18,2},{3,19},{19,3},{4,20},{20... | collective-permute-start | bytes 6291464 | tf_op jit(solution)/shard_map/ppermute | solution.py:15
  119.4 12.0 %collective-permute-start.15 = (f32[3,128,256]{2,1,0:T(8,128)S(1)}, f32[3,128,256]{2,1,0:T(8,128)S(1)}, u32[]{:S(2)}, u32[]{:S(2)}) collective-permute-start(f32[3,128,256]{2,1,0:T(8,128)S(1)} %slice.97), channel_id=1, source_target_pairs={{0,32},{32,64},{64,96},{96,0},{1,33},{33,65},{65,97},{97,1},{2,34}... | collective-permute-start | bytes 1179656 | tf_op jit(solution)/shard_map/ppermute | solution.py:15
  120.5 10.9 %collective-permute-start.16 = (f32[3,128,256]{2,1,0:T(8,128)S(1)}, f32[3,128,256]{2,1,0:T(8,128)S(1)}, u32[]{:S(2)}, u32[]{:S(2)}) collective-permute-start(f32[3,128,256]{2,1,0:T(8,128)S(1)} %slice.98), channel_id=1, source_target_pairs={{0,96},{32,0},{64,32},{96,64},{1,97},{33,1},{65,33},{97,65},{2,98}... | collective-permute-start | bytes 1179656 | tf_op jit(solution)/shard_map/ppermute | solution.py:15
  124.9 7.3 %copy-start.4 = (f32[2,256,256]{2,1,0:T(8,128)S(1)}, f32[2,256,256]{2,1,0:T(8,128)}, u32[]{:S(2)}) copy-start(f32[2,256,256]{2,1,0:T(8,128)} %copy-done.2) | copy-start | bytes 1572868
  124.9 30.8 %all-to-all-start.2 = ((f32[4,2,256,256]{3,2,1,0:T(8,128)}), f32[4,2,256,256]{3,2,1,0:T(8,128)}, u32[]{:S(2)}, u32[]{:S(2)}) async-start(f32[4,2,256,256]{3,2,1,0:T(8,128)} %add.221), calls=%async_computation.2 | async-start | bytes 4194304 | tf_op jit(solution)/shard_map/all_to_all | solution.py:176
  131.4 0.8 copy-start.6
  132.2 2.8 %copy-start.1 = (bf16[4,4,256,768]{3,2,1,0:T(8,128)(2,1)S(1)}, bf16[4,4,256,768]{3,2,1,0:T(8,128)(2,1)}, u32[]{:S(2)}) copy-start(bf16[4,4,256,768]{3,2,1,0:T(8,128)(2,1)} %copy-done) | copy-start | bytes 18874372
  135.0 1.0 copy-start.7
  145.8 1.3 copy-start.5
  155.7 5.3 %collective-permute-start.17 = (f32[4,2,256,256]{3,2,1,0:T(8,128)}, f32[4,2,256,256]{3,2,1,0:T(8,128)S(1)}, u32[]{:S(2)}, u32[]{:S(2)}) collective-permute-start(f32[4,2,256,256]{3,2,1,0:T(8,128)} %copy-done.5), channel_id=1, source_target_pairs={{0,16},{16,0},{1,17},{17,1},{2,18},{18,2},{3,19},{19,3},{4,20},{20... | collective-permute-start | bytes 6291464 | tf_op jit(solution)/shard_map/ppermute | solution.py:15
  162.7 29.7 %all-to-all-start.3 = ((f32[4,2,256,256]{3,2,1,0:T(8,128)}), f32[4,2,256,256]{3,2,1,0:T(8,128)S(1)}, u32[]{:S(2)}, u32[]{:S(2)}) async-start(f32[4,2,256,256]{3,2,1,0:T(8,128)} %add.226), calls=%async_computation.3 | async-start | bytes 4194304 | tf_op jit(solution)/shard_map/all_to_all | solution.py:181
  192.3 1.2 copy-start.9

commit v8 on v7

--- a/solution.py
+++ b/solution.py
@@ -139,13 +139,17 @@
     other = shift(lax.dynamic_index_in_dim(integ, 1 - c, 0, keepdims=False), "c", 1)
     pairs = jnp.where(c == 0, jnp.stack([mine, other]), jnp.stack([other, mine])).reshape(4, 2, w, w)
     own = lax.dynamic_index_in_dim(pairs, x, 0, keepdims=False)
+    own, pairs = lax.optimization_barrier((own, pairs))
     own_r, own_l = shift(own, "z", 1), shift(own, "z", -1)
 
-    def others(kp):
-        held = lax.all_to_all(pairs[:, kp], "x", 0, 0, tiled=True)
-        return lax.dynamic_slice_in_dim(jnp.concatenate([held, held]), x + 1, 3, 0)
-
-    rest = [others(0), others(1)]
+    came = [
+        shift(lax.dynamic_slice(pairs, (lax.rem(x + 4 - s, 4), 0, 0, 0), (1, 1, w, w)).reshape(w, w), "x", -s)
+        for s in (1, 2, 3)
+    ]
+    rest = [jnp.stack(came)]
+    pairs, rest[0], own_r, own_l = lax.optimization_barrier((pairs, rest[0], own_r, own_l))
+    held = lax.all_to_all(pairs[:, 1], "x", 0, 0, tiled=True)
+    rest.append(lax.dynamic_slice_in_dim(jnp.concatenate([held, held]), x + 1, 3, 0))
 
     def with_flags(parity):
         tile = lax.dynamic_index_in_dim(amp, parity, 1, keepdims=False)
@@ -153,7 +157,7 @@
 
     a_mine, a_other = with_flags(c), shift(with_flags(1 - c), "c", 1)
     a0 = jnp.where(c == 0, jnp.stack([a_mine, a_other]), jnp.stack([a_other, a_mine]))
-    a0, rest[0] = lax.optimization_barrier((a0, rest[0]))
+    a0, rest[1] = lax.optimization_barrier((a0, rest[1]))
     a_r, a_l = shift(a0, "x", -1), shift(a0, "x", 1)
     a_fa, a_fb = shift(a_r[:1], "x", -1), shift(a_l[1:], "x", 1)
     a3 = split_amp(a0, a_r, a_l, a_fa, a_fb)

time: 196 us -> 194 us (0.990)
  local copies, waits for them, and re-layouts: 26.8 us -> 34.7 us
  waiting for transfers between devices: 88.1 us -> 80.3 us
  other arithmetic: 15.3 us -> 11.5 us
    all_to_all x2 -> x1, waiting for transfers between devices: 26.9 us -> 8.42 us  [on_device(): held = lax.all_to_all(pairs[:, 1], 'x', 0, 0, tiled=True)]
    unnamed x24 -> x46, local copies, waits for them, and re-layouts: 7.95 us -> 21.3 us
    ppermute x18 -> x21, waiting for transfers between devices: 28.2 us -> 38.7 us  [shift(): return lax.ppermute(t, axis, [(i, (i + s) % n) for i in range(n)])]
    ppermute x18 -> x21, starting transfers between devices: 28.3 us -> 34.2 us  [shift(): return lax.ppermute(t, axis, [(i, (i + s) % n) for i in range(n)])]
    all_to_all x2 -> x1, starting transfers between devices: 8.62 us -> 4.24 us  [on_device(): held = lax.all_to_all(pairs[:, 1], 'x', 0, 0, tiled=True)]
    dynamic_slice x1, local copies, waits for them, and re-layouts: 2.27 us -> 0.09 us  [with_flags(): tile = lax.dynamic_index_in_dim(amp, parity, 1, keepdims=False)]
  transfers between devices with their start and end apart: 22 -> 24, of which waited for: 10 -> 11; matrix products, arithmetic and copies ran while one was open for 13% -> 10% of each run, Pallas kernels for 6% -> 5%
where the time goes in v8:
time: 194 us; the launch traced here: 191 us
  waiting for transfers between devices  80.3 us (41%)
  starting transfers between devices  46.6 us (24%)
  local copies, waits for them, and re-layouts  34.7 us (18%)
  Pallas kernels  17.7 us (9%)
  other arithmetic  11.5 us (6%)
    ppermute x21, waiting for transfers between devices, shift(): return lax.ppermute(t, axis, [(i, (i + s) % n) for i in range(n)])  38.7 us
    ppermute x21, starting transfers between devices, shift(): return lax.ppermute(t, axis, [(i, (i + s) % n) for i in range(n)])  34.2 us
    all_to_all x1, waiting for transfers between devices, on_device(): part = lax.all_to_all(held + shift(away, 'c', 1), 'y', 0, 0, tiled=True)  24.4 us
    unnamed x46, local copies, waits for them, and re-layouts  21.3 us
    pallas_call x2, Pallas kernels, contract(): pl.pallas_call(make_contract_kernel(kp), in_specs=[pl.BlockSpec(memory_sp...  15.5 us
    all_to_all x1, waiting for transfers between devices, on_device(): part = lax.all_to_all(part, 'y', 0, 0, tiled=True)  8.84 us
    all_to_all x1, waiting for transfers between devices, on_device(): held = lax.all_to_all(pairs[:, 1], 'x', 0, 0, tiled=True)  8.42 us
    all_to_all x1, starting transfers between devices, on_device(): part = lax.all_to_all(part, 'y', 0, 0, tiled=True)  4.59 us
  transfers between devices with their start and end apart: 24, of which 11 were waited for; matrix products, arithmetic and copies ran while one was open for 10% of the time, Pallas kernels for 5%

profile of v8, /device:TPU:1, one launch (start us, length us, event | category | flops | bytes accessed | tf_op | source)
XLA Modules:
  0.0 191.1 jit_solution(11784241652515882507)
XLA Ops:
  0.0 1.8 constant_dynamic-slice_fusion
  1.8 1.5 collective-permute-start.1
  3.4 2.2 %collective-permute-done.1 = f32[4,256,256]{2,1,0:T(8,128)S(1)} collective-permute-done((f32[4,256,256]{2,1,0:T(8,128)S(1)}, f32[4,256,256]{2,1,0:T(8,128)S(1)}, u32[]{:S(2)}, u32[]{:S(2)}) %collective-permute-start.1) | collective-permute-done | bytes 1048608 | tf_op jit(solution)/shard_map/ppermute | solution.py:15
  5.9 1.8 collective-permute-start.5
  7.7 2.2 %collective-permute-start.6 = (f32[2,256,256]{2,1,0:T(8,128)S(1)}, f32[2,256,256]{2,1,0:T(8,128)S(1)}, u32[]{:S(2)}, u32[]{:S(2)}) collective-permute-start(f32[2,256,256]{2,1,0:T(8,128)S(1)} %dynamic-slice_bitcast_fusion.1.own), channel_id=1, source_target_pairs={{0,96},{32,0},{64,32},{96,64},{1,97},{33,1},{65,33},{97,65},{2,98}... | collective-permute-start | bytes 1572872 | tf_op jit(solution)/shard_map/ppermute | solution.py:15
  9.9 2.5 %collective-permute-start.2 = (f32[256,256]{1,0:T(8,128)S(1)}, f32[256,256]{1,0:T(8,128)S(1)}, u32[]{:S(2)}, u32[]{:S(2)}) collective-permute-start(f32[256,256]{1,0:T(8,128)S(1)} %get-tuple-element.43), channel_id=1, source_target_pairs={{0,3},{1,0},{2,1},{3,2},{4,7},{5,4},{6,5},{7,6},{8,11},{9,8},{10,9... | collective-permute-start | bytes 786440 | tf_op jit(solution)/shard_map/ppermute | solution.py:15
  13.7 0.9 fusion.1
  14.6 3.7 %collective-permute-done.2 = f32[256,256]{1,0:T(8,128)S(1)} collective-permute-done((f32[256,256]{1,0:T(8,128)S(1)}, f32[256,256]{1,0:T(8,128)S(1)}, u32[]{:S(2)}, u32[]{:S(2)}) %collective-permute-start.2) | collective-permute-done | bytes 262176 | tf_op jit(solution)/shard_map/ppermute | solution.py:15
  18.3 6.4 %collective-permute-start = (f32[520,256]{1,0:T(8,128)}, f32[520,256]{1,0:T(8,128)S(1)}, u32[]{:S(2)}, u32[]{:S(2)}) collective-permute-start(f32[520,256]{1,0:T(8,128)} %get-tuple-element.53), channel_id=1, source_target_pairs={{0,16},{16,0},{1,17},{17,1},{2,18},{18,2},{3,19},{19,3},{4,20},{20... | collective-permute-start | bytes 1597448 | tf_op jit(solution)/shard_map/ppermute | solution.py:15
  24.7 3.2 %collective-permute-done.4 = f32[256,256]{1,0:T(8,128)S(1)} collective-permute-done((f32[256,256]{1,0:T(8,128)S(1)}, f32[256,256]{1,0:T(8,128)S(1)}, u32[]{:S(2)}, u32[]{:S(2)}) %collective-permute-start.4) | collective-permute-done | bytes 262176 | tf_op jit(solution)/shard_map/ppermute | solution.py:15
  27.9 1.1 slice_bitcast_fusion
  29.0 4.2 %all-to-all-start = ((f32[4,256,256]{2,1,0:T(8,128)}), f32[4,256,256]{2,1,0:T(8,128)}, u32[]{:S(2)}, u32[]{:S(2)}) async-start(f32[4,256,256]{2,1,0:T(8,128)} %slice_bitcast_fusion), calls=%async_computation | async-start | bytes 2097152 | tf_op jit(solution)/shard_map/all_to_all | solution.py:151
  33.3 0.8 copy-done.21
  34.1 1.3 maximum_select_fusion.1.a_ref
  35.5 1.5 pad_maximum_fusion
  37.0 2.7 %collective-permute-start.12 = (f32[4,256,256]{2,1,0:T(8,128)}, f32[4,256,256]{2,1,0:T(8,128)}, u32[]{:S(2)}, u32[]{:S(2)}) collective-permute-start(f32[4,256,256]{2,1,0:T(8,128)} %get-tuple-element.50), channel_id=1, source_target_pairs={{0,96},{32,0},{64,32},{96,64},{1,97},{33,1},{65,33},{97,65},{2,98}... | collective-permute-start | bytes 3145736 | tf_op jit(solution)/shard_map/ppermute | solution.py:15
  39.6 8.4 %all-to-all-done = f32[4,256,256]{2,1,0:T(8,128)} async-done(((f32[4,256,256]{2,1,0:T(8,128)}), f32[4,256,256]{2,1,0:T(8,128)}, u32[]{:S(2)}, u32[]{:S(2)}) %all-to-all-start) | async-done | bytes 1048608 | tf_op jit(solution)/shard_map/all_to_all | solution.py:151
  48.1 2.1 %fusion.rest = f32[3,256,256]{2,1,0:T(8,128)} fusion(s32[]{:T(128)S(6)} %select_n.144, f32[4,256,256]{2,1,0:T(8,128)} %all-to-all-done), kind=kLoop, calls=%fused_computation.9 | loop fusion | flops 196608 | bytes 1835012 | tf_op jit(solution)/shard_map/concatenate | solution.py:152
  50.4 2.4 %collective-permute-start.7 = (f32[2,520,256]{2,1,0:T(8,128)S(1)}, f32[2,520,256]{2,1,0:T(8,128)S(1)}, u32[]{:S(2)}, u32[]{:S(2)}) collective-permute-start(f32[2,520,256]{2,1,0:T(8,128)S(1)} %maximum_select_fusion.1.a_ref), channel_id=1, source_target_pairs={{0,3},{1,0},{2,1},{3,2},{4,7},{5,4},{6,5},{7,6},{8,11},{9,8},{10,9... | collective-permute-start | bytes 3194888 | tf_op jit(solution)/shard_map/ppermute | solution.py:15
  52.9 9.9 %collective-permute-done.11.two_r.own_fa = f32[4,256,256]{2,1,0:T(8,128)} collective-permute-done((f32[4,256,256]{2,1,0:T(8,128)}, f32[4,256,256]{2,1,0:T(8,128)}, u32[]{:S(2)}, u32[]{:S(2)}) %collective-permute-start.11) | collective-permute-done | bytes 1048608 | tf_op jit(solution)/shard_map/ppermute | solution.py:15
  62.7 2.7 %collective-permute-start.14 = (f32[3,256,256]{2,1,0:T(8,128)}, f32[3,256,256]{2,1,0:T(8,128)}, u32[]{:S(2)}, u32[]{:S(2)}) collective-permute-start(f32[3,256,256]{2,1,0:T(8,128)} %fusion.rest), channel_id=1, source_target_pairs={{0,96},{32,0},{64,32},{96,64},{1,97},{33,1},{65,33},{97,65},{2,98}... | collective-permute-start | bytes 2359304 | tf_op jit(solution)/shard_map/ppermute | solution.py:15
  65.4 9.8 %collective-permute-done.9.l_ref = f32[2,520,256]{2,1,0:T(8,128)S(1)} collective-permute-done((f32[2,520,256]{2,1,0:T(8,128)S(1)}, f32[2,520,256]{2,1,0:T(8,128)S(1)}, u32[]{:S(2)}, u32[]{:S(2)}) %collective-permute-start.9) | collective-permute-done | bytes 1064992 | tf_op jit(solution)/shard_map/ppermute | solution.py:15
  75.2 0.8 slice.103
  76.0 1.0 copy-done.3
  77.0 0.9 slice.101
  77.8 2.7 %collective-permute-start.8 = (f32[1,520,256]{2,1,0:T(8,128)}, f32[1,520,256]{2,1,0:T(8,128)}, u32[]{:S(2)}, u32[]{:S(2)}) collective-permute-start(f32[1,520,256]{2,1,0:T(8,128)} %slice.101), channel_id=1, source_target_pairs={{0,3},{1,0},{2,1},{3,2},{4,7},{5,4},{6,5},{7,6},{8,11},{9,8},{10,9... | collective-permute-start | bytes 1597448 | tf_op jit(solution)/shard_map/ppermute | solution.py:15
  80.6 1.8 slice.87
  82.4 1.8 slice.88
  84.2 0.7 slice_reduce_fusion.1
  84.9 3.9 %collective-permute-done.10.fb_ref = f32[1,520,256]{2,1,0:T(8,128)S(1)} collective-permute-done((f32[1,520,256]{2,1,0:T(8,128)}, f32[1,520,256]{2,1,0:T(8,128)S(1)}, u32[]{:S(2)}, u32[]{:S(2)}) %collective-permute-start.10) | collective-permute-done | bytes 532512 | tf_op jit(solution)/shard_map/ppermute | solution.py:15
  88.8 1.4 collective-permute-start.16
  90.4 1.2 copy-done.4
  91.6 2.2 %split_amp.1.a_ref = bf16[4,4,256,768]{3,2,1,0:T(8,128)(2,1)S(1)} custom-call(f32[2,520,256]{2,1,0:T(8,128)S(1)} %maximum_select_fusion.1.a_ref, f32[2,520,256]{2,1,0:T(8,128)S(1)} %copy-done.4, f32[2,520,256]{2,1,0:T(8,128)S(1)} %collective-permute-done.9.l_ref, f32[1,520,256]{2,1,0:T(8,128)} %collective-permute-done.8.fa_ref, ...), custom_call_target="tpu_custom_call" | custom-call | bytes 10485760 | tf_op jit(solution)/shard_map/split_amp/pallas_call | solution.py:50
  93.9 2.6 %copy-done = bf16[4,4,256,768]{3,2,1,0:T(8,128)(2,1)} copy-done((bf16[4,4,256,768]{3,2,1,0:T(8,128)(2,1)}, bf16[4,4,256,768]{3,2,1,0:T(8,128)(2,1)S(1)}, u32[]{:S(2)}) %copy-start) | copy-done | bytes 6291480
  97.6 2.8 %copy-done.1 = bf16[4,4,256,768]{3,2,1,0:T(8,128)(2,1)S(1)} copy-done((bf16[4,4,256,768]{3,2,1,0:T(8,128)(2,1)S(1)}, bf16[4,4,256,768]{3,2,1,0:T(8,128)(2,1)}, u32[]{:S(2)}) %copy-start.1) | copy-done | bytes 6291480
  100.4 1.0 copy-done.6
  101.4 1.0 copy-done.9
  102.5 1.0 copy-done.12
  103.5 8.9 %contract.2 = (f32[4,2,256,256]{3,2,1,0:T(8,128)S(1)}, f32[4,2,256,256]{3,2,1,0:T(8,128)S(1)}) custom-call(s32[130]{0:T(256)S(1)} %pad_add_fusion.flag_ref, bf16[4,4,256,768]{3,2,1,0:T(8,128)(2,1)S(1)} %copy-done.1, f32[2,256,256]{2,1,0:T(8,128)S(1)} %copy-done.6, f32[2,256,256]{2,1,0:T(8,128)S(1)} %copy-done.9, f32[2,256,256]{2,1,0:T(8,128)S(1)} %copy-done.12, ...), custom_call_target="tpu_custom_call" | custom-call | flops 40000000000 | bytes 8388608 | tf_op jit(solution)/shard_map/contract/pallas_call | solution.py:113
  112.4 2.1 %collective-permute-start.17 = (f32[4,2,256,256]{3,2,1,0:T(8,128)S(1)}, f32[4,2,256,256]{3,2,1,0:T(8,128)S(1)}, u32[]{:S(2)}, u32[]{:S(2)}) collective-permute-start(f32[4,2,256,256]{3,2,1,0:T(8,128)S(1)} %get-tuple-element.37), channel_id=1, source_target_pairs={{0,16},{16,0},{1,17},{17,1},{2,18},{18,2},{3,19},{19,3},{4,20},{20... | collective-permute-start | bytes 6291464 | tf_op jit(solution)/shard_map/ppermute | solution.py:15
  114.5 1.0 slice.93
  115.5 1.2 collective-permute-start.18
  116.8 1.0 slice.94
  117.8 2.1 %collective-permute-start.19 = (f32[3,128,256]{2,1,0:T(8,128)S(1)}, f32[3,128,256]{2,1,0:T(8,128)S(1)}, u32[]{:S(2)}, u32[]{:S(2)}) collective-permute-start(f32[3,128,256]{2,1,0:T(8,128)S(1)} %slice.94), channel_id=1, source_target_pairs={{0,96},{32,0},{64,32},{96,64},{1,97},{33,1},{65,33},{97,65},{2,98}... | collective-permute-start | bytes 1179656 | tf_op jit(solution)/shard_map/ppermute | solution.py:15
  119.8 1.7 add.240
  121.5 4.6 %all-to-all-start.1 = ((f32[4,2,256,256]{3,2,1,0:T(8,128)}), f32[4,2,256,256]{3,2,1,0:T(8,128)}, u32[]{:S(2)}, u32[]{:S(2)}) async-start(f32[4,2,256,256]{3,2,1,0:T(8,128)} %add.240), calls=%async_computation.1 | async-start | bytes 4194304 | tf_op jit(solution)/shard_map/all_to_all | solution.py:180
  126.1 2.1 %collective-permute-done.18.fa = f32[3,128,256]{2,1,0:T(8,128)S(1)} collective-permute-done((f32[3,128,256]{2,1,0:T(8,128)S(1)}, f32[3,128,256]{2,1,0:T(8,128)S(1)}, u32[]{:S(2)}, u32[]{:S(2)}) %collective-permute-start.18) | collective-permute-done | bytes 393248 | tf_op jit(solution)/shard_map/ppermute | solution.py:15
  128.2 0.8 copy-done.15
  129.0 0.7 copy-done.17
  129.7 2.8 %copy-done.2 = bf16[4,4,256,768]{3,2,1,0:T(8,128)(2,1)S(1)} copy-done((bf16[4,4,256,768]{3,2,1,0:T(8,128)(2,1)S(1)}, bf16[4,4,256,768]{3,2,1,0:T(8,128)(2,1)}, u32[]{:S(2)}) %copy-start.2) | copy-done | bytes 6291480
  132.5 1.0 copy-done.13
  133.5 1.0 copy-done.16
  134.5 1.0 copy-done.18
  135.5 6.6 %contract.3 = (f32[4,2,256,256]{3,2,1,0:T(8,128)S(1)}, f32[4,2,256,256]{3,2,1,0:T(8,128)S(1)}) custom-call(s32[130]{0:T(256)S(1)} %pad_add_fusion.flag_ref, bf16[4,4,256,768]{3,2,1,0:T(8,128)(2,1)S(1)} %copy-done.2, f32[2,256,256]{2,1,0:T(8,128)S(1)} %copy-done.7, f32[2,256,256]{2,1,0:T(8,128)S(1)} %copy-done.10, f32[2,256,256]{2,1,0:T(8,128)S(1)} %copy-done.13, ...), custom_call_target="tpu_custom_call" | custom-call | flops 40000000000 | bytes 8388608 | tf_op jit(solution)/shard_map/contract/pallas_call | solution.py:113
  142.2 1.3 copy-done.14
  143.5 8.8 %all-to-all-done.1 = f32[4,2,256,256]{3,2,1,0:T(8,128)} async-done(((f32[4,2,256,256]{3,2,1,0:T(8,128)}), f32[4,2,256,256]{3,2,1,0:T(8,128)}, u32[]{:S(2)}, u32[]{:S(2)}) %all-to-all-start.1) | async-done | bytes 2097184 | tf_op jit(solution)/shard_map/all_to_all | solution.py:180
  152.3 1.1 collective-permute-start.20
  153.4 4.0 %collective-permute-done.20 = f32[4,2,256,256]{3,2,1,0:T(8,128)S(1)} collective-permute-done((f32[4,2,256,256]{3,2,1,0:T(8,128)}, f32[4,2,256,256]{3,2,1,0:T(8,128)S(1)}, u32[]{:S(2)}, u32[]{:S(2)}) %collective-permute-start.20) | collective-permute-done | bytes 2097184 | tf_op jit(solution)/shard_map/ppermute | solution.py:15
  157.4 1.6 add.245
  159.1 3.6 %all-to-all-start.2 = ((f32[4,2,256,256]{3,2,1,0:T(8,128)}), f32[4,2,256,256]{3,2,1,0:T(8,128)S(1)}, u32[]{:S(2)}, u32[]{:S(2)}) async-start(f32[4,2,256,256]{3,2,1,0:T(8,128)} %add.245), calls=%async_computation.2 | async-start | bytes 4194304 | tf_op jit(solution)/shard_map/all_to_all | solution.py:185
  162.7 1.7 fusion.3
  164.3 24.4 %all-to-all-done.2 = f32[4,2,256,256]{3,2,1,0:T(8,128)S(1)} async-done(((f32[4,2,256,256]{3,2,1,0:T(8,128)}), f32[4,2,256,256]{3,2,1,0:T(8,128)S(1)}, u32[]{:S(2)}, u32[]{:S(2)}) %all-to-all-start.2) | async-done | bytes 2097184 | tf_op jit(solution)/shard_map/all_to_all | solution.py:185
  188.9 1.1 copy-done.19
  190.1 1.0 copy.12
  (74 shorter events, 3.7 us)
Async XLA Ops:
  0.0 3.3 %copy-start.22 = (s32[1,1,3,32]{3,1,2,0:T(1,128)S(1)}, s32[1,1,3,32]{3,1,2,0:T(1,128)}, u32[]{:S(2)}) copy-start(s32[1,1,3,32]{3,1,2,0:T(1,128)} %param.7) | copy-start | bytes 1156
  1.8 3.8 %collective-permute-start.1 = (f32[4,256,256]{2,1,0:T(8,128)S(1)}, f32[4,256,256]{2,1,0:T(8,128)S(1)}, u32[]{:S(2)}, u32[]{:S(2)}) collective-permute-start(f32[4,256,256]{2,1,0:T(8,128)S(1)} %get-tuple-element.47), channel_id=1, source_target_pairs={{0,16},{16,0},{1,17},{17,1},{2,18},{18,2},{3,19},{19,3},{4,20},{20... | collective-permute-start | bytes 3145736 | tf_op jit(solution)/shard_map/ppermute | solution.py:15
  5.8 7.8 %copy-start.20 = (f32[2,2,256,256]{3,2,1,0:T(8,128)S(1)}, f32[2,2,256,256]{3,2,1,0:T(8,128)}, u32[]{:S(2)}) copy-start(f32[2,2,256,256]{3,2,1,0:T(8,128)} %param.4) | copy-start | bytes 3145732
  5.9 8.7 %copy-start.5 = (f32[2,256,256]{2,1,0:T(8,128)}, f32[2,256,256]{2,1,0:T(8,128)S(1)}, u32[]{:S(2)}) copy-start(f32[2,256,256]{2,1,0:T(8,128)S(1)} %dynamic-slice_bitcast_fusion.1.own) | copy-start | bytes 1572868
  5.9 22.0 %collective-permute-start.5 = (f32[2,256,256]{2,1,0:T(8,128)S(1)}, f32[2,256,256]{2,1,0:T(8,128)S(1)}, u32[]{:S(2)}, u32[]{:S(2)}) collective-permute-start(f32[2,256,256]{2,1,0:T(8,128)S(1)} %dynamic-slice_bitcast_fusion.1.own), channel_id=1, source_target_pairs={{0,32},{32,64},{64,96},{96,0},{1,33},{33,65},{65,97},{97,1},{2,34}... | collective-permute-start | bytes 1572872 | tf_op jit(solution)/shard_map/ppermute | solution.py:15
  7.7 20.2 %collective-permute-start.6 = (f32[2,256,256]{2,1,0:T(8,128)S(1)}, f32[2,256,256]{2,1,0:T(8,128)S(1)}, u32[]{:S(2)}, u32[]{:S(2)}) collective-permute-start(f32[2,256,256]{2,1,0:T(8,128)S(1)} %dynamic-slice_bitcast_fusion.1.own), channel_id=1, source_target_pairs={{0,96},{32,0},{64,32},{96,64},{1,97},{33,1},{65,33},{97,65},{2,98}... | collective-permute-start | bytes 1572872 | tf_op jit(solution)/shard_map/ppermute | solution.py:15
  9.9 8.3 %collective-permute-start.2 = (f32[256,256]{1,0:T(8,128)S(1)}, f32[256,256]{1,0:T(8,128)S(1)}, u32[]{:S(2)}, u32[]{:S(2)}) collective-permute-start(f32[256,256]{1,0:T(8,128)S(1)} %get-tuple-element.43), channel_id=1, source_target_pairs={{0,3},{1,0},{2,1},{3,2},{4,7},{5,4},{6,5},{7,6},{8,11},{9,8},{10,9... | collective-permute-start | bytes 786440 | tf_op jit(solution)/shard_map/ppermute | solution.py:15
  12.5 12.2 %collective-permute-start.3 = (f32[256,256]{1,0:T(8,128)S(1)}, f32[256,256]{1,0:T(8,128)S(1)}, u32[]{:S(2)}, u32[]{:S(2)}) collective-permute-start(f32[256,256]{1,0:T(8,128)S(1)} %get-tuple-element.45), channel_id=1, source_target_pairs={{0,2},{1,3},{2,0},{3,1},{4,6},{5,7},{6,4},{7,5},{8,10},{9,11},{10,... | collective-permute-start | bytes 786440 | tf_op jit(solution)/shard_map/ppermute | solution.py:15
  13.0 14.8 %collective-permute-start.4 = (f32[256,256]{1,0:T(8,128)S(1)}, f32[256,256]{1,0:T(8,128)S(1)}, u32[]{:S(2)}, u32[]{:S(2)}) collective-permute-start(f32[256,256]{1,0:T(8,128)S(1)} %get-tuple-element.44), channel_id=1, source_target_pairs={{0,1},{1,2},{2,3},{3,0},{4,5},{5,6},{6,7},{7,4},{8,9},{9,10},{10,1... | collective-permute-start | bytes 786440 | tf_op jit(solution)/shard_map/ppermute | solution.py:15
  18.3 15.0 %collective-permute-start = (f32[520,256]{1,0:T(8,128)}, f32[520,256]{1,0:T(8,128)S(1)}, u32[]{:S(2)}, u32[]{:S(2)}) collective-permute-start(f32[520,256]{1,0:T(8,128)} %get-tuple-element.53), channel_id=1, source_target_pairs={{0,16},{16,0},{1,17},{17,1},{2,18},{18,2},{3,19},{19,3},{4,20},{20... | collective-permute-start | bytes 1597448 | tf_op jit(solution)/shard_map/ppermute | solution.py:15
  27.9 7.5 %copy-start.8 = (f32[2,256,256]{2,1,0:T(8,128)}, f32[2,256,256]{2,1,0:T(8,128)S(1)}, u32[]{:S(2)}) copy-start(f32[2,256,256]{2,1,0:T(8,128)S(1)} %collective-permute-done.5.own_r) | copy-start | bytes 1572868
  27.9 7.5 %copy-start.11 = (f32[2,256,256]{2,1,0:T(8,128)}, f32[2,256,256]{2,1,0:T(8,128)S(1)}, u32[]{:S(2)}) copy-start(f32[2,256,256]{2,1,0:T(8,128)S(1)} %collective-permute-done.6.own_l) | copy-start | bytes 1572868
  29.0 19.0 %all-to-all-start = ((f32[4,256,256]{2,1,0:T(8,128)}), f32[4,256,256]{2,1,0:T(8,128)}, u32[]{:S(2)}, u32[]{:S(2)}) async-start(f32[4,256,256]{2,1,0:T(8,128)} %slice_bitcast_fusion), calls=%async_computation | async-start | bytes 2097152 | tf_op jit(solution)/shard_map/all_to_all | solution.py:151
  33.3 0.8 copy-start.21
  37.0 25.8 %collective-permute-start.11 = (f32[4,256,256]{2,1,0:T(8,128)}, f32[4,256,256]{2,1,0:T(8,128)}, u32[]{:S(2)}, u32[]{:S(2)}) collective-permute-start(f32[4,256,256]{2,1,0:T(8,128)} %get-tuple-element.51), channel_id=1, source_target_pairs={{0,32},{32,64},{64,96},{96,0},{1,33},{33,65},{65,97},{97,1},{2,34}... | collective-permute-start | bytes 3145736 | tf_op jit(solution)/shard_map/ppermute | solution.py:15
  37.0 25.8 %collective-permute-start.12 = (f32[4,256,256]{2,1,0:T(8,128)}, f32[4,256,256]{2,1,0:T(8,128)}, u32[]{:S(2)}, u32[]{:S(2)}) collective-permute-start(f32[4,256,256]{2,1,0:T(8,128)} %get-tuple-element.50), channel_id=1, source_target_pairs={{0,96},{32,0},{64,32},{96,64},{1,97},{33,1},{65,33},{97,65},{2,98}... | collective-permute-start | bytes 3145736 | tf_op jit(solution)/shard_map/ppermute | solution.py:15
  50.2 25.0 %collective-permute-start.9 = (f32[2,520,256]{2,1,0:T(8,128)S(1)}, f32[2,520,256]{2,1,0:T(8,128)S(1)}, u32[]{:S(2)}, u32[]{:S(2)}) collective-permute-start(f32[2,520,256]{2,1,0:T(8,128)S(1)} %maximum_select_fusion.1.a_ref), channel_id=1, source_target_pairs={{0,1},{1,2},{2,3},{3,0},{4,5},{5,6},{6,7},{7,4},{8,9},{9,10},{10,1... | collective-permute-start | bytes 3194888 | tf_op jit(solution)/shard_map/ppermute | solution.py:15
  50.4 25.5 %collective-permute-start.7 = (f32[2,520,256]{2,1,0:T(8,128)S(1)}, f32[2,520,256]{2,1,0:T(8,128)S(1)}, u32[]{:S(2)}, u32[]{:S(2)}) collective-permute-start(f32[2,520,256]{2,1,0:T(8,128)S(1)} %maximum_select_fusion.1.a_ref), channel_id=1, source_target_pairs={{0,3},{1,0},{2,1},{3,2},{4,7},{5,4},{6,5},{7,6},{8,11},{9,8},{10,9... | collective-permute-start | bytes 3194888 | tf_op jit(solution)/shard_map/ppermute | solution.py:15
  62.7 33.8 %collective-permute-start.13 = (f32[3,256,256]{2,1,0:T(8,128)}, f32[3,256,256]{2,1,0:T(8,128)}, u32[]{:S(2)}, u32[]{:S(2)}) collective-permute-start(f32[3,256,256]{2,1,0:T(8,128)} %fusion.rest), channel_id=1, source_target_pairs={{0,32},{32,64},{64,96},{96,0},{1,33},{33,65},{65,97},{97,1},{2,34}... | collective-permute-start | bytes 2359304 | tf_op jit(solution)/shard_map/ppermute | solution.py:15
  62.7 33.8 %collective-permute-start.14 = (f32[3,256,256]{2,1,0:T(8,128)}, f32[3,256,256]{2,1,0:T(8,128)}, u32[]{:S(2)}, u32[]{:S(2)}) collective-permute-start(f32[3,256,256]{2,1,0:T(8,128)} %fusion.rest), channel_id=1, source_target_pairs={{0,96},{32,0},{64,32},{96,64},{1,97},{33,1},{65,33},{97,65},{2,98}... | collective-permute-start | bytes 2359304 | tf_op jit(solution)/shard_map/ppermute | solution.py:15
  76.0 12.9 %collective-permute-start.10 = (f32[1,520,256]{2,1,0:T(8,128)}, f32[1,520,256]{2,1,0:T(8,128)S(1)}, u32[]{:S(2)}, u32[]{:S(2)}) collective-permute-start(f32[1,520,256]{2,1,0:T(8,128)} %slice.103), channel_id=1, source_target_pairs={{0,1},{1,2},{2,3},{3,0},{4,5},{5,6},{6,7},{7,4},{8,9},{9,10},{10,1... | collective-permute-start | bytes 1597448 | tf_op jit(solution)/shard_map/ppermute | solution.py:15
  76.0 1.0 copy-start.3
  77.8 12.6 %collective-permute-start.8 = (f32[1,520,256]{2,1,0:T(8,128)}, f32[1,520,256]{2,1,0:T(8,128)}, u32[]{:S(2)}, u32[]{:S(2)}) collective-permute-start(f32[1,520,256]{2,1,0:T(8,128)} %slice.101), channel_id=1, source_target_pairs={{0,3},{1,0},{2,1},{3,2},{4,7},{5,4},{6,5},{7,6},{8,11},{9,8},{10,9... | collective-permute-start | bytes 1597448 | tf_op jit(solution)/shard_map/ppermute | solution.py:15
  82.4 15.2 %collective-permute-start.15 = (f32[3,128,256]{2,1,0:T(8,128)}, f32[3,128,256]{2,1,0:T(8,128)}, u32[]{:S(2)}, u32[]{:S(2)}) collective-permute-start(f32[3,128,256]{2,1,0:T(8,128)} %slice.87), channel_id=1, source_target_pairs={{0,32},{32,64},{64,96},{96,0},{1,33},{33,65},{65,97},{97,1},{2,34}... | collective-permute-start | bytes 1179656 | tf_op jit(solution)/shard_map/ppermute | solution.py:15
  88.8 8.8 %collective-permute-start.16 = (f32[3,128,256]{2,1,0:T(8,128)}, f32[3,128,256]{2,1,0:T(8,128)}, u32[]{:S(2)}, u32[]{:S(2)}) collective-permute-start(f32[3,128,256]{2,1,0:T(8,128)} %slice.88), channel_id=1, source_target_pairs={{0,96},{32,0},{64,32},{96,64},{1,97},{33,1},{65,33},{97,65},{2,98}... | collective-permute-start | bytes 1179656 | tf_op jit(solution)/shard_map/ppermute | solution.py:15
  90.4 1.2 copy-start.4
  93.9 2.6 %copy-start = (bf16[4,4,256,768]{3,2,1,0:T(8,128)(2,1)}, bf16[4,4,256,768]{3,2,1,0:T(8,128)(2,1)S(1)}, u32[]{:S(2)}) copy-start(bf16[4,4,256,768]{3,2,1,0:T(8,128)(2,1)S(1)} %split_amp.1.a_ref) | copy-start | bytes 18874372
  97.6 2.8 %copy-start.1 = (bf16[4,4,256,768]{3,2,1,0:T(8,128)(2,1)S(1)}, bf16[4,4,256,768]{3,2,1,0:T(8,128)(2,1)}, u32[]{:S(2)}) copy-start(bf16[4,4,256,768]{3,2,1,0:T(8,128)(2,1)} %copy-done) | copy-start | bytes 18874372
  100.4 1.0 copy-start.6
  101.4 1.0 copy-start.9
  102.5 1.0 copy-start.12
  112.4 7.4 %collective-permute-start.17 = (f32[4,2,256,256]{3,2,1,0:T(8,128)S(1)}, f32[4,2,256,256]{3,2,1,0:T(8,128)S(1)}, u32[]{:S(2)}, u32[]{:S(2)}) collective-permute-start(f32[4,2,256,256]{3,2,1,0:T(8,128)S(1)} %get-tuple-element.37), channel_id=1, source_target_pairs={{0,16},{16,0},{1,17},{17,1},{2,18},{18,2},{3,19},{19,3},{4,20},{20... | collective-permute-start | bytes 6291464 | tf_op jit(solution)/shard_map/ppermute | solution.py:15
  115.5 12.7 %collective-permute-start.18 = (f32[3,128,256]{2,1,0:T(8,128)S(1)}, f32[3,128,256]{2,1,0:T(8,128)S(1)}, u32[]{:S(2)}, u32[]{:S(2)}) collective-permute-start(f32[3,128,256]{2,1,0:T(8,128)S(1)} %slice.93), channel_id=1, source_target_pairs={{0,32},{32,64},{64,96},{96,0},{1,33},{33,65},{65,97},{97,1},{2,34}... | collective-permute-start | bytes 1179656 | tf_op jit(solution)/shard_map/ppermute | solution.py:15
  117.8 11.2 %collective-permute-start.19 = (f32[3,128,256]{2,1,0:T(8,128)S(1)}, f32[3,128,256]{2,1,0:T(8,128)S(1)}, u32[]{:S(2)}, u32[]{:S(2)}) collective-permute-start(f32[3,128,256]{2,1,0:T(8,128)S(1)} %slice.94), channel_id=1, source_target_pairs={{0,96},{32,0},{64,32},{96,64},{1,97},{33,1},{65,33},{97,65},{2,98}... | collective-permute-start | bytes 1179656 | tf_op jit(solution)/shard_map/ppermute | solution.py:15
  121.5 8.2 %copy-start.7 = (f32[2,256,256]{2,1,0:T(8,128)S(1)}, f32[2,256,256]{2,1,0:T(8,128)}, u32[]{:S(2)}) copy-start(f32[2,256,256]{2,1,0:T(8,128)} %copy-done.5) | copy-start | bytes 1572868
  121.5 8.2 %copy-start.10 = (f32[2,256,256]{2,1,0:T(8,128)S(1)}, f32[2,256,256]{2,1,0:T(8,128)}, u32[]{:S(2)}) copy-start(f32[2,256,256]{2,1,0:T(8,128)} %copy-done.8) | copy-start | bytes 1572868
  121.5 30.8 %all-to-all-start.1 = ((f32[4,2,256,256]{3,2,1,0:T(8,128)}), f32[4,2,256,256]{3,2,1,0:T(8,128)}, u32[]{:S(2)}, u32[]{:S(2)}) async-start(f32[4,2,256,256]{3,2,1,0:T(8,128)} %add.240), calls=%async_computation.1 | async-start | bytes 4194304 | tf_op jit(solution)/shard_map/all_to_all | solution.py:180
  128.2 0.8 copy-start.15
  129.0 0.7 copy-start.17
  129.7 2.8 %copy-start.2 = (bf16[4,4,256,768]{3,2,1,0:T(8,128)(2,1)S(1)}, bf16[4,4,256,768]{3,2,1,0:T(8,128)(2,1)}, u32[]{:S(2)}) copy-start(bf16[4,4,256,768]{3,2,1,0:T(8,128)(2,1)} %copy-done) | copy-start | bytes 18874372
  132.5 1.0 copy-start.13
  133.5 1.0 copy-start.16
  134.5 1.0 copy-start.18
  142.1 1.3 copy-start.14
  152.3 5.1 %collective-permute-start.20 = (f32[4,2,256,256]{3,2,1,0:T(8,128)}, f32[4,2,256,256]{3,2,1,0:T(8,128)S(1)}, u32[]{:S(2)}, u32[]{:S(2)}) collective-permute-start(f32[4,2,256,256]{3,2,1,0:T(8,128)} %copy-done.14), channel_id=1, source_target_pairs={{0,16},{16,0},{1,17},{17,1},{2,18},{18,2},{3,19},{19,3},{4,20},{20... | collective-permute-start | bytes 6291464 | tf_op jit(solution)/shard_map/ppermute | solution.py:15
  159.1 29.7 %all-to-all-start.2 = ((f32[4,2,256,256]{3,2,1,0:T(8,128)}), f32[4,2,256,256]{3,2,1,0:T(8,128)S(1)}, u32[]{:S(2)}, u32[]{:S(2)}) async-start(f32[4,2,256,256]{3,2,1,0:T(8,128)} %add.245), calls=%async_computation.2 | async-start | bytes 4194304 | tf_op jit(solution)/shard_map/all_to_all | solution.py:185
  188.7 1.2 copy-start.19

commit v9 on v8

--- a/solution.py
+++ b/solution.py
@@ -60,41 +60,57 @@
 
 
 def make_contract_kernel(kp):
-    def kernel(flag_ref, a_ref, own, own_r, own_l, rest, two_r, two_l, own_fa, own_fb, fa, fb, *refs):
-        outs, b_ref = refs[:-1], refs[-1]
+    def kernel(flag_ref, amp_ref, own, own_r, own_l, rest, two_r, two_l, own_fa, own_fb, fa, fb,
+               mine_ref, other_ref, a_ref, near_ref, far_ref, b_ref, sems):
         w = b_ref.shape[2]
         h = w // 2
-
-        def load(s, b, at=0):
-            n = b.shape[0]
-            hi, lo = halves(b)
-            b_ref[s, at : at + n] = hi
-            b_ref[s, w + at : w + at + n] = hi
-            b_ref[s, 2 * w + at : 2 * w + at + n] = lo
+        three = pl.ds(0, 3)
+        pairs = []
+        for step, (mine, others) in enumerate(((own, rest), (own_r, two_r), (own_l, two_l))):
+            pairs.append((mine.at[kp], near_ref.at[step, 0]))
+            pairs.append((others.at[three], near_ref.at[step, pl.ds(1, 3)]))
+        for part, (mine, others) in enumerate(((own_fa, fa), (own_fb, fb))):
+            rows = pl.ds(part * h, h)
+            pairs.append((mine.at[3, pl.ds(kp * h, h)], far_ref.at[0, rows]))
+            pairs.append((others.at[three], far_ref.at[pl.ds(1, 3), rows]))
+        pairs.append((amp_ref, a_ref))
+        copies = [pltpu.make_async_copy(*pair, sems.at[n]) for n, pair in enumerate(pairs)]
+        for n in (0, 1, 10, 2, 3, 4, 5, 6, 7, 8, 9):
+            copies[n].start()
+
+        def load(ref):
+            for s in range(4):
+                hi, lo = halves(ref[s])
+                b_ref[s, :w] = hi
+                b_ref[s, w : 2 * w] = hi
+                b_ref[s, 2 * w :] = lo
 
         z, c = flag_ref[128], flag_ref[129]
 
         @pl.loop(0, 4)
         def _(step):
             ka = lax.rem(z + jnp.where(step == 1, 3, jnp.where(step == 2, 1, jnp.where(step == 3, 2, 0))), 4)
-            for at, (mine, others) in enumerate(((own, rest), (own_r, two_r), (own_l, two_l))):
+            for at in range(3):
                 @pl.when(step == at)
                 def _():
-                    load(0, mine[kp])
-                    for s in range(3):
-                        load(s + 1, others[s])
+                    copies[2 * at].wait()
+                    copies[2 * at + 1].wait()
+                    load(near_ref.at[at])
+
+            @pl.when(step == 0)
+            def _():
+                copies[10].wait()
 
             @pl.when(step == 3)
             def _():
-                for part, (mine, others) in enumerate(((own_fa, fa), (own_fb, fb))):
-                    load(0, mine[3, kp * h : kp * h + h], part * h)
-                    for s in range(3):
-                        load(s + 1, others[s], part * h)
+                for n in range(6, 10):
+                    copies[n].wait()
+                load(far_ref)
 
             for turn in range(2):
                 core = lax.rem(c + turn, 2)
                 for il in range(2):
-                    out, at = outs[turn], (ka, il)
+                    out, at = (mine_ref, other_ref)[turn], (ka, il)
                     out[at] = jnp.zeros((w, w), jnp.float32)
                     for s in range(4):
                         @pl.when(flag_ref[(s * 2 + core) * 16 + kp * 8 + ka * 2 + il] != 0)
@@ -109,12 +125,19 @@
 def contract(kp, flags, a3, pieces):
     w = a3.shape[2]
     inside = pl.BlockSpec(memory_space=pltpu.VMEM)
+    anywhere = pl.BlockSpec(memory_space=pl.ANY)
     out = [jax.ShapeDtypeStruct((4, 2, w, w), jnp.float32)] * 2
     return pl.pallas_call(
         make_contract_kernel(kp),
-        in_specs=[pl.BlockSpec(memory_space=pltpu.SMEM)] + [inside] * (len(pieces) + 1),
-        out_specs=[inside] * len(out),
-        scratch_shapes=[pltpu.VMEM((4, 3 * w, w), jnp.bfloat16)],
+        in_specs=[pl.BlockSpec(memory_space=pltpu.SMEM)] + [anywhere] * (len(pieces) + 1),
+        out_specs=[inside] * 2,
+        scratch_shapes=[
+            pltpu.VMEM(a3.shape, jnp.bfloat16),
+            pltpu.VMEM((3, 4, w, w), jnp.float32),
+            pltpu.VMEM((4, w, w), jnp.float32),
+            pltpu.VMEM((4, 3 * w, w), jnp.bfloat16),
+            pltpu.SemaphoreType.DMA((11,)),
+        ],
         out_shape=out,
         compiler_params=pltpu.CompilerParams(vmem_limit_bytes=28 * MIB),
         cost_estimate=pl.CostEstimate(flops=COST[kp] * 10**9, bytes_accessed=8 * MIB, transcendentals=0),
@@ -147,9 +170,6 @@
         for s in (1, 2, 3)
     ]
     rest = [jnp.stack(came)]
-    pairs, rest[0], own_r, own_l = lax.optimization_barrier((pairs, rest[0], own_r, own_l))
-    held = lax.all_to_all(pairs[:, 1], "x", 0, 0, tiled=True)
-    rest.append(lax.dynamic_slice_in_dim(jnp.concatenate([held, held]), x + 1, 3, 0))
 
     def with_flags(parity):
         tile = lax.dynamic_index_in_dim(amp, parity, 1, keepdims=False)
@@ -157,6 +177,12 @@
 
     a_mine, a_other = with_flags(c), shift(with_flags(1 - c), "c", 1)
     a0 = jnp.where(c == 0, jnp.stack([a_mine, a_other]), jnp.stack([a_other, a_mine]))
+    send_r = jnp.concatenate([rest[0], own_r[:, :h].reshape(1, w, w)])
+    send_l = jnp.concatenate([rest[0], own_l[:, h:].reshape(1, w, w)])
+    pairs, a0, send_r, send_l = lax.optimization_barrier((pairs, a0, send_r, send_l))
+    two_r, two_l = shift(send_r, "z", 1), shift(send_l, "z", -1)
+    held = lax.all_to_all(pairs[:, 1], "x", 0, 0, tiled=True)
+    rest.append(lax.dynamic_slice_in_dim(jnp.concatenate([held, held]), x + 1, 3, 0))
     a0, rest[1] = lax.optimization_barrier((a0, rest[1]))
     a_r, a_l = shift(a0, "x", -1), shift(a0, "x", 1)
     a_fa, a_fb = shift(a_r[:1], "x", -1), shift(a_l[1:], "x", 1)
@@ -166,8 +192,6 @@
     flags = lax.dynamic_index_in_dim(rows.reshape(4, 2, 8, 16), c * 4 + x, 2, keepdims=False)
     flags = jnp.concatenate([flags.reshape(-1).astype(jnp.int32), jnp.stack([z, c])])
 
-    two_r = shift(jnp.concatenate([rest[0], own_r[:, :h].reshape(1, w, w)]), "z", 1)
-    two_l = shift(jnp.concatenate([rest[0], own_l[:, h:].reshape(1, w, w)]), "z", -1)
     two_r, two_l, rest[1] = lax.optimization_barrier((two_r, two_l, rest[1]))
     far0 = shift(two_r[:3, :h], "z", 1), shift(two_l[:3, h:], "z", -1)
     rest1_r, rest1_l = shift(rest[1], "z", 1), shift(rest[1], "z", -1)

time: 194 us -> 198 us (1.021)
  waiting for transfers between devices: 80.3 us -> 88.9 us
  starting transfers between devices: 46.6 us -> 42.5 us
  other arithmetic: 11.5 us -> 13.9 us
    ppermute x21, waiting for transfers between devices: 38.7 us -> 43.7 us  [shift(): return lax.ppermute(t, axis, [(i, (i + s) % n) for i in range(n)])]
    all_to_all x1, waiting for transfers between devices: 8.42 us -> 11.9 us  [on_device(): held = lax.all_to_all(pairs[:, 1], 'x', 0, 0, tiled=True)]
    ppermute x21, starting transfers between devices: 34.2 us -> 30.7 us  [shift(): return lax.ppermute(t, axis, [(i, (i + s) % n) for i in range(n)])]
    unnamed x46, local copies, waits for them, and re-layouts: 21.3 us -> 19 us
  transfers between devices with their start and end apart: 24 -> 24, of which waited for: 11 -> 11; matrix products, arithmetic and copies ran while one was open for 10% -> 11% of each run, Pallas kernels for 5% -> 5%
where the time goes in v9:
time: 198 us; the launch traced here: 197 us
  waiting for transfers between devices  88.9 us (45%)
  starting transfers between devices  42.5 us (21%)
  local copies, waits for them, and re-layouts  34.5 us (17%)
  Pallas kernels  16.7 us (8%)
  other arithmetic  13.9 us (7%)
    ppermute x21, waiting for transfers between devices, shift(): return lax.ppermute(t, axis, [(i, (i + s) % n) for i in range(n)])  43.7 us
    ppermute x21, starting transfers between devices, shift(): return lax.ppermute(t, axis, [(i, (i + s) % n) for i in range(n)])  30.7 us
    all_to_all x1, waiting for transfers between devices, on_device(): part = lax.all_to_all(held + shift(away, 'c', 1), 'y', 0, 0, tiled=True)  24.4 us
    unnamed x46, local copies, waits for them, and re-layouts  19 us
    pallas_call x2, Pallas kernels, contract(): pl.pallas_call(make_contract_kernel(kp), in_specs=[pl.BlockSpec(memory_sp...  14.3 us
    all_to_all x1, waiting for transfers between devices, on_device(): held = lax.all_to_all(pairs[:, 1], 'x', 0, 0, tiled=True)  11.9 us
    all_to_all x1, waiting for transfers between devices, on_device(): part = lax.all_to_all(part, 'y', 0, 0, tiled=True)  8.85 us
    all_to_all x1, starting transfers between devices, on_device(): part = lax.all_to_all(part, 'y', 0, 0, tiled=True)  4.59 us
  transfers between devices with their start and end apart: 24, of which 11 were waited for; matrix products, arithmetic and copies ran while one was open for 11% of the time, Pallas kernels for 5%

profile of v9, /device:TPU:1, one launch (start us, length us, event | category | flops | bytes accessed | tf_op | source)
XLA Modules:
  0.0 196.7 jit_solution(3629505168993549914)
XLA Ops:
  0.0 2.8 %constant_dynamic-slice_fusion.2 = (f32[1,4,256,256]{3,2,1,0:T(8,128)S(1)}, f32[4,256,256]{2,1,0:T(8,128)}) fusion(f32[2,4,256,256]{3,2,1,0:T(8,128)} %param.5, s32[]{:T(128)S(6)} %select_n.125, s32[]{:T(128)S(6)} %select_n.126), kind=kLoop, calls=%fused_computation.41 | loop fusion | bytes 4194312 | tf_op jit(solution)/shard_map/jit(dynamic_index_in_dim)/dynamic_slice | solution.py:161
  2.8 1.4 collective-permute-start
  4.5 0.9 fusion.1
  5.3 1.5 collective-permute-done
  6.9 1.9 maximum_select_fusion
  8.8 1.3 copy-done.16
  10.1 1.7 collective-permute-start.5
  11.8 2.1 %collective-permute-start.6 = (f32[2,256,256]{2,1,0:T(8,128)S(1)}, f32[2,256,256]{2,1,0:T(8,128)S(1)}, u32[]{:S(2)}, u32[]{:S(2)}) collective-permute-start(f32[2,256,256]{2,1,0:T(8,128)S(1)} %dynamic-slice_bitcast_fusion.1.own), channel_id=1, source_target_pairs={{0,96},{32,0},{64,32},{96,64},{1,97},{33,1},{65,33},{97,65},{2,98}... | collective-permute-start | bytes 1572872 | tf_op jit(solution)/shard_map/ppermute | solution.py:15
  13.9 1.2 dynamic-slice_bitcast_fusion.4
  15.1 2.5 %collective-permute-start.2 = (f32[256,256]{1,0:T(8,128)S(1)}, f32[256,256]{1,0:T(8,128)S(1)}, u32[]{:S(2)}, u32[]{:S(2)}) collective-permute-start(f32[256,256]{1,0:T(8,128)S(1)} %get-tuple-element.43), channel_id=1, source_target_pairs={{0,3},{1,0},{2,1},{3,2},{4,7},{5,4},{6,5},{7,6},{8,11},{9,8},{10,9... | collective-permute-start | bytes 786440 | tf_op jit(solution)/shard_map/ppermute | solution.py:15
  18.1 0.6 collective-permute-start.4
  18.8 1.3 maximum_select_fusion.1.a_ref
  20.1 5.8 %collective-permute-done.5.own_r = f32[2,256,256]{2,1,0:T(8,128)S(1)} collective-permute-done((f32[2,256,256]{2,1,0:T(8,128)S(1)}, f32[2,256,256]{2,1,0:T(8,128)S(1)}, u32[]{:S(2)}, u32[]{:S(2)}) %collective-permute-start.5) | collective-permute-done | bytes 524320 | tf_op jit(solution)/shard_map/ppermute | solution.py:15
  26.0 6.9 %collective-permute-done.4 = f32[256,256]{1,0:T(8,128)S(1)} collective-permute-done((f32[256,256]{1,0:T(8,128)S(1)}, f32[256,256]{1,0:T(8,128)S(1)}, u32[]{:S(2)}, u32[]{:S(2)}) %collective-permute-start.4) | collective-permute-done | bytes 262176 | tf_op jit(solution)/shard_map/ppermute | solution.py:15
  33.0 1.5 pad_maximum_fusion.2
  34.5 1.0 slice_bitcast_fusion
  35.5 3.5 %all-to-all-start = ((f32[4,256,256]{2,1,0:T(8,128)}), f32[4,256,256]{2,1,0:T(8,128)S(1)}, u32[]{:S(2)}, u32[]{:S(2)}) async-start(f32[4,256,256]{2,1,0:T(8,128)} %slice_bitcast_fusion), calls=%async_computation | async-start | bytes 2097152 | tf_op jit(solution)/shard_map/all_to_all | solution.py:184
  39.1 2.7 %collective-permute-start.12 = (f32[4,256,256]{2,1,0:T(8,128)}, f32[4,256,256]{2,1,0:T(8,128)}, u32[]{:S(2)}, u32[]{:S(2)}) collective-permute-start(f32[4,256,256]{2,1,0:T(8,128)} %get-tuple-element.30), channel_id=1, source_target_pairs={{0,96},{32,0},{64,32},{96,64},{1,97},{33,1},{65,33},{97,65},{2,98}... | collective-permute-start | bytes 3145736 | tf_op jit(solution)/shard_map/ppermute | solution.py:15
  41.8 11.9 %all-to-all-done = f32[4,256,256]{2,1,0:T(8,128)S(1)} async-done(((f32[4,256,256]{2,1,0:T(8,128)}), f32[4,256,256]{2,1,0:T(8,128)S(1)}, u32[]{:S(2)}, u32[]{:S(2)}) %all-to-all-start) | async-done | bytes 1048608 | tf_op jit(solution)/shard_map/all_to_all | solution.py:184
  53.7 1.0 fusion.rest
  55.1 2.3 %collective-permute-start.7 = (f32[2,520,256]{2,1,0:T(8,128)S(1)}, f32[2,520,256]{2,1,0:T(8,128)S(1)}, u32[]{:S(2)}, u32[]{:S(2)}) collective-permute-start(f32[2,520,256]{2,1,0:T(8,128)S(1)} %maximum_select_fusion.1.a_ref), channel_id=1, source_target_pairs={{0,3},{1,0},{2,1},{3,2},{4,7},{5,4},{6,5},{7,6},{8,11},{9,8},{10,9... | collective-permute-start | bytes 3194888 | tf_op jit(solution)/shard_map/ppermute | solution.py:15
  57.4 7.5 %collective-permute-done.11.two_r.own_fa = f32[4,256,256]{2,1,0:T(8,128)} collective-permute-done((f32[4,256,256]{2,1,0:T(8,128)}, f32[4,256,256]{2,1,0:T(8,128)}, u32[]{:S(2)}, u32[]{:S(2)}) %collective-permute-start.11) | collective-permute-done | bytes 1048608 | tf_op jit(solution)/shard_map/ppermute | solution.py:15
  64.9 2.7 %collective-permute-start.14 = (f32[3,256,256]{2,1,0:T(8,128)}, f32[3,256,256]{2,1,0:T(8,128)}, u32[]{:S(2)}, u32[]{:S(2)}) collective-permute-start(f32[3,256,256]{2,1,0:T(8,128)} %fusion.rest), channel_id=1, source_target_pairs={{0,96},{32,0},{64,32},{96,64},{1,97},{33,1},{65,33},{97,65},{2,98}... | collective-permute-start | bytes 2359304 | tf_op jit(solution)/shard_map/ppermute | solution.py:15
  67.6 12.1 %collective-permute-done.9.l_ref = f32[2,520,256]{2,1,0:T(8,128)S(1)} collective-permute-done((f32[2,520,256]{2,1,0:T(8,128)S(1)}, f32[2,520,256]{2,1,0:T(8,128)S(1)}, u32[]{:S(2)}, u32[]{:S(2)}) %collective-permute-start.9) | collective-permute-done | bytes 1064992 | tf_op jit(solution)/shard_map/ppermute | solution.py:15
  79.7 0.9 slice.105
  80.6 0.8 slice.103
  81.4 2.7 %collective-permute-start.8 = (f32[1,520,256]{2,1,0:T(8,128)}, f32[1,520,256]{2,1,0:T(8,128)}, u32[]{:S(2)}, u32[]{:S(2)}) collective-permute-start(f32[1,520,256]{2,1,0:T(8,128)} %slice.103), channel_id=1, source_target_pairs={{0,3},{1,0},{2,1},{3,2},{4,7},{5,4},{6,5},{7,6},{8,11},{9,8},{10,9... | collective-permute-start | bytes 1597448 | tf_op jit(solution)/shard_map/ppermute | solution.py:15
  84.1 2.0 pad_maximum_fusion.3.rest
  86.2 1.8 slice.87
  88.0 1.8 slice.88
  89.8 3.8 %collective-permute-done.10.fb_ref = f32[1,520,256]{2,1,0:T(8,128)} collective-permute-done((f32[1,520,256]{2,1,0:T(8,128)}, f32[1,520,256]{2,1,0:T(8,128)}, u32[]{:S(2)}, u32[]{:S(2)}) %collective-permute-start.10) | collective-permute-done | bytes 532512 | tf_op jit(solution)/shard_map/ppermute | solution.py:15
  93.6 1.5 collective-permute-start.16
  95.2 2.4 %split_amp.1.amp_ref = bf16[4,4,256,768]{3,2,1,0:T(8,128)(2,1)S(1)} custom-call(f32[2,520,256]{2,1,0:T(8,128)S(1)} %maximum_select_fusion.1.a_ref, f32[2,520,256]{2,1,0:T(8,128)S(1)} %collective-permute-done.7.r_ref, f32[2,520,256]{2,1,0:T(8,128)S(1)} %collective-permute-done.9.l_ref, f32[1,520,256]{2,1,0:T(8,128)} %collective-permute-done.8.fa_ref, ...), custom_call_target="tpu_custom_call" | custom-call | bytes 10485760 | tf_op jit(solution)/shard_map/split_amp/pallas_call | solution.py:50
  97.6 2.6 %copy-done = bf16[4,4,256,768]{3,2,1,0:T(8,128)(2,1)} copy-done((bf16[4,4,256,768]{3,2,1,0:T(8,128)(2,1)}, bf16[4,4,256,768]{3,2,1,0:T(8,128)(2,1)S(1)}, u32[]{:S(2)}) %copy-start) | copy-done | bytes 6291480
  100.3 0.7 slice_reduce_fusion.4
  101.0 0.7 slice_reduce_fusion.3
  102.0 2.8 %copy-done.1 = bf16[4,4,256,768]{3,2,1,0:T(8,128)(2,1)S(1)} copy-done((bf16[4,4,256,768]{3,2,1,0:T(8,128)(2,1)S(1)}, bf16[4,4,256,768]{3,2,1,0:T(8,128)(2,1)}, u32[]{:S(2)}) %copy-start.1) | copy-done | bytes 6291480
  104.8 1.1 copy-done.3
  106.0 1.0 copy-done.5
  107.0 1.0 copy-done.8
  108.0 1.0 copy-done.11
  109.1 6.2 %contract.2 = (f32[4,2,256,256]{3,2,1,0:T(8,128)S(1)}, f32[4,2,256,256]{3,2,1,0:T(8,128)S(1)}) custom-call(s32[130]{0:T(256)S(1)} %pad_add_fusion.flag_ref, bf16[4,4,256,768]{3,2,1,0:T(8,128)(2,1)S(1)} %copy-done.1, f32[2,256,256]{2,1,0:T(8,128)S(1)} %copy-done.5, f32[2,256,256]{2,1,0:T(8,128)S(1)} %copy-done.8, f32[2,256,256]{2,1,0:T(8,128)S(1)} %copy-done.11, ...), custom_call_target="tpu_custom_call" | custom-call | flops 40000000000 | bytes 8388608 | tf_op jit(solution)/shard_map/contract/pallas_call | solution.py:130
  115.3 5.3 %collective-permute-start.17 = (f32[4,2,256,256]{3,2,1,0:T(8,128)S(1)}, f32[4,2,256,256]{3,2,1,0:T(8,128)S(1)}, u32[]{:S(2)}, u32[]{:S(2)}) collective-permute-start(f32[4,2,256,256]{3,2,1,0:T(8,128)S(1)} %get-tuple-element.37), channel_id=1, source_target_pairs={{0,16},{16,0},{1,17},{17,1},{2,18},{18,2},{3,19},{19,3},{4,20},{20... | collective-permute-start | bytes 6291464 | tf_op jit(solution)/shard_map/ppermute | solution.py:15
  120.6 1.0 slice.93
  121.7 1.0 slice.94
  122.7 2.7 %collective-permute-start.19 = (f32[3,128,256]{2,1,0:T(8,128)S(1)}, f32[3,128,256]{2,1,0:T(8,128)S(1)}, u32[]{:S(2)}, u32[]{:S(2)}) collective-permute-start(f32[3,128,256]{2,1,0:T(8,128)S(1)} %slice.94), channel_id=1, source_target_pairs={{0,96},{32,0},{64,32},{96,64},{1,97},{33,1},{65,33},{97,65},{2,98}... | collective-permute-start | bytes 1179656 | tf_op jit(solution)/shard_map/ppermute | solution.py:15
  125.5 1.7 add.240
  127.1 4.6 %all-to-all-start.1 = ((f32[4,2,256,256]{3,2,1,0:T(8,128)}), f32[4,2,256,256]{3,2,1,0:T(8,128)}, u32[]{:S(2)}, u32[]{:S(2)}) async-start(f32[4,2,256,256]{3,2,1,0:T(8,128)} %add.240), calls=%async_computation.1 | async-start | bytes 4194304 | tf_op jit(solution)/shard_map/all_to_all | solution.py:204
  131.7 1.9 collective-permute-done.18.fa
  133.7 0.8 copy-done.14
  134.4 2.8 %copy-done.2 = bf16[4,4,256,768]{3,2,1,0:T(8,128)(2,1)S(1)} copy-done((bf16[4,4,256,768]{3,2,1,0:T(8,128)(2,1)S(1)}, bf16[4,4,256,768]{3,2,1,0:T(8,128)(2,1)}, u32[]{:S(2)}) %copy-start.2) | copy-done | bytes 6291480
  137.2 1.0 copy-done.12
  138.3 1.0 copy-done.15
  139.3 8.2 %contract.3 = (f32[4,2,256,256]{3,2,1,0:T(8,128)S(1)}, f32[4,2,256,256]{3,2,1,0:T(8,128)S(1)}) custom-call(s32[130]{0:T(256)S(1)} %pad_add_fusion.flag_ref, bf16[4,4,256,768]{3,2,1,0:T(8,128)(2,1)S(1)} %copy-done.2, f32[2,256,256]{2,1,0:T(8,128)S(1)} %copy-done.6, f32[2,256,256]{2,1,0:T(8,128)S(1)} %copy-done.9, f32[2,256,256]{2,1,0:T(8,128)S(1)} %copy-done.12, ...), custom_call_target="tpu_custom_call" | custom-call | flops 40000000000 | bytes 8388608 | tf_op jit(solution)/shard_map/contract/pallas_call | solution.py:130
  147.4 1.3 copy-done.13
  148.8 8.8 %all-to-all-done.1 = f32[4,2,256,256]{3,2,1,0:T(8,128)} async-done(((f32[4,2,256,256]{3,2,1,0:T(8,128)}), f32[4,2,256,256]{3,2,1,0:T(8,128)}, u32[]{:S(2)}, u32[]{:S(2)}) %all-to-all-start.1) | async-done | bytes 2097184 | tf_op jit(solution)/shard_map/all_to_all | solution.py:204
  157.6 1.4 collective-permute-start.20
  159.1 4.0 %collective-permute-done.20 = f32[4,2,256,256]{3,2,1,0:T(8,128)S(1)} collective-permute-done((f32[4,2,256,256]{3,2,1,0:T(8,128)}, f32[4,2,256,256]{3,2,1,0:T(8,128)S(1)}, u32[]{:S(2)}, u32[]{:S(2)}) %collective-permute-start.20) | collective-permute-done | bytes 2097184 | tf_op jit(solution)/shard_map/ppermute | solution.py:15
  163.1 1.6 add.245
  164.7 3.6 %all-to-all-start.2 = ((f32[4,2,256,256]{3,2,1,0:T(8,128)}), f32[4,2,256,256]{3,2,1,0:T(8,128)S(1)}, u32[]{:S(2)}, u32[]{:S(2)}) async-start(f32[4,2,256,256]{3,2,1,0:T(8,128)} %add.245), calls=%async_computation.2 | async-start | bytes 4194304 | tf_op jit(solution)/shard_map/all_to_all | solution.py:209
  168.3 1.7 fusion.3
  169.9 24.4 %all-to-all-done.2 = f32[4,2,256,256]{3,2,1,0:T(8,128)S(1)} async-done(((f32[4,2,256,256]{3,2,1,0:T(8,128)}), f32[4,2,256,256]{3,2,1,0:T(8,128)S(1)}, u32[]{:S(2)}, u32[]{:S(2)}) %all-to-all-start.2) | async-done | bytes 2097184 | tf_op jit(solution)/shard_map/all_to_all | solution.py:209
  194.5 1.1 copy-done.18
  195.7 1.0 copy.12
  (74 shorter events, 2.4 us)
Async XLA Ops:
  0.0 4.2 %copy-start.22 = (s32[1,1,3,32]{3,1,2,0:T(1,128)S(1)}, s32[1,1,3,32]{3,1,2,0:T(1,128)}, u32[]{:S(2)}) copy-start(s32[1,1,3,32]{3,1,2,0:T(1,128)} %param.7) | copy-start | bytes 1156
  0.0 4.4 %copy-start.19 = (f32[2,2,256,256]{3,2,1,0:T(8,128)S(1)}, f32[2,2,256,256]{3,2,1,0:T(8,128)}, u32[]{:S(2)}) copy-start(f32[2,2,256,256]{3,2,1,0:T(8,128)} %param.4) | copy-start | bytes 3145732
  2.8 4.1 %collective-permute-start = (f32[4,256,256]{2,1,0:T(8,128)}, f32[4,256,256]{2,1,0:T(8,128)}, u32[]{:S(2)}, u32[]{:S(2)}) collective-permute-start(f32[4,256,256]{2,1,0:T(8,128)} %get-tuple-element.47), channel_id=1, source_target_pairs={{0,16},{16,0},{1,17},{17,1},{2,18},{18,2},{3,19},{19,3},{4,20},{20... | collective-permute-start | bytes 3145736 | tf_op jit(solution)/shard_map/ppermute | solution.py:15
  5.3 12.8 %collective-permute-start.1 = (f32[520,256]{1,0:T(8,128)}, f32[520,256]{1,0:T(8,128)}, u32[]{:S(2)}, u32[]{:S(2)}) collective-permute-start(f32[520,256]{1,0:T(8,128)} %get-tuple-element.53), channel_id=1, source_target_pairs={{0,16},{16,0},{1,17},{17,1},{2,18},{18,2},{3,19},{19,3},{4,20},{20... | collective-permute-start | bytes 1597448 | tf_op jit(solution)/shard_map/ppermute | solution.py:15
  8.7 1.3 copy-start.16
  10.1 15.9 %copy-start.4 = (f32[2,256,256]{2,1,0:T(8,128)}, f32[2,256,256]{2,1,0:T(8,128)S(1)}, u32[]{:S(2)}) copy-start(f32[2,256,256]{2,1,0:T(8,128)S(1)} %dynamic-slice_bitcast_fusion.1.own) | copy-start | bytes 1572868
  10.1 15.8 %collective-permute-start.5 = (f32[2,256,256]{2,1,0:T(8,128)S(1)}, f32[2,256,256]{2,1,0:T(8,128)S(1)}, u32[]{:S(2)}, u32[]{:S(2)}) collective-permute-start(f32[2,256,256]{2,1,0:T(8,128)S(1)} %dynamic-slice_bitcast_fusion.1.own), channel_id=1, source_target_pairs={{0,32},{32,64},{64,96},{96,0},{1,33},{33,65},{65,97},{97,1},{2,34}... | collective-permute-start | bytes 1572872 | tf_op jit(solution)/shard_map/ppermute | solution.py:15
  11.8 14.2 %collective-permute-start.6 = (f32[2,256,256]{2,1,0:T(8,128)S(1)}, f32[2,256,256]{2,1,0:T(8,128)S(1)}, u32[]{:S(2)}, u32[]{:S(2)}) collective-permute-start(f32[2,256,256]{2,1,0:T(8,128)S(1)} %dynamic-slice_bitcast_fusion.1.own), channel_id=1, source_target_pairs={{0,96},{32,0},{64,32},{96,64},{1,97},{33,1},{65,33},{97,65},{2,98}... | collective-permute-start | bytes 1572872 | tf_op jit(solution)/shard_map/ppermute | solution.py:15
  15.1 10.9 %collective-permute-start.2 = (f32[256,256]{1,0:T(8,128)S(1)}, f32[256,256]{1,0:T(8,128)S(1)}, u32[]{:S(2)}, u32[]{:S(2)}) collective-permute-start(f32[256,256]{1,0:T(8,128)S(1)} %get-tuple-element.43), channel_id=1, source_target_pairs={{0,3},{1,0},{2,1},{3,2},{4,7},{5,4},{6,5},{7,6},{8,11},{9,8},{10,9... | collective-permute-start | bytes 786440 | tf_op jit(solution)/shard_map/ppermute | solution.py:15
  17.6 8.4 %collective-permute-start.3 = (f32[256,256]{1,0:T(8,128)S(1)}, f32[256,256]{1,0:T(8,128)S(1)}, u32[]{:S(2)}, u32[]{:S(2)}) collective-permute-start(f32[256,256]{1,0:T(8,128)S(1)} %get-tuple-element.45), channel_id=1, source_target_pairs={{0,2},{1,3},{2,0},{3,1},{4,6},{5,7},{6,4},{7,5},{8,10},{9,11},{10,... | collective-permute-start | bytes 786440 | tf_op jit(solution)/shard_map/ppermute | solution.py:15
  18.1 14.8 %collective-permute-start.4 = (f32[256,256]{1,0:T(8,128)S(1)}, f32[256,256]{1,0:T(8,128)S(1)}, u32[]{:S(2)}, u32[]{:S(2)}) collective-permute-start(f32[256,256]{1,0:T(8,128)S(1)} %get-tuple-element.44), channel_id=1, source_target_pairs={{0,1},{1,2},{2,3},{3,0},{4,5},{5,6},{6,7},{7,4},{8,9},{9,10},{10,1... | collective-permute-start | bytes 786440 | tf_op jit(solution)/shard_map/ppermute | solution.py:15
  25.9 8.6 %copy-start.7 = (f32[2,256,256]{2,1,0:T(8,128)}, f32[2,256,256]{2,1,0:T(8,128)S(1)}, u32[]{:S(2)}) copy-start(f32[2,256,256]{2,1,0:T(8,128)S(1)} %collective-permute-done.5.own_r) | copy-start | bytes 1572868
  25.9 8.6 %copy-start.17 = (f32[2,4,256,256]{3,2,1,0:T(8,128)S(1)}, f32[2,4,256,256]{3,2,1,0:T(8,128)}, u32[]{:S(2)}) copy-start(f32[2,4,256,256]{3,2,1,0:T(8,128)} %copy-done.16) | copy-start | bytes 6291460
  26.0 9.6 %copy-start.10 = (f32[2,256,256]{2,1,0:T(8,128)}, f32[2,256,256]{2,1,0:T(8,128)S(1)}, u32[]{:S(2)}) copy-start(f32[2,256,256]{2,1,0:T(8,128)S(1)} %collective-permute-done.6.own_l) | copy-start | bytes 1572868
  26.0 8.4 %copy-start.20 = (f32[256,256]{1,0:T(8,128)}, f32[256,256]{1,0:T(8,128)S(1)}, u32[]{:S(2)}) copy-start(f32[256,256]{1,0:T(8,128)S(1)} %collective-permute-done.3) | copy-start | bytes 786436
  33.0 1.5 copy-start.21
  35.5 18.2 %all-to-all-start = ((f32[4,256,256]{2,1,0:T(8,128)}), f32[4,256,256]{2,1,0:T(8,128)S(1)}, u32[]{:S(2)}, u32[]{:S(2)}) async-start(f32[4,256,256]{2,1,0:T(8,128)} %slice_bitcast_fusion), calls=%async_computation | async-start | bytes 2097152 | tf_op jit(solution)/shard_map/all_to_all | solution.py:184
  39.1 25.8 %collective-permute-start.11 = (f32[4,256,256]{2,1,0:T(8,128)}, f32[4,256,256]{2,1,0:T(8,128)}, u32[]{:S(2)}, u32[]{:S(2)}) collective-permute-start(f32[4,256,256]{2,1,0:T(8,128)} %get-tuple-element.29), channel_id=1, source_target_pairs={{0,32},{32,64},{64,96},{96,0},{1,33},{33,65},{65,97},{97,1},{2,34}... | collective-permute-start | bytes 3145736 | tf_op jit(solution)/shard_map/ppermute | solution.py:15
  39.1 25.8 %collective-permute-start.12 = (f32[4,256,256]{2,1,0:T(8,128)}, f32[4,256,256]{2,1,0:T(8,128)}, u32[]{:S(2)}, u32[]{:S(2)}) collective-permute-start(f32[4,256,256]{2,1,0:T(8,128)} %get-tuple-element.30), channel_id=1, source_target_pairs={{0,96},{32,0},{64,32},{96,64},{1,97},{33,1},{65,33},{97,65},{2,98}... | collective-permute-start | bytes 3145736 | tf_op jit(solution)/shard_map/ppermute | solution.py:15
  54.7 25.0 %collective-permute-start.9 = (f32[2,520,256]{2,1,0:T(8,128)S(1)}, f32[2,520,256]{2,1,0:T(8,128)S(1)}, u32[]{:S(2)}, u32[]{:S(2)}) collective-permute-start(f32[2,520,256]{2,1,0:T(8,128)S(1)} %maximum_select_fusion.1.a_ref), channel_id=1, source_target_pairs={{0,1},{1,2},{2,3},{3,0},{4,5},{5,6},{6,7},{7,4},{8,9},{9,10},{10,1... | collective-permute-start | bytes 3194888 | tf_op jit(solution)/shard_map/ppermute | solution.py:15
  55.1 25.5 %collective-permute-start.7 = (f32[2,520,256]{2,1,0:T(8,128)S(1)}, f32[2,520,256]{2,1,0:T(8,128)S(1)}, u32[]{:S(2)}, u32[]{:S(2)}) collective-permute-start(f32[2,520,256]{2,1,0:T(8,128)S(1)} %maximum_select_fusion.1.a_ref), channel_id=1, source_target_pairs={{0,3},{1,0},{2,1},{3,2},{4,7},{5,4},{6,5},{7,6},{8,11},{9,8},{10,9... | collective-permute-start | bytes 3194888 | tf_op jit(solution)/shard_map/ppermute | solution.py:15
  64.9 35.4 %collective-permute-start.13 = (f32[3,256,256]{2,1,0:T(8,128)}, f32[3,256,256]{2,1,0:T(8,128)}, u32[]{:S(2)}, u32[]{:S(2)}) collective-permute-start(f32[3,256,256]{2,1,0:T(8,128)} %fusion.rest), channel_id=1, source_target_pairs={{0,32},{32,64},{64,96},{96,0},{1,33},{33,65},{65,97},{97,1},{2,34}... | collective-permute-start | bytes 2359304 | tf_op jit(solution)/shard_map/ppermute | solution.py:15
  64.9 35.4 %collective-permute-start.14 = (f32[3,256,256]{2,1,0:T(8,128)}, f32[3,256,256]{2,1,0:T(8,128)}, u32[]{:S(2)}, u32[]{:S(2)}) collective-permute-start(f32[3,256,256]{2,1,0:T(8,128)} %fusion.rest), channel_id=1, source_target_pairs={{0,96},{32,0},{64,32},{96,64},{1,97},{33,1},{65,33},{97,65},{2,98}... | collective-permute-start | bytes 2359304 | tf_op jit(solution)/shard_map/ppermute | solution.py:15
  80.6 13.0 %collective-permute-start.10 = (f32[1,520,256]{2,1,0:T(8,128)}, f32[1,520,256]{2,1,0:T(8,128)}, u32[]{:S(2)}, u32[]{:S(2)}) collective-permute-start(f32[1,520,256]{2,1,0:T(8,128)} %slice.105), channel_id=1, source_target_pairs={{0,1},{1,2},{2,3},{3,0},{4,5},{5,6},{6,7},{7,4},{8,9},{9,10},{10,1... | collective-permute-start | bytes 1597448 | tf_op jit(solution)/shard_map/ppermute | solution.py:15
  81.4 13.8 %collective-permute-start.8 = (f32[1,520,256]{2,1,0:T(8,128)}, f32[1,520,256]{2,1,0:T(8,128)}, u32[]{:S(2)}, u32[]{:S(2)}) collective-permute-start(f32[1,520,256]{2,1,0:T(8,128)} %slice.103), channel_id=1, source_target_pairs={{0,3},{1,0},{2,1},{3,2},{4,7},{5,4},{6,5},{7,6},{8,11},{9,8},{10,9... | collective-permute-start | bytes 1597448 | tf_op jit(solution)/shard_map/ppermute | solution.py:15
  88.0 14.1 %collective-permute-start.15 = (f32[3,128,256]{2,1,0:T(8,128)}, f32[3,128,256]{2,1,0:T(8,128)}, u32[]{:S(2)}, u32[]{:S(2)}) collective-permute-start(f32[3,128,256]{2,1,0:T(8,128)} %slice.87), channel_id=1, source_target_pairs={{0,32},{32,64},{64,96},{96,0},{1,33},{33,65},{65,97},{97,1},{2,34}... | collective-permute-start | bytes 1179656 | tf_op jit(solution)/shard_map/ppermute | solution.py:15
  93.6 8.5 %collective-permute-start.16 = (f32[3,128,256]{2,1,0:T(8,128)}, f32[3,128,256]{2,1,0:T(8,128)}, u32[]{:S(2)}, u32[]{:S(2)}) collective-permute-start(f32[3,128,256]{2,1,0:T(8,128)} %slice.88), channel_id=1, source_target_pairs={{0,96},{32,0},{64,32},{96,64},{1,97},{33,1},{65,33},{97,65},{2,98}... | collective-permute-start | bytes 1179656 | tf_op jit(solution)/shard_map/ppermute | solution.py:15
  97.6 2.6 %copy-start = (bf16[4,4,256,768]{3,2,1,0:T(8,128)(2,1)}, bf16[4,4,256,768]{3,2,1,0:T(8,128)(2,1)S(1)}, u32[]{:S(2)}) copy-start(bf16[4,4,256,768]{3,2,1,0:T(8,128)(2,1)S(1)} %split_amp.1.amp_ref) | copy-start | bytes 18874372
  102.0 2.8 %copy-start.1 = (bf16[4,4,256,768]{3,2,1,0:T(8,128)(2,1)S(1)}, bf16[4,4,256,768]{3,2,1,0:T(8,128)(2,1)}, u32[]{:S(2)}) copy-start(bf16[4,4,256,768]{3,2,1,0:T(8,128)(2,1)} %copy-done) | copy-start | bytes 18874372
  104.8 1.1 copy-start.3
  106.0 1.0 copy-start.5
  107.0 1.0 copy-start.8
  108.0 1.0 copy-start.11
  115.3 10.2 %collective-permute-start.17 = (f32[4,2,256,256]{3,2,1,0:T(8,128)S(1)}, f32[4,2,256,256]{3,2,1,0:T(8,128)S(1)}, u32[]{:S(2)}, u32[]{:S(2)}) collective-permute-start(f32[4,2,256,256]{3,2,1,0:T(8,128)S(1)} %get-tuple-element.37), channel_id=1, source_target_pairs={{0,16},{16,0},{1,17},{17,1},{2,18},{18,2},{3,19},{19,3},{4,20},{20... | collective-permute-start | bytes 6291464 | tf_op jit(solution)/shard_map/ppermute | solution.py:15
  121.6 12.0 %collective-permute-start.18 = (f32[3,128,256]{2,1,0:T(8,128)S(1)}, f32[3,128,256]{2,1,0:T(8,128)S(1)}, u32[]{:S(2)}, u32[]{:S(2)}) collective-permute-start(f32[3,128,256]{2,1,0:T(8,128)S(1)} %slice.93), channel_id=1, source_target_pairs={{0,32},{32,64},{64,96},{96,0},{1,33},{33,65},{65,97},{97,1},{2,34}... | collective-permute-start | bytes 1179656 | tf_op jit(solution)/shard_map/ppermute | solution.py:15
  122.7 10.9 %collective-permute-start.19 = (f32[3,128,256]{2,1,0:T(8,128)S(1)}, f32[3,128,256]{2,1,0:T(8,128)S(1)}, u32[]{:S(2)}, u32[]{:S(2)}) collective-permute-start(f32[3,128,256]{2,1,0:T(8,128)S(1)} %slice.94), channel_id=1, source_target_pairs={{0,96},{32,0},{64,32},{96,64},{1,97},{33,1},{65,33},{97,65},{2,98}... | collective-permute-start | bytes 1179656 | tf_op jit(solution)/shard_map/ppermute | solution.py:15
  127.1 7.3 %copy-start.6 = (f32[2,256,256]{2,1,0:T(8,128)S(1)}, f32[2,256,256]{2,1,0:T(8,128)}, u32[]{:S(2)}) copy-start(f32[2,256,256]{2,1,0:T(8,128)} %copy-done.4) | copy-start | bytes 1572868
  127.1 7.3 %copy-start.9 = (f32[2,256,256]{2,1,0:T(8,128)S(1)}, f32[2,256,256]{2,1,0:T(8,128)}, u32[]{:S(2)}) copy-start(f32[2,256,256]{2,1,0:T(8,128)} %copy-done.7) | copy-start | bytes 1572868
  127.1 30.5 %all-to-all-start.1 = ((f32[4,2,256,256]{3,2,1,0:T(8,128)}), f32[4,2,256,256]{3,2,1,0:T(8,128)}, u32[]{:S(2)}, u32[]{:S(2)}) async-start(f32[4,2,256,256]{3,2,1,0:T(8,128)} %add.240), calls=%async_computation.1 | async-start | bytes 4194304 | tf_op jit(solution)/shard_map/all_to_all | solution.py:204
  133.7 0.8 copy-start.14
  134.4 2.8 %copy-start.2 = (bf16[4,4,256,768]{3,2,1,0:T(8,128)(2,1)S(1)}, bf16[4,4,256,768]{3,2,1,0:T(8,128)(2,1)}, u32[]{:S(2)}) copy-start(bf16[4,4,256,768]{3,2,1,0:T(8,128)(2,1)} %copy-done) | copy-start | bytes 18874372
  137.2 1.0 copy-start.12
  138.3 1.0 copy-start.15
  147.4 1.3 copy-start.13
  157.6 5.4 %collective-permute-start.20 = (f32[4,2,256,256]{3,2,1,0:T(8,128)}, f32[4,2,256,256]{3,2,1,0:T(8,128)S(1)}, u32[]{:S(2)}, u32[]{:S(2)}) collective-permute-start(f32[4,2,256,256]{3,2,1,0:T(8,128)} %copy-done.13), channel_id=1, source_target_pairs={{0,16},{16,0},{1,17},{17,1},{2,18},{18,2},{3,19},{19,3},{4,20},{20... | collective-permute-start | bytes 6291464 | tf_op jit(solution)/shard_map/ppermute | solution.py:15
  164.7 29.7 %all-to-all-start.2 = ((f32[4,2,256,256]{3,2,1,0:T(8,128)}), f32[4,2,256,256]{3,2,1,0:T(8,128)S(1)}, u32[]{:S(2)}, u32[]{:S(2)}) async-start(f32[4,2,256,256]{3,2,1,0:T(8,128)} %add.245), calls=%async_computation.2 | async-start | bytes 4194304 | tf_op jit(solution)/shard_map/all_to_all | solution.py:209
  194.3 1.2 copy-start.18

commit v10 on v6

--- a/solution.py
+++ b/solution.py
@@ -8,6 +8,7 @@
 NAMES = ("z", "c", "y", "x")
 SIZE = {"z": 4, "c": 2, "y": 4, "x": 4}
 MIB = 1024 * 1024
+COST = (50, 50)
 
 def shift(t, axis, s):
     n = SIZE[axis]
@@ -108,7 +109,7 @@
         scratch_shapes=[pltpu.VMEM((4, 3 * w, w), jnp.bfloat16)],
         out_shape=out,
         compiler_params=pltpu.CompilerParams(vmem_limit_bytes=28 * MIB),
-        cost_estimate=pl.CostEstimate(flops=40 * 10**9, bytes_accessed=8 * MIB, transcendentals=0),
+        cost_estimate=pl.CostEstimate(flops=COST[kp] * 10**9, bytes_accessed=8 * MIB, transcendentals=0),
         name="contract",
     )(flags, a3, *pieces)
 
@@ -143,7 +144,11 @@
         held = lax.all_to_all(pairs[:, kp], "x", 0, 0, tiled=True)
         return lax.dynamic_slice_in_dim(jnp.concatenate([held, held]), x + 1, 3, 0)
 
-    rest = [others(0), others(1)]
+    came = [
+        shift(lax.dynamic_slice(pairs, (lax.rem(x + 4 - s, 4), 1, 0, 0), (1, 1, w, w)).reshape(w, w), "x", -s)
+        for s in (1, 2, 3)
+    ]
+    rest = [others(0), jnp.stack(came)]
 
     two_r = shift(jnp.concatenate([rest[0], own_r[:, :h].reshape(1, w, w)]), "z", 1)
     two_l = shift(jnp.concatenate([rest[0], own_l[:, h:].reshape(1, w, w)]), "z", -1)
@@ -156,8 +161,10 @@
     (part,) = contract(0, False, flags, a3, pieces + (rest[0], two_r, two_l, two_r, two_l) + far0)
     even = lax.psum_scatter(part.reshape(16, w, w), ("y", "c"), scatter_dimension=0, tiled=True)
     held, away = contract(1, True, flags, a3, pieces + (rest[1], rest1_r, rest1_l, two_r, two_l) + far1)
-    part = lax.all_to_all(held + shift(away, "c", 1), "y", 0, 0, tiled=True)
-    return resid + jnp.stack([even, part[0] + part[1] + part[2] + part[3]], axis=1)
+    part = held + shift(away, "c", 1)
+    part = [lax.dynamic_index_in_dim(part, lax.rem(y + s, 4), 0, keepdims=False) for s in range(4)]
+    odd = part[0] + shift(part[1], "y", 1) + shift(part[2], "y", 2) + shift(part[3], "y", 3)
+    return resid + jnp.stack([even, odd], axis=1)
 
 
 def solution(mesh):

time: 187 us -> 191 us (1.021); the launches traced: 184 us -> 190 us
  blocking collectives: 56 us -> 0 us
  waiting for transfers between devices: 42.3 us -> 85.8 us
  starting transfers between devices: 24.8 us -> 33.4 us
  other arithmetic: 9.28 us -> 14.8 us
  Pallas kernels: 15.2 us -> 18.5 us
    all_to_all x2 -> x0, blocking collectives: 56 us -> none  [the longest x1 29.3 us: on_device(): part = lax.all_to_all(held + shift(away, 'c', 1), 'y', 0, 0, tiled=True)]
    ppermute x12 -> x18, waiting for transfers between devices: 34.1 us -> 78.9 us  [shift(): return lax.ppermute(t, axis, [(i, (i + s) % n) for i in range(n)])]
    ppermute x12 -> x18, starting transfers between devices: 20.5 us -> 29.1 us  [shift(): return lax.ppermute(t, axis, [(i, (i + s) % n) for i in range(n)])]
    add x3 -> x2, other arithmetic: 1.71 us -> 5.43 us  [the longest x1 3.28 us: on_device(): part = held + shift(away, 'c', 1)]
    pallas_call x2, Pallas kernels: 13.9 us -> 17.2 us  [contract(): pl.pallas_call(make_contract_kernel(kp, split), in_specs=[pl.BlockSpec(me...]
    unnamed x34 -> x38, local copies, waits for them, and re-layouts: 15.2 us -> 14.7 us
  transfers between devices with their start and end apart: 15 -> 21, of which waited for: 9 -> 14; matrix products, arithmetic and copies ran while one was open for 6% -> 10% of each run, Pallas kernels for 8% -> 10%
where the time goes in v10:
time: 191 us; the launch traced here: 190 us
  waiting for transfers between devices  85.8 us (45%)
  starting transfers between devices  33.4 us (17%)
  local copies, waits for them, and re-layouts  24.3 us (13%)
  Pallas kernels  18.5 us (10%)
  other arithmetic  14.8 us (8%)
  between operations  13.6 us (7%)
    ppermute x18, waiting for transfers between devices, shift(): return lax.ppermute(t, axis, [(i, (i + s) % n) for i in range(n)])  78.9 us
    ppermute x18, starting transfers between devices, shift(): return lax.ppermute(t, axis, [(i, (i + s) % n) for i in range(n)])  29.1 us
    pallas_call x2, Pallas kernels, contract(): pl.pallas_call(make_contract_kernel(kp, split), in_specs=[pl.BlockSpec(me...  17.2 us
    unnamed x38, local copies, waits for them, and re-layouts  14.7 us
    all_to_all x1, waiting for transfers between devices, others(): held = lax.all_to_all(pairs[:, kp], 'x', 0, 0, tiled=True)  6.87 us
    all_to_all x1, starting transfers between devices, others(): held = lax.all_to_all(pairs[:, kp], 'x', 0, 0, tiled=True)  4.27 us
  transfers between devices with their start and end apart: 21, of which 14 were waited for; matrix products, arithmetic and copies ran while one was open for 10% of the time, Pallas kernels for 10%

profile of v10, /device:TPU:1, one launch (start us, length us, event | category | flops | bytes accessed | tf_op | source)
XLA Modules:
  0.0 190.4 jit_solution(13563802807319732880)
XLA Ops:
  6.5 0.9 fusion.6
  7.4 0.1 convert_reduce_fusion
  7.5 2.3 %pad_maximum_fusion.2 = f32[1032,256]{1,0:T(8,128)} fusion(f32[8,256]{1,0:T(8,128)S(1)} %broadcast_in_dim.2, f32[1024,256]{1,0:T(8,128)} %bitcast.72), kind=kLoop, calls=%fused_computation.5 | loop fusion | flops 264192 | bytes 2113536 | tf_op jit(solution)/shard_map/concatenate | solution.py:131
  9.8 1.2 constant_dynamic-slice_fusion
  11.0 1.4 collective-permute-start
  12.4 2.5 %collective-permute-done = f32[4,256,256]{2,1,0:T(8,128)S(1)} collective-permute-done((f32[4,256,256]{2,1,0:T(8,128)}, f32[4,256,256]{2,1,0:T(8,128)S(1)}, u32[]{:S(2)}, u32[]{:S(2)}) %collective-permute-start) | collective-permute-done | bytes 1048608 | tf_op jit(solution)/shard_map/ppermute | solution.py:15
  14.9 1.0 copy-done.18
  15.9 1.8 maximum_select_fusion
  17.7 1.1 slice_bitcast_fusion
  18.8 4.3 %all-to-all-start = ((f32[4,256,256]{2,1,0:T(8,128)}), f32[4,256,256]{2,1,0:T(8,128)}, u32[]{:S(2)}, u32[]{:S(2)}) async-start(f32[4,256,256]{2,1,0:T(8,128)} %slice_bitcast_fusion), calls=%async_computation | async-start | bytes 2097152 | tf_op jit(solution)/shard_map/all_to_all | solution.py:144
  23.2 3.9 %collective-permute-start.2 = (f32[2,256,256]{2,1,0:T(8,128)S(1)}, f32[2,256,256]{2,1,0:T(8,128)S(1)}, u32[]{:S(2)}, u32[]{:S(2)}) collective-permute-start(f32[2,256,256]{2,1,0:T(8,128)S(1)} %dynamic-slice_bitcast_fusion.4.own), channel_id=1, source_target_pairs={{0,96},{32,0},{64,32},{96,64},{1,97},{33,1},{65,33},{97,65},{2,98}... | collective-permute-start | bytes 1572872 | tf_op jit(solution)/shard_map/ppermute | solution.py:15
  27.1 10.9 %collective-permute-done.2.own_l = f32[2,256,256]{2,1,0:T(8,128)S(1)} collective-permute-done((f32[2,256,256]{2,1,0:T(8,128)S(1)}, f32[2,256,256]{2,1,0:T(8,128)S(1)}, u32[]{:S(2)}, u32[]{:S(2)}) %collective-permute-start.2) | collective-permute-done | bytes 524320 | tf_op jit(solution)/shard_map/ppermute | solution.py:15
  38.1 3.2 %collective-permute-done.1.own_r = f32[2,256,256]{2,1,0:T(8,128)S(1)} collective-permute-done((f32[2,256,256]{2,1,0:T(8,128)S(1)}, f32[2,256,256]{2,1,0:T(8,128)S(1)}, u32[]{:S(2)}, u32[]{:S(2)}) %collective-permute-start.1) | collective-permute-done | bytes 524320 | tf_op jit(solution)/shard_map/ppermute | solution.py:15
  41.3 0.8 copy-done.12
  42.1 6.9 %all-to-all-done = f32[4,256,256]{2,1,0:T(8,128)} async-done(((f32[4,256,256]{2,1,0:T(8,128)}), f32[4,256,256]{2,1,0:T(8,128)}, u32[]{:S(2)}, u32[]{:S(2)}) %all-to-all-start) | async-done | bytes 1048608 | tf_op jit(solution)/shard_map/all_to_all | solution.py:144
  48.9 1.2 fusion.rest
  50.2 1.5 pad_maximum_fusion
  51.7 2.6 %collective-permute-start.3 = (f32[4,256,256]{2,1,0:T(8,128)}, f32[4,256,256]{2,1,0:T(8,128)S(1)}, u32[]{:S(2)}, u32[]{:S(2)}) collective-permute-start(f32[4,256,256]{2,1,0:T(8,128)} %get-tuple-element.24), channel_id=1, source_target_pairs={{0,32},{32,64},{64,96},{96,0},{1,33},{33,65},{65,97},{97,1},{2,34}... | collective-permute-start | bytes 3145736 | tf_op jit(solution)/shard_map/ppermute | solution.py:15
  54.3 1.6 collective-permute-start.4
  55.9 1.2 dynamic-slice_bitcast_fusion.7
  57.1 0.7 collective-permute-start.7
  57.8 1.8 collective-permute-start.6
  59.6 0.7 collective-permute-start.5
  60.3 11.5 %collective-permute-done.7 = f32[256,256]{1,0:T(8,128)S(1)} collective-permute-done((f32[256,256]{1,0:T(8,128)S(1)}, f32[256,256]{1,0:T(8,128)S(1)}, u32[]{:S(2)}, u32[]{:S(2)}) %collective-permute-start.7) | collective-permute-done | bytes 262176 | tf_op jit(solution)/shard_map/ppermute | solution.py:15
  71.7 10.9 %collective-permute-done.6 = f32[256,256]{1,0:T(8,128)S(1)} collective-permute-done((f32[256,256]{1,0:T(8,128)S(1)}, f32[256,256]{1,0:T(8,128)S(1)}, u32[]{:S(2)}, u32[]{:S(2)}) %collective-permute-start.6) | collective-permute-done | bytes 262176 | tf_op jit(solution)/shard_map/ppermute | solution.py:15
  82.7 0.1 pad_maximum_fusion.3.rest
  82.8 0.8 slice.39
  83.6 0.7 collective-permute-start.8
  84.3 1.8 slice.40
  86.1 2.0 %collective-permute-start.9 = (f32[3,128,256]{2,1,0:T(8,128)}, f32[3,128,256]{2,1,0:T(8,128)}, u32[]{:S(2)}, u32[]{:S(2)}) collective-permute-start(f32[3,128,256]{2,1,0:T(8,128)} %slice.40), channel_id=1, source_target_pairs={{0,96},{32,0},{64,32},{96,64},{1,97},{33,1},{65,33},{97,65},{2,98}... | collective-permute-start | bytes 1179656 | tf_op jit(solution)/shard_map/ppermute | solution.py:15
  88.1 2.7 %collective-permute-start.11 = (f32[3,256,256]{2,1,0:T(8,128)S(1)}, f32[3,256,256]{2,1,0:T(8,128)}, u32[]{:S(2)}, u32[]{:S(2)}) collective-permute-start(f32[3,256,256]{2,1,0:T(8,128)S(1)} %pad_maximum_fusion.3.rest), channel_id=1, source_target_pairs={{0,96},{32,0},{64,32},{96,64},{1,97},{33,1},{65,33},{97,65},{2,98}... | collective-permute-start | bytes 2359304 | tf_op jit(solution)/shard_map/ppermute | solution.py:15
  90.7 0.8 slice_reduce_fusion
  91.5 0.1 reshape_squeeze.3
  91.6 0.1 convert_element_type.11
  91.7 3.4 %copy-done = f32[8256,256]{1,0:T(8,128)S(1)} copy-done((f32[8256,256]{1,0:T(8,128)S(1)}, f32[8256,256]{1,0:T(8,128)}, u32[]{:S(2)}) %copy-start) | copy-done | bytes 8454168
  95.1 1.3 split_amp.1.a_ref
  96.4 0.1 pad_add_fusion.flag_ref
  96.5 0.1 copy-done.13
  96.6 8.9 %contract.2 = f32[4,4,256,256]{3,2,1,0:T(8,128)S(1)} custom-call(s32[131]{0:T(256)S(1)} %pad_add_fusion.flag_ref, bf16[4,4,256,768]{3,2,1,0:T(8,128)(2,1)S(1)} %split_amp.1.a_ref, f32[2,256,256]{2,1,0:T(8,128)S(1)} %dynamic-slice_bitcast_fusion.4.own, f32[2,256,256]{2,1,0:T(8,128)S(1)} %copy-done.13, f32[2,256,256]{2,1,0:T(8,128)S(1)} %copy-done.10, ...), custom_call_target="tpu_custom_call" | custom-call | flops 49999998976 | bytes 8388608 | tf_op jit(solution)/shard_map/contract/pallas_call | solution.py:105
  105.6 2.1 %copy-done.3 = f32[4,4,256,256]{3,2,1,0:T(8,128)} copy-done((f32[4,4,256,256]{3,2,1,0:T(8,128)}, f32[4,4,256,256]{3,2,1,0:T(8,128)S(1)}, u32[]{:S(2)}) %copy-start.3) | copy-done | bytes 4194328
  107.7 3.2 %collective-permute-done.10.two_r = f32[3,256,256]{2,1,0:T(8,128)S(1)} collective-permute-done((f32[3,256,256]{2,1,0:T(8,128)S(1)}, f32[3,256,256]{2,1,0:T(8,128)S(1)}, u32[]{:S(2)}, u32[]{:S(2)}) %collective-permute-start.10) | collective-permute-done | bytes 786464 | tf_op jit(solution)/shard_map/ppermute | solution.py:15
  110.9 0.1 collective-permute-start.12
  111.1 1.4 collective-permute-done.11.two_l
  112.4 1.0 slice.48
  113.5 3.0 %collective-permute-start.13 = (f32[3,128,256]{2,1,0:T(8,128)S(1)}, f32[3,128,256]{2,1,0:T(8,128)S(1)}, u32[]{:S(2)}, u32[]{:S(2)}) collective-permute-start(f32[3,128,256]{2,1,0:T(8,128)S(1)} %slice.48), channel_id=1, source_target_pairs={{0,96},{32,0},{64,32},{96,64},{1,97},{33,1},{65,33},{97,65},{2,98}... | collective-permute-start | bytes 1179656 | tf_op jit(solution)/shard_map/ppermute | solution.py:15
  116.4 3.8 %collective-permute-done.12.fa = f32[3,128,256]{2,1,0:T(8,128)S(1)} collective-permute-done((f32[3,128,256]{2,1,0:T(8,128)S(1)}, f32[3,128,256]{2,1,0:T(8,128)S(1)}, u32[]{:S(2)}, u32[]{:S(2)}) %collective-permute-start.12) | collective-permute-done | bytes 393248 | tf_op jit(solution)/shard_map/ppermute | solution.py:15
  120.3 1.7 collective-permute-done.13.fb
  122.0 2.8 %copy-done.2 = bf16[4,4,256,768]{3,2,1,0:T(8,128)(2,1)S(1)} copy-done((bf16[4,4,256,768]{3,2,1,0:T(8,128)(2,1)S(1)}, bf16[4,4,256,768]{3,2,1,0:T(8,128)(2,1)}, u32[]{:S(2)}) %copy-start.2) | copy-done | bytes 6291480
  124.8 1.1 copy-done.5
  125.9 1.3 copy-done.8
  127.2 1.1 copy-done.11
  128.3 1.1 copy-done.14
  129.3 8.3 %contract.3 = (f32[4,2,256,256]{3,2,1,0:T(8,128)S(1)}, f32[4,2,256,256]{3,2,1,0:T(8,128)}) custom-call(s32[131]{0:T(256)S(1)} %pad_add_fusion.flag_ref, bf16[4,4,256,768]{3,2,1,0:T(8,128)(2,1)S(1)} %copy-done.2, f32[2,256,256]{2,1,0:T(8,128)S(1)} %dynamic-slice_bitcast_fusion.4.own, f32[2,256,256]{2,1,0:T(8,128)S(1)} %copy-done.14, ...), custom_call_target="tpu_custom_call" | custom-call | flops 49999998976 | bytes 8388608 | tf_op jit(solution)/shard_map/contract/pallas_call | solution.py:105
  137.6 5.2 %collective-permute-start.14 = (f32[4,2,256,256]{3,2,1,0:T(8,128)}, f32[4,2,256,256]{3,2,1,0:T(8,128)}, u32[]{:S(2)}, u32[]{:S(2)}) collective-permute-start(f32[4,2,256,256]{3,2,1,0:T(8,128)} %get-tuple-element.14), channel_id=1, source_target_pairs={{0,16},{16,0},{1,17},{17,1},{2,18},{18,2},{3,19},{19,3},{4,20},{20... | collective-permute-start | bytes 6291464 | tf_op jit(solution)/shard_map/ppermute | solution.py:15
  142.8 4.2 %collective-permute-done.14 = f32[4,2,256,256]{3,2,1,0:T(8,128)} collective-permute-done((f32[4,2,256,256]{3,2,1,0:T(8,128)}, f32[4,2,256,256]{3,2,1,0:T(8,128)}, u32[]{:S(2)}, u32[]{:S(2)}) %collective-permute-start.14) | collective-permute-done | bytes 2097184 | tf_op jit(solution)/shard_map/ppermute | solution.py:15
  147.0 3.3 %add.199 = f32[4,2,256,256]{3,2,1,0:T(8,128)} add(f32[4,2,256,256]{3,2,1,0:T(8,128)S(1)} %get-tuple-element.13, f32[4,2,256,256]{3,2,1,0:T(8,128)} %collective-permute-done.14) | non-fusion elementwise | flops 524288 | bytes 6291456 | tf_op jit(solution)/shard_map/add | solution.py:164
  150.3 1.5 dynamic-slice_bitcast_fusion.3
  151.8 2.0 %collective-permute-start.17 = (f32[2,256,256]{2,1,0:T(8,128)S(1)}, f32[2,256,256]{2,1,0:T(8,128)S(1)}, u32[]{:S(2)}, u32[]{:S(2)}) collective-permute-start(f32[2,256,256]{2,1,0:T(8,128)S(1)} %get-tuple-element.16), channel_id=1, source_target_pairs={{0,12},{4,0},{8,4},{12,8},{1,13},{5,1},{9,5},{13,9},{2,14},{6,2},{... | collective-permute-start | bytes 1572872 | tf_op jit(solution)/shard_map/ppermute | solution.py:15
  153.8 0.7 collective-permute-start.15
  154.5 10.7 %collective-permute-done.17 = f32[2,256,256]{2,1,0:T(8,128)S(1)} collective-permute-done((f32[2,256,256]{2,1,0:T(8,128)S(1)}, f32[2,256,256]{2,1,0:T(8,128)S(1)}, u32[]{:S(2)}, u32[]{:S(2)}) %collective-permute-start.17) | collective-permute-done | bytes 524320 | tf_op jit(solution)/shard_map/ppermute | solution.py:15
  165.2 3.1 %collective-permute-done.16 = f32[2,256,256]{2,1,0:T(8,128)} collective-permute-done((f32[2,256,256]{2,1,0:T(8,128)S(1)}, f32[2,256,256]{2,1,0:T(8,128)}, u32[]{:S(2)}, u32[]{:S(2)}) %collective-permute-start.16) | collective-permute-done | bytes 524320 | tf_op jit(solution)/shard_map/ppermute | solution.py:15
  168.3 11.6 %collective-permute-done.15 = f32[2,256,256]{2,1,0:T(8,128)} collective-permute-done((f32[2,256,256]{2,1,0:T(8,128)S(1)}, f32[2,256,256]{2,1,0:T(8,128)}, u32[]{:S(2)}, u32[]{:S(2)}) %collective-permute-start.15) | collective-permute-done | bytes 524320 | tf_op jit(solution)/shard_map/ppermute | solution.py:15
  179.9 1.5 fusion.3
  181.4 2.1 %maximum_add_fusion = f32[2,2,256,256]{3,2,1,0:T(8,128)} fusion(f32[2,2,256,256]{3,2,1,0:T(8,128)S(1)} %copy-done.17, f32[2,1,256,256]{3,2,1,0:T(8,128)S(1)} %fusion.3, f32[2,1,256,256]{3,2,1,0:T(8,128)} %bitcast.75), kind=kLoop, calls=%fused_computation.7 | loop fusion | flops 524288 | bytes 3145728 | tf_op jit(solution)/shard_map/add | solution.py:167
  (49 shorter events, 0.3 us)
Async XLA Ops:
  6.5 3.3 %copy-start.16 = (f32[2,4,256,256]{3,2,1,0:T(8,128)S(1)}, f32[2,4,256,256]{3,2,1,0:T(8,128)}, u32[]{:S(2)}) copy-start(f32[2,4,256,256]{3,2,1,0:T(8,128)} %param.5) | copy-start | bytes 6291460
  6.5 84.2 %all-gather.3.cloned.1.call-start = ((), (), s32[]{:S(2)}) async-start(), calls=%async_computation.3 | async-start | bytes 9510912 | tf_op jit(solution)/shard_map/all_gather | solution.py:130
  11.0 3.9 %collective-permute-start = (f32[4,256,256]{2,1,0:T(8,128)}, f32[4,256,256]{2,1,0:T(8,128)S(1)}, u32[]{:S(2)}, u32[]{:S(2)}) collective-permute-start(f32[4,256,256]{2,1,0:T(8,128)} %get-tuple-element.22), channel_id=1, source_target_pairs={{0,16},{16,0},{1,17},{17,1},{2,18},{18,2},{3,19},{19,3},{4,20},{20... | collective-permute-start | bytes 3145736 | tf_op jit(solution)/shard_map/ppermute | solution.py:15
  14.9 1.0 copy-start.18
  17.7 5.5 %copy-start.15 = (f32[2,4,256,256]{3,2,1,0:T(8,128)}, f32[2,4,256,256]{3,2,1,0:T(8,128)S(1)}, u32[]{:S(2)}) copy-start(f32[2,4,256,256]{3,2,1,0:T(8,128)S(1)} %maximum_select_fusion) | copy-start | bytes 6291460
  18.8 30.1 %all-to-all-start = ((f32[4,256,256]{2,1,0:T(8,128)}), f32[4,256,256]{2,1,0:T(8,128)}, u32[]{:S(2)}, u32[]{:S(2)}) async-start(f32[4,256,256]{2,1,0:T(8,128)} %slice_bitcast_fusion), calls=%async_computation | async-start | bytes 2097152 | tf_op jit(solution)/shard_map/all_to_all | solution.py:144
  23.1 158.3 %reduce-scatter.2.cloned.1.call-start = ((), (), s32[]{:S(2)}) async-start(), calls=%async_computation.2 | async-start | bytes 4718592 | tf_op jit(solution)/shard_map/reduce_scatter | solution.py:162
  23.2 14.9 %collective-permute-start.2 = (f32[2,256,256]{2,1,0:T(8,128)S(1)}, f32[2,256,256]{2,1,0:T(8,128)S(1)}, u32[]{:S(2)}, u32[]{:S(2)}) collective-permute-start(f32[2,256,256]{2,1,0:T(8,128)S(1)} %dynamic-slice_bitcast_fusion.4.own), channel_id=1, source_target_pairs={{0,96},{32,0},{64,32},{96,64},{1,97},{33,1},{65,33},{97,65},{2,98}... | collective-permute-start | bytes 1572872 | tf_op jit(solution)/shard_map/ppermute | solution.py:15
  27.1 14.1 %collective-permute-start.1 = (f32[2,256,256]{2,1,0:T(8,128)S(1)}, f32[2,256,256]{2,1,0:T(8,128)S(1)}, u32[]{:S(2)}, u32[]{:S(2)}) collective-permute-start(f32[2,256,256]{2,1,0:T(8,128)S(1)} %dynamic-slice_bitcast_fusion.4.own), channel_id=1, source_target_pairs={{0,32},{32,64},{64,96},{96,0},{1,33},{33,65},{65,97},{97,1},{2,34}... | collective-permute-start | bytes 1572872 | tf_op jit(solution)/shard_map/ppermute | solution.py:15
  38.1 3.2 %copy-start.9 = (f32[2,256,256]{2,1,0:T(8,128)}, f32[2,256,256]{2,1,0:T(8,128)S(1)}, u32[]{:S(2)}) copy-start(f32[2,256,256]{2,1,0:T(8,128)S(1)} %collective-permute-done.2.own_l) | copy-start | bytes 1572868
  41.3 0.8 copy-start.12
  51.7 31.0 %collective-permute-start.3 = (f32[4,256,256]{2,1,0:T(8,128)}, f32[4,256,256]{2,1,0:T(8,128)S(1)}, u32[]{:S(2)}, u32[]{:S(2)}) collective-permute-start(f32[4,256,256]{2,1,0:T(8,128)} %get-tuple-element.24), channel_id=1, source_target_pairs={{0,32},{32,64},{64,96},{96,0},{1,33},{33,65},{65,97},{97,1},{2,34}... | collective-permute-start | bytes 3145736 | tf_op jit(solution)/shard_map/ppermute | solution.py:15
  54.3 28.4 %collective-permute-start.4 = (f32[4,256,256]{2,1,0:T(8,128)}, f32[4,256,256]{2,1,0:T(8,128)}, u32[]{:S(2)}, u32[]{:S(2)}) collective-permute-start(f32[4,256,256]{2,1,0:T(8,128)} %get-tuple-element.23), channel_id=1, source_target_pairs={{0,96},{32,0},{64,32},{96,64},{1,97},{33,1},{65,33},{97,65},{2,98}... | collective-permute-start | bytes 3145736 | tf_op jit(solution)/shard_map/ppermute | solution.py:15
  57.1 14.6 %collective-permute-start.7 = (f32[256,256]{1,0:T(8,128)S(1)}, f32[256,256]{1,0:T(8,128)S(1)}, u32[]{:S(2)}, u32[]{:S(2)}) collective-permute-start(f32[256,256]{1,0:T(8,128)S(1)} %get-tuple-element.19), channel_id=1, source_target_pairs={{0,1},{1,2},{2,3},{3,0},{4,5},{5,6},{6,7},{7,4},{8,9},{9,10},{10,1... | collective-permute-start | bytes 786440 | tf_op jit(solution)/shard_map/ppermute | solution.py:15
  57.8 24.9 %collective-permute-start.6 = (f32[256,256]{1,0:T(8,128)S(1)}, f32[256,256]{1,0:T(8,128)S(1)}, u32[]{:S(2)}, u32[]{:S(2)}) collective-permute-start(f32[256,256]{1,0:T(8,128)S(1)} %get-tuple-element.20), channel_id=1, source_target_pairs={{0,2},{1,3},{2,0},{3,1},{4,6},{5,7},{6,4},{7,5},{8,10},{9,11},{10,... | collective-permute-start | bytes 786440 | tf_op jit(solution)/shard_map/ppermute | solution.py:15
  59.6 23.1 %collective-permute-start.5 = (f32[256,256]{1,0:T(8,128)S(1)}, f32[256,256]{1,0:T(8,128)S(1)}, u32[]{:S(2)}, u32[]{:S(2)}) collective-permute-start(f32[256,256]{1,0:T(8,128)S(1)} %get-tuple-element.18), channel_id=1, source_target_pairs={{0,3},{1,0},{2,1},{3,2},{4,7},{5,4},{6,5},{7,6},{8,11},{9,8},{10,9... | collective-permute-start | bytes 786440 | tf_op jit(solution)/shard_map/ppermute | solution.py:15
  82.7 5.3 %copy-start.6 = (f32[4,256,256]{2,1,0:T(8,128)}, f32[4,256,256]{2,1,0:T(8,128)S(1)}, u32[]{:S(2)}) copy-start(f32[4,256,256]{2,1,0:T(8,128)S(1)} %collective-permute-done.3.two_r.own_fa) | copy-start | bytes 3145732
  83.6 12.8 %collective-permute-start.8 = (f32[3,128,256]{2,1,0:T(8,128)}, f32[3,128,256]{2,1,0:T(8,128)}, u32[]{:S(2)}, u32[]{:S(2)}) collective-permute-start(f32[3,128,256]{2,1,0:T(8,128)} %slice.39), channel_id=1, source_target_pairs={{0,32},{32,64},{64,96},{96,0},{1,33},{33,65},{65,97},{97,1},{2,34}... | collective-permute-start | bytes 1179656 | tf_op jit(solution)/shard_map/ppermute | solution.py:15
  86.1 10.4 %collective-permute-start.9 = (f32[3,128,256]{2,1,0:T(8,128)}, f32[3,128,256]{2,1,0:T(8,128)}, u32[]{:S(2)}, u32[]{:S(2)}) collective-permute-start(f32[3,128,256]{2,1,0:T(8,128)} %slice.40), channel_id=1, source_target_pairs={{0,96},{32,0},{64,32},{96,64},{1,97},{33,1},{65,33},{97,65},{2,98}... | collective-permute-start | bytes 1179656 | tf_op jit(solution)/shard_map/ppermute | solution.py:15
  88.1 22.8 %collective-permute-start.10 = (f32[3,256,256]{2,1,0:T(8,128)S(1)}, f32[3,256,256]{2,1,0:T(8,128)S(1)}, u32[]{:S(2)}, u32[]{:S(2)}) collective-permute-start(f32[3,256,256]{2,1,0:T(8,128)S(1)} %pad_maximum_fusion.3.rest), channel_id=1, source_target_pairs={{0,32},{32,64},{64,96},{96,0},{1,33},{33,65},{65,97},{97,1},{2,34}... | collective-permute-start | bytes 2359304 | tf_op jit(solution)/shard_map/ppermute | solution.py:15
  88.1 24.4 %collective-permute-start.11 = (f32[3,256,256]{2,1,0:T(8,128)S(1)}, f32[3,256,256]{2,1,0:T(8,128)}, u32[]{:S(2)}, u32[]{:S(2)}) collective-permute-start(f32[3,256,256]{2,1,0:T(8,128)S(1)} %pad_maximum_fusion.3.rest), channel_id=1, source_target_pairs={{0,96},{32,0},{64,32},{96,64},{1,97},{33,1},{65,33},{97,65},{2,98}... | collective-permute-start | bytes 2359304 | tf_op jit(solution)/shard_map/ppermute | solution.py:15
  91.7 3.4 %copy-start = (f32[8256,256]{1,0:T(8,128)S(1)}, f32[8256,256]{1,0:T(8,128)}, u32[]{:S(2)}) copy-start(f32[8256,256]{1,0:T(8,128)} %all-gather.3.cloned.1.call-done) | copy-start | bytes 25362436
  95.1 1.4 copy-start.7
  95.1 1.4 copy-start.10
  95.1 1.5 copy-start.13
  96.4 9.2 %copy-start.1 = (bf16[4,4,256,768]{3,2,1,0:T(8,128)(2,1)}, bf16[4,4,256,768]{3,2,1,0:T(8,128)(2,1)S(1)}, u32[]{:S(2)}) copy-start(bf16[4,4,256,768]{3,2,1,0:T(8,128)(2,1)S(1)} %split_amp.1.a_ref) | copy-start | bytes 18874372
  105.5 2.1 %copy-start.3 = (f32[4,4,256,256]{3,2,1,0:T(8,128)}, f32[4,4,256,256]{3,2,1,0:T(8,128)S(1)}, u32[]{:S(2)}) copy-start(f32[4,4,256,256]{3,2,1,0:T(8,128)S(1)} %contract.2) | copy-start | bytes 12582916
  110.9 9.4 %copy-start.4 = (f32[3,256,256]{2,1,0:T(8,128)}, f32[3,256,256]{2,1,0:T(8,128)S(1)}, u32[]{:S(2)}) copy-start(f32[3,256,256]{2,1,0:T(8,128)S(1)} %collective-permute-done.10.two_r) | copy-start | bytes 2359300
  110.9 9.3 %collective-permute-start.12 = (f32[3,128,256]{2,1,0:T(8,128)S(1)}, f32[3,128,256]{2,1,0:T(8,128)S(1)}, u32[]{:S(2)}, u32[]{:S(2)}) collective-permute-start(f32[3,128,256]{2,1,0:T(8,128)S(1)} %slice.47), channel_id=1, source_target_pairs={{0,32},{32,64},{64,96},{96,0},{1,33},{33,65},{65,97},{97,1},{2,34}... | collective-permute-start | bytes 1179656 | tf_op jit(solution)/shard_map/ppermute | solution.py:15
  113.5 8.5 %collective-permute-start.13 = (f32[3,128,256]{2,1,0:T(8,128)S(1)}, f32[3,128,256]{2,1,0:T(8,128)S(1)}, u32[]{:S(2)}, u32[]{:S(2)}) collective-permute-start(f32[3,128,256]{2,1,0:T(8,128)S(1)} %slice.48), channel_id=1, source_target_pairs={{0,96},{32,0},{64,32},{96,64},{1,97},{33,1},{65,33},{97,65},{2,98}... | collective-permute-start | bytes 1179656 | tf_op jit(solution)/shard_map/ppermute | solution.py:15
  122.0 2.8 %copy-start.2 = (bf16[4,4,256,768]{3,2,1,0:T(8,128)(2,1)S(1)}, bf16[4,4,256,768]{3,2,1,0:T(8,128)(2,1)}, u32[]{:S(2)}) copy-start(bf16[4,4,256,768]{3,2,1,0:T(8,128)(2,1)} %copy-done.1) | copy-start | bytes 18874372
  124.8 1.1 copy-start.5
  125.9 1.3 copy-start.8
  127.2 1.1 copy-start.11
  128.3 1.1 copy-start.14
  137.6 9.4 %collective-permute-start.14 = (f32[4,2,256,256]{3,2,1,0:T(8,128)}, f32[4,2,256,256]{3,2,1,0:T(8,128)}, u32[]{:S(2)}, u32[]{:S(2)}) collective-permute-start(f32[4,2,256,256]{3,2,1,0:T(8,128)} %get-tuple-element.14), channel_id=1, source_target_pairs={{0,16},{16,0},{1,17},{17,1},{2,18},{18,2},{3,19},{19,3},{4,20},{20... | collective-permute-start | bytes 6291464 | tf_op jit(solution)/shard_map/ppermute | solution.py:15
  151.8 29.6 %copy-start.17 = (f32[2,2,256,256]{3,2,1,0:T(8,128)S(1)}, f32[2,2,256,256]{3,2,1,0:T(8,128)}, u32[]{:S(2)}) copy-start(f32[2,2,256,256]{3,2,1,0:T(8,128)} %param.6) | copy-start | bytes 3145732
  151.8 13.4 %collective-permute-start.17 = (f32[2,256,256]{2,1,0:T(8,128)S(1)}, f32[2,256,256]{2,1,0:T(8,128)S(1)}, u32[]{:S(2)}, u32[]{:S(2)}) collective-permute-start(f32[2,256,256]{2,1,0:T(8,128)S(1)} %get-tuple-element.16), channel_id=1, source_target_pairs={{0,12},{4,0},{8,4},{12,8},{1,13},{5,1},{9,5},{13,9},{2,14},{6,2},{... | collective-permute-start | bytes 1572872 | tf_op jit(solution)/shard_map/ppermute | solution.py:15
  153.8 14.5 %collective-permute-start.16 = (f32[2,256,256]{2,1,0:T(8,128)S(1)}, f32[2,256,256]{2,1,0:T(8,128)}, u32[]{:S(2)}, u32[]{:S(2)}) collective-permute-start(f32[2,256,256]{2,1,0:T(8,128)S(1)} %get-tuple-element.17), channel_id=1, source_target_pairs={{0,8},{4,12},{8,0},{12,4},{1,9},{5,13},{9,1},{13,5},{2,10},{6,14},... | collective-permute-start | bytes 1572872 | tf_op jit(solution)/shard_map/ppermute | solution.py:15
  153.8 26.1 %collective-permute-start.15 = (f32[2,256,256]{2,1,0:T(8,128)S(1)}, f32[2,256,256]{2,1,0:T(8,128)}, u32[]{:S(2)}, u32[]{:S(2)}) collective-permute-start(f32[2,256,256]{2,1,0:T(8,128)S(1)} %get-tuple-element.15), channel_id=1, source_target_pairs={{0,4},{4,8},{8,12},{12,0},{1,5},{5,9},{9,13},{13,1},{2,6},{6,10},{... | collective-permute-start | bytes 1572872 | tf_op jit(solution)/shard_map/ppermute | solution.py:15
Sparse Core Ops, SparseCore 0:
  9.9 75.2 all-gather.2
  107.8 40.6 reduce-scatter.1

commit v11 on v7

--- a/solution.py
+++ b/solution.py
@@ -8,7 +8,7 @@
 NAMES = ("z", "c", "y", "x")
 SIZE = {"z": 4, "c": 2, "y": 4, "x": 4}
 MIB = 1024 * 1024
-COST = (40, 40)
+COST = (8, 8)
 
 def shift(t, axis, s):
     n = SIZE[axis]
@@ -139,13 +139,14 @@
     other = shift(lax.dynamic_index_in_dim(integ, 1 - c, 0, keepdims=False), "c", 1)
     pairs = jnp.where(c == 0, jnp.stack([mine, other]), jnp.stack([other, mine])).reshape(4, 2, w, w)
     own = lax.dynamic_index_in_dim(pairs, x, 0, keepdims=False)
+    own, pairs = lax.optimization_barrier((own, pairs))
     own_r, own_l = shift(own, "z", 1), shift(own, "z", -1)
 
-    def others(kp):
-        held = lax.all_to_all(pairs[:, kp], "x", 0, 0, tiled=True)
-        return lax.dynamic_slice_in_dim(jnp.concatenate([held, held]), x + 1, 3, 0)
-
-    rest = [others(0), others(1)]
+    came = [
+        shift(lax.dynamic_index_in_dim(pairs, lax.rem(x + 4 - s, 4), 0, keepdims=False), "x", -s) for s in (1, 2, 3)
+    ]
+    rest = [jnp.stack([t[kp] for t in came]) for kp in range(2)]
+    own_r, own_l, rest[0], rest[1] = lax.optimization_barrier((own_r, own_l, rest[0], rest[1]))
 
     def with_flags(parity):
         tile = lax.dynamic_index_in_dim(amp, parity, 1, keepdims=False)
@@ -167,7 +168,6 @@
     two_r, two_l, rest[1] = lax.optimization_barrier((two_r, two_l, rest[1]))
     far0 = shift(two_r[:3, :h], "z", 1), shift(two_l[:3, h:], "z", -1)
     rest1_r, rest1_l = shift(rest[1], "z", 1), shift(rest[1], "z", -1)
-    a3, rest1_r, rest1_l = lax.optimization_barrier((a3, rest1_r, rest1_l))
     far1 = shift(rest1_r[:, :h], "z", 1), shift(rest1_l[:, h:], "z", -1)
 
     pieces = own, own_r, own_l

time: 196 us -> 187 us (0.954)
  starting transfers between devices: 45.1 us -> 38 us
  other arithmetic: 15.3 us -> 9.18 us
  waiting for transfers between devices: 88.1 us -> 93.3 us
  local copies, waits for them, and re-layouts: 26.8 us -> 24.2 us
  Pallas kernels: 19.2 us -> 21.4 us
    ppermute x18 -> x21, waiting for transfers between devices: 28.2 us -> 69.2 us  [shift(): return lax.ppermute(t, axis, [(i, (i + s) % n) for i in range(n)])]
    all_to_all x2 -> x0, waiting for transfers between devices: 26.9 us -> none  [others(): held = lax.all_to_all(pairs[:, kp], 'x', 0, 0, tiled=True)]
    all_to_all x2 -> x0, starting transfers between devices: 8.62 us -> none  [others(): held = lax.all_to_all(pairs[:, kp], 'x', 0, 0, tiled=True)]
    all_to_all x1, waiting for transfers between devices: 8.6 us -> 0.01 us  [on_device(): part = lax.all_to_all(part, 'y', 0, 0, tiled=True)]
    unnamed x24 -> x44, local copies, waits for them, and re-layouts: 7.95 us -> 12.6 us
    concatenate x2 -> x0, other arithmetic: 3.35 us -> none  [others(): return lax.dynamic_slice_in_dim(jnp.concatenate([held, held]), x + 1, 3, 0)]
    pallas_call x2, Pallas kernels: 16.7 us -> 19.1 us  [contract(): pl.pallas_call(make_contract_kernel(kp), in_specs=[pl.BlockSpec(memory_sp...]
    dynamic_slice x1, local copies, waits for them, and re-layouts: 2.27 us -> 0.08 us  [with_flags(): tile = lax.dynamic_index_in_dim(amp, parity, 1, keepdims=False)]
  transfers between devices with their start and end apart: 22 -> 23, of which waited for: 10 -> 11; matrix products, arithmetic and copies ran while one was open for 13% -> 8% of each run, Pallas kernels for 6% -> 5%
where the time goes in v11:
time: 187 us; the launch traced here: 186 us
  waiting for transfers between devices  93.3 us (50%)
  starting transfers between devices  38 us (20%)
  local copies, waits for them, and re-layouts  24.2 us (13%)
  Pallas kernels  21.4 us (11%)
  other arithmetic  9.18 us (5%)
    ppermute x21, waiting for transfers between devices, shift(): return lax.ppermute(t, axis, [(i, (i + s) % n) for i in range(n)])  69.2 us
    ppermute x21, starting transfers between devices, shift(): return lax.ppermute(t, axis, [(i, (i + s) % n) for i in range(n)])  27.8 us
    all_to_all x1, waiting for transfers between devices, on_device(): part = lax.all_to_all(held + shift(away, 'c', 1), 'y', 0, 0, tiled=True)  24.1 us
    pallas_call x2, Pallas kernels, contract(): pl.pallas_call(make_contract_kernel(kp), in_specs=[pl.BlockSpec(memory_sp...  19.1 us
    unnamed x44, local copies, waits for them, and re-layouts  12.6 us
    all_to_all x1, starting transfers between devices, on_device(): part = lax.all_to_all(held + shift(away, 'c', 1), 'y', 0, 0, tiled=True)  5.63 us
    all_to_all x1, starting transfers between devices, on_device(): part = lax.all_to_all(part, 'y', 0, 0, tiled=True)  4.58 us
  transfers between devices with their start and end apart: 23, of which 11 were waited for; matrix products, arithmetic and copies ran while one was open for 8% of the time, Pallas kernels for 5%

profile of v11, /device:TPU:1, one launch (start us, length us, event | category | flops | bytes accessed | tf_op | source)
XLA Modules:
  0.0 186.4 jit_solution(7252126571671092053)
XLA Ops:
  0.0 2.8 %constant_dynamic-slice_fusion = (f32[1,4,256,256]{3,2,1,0:T(8,128)S(1)}, f32[4,256,256]{2,1,0:T(8,128)}) fusion(f32[2,4,256,256]{3,2,1,0:T(8,128)} %param.5, s32[]{:T(128)S(6)} %select_n.122, s32[]{:T(128)S(6)} %select_n.132), kind=kLoop, calls=%fused_computation.35 | loop fusion | bytes 4194312 | tf_op jit(solution)/shard_map/jit(dynamic_index_in_dim)/dynamic_slice | solution.py:138
  2.8 1.4 collective-permute-start.1
  4.3 0.1 convert_reduce_fusion
  4.5 0.9 fusion
  5.3 1.4 collective-permute-done.1
  6.7 0.2 maximum_select_fusion
  7.0 0.1 dynamic-slice_bitcast_fusion.3
  7.1 2.6 %collective-permute-start.4 = (f32[2,256,256]{2,1,0:T(8,128)S(1)}, f32[2,256,256]{2,1,0:T(8,128)S(1)}, u32[]{:S(2)}, u32[]{:S(2)}) collective-permute-start(f32[2,256,256]{2,1,0:T(8,128)S(1)} %get-tuple-element.37), channel_id=1, source_target_pairs={{0,3},{1,0},{2,1},{3,2},{4,7},{5,4},{6,5},{7,6},{8,11},{9,8},{10,9... | collective-permute-start | bytes 1572872 | tf_op jit(solution)/shard_map/ppermute | solution.py:15
  9.8 0.5 collective-permute-start.5
  10.3 0.6 collective-permute-start.6
  11.0 1.7 collective-permute-start.2
  12.7 2.2 %collective-permute-start.3 = (f32[2,256,256]{2,1,0:T(8,128)S(1)}, f32[2,256,256]{2,1,0:T(8,128)S(1)}, u32[]{:S(2)}, u32[]{:S(2)}) collective-permute-start(f32[2,256,256]{2,1,0:T(8,128)S(1)} %dynamic-slice_bitcast_fusion.4.own), channel_id=1, source_target_pairs={{0,96},{32,0},{64,32},{96,64},{1,97},{33,1},{65,33},{97,65},{2,98}... | collective-permute-start | bytes 1572872 | tf_op jit(solution)/shard_map/ppermute | solution.py:15
  14.9 16.9 %collective-permute-done.4 = f32[2,256,256]{2,1,0:T(8,128)S(1)} collective-permute-done((f32[2,256,256]{2,1,0:T(8,128)S(1)}, f32[2,256,256]{2,1,0:T(8,128)S(1)}, u32[]{:S(2)}, u32[]{:S(2)}) %collective-permute-start.4) | collective-permute-done | bytes 524320 | tf_op jit(solution)/shard_map/ppermute | solution.py:15
  31.9 4.5 %collective-permute-done.6 = f32[2,256,256]{2,1,0:T(8,128)S(1)} collective-permute-done((f32[2,256,256]{2,1,0:T(8,128)S(1)}, f32[2,256,256]{2,1,0:T(8,128)S(1)}, u32[]{:S(2)}, u32[]{:S(2)}) %collective-permute-start.6) | collective-permute-done | bytes 524320 | tf_op jit(solution)/shard_map/ppermute | solution.py:15
  36.4 1.0 pad_maximum_fusion.2
  37.5 1.5 collective-permute-start.9
  39.0 0.8 copy-done.12
  39.8 1.5 pad_maximum_fusion
  41.3 1.6 collective-permute-start.11
  42.9 2.1 %collective-permute-start.12 = (f32[4,256,256]{2,1,0:T(8,128)}, f32[4,256,256]{2,1,0:T(8,128)}, u32[]{:S(2)}, u32[]{:S(2)}) collective-permute-start(f32[4,256,256]{2,1,0:T(8,128)} %get-tuple-element.44), channel_id=1, source_target_pairs={{0,96},{32,0},{64,32},{96,64},{1,97},{33,1},{65,33},{97,65},{2,98}... | collective-permute-start | bytes 3145736 | tf_op jit(solution)/shard_map/ppermute | solution.py:15
  45.1 17.1 %collective-permute-done.7.r_ref = f32[2,520,256]{2,1,0:T(8,128)S(1)} collective-permute-done((f32[2,520,256]{2,1,0:T(8,128)S(1)}, f32[2,520,256]{2,1,0:T(8,128)S(1)}, u32[]{:S(2)}, u32[]{:S(2)}) %collective-permute-start.7) | collective-permute-done | bytes 1064992 | tf_op jit(solution)/shard_map/ppermute | solution.py:15
  62.1 0.9 slice.126
  63.0 0.8 collective-permute-start.8
  63.9 1.0 copy-done.2
  64.8 0.9 slice.128
  65.7 0.6 collective-permute-start.10
  66.5 1.3 collective-permute-done.11.two_r.own_fa
  67.8 1.8 slice.107
  69.6 0.4 collective-permute-start.13
  70.0 1.8 slice.108
  71.8 2.3 %collective-permute-start.14 = (f32[3,128,256]{2,1,0:T(8,128)}, f32[3,128,256]{2,1,0:T(8,128)}, u32[]{:S(2)}, u32[]{:S(2)}) collective-permute-start(f32[3,128,256]{2,1,0:T(8,128)} %slice.108), channel_id=1, source_target_pairs={{0,96},{32,0},{64,32},{96,64},{1,97},{33,1},{65,33},{97,65},{2,98}... | collective-permute-start | bytes 1179656 | tf_op jit(solution)/shard_map/ppermute | solution.py:15
  74.1 0.7 slice_reduce_fusion
  74.9 0.7 collective-permute-done.8.fa_ref
  75.8 3.2 %collective-permute-done.10.fb_ref = f32[1,520,256]{2,1,0:T(8,128)} collective-permute-done((f32[1,520,256]{2,1,0:T(8,128)}, f32[1,520,256]{2,1,0:T(8,128)}, u32[]{:S(2)}, u32[]{:S(2)}) %collective-permute-start.10) | collective-permute-done | bytes 532512 | tf_op jit(solution)/shard_map/ppermute | solution.py:15
  79.0 0.7 slice_reduce_fusion.3
  79.8 0.1 convert_element_type.11
  79.9 1.2 copy-done.3
  81.1 2.3 %split_amp.1.a_ref = bf16[4,4,256,768]{3,2,1,0:T(8,128)(2,1)S(1)} custom-call(f32[2,520,256]{2,1,0:T(8,128)S(1)} %maximum_select_fusion.1.a_ref, f32[2,520,256]{2,1,0:T(8,128)S(1)} %collective-permute-done.7.r_ref, f32[2,520,256]{2,1,0:T(8,128)S(1)} %copy-done.3, f32[1,520,256]{2,1,0:T(8,128)S(1)} %collective-permute-done.8.fa_ref, ...), custom_call_target="tpu_custom_call" | custom-call | bytes 10485760 | tf_op jit(solution)/shard_map/split_amp/pallas_call | solution.py:50
  83.6 12.4 %contract.2 = (f32[4,2,256,256]{3,2,1,0:T(8,128)S(1)}, f32[4,2,256,256]{3,2,1,0:T(8,128)S(1)}) custom-call(s32[130]{0:T(256)S(1)} %pad_add_fusion.flag_ref, bf16[4,4,256,768]{3,2,1,0:T(8,128)(2,1)S(1)} %split_amp.1.a_ref, f32[2,256,256]{2,1,0:T(8,128)S(1)} %copy-done.6, f32[2,256,256]{2,1,0:T(8,128)S(1)} %copy-done.13, f32[2,256,256]{2,1,0:T(8,128)S(1)} %copy-done.16, ...), custom_call_target="tpu_custom_call" | custom-call | flops 8000000000 | bytes 8388608 | tf_op jit(solution)/shard_map/contract/pallas_call | solution.py:113
  96.0 0.1 collective-permute-start.15
  96.1 3.0 %collective-permute-start.16 = (f32[3,256,256]{2,1,0:T(8,128)S(1)}, f32[3,256,256]{2,1,0:T(8,128)S(1)}, u32[]{:S(2)}, u32[]{:S(2)}) collective-permute-start(f32[3,256,256]{2,1,0:T(8,128)S(1)} %copy-done.4), channel_id=1, source_target_pairs={{0,32},{32,64},{64,96},{96,0},{1,33},{33,65},{65,97},{97,1},{2,34}... | collective-permute-start | bytes 2359304 | tf_op jit(solution)/shard_map/ppermute | solution.py:15
  99.1 1.7 collective-permute-start.17
  100.8 1.7 add.233
  102.5 4.6 %all-to-all-start = ((f32[4,2,256,256]{3,2,1,0:T(8,128)}), f32[4,2,256,256]{3,2,1,0:T(8,128)}, u32[]{:S(2)}, u32[]{:S(2)}) async-start(f32[4,2,256,256]{3,2,1,0:T(8,128)} %add.233), calls=%async_computation | async-start | bytes 4194304 | tf_op jit(solution)/shard_map/all_to_all | solution.py:176
  107.0 11.6 %collective-permute-done.16.two_r = f32[3,256,256]{2,1,0:T(8,128)S(1)} collective-permute-done((f32[3,256,256]{2,1,0:T(8,128)S(1)}, f32[3,256,256]{2,1,0:T(8,128)S(1)}, u32[]{:S(2)}, u32[]{:S(2)}) %collective-permute-start.16) | collective-permute-done | bytes 786464 | tf_op jit(solution)/shard_map/ppermute | solution.py:15
  118.8 2.7 %collective-permute-start.19 = (f32[3,128,256]{2,1,0:T(8,128)S(1)}, f32[3,128,256]{2,1,0:T(8,128)S(1)}, u32[]{:S(2)}, u32[]{:S(2)}) collective-permute-start(f32[3,128,256]{2,1,0:T(8,128)S(1)} %slice.136), channel_id=1, source_target_pairs={{0,96},{32,0},{64,32},{96,64},{1,97},{33,1},{65,33},{97,65},{2,98}... | collective-permute-start | bytes 1179656 | tf_op jit(solution)/shard_map/ppermute | solution.py:15
  121.5 8.5 %collective-permute-done.18.fa = f32[3,128,256]{2,1,0:T(8,128)S(1)} collective-permute-done((f32[3,128,256]{2,1,0:T(8,128)S(1)}, f32[3,128,256]{2,1,0:T(8,128)S(1)}, u32[]{:S(2)}, u32[]{:S(2)}) %collective-permute-start.18) | collective-permute-done | bytes 393248 | tf_op jit(solution)/shard_map/ppermute | solution.py:15
  130.1 2.8 %copy-done.1 = bf16[4,4,256,768]{3,2,1,0:T(8,128)(2,1)S(1)} copy-done((bf16[4,4,256,768]{3,2,1,0:T(8,128)(2,1)S(1)}, bf16[4,4,256,768]{3,2,1,0:T(8,128)(2,1)}, u32[]{:S(2)}) %copy-start.1) | copy-done | bytes 6291480
  132.8 1.1 copy-done.9
  134.0 1.1 copy-done.11
  135.1 1.0 copy-done.14
  136.1 1.0 copy-done.17
  137.2 6.7 %contract.3 = (f32[4,2,256,256]{3,2,1,0:T(8,128)S(1)}, f32[4,2,256,256]{3,2,1,0:T(8,128)S(1)}) custom-call(s32[130]{0:T(256)S(1)} %pad_add_fusion.flag_ref, bf16[4,4,256,768]{3,2,1,0:T(8,128)(2,1)S(1)} %copy-done.1, f32[2,256,256]{2,1,0:T(8,128)S(1)} %copy-done.7, f32[2,256,256]{2,1,0:T(8,128)S(1)} %copy-done.14, f32[2,256,256]{2,1,0:T(8,128)S(1)} %copy-done.17, ...), custom_call_target="tpu_custom_call" | custom-call | flops 8000000000 | bytes 8388608 | tf_op jit(solution)/shard_map/contract/pallas_call | solution.py:113
  143.9 1.3 copy-done.18
  145.2 1.7 collective-permute-start.20
  146.9 4.0 %collective-permute-done.20 = f32[4,2,256,256]{3,2,1,0:T(8,128)S(1)} collective-permute-done((f32[4,2,256,256]{3,2,1,0:T(8,128)}, f32[4,2,256,256]{3,2,1,0:T(8,128)S(1)}, u32[]{:S(2)}, u32[]{:S(2)}) %collective-permute-start.20) | collective-permute-done | bytes 2097184 | tf_op jit(solution)/shard_map/ppermute | solution.py:15
  150.9 1.7 add.238
  152.6 5.6 %all-to-all-start.1 = ((f32[4,2,256,256]{3,2,1,0:T(8,128)}), f32[4,2,256,256]{3,2,1,0:T(8,128)S(1)}, u32[]{:S(2)}, u32[]{:S(2)}) async-start(f32[4,2,256,256]{3,2,1,0:T(8,128)} %add.238), calls=%async_computation.1 | async-start | bytes 4194304 | tf_op jit(solution)/shard_map/all_to_all | solution.py:181
  158.3 1.6 fusion.2
  159.9 24.1 %all-to-all-done.1 = f32[4,2,256,256]{3,2,1,0:T(8,128)S(1)} async-done(((f32[4,2,256,256]{3,2,1,0:T(8,128)}), f32[4,2,256,256]{3,2,1,0:T(8,128)S(1)}, u32[]{:S(2)}, u32[]{:S(2)}) %all-to-all-start.1) | async-done | bytes 2097184 | tf_op jit(solution)/shard_map/all_to_all | solution.py:181
  184.0 0.1 fusion.1
  184.2 1.1 copy-done.19
  185.2 0.1 maximum_add_fusion
  185.4 1.0 copy.8
  (71 shorter events, 1.2 us)
Async XLA Ops:
  0.0 4.2 %copy-start.21 = (s32[1,1,3,32]{3,1,2,0:T(1,128)S(1)}, s32[1,1,3,32]{3,1,2,0:T(1,128)}, u32[]{:S(2)}) copy-start(s32[1,1,3,32]{3,1,2,0:T(1,128)} %param.7) | copy-start | bytes 1156
  0.0 4.4 %copy-start.20 = (f32[2,2,256,256]{3,2,1,0:T(8,128)S(1)}, f32[2,2,256,256]{3,2,1,0:T(8,128)}, u32[]{:S(2)}) copy-start(f32[2,2,256,256]{3,2,1,0:T(8,128)} %param.4) | copy-start | bytes 3145732
  2.8 3.9 %collective-permute-start.1 = (f32[4,256,256]{2,1,0:T(8,128)}, f32[4,256,256]{2,1,0:T(8,128)S(1)}, u32[]{:S(2)}, u32[]{:S(2)}) collective-permute-start(f32[4,256,256]{2,1,0:T(8,128)} %get-tuple-element.41), channel_id=1, source_target_pairs={{0,16},{16,0},{1,17},{17,1},{2,18},{18,2},{3,19},{19,3},{4,20},{20... | collective-permute-start | bytes 3145736 | tf_op jit(solution)/shard_map/ppermute | solution.py:15
  5.3 5.5 %collective-permute-start = (f32[520,256]{1,0:T(8,128)}, f32[520,256]{1,0:T(8,128)S(1)}, u32[]{:S(2)}, u32[]{:S(2)}) collective-permute-start(f32[520,256]{1,0:T(8,128)} %get-tuple-element.53), channel_id=1, source_target_pairs={{0,16},{16,0},{1,17},{17,1},{2,18},{18,2},{3,19},{19,3},{4,20},{20... | collective-permute-start | bytes 1597448 | tf_op jit(solution)/shard_map/ppermute | solution.py:15
  7.0 5.7 %copy-start.5 = (f32[2,256,256]{2,1,0:T(8,128)}, f32[2,256,256]{2,1,0:T(8,128)S(1)}, u32[]{:S(2)}) copy-start(f32[2,256,256]{2,1,0:T(8,128)S(1)} %dynamic-slice_bitcast_fusion.4.own) | copy-start | bytes 1572868
  7.1 24.7 %collective-permute-start.4 = (f32[2,256,256]{2,1,0:T(8,128)S(1)}, f32[2,256,256]{2,1,0:T(8,128)S(1)}, u32[]{:S(2)}, u32[]{:S(2)}) collective-permute-start(f32[2,256,256]{2,1,0:T(8,128)S(1)} %get-tuple-element.37), channel_id=1, source_target_pairs={{0,3},{1,0},{2,1},{3,2},{4,7},{5,4},{6,5},{7,6},{8,11},{9,8},{10,9... | collective-permute-start | bytes 1572872 | tf_op jit(solution)/shard_map/ppermute | solution.py:15
  9.8 22.1 %collective-permute-start.5 = (f32[2,256,256]{2,1,0:T(8,128)S(1)}, f32[2,256,256]{2,1,0:T(8,128)S(1)}, u32[]{:S(2)}, u32[]{:S(2)}) collective-permute-start(f32[2,256,256]{2,1,0:T(8,128)S(1)} %get-tuple-element.39), channel_id=1, source_target_pairs={{0,2},{1,3},{2,0},{3,1},{4,6},{5,7},{6,4},{7,5},{8,10},{9,11},{10,... | collective-permute-start | bytes 1572872 | tf_op jit(solution)/shard_map/ppermute | solution.py:15
  10.3 26.1 %collective-permute-start.6 = (f32[2,256,256]{2,1,0:T(8,128)S(1)}, f32[2,256,256]{2,1,0:T(8,128)S(1)}, u32[]{:S(2)}, u32[]{:S(2)}) collective-permute-start(f32[2,256,256]{2,1,0:T(8,128)S(1)} %get-tuple-element.38), channel_id=1, source_target_pairs={{0,1},{1,2},{2,3},{3,0},{4,5},{5,6},{6,7},{7,4},{8,9},{9,10},{10,1... | collective-permute-start | bytes 1572872 | tf_op jit(solution)/shard_map/ppermute | solution.py:15
  11.0 26.4 %collective-permute-start.2 = (f32[2,256,256]{2,1,0:T(8,128)S(1)}, f32[2,256,256]{2,1,0:T(8,128)S(1)}, u32[]{:S(2)}, u32[]{:S(2)}) collective-permute-start(f32[2,256,256]{2,1,0:T(8,128)S(1)} %dynamic-slice_bitcast_fusion.4.own), channel_id=1, source_target_pairs={{0,32},{32,64},{64,96},{96,0},{1,33},{33,65},{65,97},{97,1},{2,34}... | collective-permute-start | bytes 1572872 | tf_op jit(solution)/shard_map/ppermute | solution.py:15
  12.7 24.7 %collective-permute-start.3 = (f32[2,256,256]{2,1,0:T(8,128)S(1)}, f32[2,256,256]{2,1,0:T(8,128)S(1)}, u32[]{:S(2)}, u32[]{:S(2)}) collective-permute-start(f32[2,256,256]{2,1,0:T(8,128)S(1)} %dynamic-slice_bitcast_fusion.4.own), channel_id=1, source_target_pairs={{0,96},{32,0},{64,32},{96,64},{1,97},{33,1},{65,33},{97,65},{2,98}... | collective-permute-start | bytes 1572872 | tf_op jit(solution)/shard_map/ppermute | solution.py:15
  37.4 1.6 copy-start.15
  37.4 24.8 %collective-permute-start.7 = (f32[2,520,256]{2,1,0:T(8,128)S(1)}, f32[2,520,256]{2,1,0:T(8,128)S(1)}, u32[]{:S(2)}, u32[]{:S(2)}) collective-permute-start(f32[2,520,256]{2,1,0:T(8,128)S(1)} %maximum_select_fusion.1.a_ref), channel_id=1, source_target_pairs={{0,3},{1,0},{2,1},{3,2},{4,7},{5,4},{6,5},{7,6},{8,11},{9,8},{10,9... | collective-permute-start | bytes 3194888 | tf_op jit(solution)/shard_map/ppermute | solution.py:15
  37.5 26.4 %collective-permute-start.9 = (f32[2,520,256]{2,1,0:T(8,128)S(1)}, f32[2,520,256]{2,1,0:T(8,128)S(1)}, u32[]{:S(2)}, u32[]{:S(2)}) collective-permute-start(f32[2,520,256]{2,1,0:T(8,128)S(1)} %maximum_select_fusion.1.a_ref), channel_id=1, source_target_pairs={{0,1},{1,2},{2,3},{3,0},{4,5},{5,6},{6,7},{7,4},{8,9},{9,10},{10,1... | collective-permute-start | bytes 3194888 | tf_op jit(solution)/shard_map/ppermute | solution.py:15
  39.0 0.8 copy-start.12
  41.3 26.5 %collective-permute-start.11 = (f32[4,256,256]{2,1,0:T(8,128)}, f32[4,256,256]{2,1,0:T(8,128)}, u32[]{:S(2)}, u32[]{:S(2)}) collective-permute-start(f32[4,256,256]{2,1,0:T(8,128)} %get-tuple-element.45), channel_id=1, source_target_pairs={{0,32},{32,64},{64,96},{96,0},{1,33},{33,65},{65,97},{97,1},{2,34}... | collective-permute-start | bytes 3145736 | tf_op jit(solution)/shard_map/ppermute | solution.py:15
  42.9 24.9 %collective-permute-start.12 = (f32[4,256,256]{2,1,0:T(8,128)}, f32[4,256,256]{2,1,0:T(8,128)}, u32[]{:S(2)}, u32[]{:S(2)}) collective-permute-start(f32[4,256,256]{2,1,0:T(8,128)} %get-tuple-element.44), channel_id=1, source_target_pairs={{0,96},{32,0},{64,32},{96,64},{1,97},{33,1},{65,33},{97,65},{2,98}... | collective-permute-start | bytes 3145736 | tf_op jit(solution)/shard_map/ppermute | solution.py:15
  63.0 12.7 %collective-permute-start.8 = (f32[1,520,256]{2,1,0:T(8,128)}, f32[1,520,256]{2,1,0:T(8,128)S(1)}, u32[]{:S(2)}, u32[]{:S(2)}) collective-permute-start(f32[1,520,256]{2,1,0:T(8,128)} %slice.126), channel_id=1, source_target_pairs={{0,3},{1,0},{2,1},{3,2},{4,7},{5,4},{6,5},{7,6},{8,11},{9,8},{10,9... | collective-permute-start | bytes 1597448 | tf_op jit(solution)/shard_map/ppermute | solution.py:15
  63.9 1.0 copy-start.2
  65.7 13.2 %collective-permute-start.10 = (f32[1,520,256]{2,1,0:T(8,128)}, f32[1,520,256]{2,1,0:T(8,128)}, u32[]{:S(2)}, u32[]{:S(2)}) collective-permute-start(f32[1,520,256]{2,1,0:T(8,128)} %slice.128), channel_id=1, source_target_pairs={{0,1},{1,2},{2,3},{3,0},{4,5},{5,6},{6,7},{7,4},{8,9},{9,10},{10,1... | collective-permute-start | bytes 1597448 | tf_op jit(solution)/shard_map/ppermute | solution.py:15
  69.6 14.0 %collective-permute-start.13 = (f32[3,128,256]{2,1,0:T(8,128)}, f32[3,128,256]{2,1,0:T(8,128)}, u32[]{:S(2)}, u32[]{:S(2)}) collective-permute-start(f32[3,128,256]{2,1,0:T(8,128)} %slice.107), channel_id=1, source_target_pairs={{0,32},{32,64},{64,96},{96,0},{1,33},{33,65},{65,97},{97,1},{2,34}... | collective-permute-start | bytes 1179656 | tf_op jit(solution)/shard_map/ppermute | solution.py:15
  71.8 11.8 %collective-permute-start.14 = (f32[3,128,256]{2,1,0:T(8,128)}, f32[3,128,256]{2,1,0:T(8,128)}, u32[]{:S(2)}, u32[]{:S(2)}) collective-permute-start(f32[3,128,256]{2,1,0:T(8,128)} %slice.108), channel_id=1, source_target_pairs={{0,96},{32,0},{64,32},{96,64},{1,97},{33,1},{65,33},{97,65},{2,98}... | collective-permute-start | bytes 1179656 | tf_op jit(solution)/shard_map/ppermute | solution.py:15
  79.9 1.2 copy-start.3
  81.1 2.5 %copy-start.6 = (f32[2,256,256]{2,1,0:T(8,128)S(1)}, f32[2,256,256]{2,1,0:T(8,128)}, u32[]{:S(2)}) copy-start(f32[2,256,256]{2,1,0:T(8,128)} %copy-done.5) | copy-start | bytes 1572868
  81.1 2.5 %copy-start.13 = (f32[2,256,256]{2,1,0:T(8,128)S(1)}, f32[2,256,256]{2,1,0:T(8,128)}, u32[]{:S(2)}) copy-start(f32[2,256,256]{2,1,0:T(8,128)} %copy-done.12) | copy-start | bytes 1572868
  81.1 2.5 %copy-start.16 = (f32[2,256,256]{2,1,0:T(8,128)S(1)}, f32[2,256,256]{2,1,0:T(8,128)}, u32[]{:S(2)}) copy-start(f32[2,256,256]{2,1,0:T(8,128)} %copy-done.15) | copy-start | bytes 1572868
  83.5 12.5 %copy-start = (bf16[4,4,256,768]{3,2,1,0:T(8,128)(2,1)}, bf16[4,4,256,768]{3,2,1,0:T(8,128)(2,1)S(1)}, u32[]{:S(2)}) copy-start(bf16[4,4,256,768]{3,2,1,0:T(8,128)(2,1)S(1)} %split_amp.1.a_ref) | copy-start | bytes 18874372
  83.6 12.5 %copy-start.4 = (f32[3,256,256]{2,1,0:T(8,128)S(1)}, f32[3,256,256]{2,1,0:T(8,128)}, u32[]{:S(2)}) copy-start(f32[3,256,256]{2,1,0:T(8,128)} %get-tuple-element.33.rest) | copy-start | bytes 2359300
  96.0 4.8 %collective-permute-start.15 = (f32[4,2,256,256]{3,2,1,0:T(8,128)S(1)}, f32[4,2,256,256]{3,2,1,0:T(8,128)S(1)}, u32[]{:S(2)}, u32[]{:S(2)}) collective-permute-start(f32[4,2,256,256]{3,2,1,0:T(8,128)S(1)} %get-tuple-element.32), channel_id=1, source_target_pairs={{0,16},{16,0},{1,17},{17,1},{2,18},{18,2},{3,19},{19,3},{4,20},{20... | collective-permute-start | bytes 6291464 | tf_op jit(solution)/shard_map/ppermute | solution.py:15
  96.1 22.5 %collective-permute-start.16 = (f32[3,256,256]{2,1,0:T(8,128)S(1)}, f32[3,256,256]{2,1,0:T(8,128)S(1)}, u32[]{:S(2)}, u32[]{:S(2)}) collective-permute-start(f32[3,256,256]{2,1,0:T(8,128)S(1)} %copy-done.4), channel_id=1, source_target_pairs={{0,32},{32,64},{64,96},{96,0},{1,33},{33,65},{65,97},{97,1},{2,34}... | collective-permute-start | bytes 2359304 | tf_op jit(solution)/shard_map/ppermute | solution.py:15
  99.1 19.6 %collective-permute-start.17 = (f32[3,256,256]{2,1,0:T(8,128)S(1)}, f32[3,256,256]{2,1,0:T(8,128)S(1)}, u32[]{:S(2)}, u32[]{:S(2)}) collective-permute-start(f32[3,256,256]{2,1,0:T(8,128)S(1)} %copy-done.4), channel_id=1, source_target_pairs={{0,96},{32,0},{64,32},{96,64},{1,97},{33,1},{65,33},{97,65},{2,98}... | collective-permute-start | bytes 2359304 | tf_op jit(solution)/shard_map/ppermute | solution.py:15
  102.5 27.6 %copy-start.7 = (f32[2,256,256]{2,1,0:T(8,128)S(1)}, f32[2,256,256]{2,1,0:T(8,128)}, u32[]{:S(2)}) copy-start(f32[2,256,256]{2,1,0:T(8,128)} %copy-done.5) | copy-start | bytes 1572868
  102.5 42.8 %all-to-all-start = ((f32[4,2,256,256]{3,2,1,0:T(8,128)}), f32[4,2,256,256]{3,2,1,0:T(8,128)}, u32[]{:S(2)}, u32[]{:S(2)}) async-start(f32[4,2,256,256]{3,2,1,0:T(8,128)} %add.233), calls=%async_computation | async-start | bytes 4194304 | tf_op jit(solution)/shard_map/all_to_all | solution.py:176
  118.6 11.4 %copy-start.8 = (f32[3,256,256]{2,1,0:T(8,128)}, f32[3,256,256]{2,1,0:T(8,128)S(1)}, u32[]{:S(2)}) copy-start(f32[3,256,256]{2,1,0:T(8,128)S(1)} %collective-permute-done.16.two_r) | copy-start | bytes 2359300
  118.7 11.4 %collective-permute-start.18 = (f32[3,128,256]{2,1,0:T(8,128)S(1)}, f32[3,128,256]{2,1,0:T(8,128)S(1)}, u32[]{:S(2)}, u32[]{:S(2)}) collective-permute-start(f32[3,128,256]{2,1,0:T(8,128)S(1)} %slice.135), channel_id=1, source_target_pairs={{0,32},{32,64},{64,96},{96,0},{1,33},{33,65},{65,97},{97,1},{2,34}... | collective-permute-start | bytes 1179656 | tf_op jit(solution)/shard_map/ppermute | solution.py:15
  118.7 11.3 %copy-start.10 = (f32[3,256,256]{2,1,0:T(8,128)}, f32[3,256,256]{2,1,0:T(8,128)S(1)}, u32[]{:S(2)}) copy-start(f32[3,256,256]{2,1,0:T(8,128)S(1)} %collective-permute-done.17.two_l) | copy-start | bytes 2359300
  118.8 11.2 %collective-permute-start.19 = (f32[3,128,256]{2,1,0:T(8,128)S(1)}, f32[3,128,256]{2,1,0:T(8,128)S(1)}, u32[]{:S(2)}, u32[]{:S(2)}) collective-permute-start(f32[3,128,256]{2,1,0:T(8,128)S(1)} %slice.136), channel_id=1, source_target_pairs={{0,96},{32,0},{64,32},{96,64},{1,97},{33,1},{65,33},{97,65},{2,98}... | collective-permute-start | bytes 1179656 | tf_op jit(solution)/shard_map/ppermute | solution.py:15
  130.0 2.8 %copy-start.1 = (bf16[4,4,256,768]{3,2,1,0:T(8,128)(2,1)S(1)}, bf16[4,4,256,768]{3,2,1,0:T(8,128)(2,1)}, u32[]{:S(2)}) copy-start(bf16[4,4,256,768]{3,2,1,0:T(8,128)(2,1)} %copy-done) | copy-start | bytes 18874372
  132.8 1.1 copy-start.9
  134.0 1.1 copy-start.11
  135.1 1.0 copy-start.14
  136.1 1.0 copy-start.17
  143.9 1.4 copy-start.18
  145.2 5.7 %collective-permute-start.20 = (f32[4,2,256,256]{3,2,1,0:T(8,128)}, f32[4,2,256,256]{3,2,1,0:T(8,128)S(1)}, u32[]{:S(2)}, u32[]{:S(2)}) collective-permute-start(f32[4,2,256,256]{3,2,1,0:T(8,128)} %copy-done.18), channel_id=1, source_target_pairs={{0,16},{16,0},{1,17},{17,1},{2,18},{18,2},{3,19},{19,3},{4,20},{20... | collective-permute-start | bytes 6291464 | tf_op jit(solution)/shard_map/ppermute | solution.py:15
  152.6 31.4 %all-to-all-start.1 = ((f32[4,2,256,256]{3,2,1,0:T(8,128)}), f32[4,2,256,256]{3,2,1,0:T(8,128)S(1)}, u32[]{:S(2)}, u32[]{:S(2)}) async-start(f32[4,2,256,256]{3,2,1,0:T(8,128)} %add.238), calls=%async_computation.1 | async-start | bytes 4194304 | tf_op jit(solution)/shard_map/all_to_all | solution.py:181
  184.0 1.2 copy-start.19

commit v12 on v11

--- a/solution.py
+++ b/solution.py
@@ -8,7 +8,7 @@
 NAMES = ("z", "c", "y", "x")
 SIZE = {"z": 4, "c": 2, "y": 4, "x": 4}
 MIB = 1024 * 1024
-COST = (8, 8)
+COST = (40, 40)
 
 def shift(t, axis, s):
     n = SIZE[axis]
@@ -168,6 +168,7 @@
     two_r, two_l, rest[1] = lax.optimization_barrier((two_r, two_l, rest[1]))
     far0 = shift(two_r[:3, :h], "z", 1), shift(two_l[:3, h:], "z", -1)
     rest1_r, rest1_l = shift(rest[1], "z", 1), shift(rest[1], "z", -1)
+    a3, rest1_r, rest1_l = lax.optimization_barrier((a3, rest1_r, rest1_l))
     far1 = shift(rest1_r[:, :h], "z", 1), shift(rest1_l[:, h:], "z", -1)
 
     pieces = own, own_r, own_l

time: 187 us -> 183 us (0.979)
  Pallas kernels: 21.4 us -> 14.9 us
  local copies, waits for them, and re-layouts: 24.2 us -> 29.2 us
  waiting for transfers between devices: 93.3 us -> 91.4 us
    ppermute x21, waiting for transfers between devices: 69.2 us -> 59.1 us  [shift(): return lax.ppermute(t, axis, [(i, (i + s) % n) for i in range(n)])]
    all_to_all x1, waiting for transfers between devices: 0.01 us -> 7.95 us  [on_device(): part = lax.all_to_all(part, 'y', 0, 0, tiled=True)]
    pallas_call x2, Pallas kernels: 19.1 us -> 12.5 us  [contract(): pl.pallas_call(make_contract_kernel(kp), in_specs=[pl.BlockSpec(memory_sp...]
    slice x2, local copies, waits for them, and re-layouts: 0.05 us -> 3.56 us  [on_device(): far1 = (shift(rest1_r[:, :h], 'z', 1), shift(rest1_l[:, h:], 'z', -1))]
    ppermute x21, starting transfers between devices: 27.8 us -> 30.1 us  [shift(): return lax.ppermute(t, axis, [(i, (i + s) % n) for i in range(n)])]
    all_to_all x1, starting transfers between devices: 5.63 us -> 3.61 us  [on_device(): part = lax.all_to_all(held + shift(away, 'c', 1), 'y', 0, 0, tiled=True)]
    unnamed x44 -> x50, local copies, waits for them, and re-layouts: 12.6 us -> 14.3 us
  transfers between devices with their start and end apart: 23 -> 23, of which waited for: 11 -> 13; matrix products, arithmetic and copies ran while one was open for 8% -> 9% of each run, Pallas kernels for 5% -> 5%
where the time goes in v12:
time: 183 us; the launch traced here: 182 us
  waiting for transfers between devices  91.4 us (50%)
  starting transfers between devices  38.9 us (21%)
  local copies, waits for them, and re-layouts  29.2 us (16%)
  Pallas kernels  14.9 us (8%)
  other arithmetic  7.78 us (4%)
    ppermute x21, waiting for transfers between devices, shift(): return lax.ppermute(t, axis, [(i, (i + s) % n) for i in range(n)])  59.1 us
    ppermute x21, starting transfers between devices, shift(): return lax.ppermute(t, axis, [(i, (i + s) % n) for i in range(n)])  30.1 us
    all_to_all x1, waiting for transfers between devices, on_device(): part = lax.all_to_all(held + shift(away, 'c', 1), 'y', 0, 0, tiled=True)  24.4 us
    unnamed x50, local copies, waits for them, and re-layouts  14.3 us
    pallas_call x2, Pallas kernels, contract(): pl.pallas_call(make_contract_kernel(kp), in_specs=[pl.BlockSpec(memory_sp...  12.5 us
    all_to_all x1, waiting for transfers between devices, on_device(): part = lax.all_to_all(part, 'y', 0, 0, tiled=True)  7.95 us
    all_to_all x1, starting transfers between devices, on_device(): part = lax.all_to_all(part, 'y', 0, 0, tiled=True)  5.1 us
  transfers between devices with their start and end apart: 23, of which 13 were waited for; matrix products, arithmetic and copies ran while one was open for 9% of the time, Pallas kernels for 5%

profile of v12, /device:TPU:1, one launch (start us, length us, event | category | flops | bytes accessed | tf_op | source)
XLA Modules:
  0.0 182.4 jit_solution(13835274923673814456)
XLA Ops:
  0.0 2.8 %constant_dynamic-slice_fusion = (f32[1,4,256,256]{3,2,1,0:T(8,128)S(1)}, f32[4,256,256]{2,1,0:T(8,128)}) fusion(f32[2,4,256,256]{3,2,1,0:T(8,128)} %param.5, s32[]{:T(128)S(6)} %select_n.122, s32[]{:T(128)S(6)} %select_n.132), kind=kLoop, calls=%fused_computation.35 | loop fusion | bytes 4194312 | tf_op jit(solution)/shard_map/jit(dynamic_index_in_dim)/dynamic_slice | solution.py:138
  2.8 1.4 collective-permute-start.1
  4.5 0.9 fusion
  5.3 1.4 collective-permute-done.1
  6.7 0.2 maximum_select_fusion
  7.1 2.6 %collective-permute-start.4 = (f32[2,256,256]{2,1,0:T(8,128)S(1)}, f32[2,256,256]{2,1,0:T(8,128)S(1)}, u32[]{:S(2)}, u32[]{:S(2)}) collective-permute-start(f32[2,256,256]{2,1,0:T(8,128)S(1)} %get-tuple-element.43), channel_id=1, source_target_pairs={{0,3},{1,0},{2,1},{3,2},{4,7},{5,4},{6,5},{7,6},{8,11},{9,8},{10,9... | collective-permute-start | bytes 1572872 | tf_op jit(solution)/shard_map/ppermute | solution.py:15
  9.8 0.5 collective-permute-start.5
  10.3 0.6 collective-permute-start.6
  11.0 1.7 collective-permute-start.2
  12.7 2.2 %collective-permute-start.3 = (f32[2,256,256]{2,1,0:T(8,128)S(1)}, f32[2,256,256]{2,1,0:T(8,128)S(1)}, u32[]{:S(2)}, u32[]{:S(2)}) collective-permute-start(f32[2,256,256]{2,1,0:T(8,128)S(1)} %dynamic-slice_bitcast_fusion.4.own), channel_id=1, source_target_pairs={{0,96},{32,0},{64,32},{96,64},{1,97},{33,1},{65,33},{97,65},{2,98}... | collective-permute-start | bytes 1572872 | tf_op jit(solution)/shard_map/ppermute | solution.py:15
  14.9 16.9 %collective-permute-done.4 = f32[2,256,256]{2,1,0:T(8,128)S(1)} collective-permute-done((f32[2,256,256]{2,1,0:T(8,128)S(1)}, f32[2,256,256]{2,1,0:T(8,128)S(1)}, u32[]{:S(2)}, u32[]{:S(2)}) %collective-permute-start.4) | collective-permute-done | bytes 524320 | tf_op jit(solution)/shard_map/ppermute | solution.py:15
  31.9 4.5 %collective-permute-done.6 = f32[2,256,256]{2,1,0:T(8,128)S(1)} collective-permute-done((f32[2,256,256]{2,1,0:T(8,128)S(1)}, f32[2,256,256]{2,1,0:T(8,128)S(1)}, u32[]{:S(2)}, u32[]{:S(2)}) %collective-permute-start.6) | collective-permute-done | bytes 524320 | tf_op jit(solution)/shard_map/ppermute | solution.py:15
  36.4 1.0 pad_maximum_fusion.2
  37.5 0.7 copy-done.16
  38.2 0.8 copy-done.13
  39.1 0.2 pad_maximum_fusion
  39.2 1.7 collective-permute-start.11
  40.9 2.2 %collective-permute-start.12 = (f32[4,256,256]{2,1,0:T(8,128)S(1)}, f32[4,256,256]{2,1,0:T(8,128)S(1)}, u32[]{:S(2)}, u32[]{:S(2)}) collective-permute-start(f32[4,256,256]{2,1,0:T(8,128)S(1)} %get-tuple-element.50), channel_id=1, source_target_pairs={{0,96},{32,0},{64,32},{96,64},{1,97},{33,1},{65,33},{97,65},{2,98}... | collective-permute-start | bytes 3145736 | tf_op jit(solution)/shard_map/ppermute | solution.py:15
  43.1 0.8 collective-permute-start.9
  43.9 18.2 %collective-permute-done.7.r_ref = f32[2,520,256]{2,1,0:T(8,128)S(1)} collective-permute-done((f32[2,520,256]{2,1,0:T(8,128)S(1)}, f32[2,520,256]{2,1,0:T(8,128)S(1)}, u32[]{:S(2)}, u32[]{:S(2)}) %collective-permute-start.7) | collective-permute-done | bytes 1064992 | tf_op jit(solution)/shard_map/ppermute | solution.py:15
  62.0 0.8 slice.126
  62.9 0.8 collective-permute-start.8
  63.7 2.4 %collective-permute-done.11.two_r.own_fa = f32[4,256,256]{2,1,0:T(8,128)S(1)} collective-permute-done((f32[4,256,256]{2,1,0:T(8,128)S(1)}, f32[4,256,256]{2,1,0:T(8,128)S(1)}, u32[]{:S(2)}, u32[]{:S(2)}) %collective-permute-start.11) | collective-permute-done | bytes 1048608 | tf_op jit(solution)/shard_map/ppermute | solution.py:15
  66.2 0.3 collective-permute-start.13
  66.5 2.4 %collective-permute-start.14 = (f32[3,256,256]{2,1,0:T(8,128)}, f32[3,256,256]{2,1,0:T(8,128)}, u32[]{:S(2)}, u32[]{:S(2)}) collective-permute-start(f32[3,256,256]{2,1,0:T(8,128)} %get-tuple-element.32.rest), channel_id=1, source_target_pairs={{0,96},{32,0},{64,32},{96,64},{1,97},{33,1},{65,33},{97,65},{2,98}... | collective-permute-start | bytes 2359304 | tf_op jit(solution)/shard_map/ppermute | solution.py:15
  68.9 1.0 copy-done.2
  69.9 0.8 slice.128
  70.8 0.4 collective-permute-start.10
  71.3 1.8 slice.107
  73.1 1.8 slice.108
  74.8 0.6 collective-permute-done.8.fa_ref
  75.4 3.8 %collective-permute-start.16 = (f32[3,128,256]{2,1,0:T(8,128)}, f32[3,128,256]{2,1,0:T(8,128)}, u32[]{:S(2)}, u32[]{:S(2)}) collective-permute-start(f32[3,128,256]{2,1,0:T(8,128)} %slice.108), channel_id=1, source_target_pairs={{0,96},{32,0},{64,32},{96,64},{1,97},{33,1},{65,33},{97,65},{2,98}... | collective-permute-start | bytes 1179656 | tf_op jit(solution)/shard_map/ppermute | solution.py:15
  79.2 0.7 slice_reduce_fusion
  80.2 4.1 %collective-permute-done.10.fb_ref = f32[1,520,256]{2,1,0:T(8,128)} collective-permute-done((f32[1,520,256]{2,1,0:T(8,128)}, f32[1,520,256]{2,1,0:T(8,128)}, u32[]{:S(2)}, u32[]{:S(2)}) %collective-permute-start.10) | collective-permute-done | bytes 532512 | tf_op jit(solution)/shard_map/ppermute | solution.py:15
  84.3 0.7 slice_reduce_fusion.3
  85.2 1.2 copy-done.3
  86.4 2.4 %split_amp.1.a_ref = bf16[4,4,256,768]{3,2,1,0:T(8,128)(2,1)S(1)} custom-call(f32[2,520,256]{2,1,0:T(8,128)S(1)} %maximum_select_fusion.1.a_ref, f32[2,520,256]{2,1,0:T(8,128)S(1)} %collective-permute-done.7.r_ref, f32[2,520,256]{2,1,0:T(8,128)S(1)} %copy-done.3, f32[1,520,256]{2,1,0:T(8,128)S(1)} %collective-permute-done.8.fa_ref, ...), custom_call_target="tpu_custom_call" | custom-call | bytes 10485760 | tf_op jit(solution)/shard_map/split_amp/pallas_call | solution.py:50
  88.9 5.3 %collective-permute-done.15.fa = f32[3,128,256]{2,1,0:T(8,128)} collective-permute-done((f32[3,128,256]{2,1,0:T(8,128)}, f32[3,128,256]{2,1,0:T(8,128)}, u32[]{:S(2)}, u32[]{:S(2)}) %collective-permute-start.15) | collective-permute-done | bytes 393248 | tf_op jit(solution)/shard_map/ppermute | solution.py:15
  94.2 5.5 %contract.2 = (f32[4,2,256,256]{3,2,1,0:T(8,128)S(1)}, f32[4,2,256,256]{3,2,1,0:T(8,128)S(1)}) custom-call(s32[130]{0:T(256)S(1)} %pad_add_fusion.flag_ref, bf16[4,4,256,768]{3,2,1,0:T(8,128)(2,1)S(1)} %split_amp.1.a_ref, f32[2,256,256]{2,1,0:T(8,128)S(1)} %copy-done.5, f32[2,256,256]{2,1,0:T(8,128)S(1)} %copy-done.14, f32[2,256,256]{2,1,0:T(8,128)S(1)} %copy-done.17, ...), custom_call_target="tpu_custom_call" | custom-call | flops 40000000000 | bytes 8388608 | tf_op jit(solution)/shard_map/contract/pallas_call | solution.py:113
  99.7 4.4 %collective-permute-start.17 = (f32[4,2,256,256]{3,2,1,0:T(8,128)S(1)}, f32[4,2,256,256]{3,2,1,0:T(8,128)S(1)}, u32[]{:S(2)}, u32[]{:S(2)}) collective-permute-start(f32[4,2,256,256]{3,2,1,0:T(8,128)S(1)} %get-tuple-element.37), channel_id=1, source_target_pairs={{0,16},{16,0},{1,17},{17,1},{2,18},{18,2},{3,19},{19,3},{4,20},{20... | collective-permute-start | bytes 6291464 | tf_op jit(solution)/shard_map/ppermute | solution.py:15
  104.1 1.8 slice.113
  105.9 1.8 slice.114
  107.6 2.7 %collective-permute-start.19 = (f32[3,128,256]{2,1,0:T(8,128)}, f32[3,128,256]{2,1,0:T(8,128)S(1)}, u32[]{:S(2)}, u32[]{:S(2)}) collective-permute-start(f32[3,128,256]{2,1,0:T(8,128)} %slice.114), channel_id=1, source_target_pairs={{0,96},{32,0},{64,32},{96,64},{1,97},{33,1},{65,33},{97,65},{2,98}... | collective-permute-start | bytes 1179656 | tf_op jit(solution)/shard_map/ppermute | solution.py:15
  110.3 1.6 add.233
  112.0 5.1 %all-to-all-start = ((f32[4,2,256,256]{3,2,1,0:T(8,128)}), f32[4,2,256,256]{3,2,1,0:T(8,128)}, u32[]{:S(2)}, u32[]{:S(2)}) async-start(f32[4,2,256,256]{3,2,1,0:T(8,128)} %add.233), calls=%async_computation | async-start | bytes 4194304 | tf_op jit(solution)/shard_map/all_to_all | solution.py:177
  117.1 0.9 collective-permute-done.18.fa
  118.0 0.8 collective-permute-done.19.fb
  118.8 0.8 copy-done.20
  119.6 2.8 %copy-done.1 = bf16[4,4,256,768]{3,2,1,0:T(8,128)(2,1)S(1)} copy-done((bf16[4,4,256,768]{3,2,1,0:T(8,128)(2,1)S(1)}, bf16[4,4,256,768]{3,2,1,0:T(8,128)(2,1)}, u32[]{:S(2)}) %copy-start.1) | copy-done | bytes 6291480
  122.4 1.2 copy-done.9
  123.6 1.2 copy-done.12
  124.8 1.0 copy-done.18
  125.9 1.0 copy-done.21
  126.9 7.0 %contract.3 = (f32[4,2,256,256]{3,2,1,0:T(8,128)S(1)}, f32[4,2,256,256]{3,2,1,0:T(8,128)S(1)}) custom-call(s32[130]{0:T(256)S(1)} %pad_add_fusion.flag_ref, bf16[4,4,256,768]{3,2,1,0:T(8,128)(2,1)S(1)} %copy-done.1, f32[2,256,256]{2,1,0:T(8,128)S(1)} %copy-done.6, f32[2,256,256]{2,1,0:T(8,128)S(1)} %copy-done.15, f32[2,256,256]{2,1,0:T(8,128)S(1)} %copy-done.18, ...), custom_call_target="tpu_custom_call" | custom-call | flops 40000000000 | bytes 8388608 | tf_op jit(solution)/shard_map/contract/pallas_call | solution.py:113
  133.9 1.3 copy-done.19
  135.2 8.0 %all-to-all-done = f32[4,2,256,256]{3,2,1,0:T(8,128)} async-done(((f32[4,2,256,256]{3,2,1,0:T(8,128)}), f32[4,2,256,256]{3,2,1,0:T(8,128)}, u32[]{:S(2)}, u32[]{:S(2)}) %all-to-all-start) | async-done | bytes 2097184 | tf_op jit(solution)/shard_map/all_to_all | solution.py:177
  143.2 1.5 collective-permute-start.20
  144.7 4.0 %collective-permute-done.20 = f32[4,2,256,256]{3,2,1,0:T(8,128)S(1)} collective-permute-done((f32[4,2,256,256]{3,2,1,0:T(8,128)}, f32[4,2,256,256]{3,2,1,0:T(8,128)S(1)}, u32[]{:S(2)}, u32[]{:S(2)}) %collective-permute-start.20) | collective-permute-done | bytes 2097184 | tf_op jit(solution)/shard_map/ppermute | solution.py:15
  148.7 1.6 add.238
  150.3 3.6 %all-to-all-start.1 = ((f32[4,2,256,256]{3,2,1,0:T(8,128)}), f32[4,2,256,256]{3,2,1,0:T(8,128)S(1)}, u32[]{:S(2)}, u32[]{:S(2)}) async-start(f32[4,2,256,256]{3,2,1,0:T(8,128)} %add.238), calls=%async_computation.1 | async-start | bytes 4194304 | tf_op jit(solution)/shard_map/all_to_all | solution.py:182
  153.9 1.7 fusion.2
  155.6 24.4 %all-to-all-done.1 = f32[4,2,256,256]{3,2,1,0:T(8,128)S(1)} async-done(((f32[4,2,256,256]{3,2,1,0:T(8,128)}), f32[4,2,256,256]{3,2,1,0:T(8,128)S(1)}, u32[]{:S(2)}, u32[]{:S(2)}) %all-to-all-start.1) | async-done | bytes 2097184 | tf_op jit(solution)/shard_map/all_to_all | solution.py:182
  180.1 1.1 copy-done.22
  181.4 1.0 copy.8
  (77 shorter events, 1.7 us)
Async XLA Ops:
  0.0 4.2 %copy-start.24 = (s32[1,1,3,32]{3,1,2,0:T(1,128)S(1)}, s32[1,1,3,32]{3,1,2,0:T(1,128)}, u32[]{:S(2)}) copy-start(s32[1,1,3,32]{3,1,2,0:T(1,128)} %param.7) | copy-start | bytes 1156
  0.0 4.4 %copy-start.23 = (f32[2,2,256,256]{3,2,1,0:T(8,128)S(1)}, f32[2,2,256,256]{3,2,1,0:T(8,128)}, u32[]{:S(2)}) copy-start(f32[2,2,256,256]{3,2,1,0:T(8,128)} %param.4) | copy-start | bytes 3145732
  2.8 3.9 %collective-permute-start.1 = (f32[4,256,256]{2,1,0:T(8,128)}, f32[4,256,256]{2,1,0:T(8,128)S(1)}, u32[]{:S(2)}, u32[]{:S(2)}) collective-permute-start(f32[4,256,256]{2,1,0:T(8,128)} %get-tuple-element.47), channel_id=1, source_target_pairs={{0,16},{16,0},{1,17},{17,1},{2,18},{18,2},{3,19},{19,3},{4,20},{20... | collective-permute-start | bytes 3145736 | tf_op jit(solution)/shard_map/ppermute | solution.py:15
  5.3 5.5 %collective-permute-start = (f32[520,256]{1,0:T(8,128)}, f32[520,256]{1,0:T(8,128)S(1)}, u32[]{:S(2)}, u32[]{:S(2)}) collective-permute-start(f32[520,256]{1,0:T(8,128)} %get-tuple-element.59), channel_id=1, source_target_pairs={{0,16},{16,0},{1,17},{17,1},{2,18},{18,2},{3,19},{19,3},{4,20},{20... | collective-permute-start | bytes 1597448 | tf_op jit(solution)/shard_map/ppermute | solution.py:15
  7.0 5.7 %copy-start.4 = (f32[2,256,256]{2,1,0:T(8,128)}, f32[2,256,256]{2,1,0:T(8,128)S(1)}, u32[]{:S(2)}) copy-start(f32[2,256,256]{2,1,0:T(8,128)S(1)} %dynamic-slice_bitcast_fusion.4.own) | copy-start | bytes 1572868
  7.1 24.7 %collective-permute-start.4 = (f32[2,256,256]{2,1,0:T(8,128)S(1)}, f32[2,256,256]{2,1,0:T(8,128)S(1)}, u32[]{:S(2)}, u32[]{:S(2)}) collective-permute-start(f32[2,256,256]{2,1,0:T(8,128)S(1)} %get-tuple-element.43), channel_id=1, source_target_pairs={{0,3},{1,0},{2,1},{3,2},{4,7},{5,4},{6,5},{7,6},{8,11},{9,8},{10,9... | collective-permute-start | bytes 1572872 | tf_op jit(solution)/shard_map/ppermute | solution.py:15
  9.8 22.1 %collective-permute-start.5 = (f32[2,256,256]{2,1,0:T(8,128)S(1)}, f32[2,256,256]{2,1,0:T(8,128)S(1)}, u32[]{:S(2)}, u32[]{:S(2)}) collective-permute-start(f32[2,256,256]{2,1,0:T(8,128)S(1)} %get-tuple-element.45), channel_id=1, source_target_pairs={{0,2},{1,3},{2,0},{3,1},{4,6},{5,7},{6,4},{7,5},{8,10},{9,11},{10,... | collective-permute-start | bytes 1572872 | tf_op jit(solution)/shard_map/ppermute | solution.py:15
  10.3 26.1 %collective-permute-start.6 = (f32[2,256,256]{2,1,0:T(8,128)S(1)}, f32[2,256,256]{2,1,0:T(8,128)S(1)}, u32[]{:S(2)}, u32[]{:S(2)}) collective-permute-start(f32[2,256,256]{2,1,0:T(8,128)S(1)} %get-tuple-element.44), channel_id=1, source_target_pairs={{0,1},{1,2},{2,3},{3,0},{4,5},{5,6},{6,7},{7,4},{8,9},{9,10},{10,1... | collective-permute-start | bytes 1572872 | tf_op jit(solution)/shard_map/ppermute | solution.py:15
  11.0 26.4 %collective-permute-start.2 = (f32[2,256,256]{2,1,0:T(8,128)S(1)}, f32[2,256,256]{2,1,0:T(8,128)S(1)}, u32[]{:S(2)}, u32[]{:S(2)}) collective-permute-start(f32[2,256,256]{2,1,0:T(8,128)S(1)} %dynamic-slice_bitcast_fusion.4.own), channel_id=1, source_target_pairs={{0,32},{32,64},{64,96},{96,0},{1,33},{33,65},{65,97},{97,1},{2,34}... | collective-permute-start | bytes 1572872 | tf_op jit(solution)/shard_map/ppermute | solution.py:15
  12.7 24.7 %collective-permute-start.3 = (f32[2,256,256]{2,1,0:T(8,128)S(1)}, f32[2,256,256]{2,1,0:T(8,128)S(1)}, u32[]{:S(2)}, u32[]{:S(2)}) collective-permute-start(f32[2,256,256]{2,1,0:T(8,128)S(1)} %dynamic-slice_bitcast_fusion.4.own), channel_id=1, source_target_pairs={{0,96},{32,0},{64,32},{96,64},{1,97},{33,1},{65,33},{97,65},{2,98}... | collective-permute-start | bytes 1572872 | tf_op jit(solution)/shard_map/ppermute | solution.py:15
  37.4 0.8 copy-start.16
  37.4 24.7 %collective-permute-start.7 = (f32[2,520,256]{2,1,0:T(8,128)S(1)}, f32[2,520,256]{2,1,0:T(8,128)S(1)}, u32[]{:S(2)}, u32[]{:S(2)}) collective-permute-start(f32[2,520,256]{2,1,0:T(8,128)S(1)} %maximum_select_fusion.1.a_ref), channel_id=1, source_target_pairs={{0,3},{1,0},{2,1},{3,2},{4,7},{5,4},{6,5},{7,6},{8,11},{9,8},{10,9... | collective-permute-start | bytes 3194888 | tf_op jit(solution)/shard_map/ppermute | solution.py:15
  38.2 0.8 copy-start.13
  39.2 26.9 %collective-permute-start.11 = (f32[4,256,256]{2,1,0:T(8,128)S(1)}, f32[4,256,256]{2,1,0:T(8,128)S(1)}, u32[]{:S(2)}, u32[]{:S(2)}) collective-permute-start(f32[4,256,256]{2,1,0:T(8,128)S(1)} %get-tuple-element.51), channel_id=1, source_target_pairs={{0,32},{32,64},{64,96},{96,0},{1,33},{33,65},{65,97},{97,1},{2,34}... | collective-permute-start | bytes 3145736 | tf_op jit(solution)/shard_map/ppermute | solution.py:15
  40.9 25.2 %collective-permute-start.12 = (f32[4,256,256]{2,1,0:T(8,128)S(1)}, f32[4,256,256]{2,1,0:T(8,128)S(1)}, u32[]{:S(2)}, u32[]{:S(2)}) collective-permute-start(f32[4,256,256]{2,1,0:T(8,128)S(1)} %get-tuple-element.50), channel_id=1, source_target_pairs={{0,96},{32,0},{64,32},{96,64},{1,97},{33,1},{65,33},{97,65},{2,98}... | collective-permute-start | bytes 3145736 | tf_op jit(solution)/shard_map/ppermute | solution.py:15
  43.1 25.8 %collective-permute-start.9 = (f32[2,520,256]{2,1,0:T(8,128)S(1)}, f32[2,520,256]{2,1,0:T(8,128)S(1)}, u32[]{:S(2)}, u32[]{:S(2)}) collective-permute-start(f32[2,520,256]{2,1,0:T(8,128)S(1)} %maximum_select_fusion.1.a_ref), channel_id=1, source_target_pairs={{0,1},{1,2},{2,3},{3,0},{4,5},{5,6},{6,7},{7,4},{8,9},{9,10},{10,1... | collective-permute-start | bytes 3194888 | tf_op jit(solution)/shard_map/ppermute | solution.py:15
  62.9 12.6 %collective-permute-start.8 = (f32[1,520,256]{2,1,0:T(8,128)}, f32[1,520,256]{2,1,0:T(8,128)S(1)}, u32[]{:S(2)}, u32[]{:S(2)}) collective-permute-start(f32[1,520,256]{2,1,0:T(8,128)} %slice.126), channel_id=1, source_target_pairs={{0,3},{1,0},{2,1},{3,2},{4,7},{5,4},{6,5},{7,6},{8,11},{9,8},{10,9... | collective-permute-start | bytes 1597448 | tf_op jit(solution)/shard_map/ppermute | solution.py:15
  66.2 4.6 %copy-start.7 = (f32[4,256,256]{2,1,0:T(8,128)}, f32[4,256,256]{2,1,0:T(8,128)S(1)}, u32[]{:S(2)}) copy-start(f32[4,256,256]{2,1,0:T(8,128)S(1)} %collective-permute-done.11.two_r.own_fa) | copy-start | bytes 3145732
  66.2 4.6 %copy-start.10 = (f32[4,256,256]{2,1,0:T(8,128)}, f32[4,256,256]{2,1,0:T(8,128)S(1)}, u32[]{:S(2)}) copy-start(f32[4,256,256]{2,1,0:T(8,128)S(1)} %collective-permute-done.12.two_l.own_fb) | copy-start | bytes 3145732
  66.2 22.8 %collective-permute-start.13 = (f32[3,256,256]{2,1,0:T(8,128)}, f32[3,256,256]{2,1,0:T(8,128)}, u32[]{:S(2)}, u32[]{:S(2)}) collective-permute-start(f32[3,256,256]{2,1,0:T(8,128)} %get-tuple-element.32.rest), channel_id=1, source_target_pairs={{0,32},{32,64},{64,96},{96,0},{1,33},{33,65},{65,97},{97,1},{2,34}... | collective-permute-start | bytes 2359304 | tf_op jit(solution)/shard_map/ppermute | solution.py:15
  66.5 22.4 %collective-permute-start.14 = (f32[3,256,256]{2,1,0:T(8,128)}, f32[3,256,256]{2,1,0:T(8,128)}, u32[]{:S(2)}, u32[]{:S(2)}) collective-permute-start(f32[3,256,256]{2,1,0:T(8,128)} %get-tuple-element.32.rest), channel_id=1, source_target_pairs={{0,96},{32,0},{64,32},{96,64},{1,97},{33,1},{65,33},{97,65},{2,98}... | collective-permute-start | bytes 2359304 | tf_op jit(solution)/shard_map/ppermute | solution.py:15
  68.9 1.0 copy-start.2
  70.8 13.5 %collective-permute-start.10 = (f32[1,520,256]{2,1,0:T(8,128)}, f32[1,520,256]{2,1,0:T(8,128)}, u32[]{:S(2)}, u32[]{:S(2)}) collective-permute-start(f32[1,520,256]{2,1,0:T(8,128)} %slice.128), channel_id=1, source_target_pairs={{0,1},{1,2},{2,3},{3,0},{4,5},{5,6},{6,7},{7,4},{8,9},{9,10},{10,1... | collective-permute-start | bytes 1597448 | tf_op jit(solution)/shard_map/ppermute | solution.py:15
  73.0 21.1 %collective-permute-start.15 = (f32[3,128,256]{2,1,0:T(8,128)}, f32[3,128,256]{2,1,0:T(8,128)}, u32[]{:S(2)}, u32[]{:S(2)}) collective-permute-start(f32[3,128,256]{2,1,0:T(8,128)} %slice.107), channel_id=1, source_target_pairs={{0,32},{32,64},{64,96},{96,0},{1,33},{33,65},{65,97},{97,1},{2,34}... | collective-permute-start | bytes 1179656 | tf_op jit(solution)/shard_map/ppermute | solution.py:15
  75.4 18.8 %collective-permute-start.16 = (f32[3,128,256]{2,1,0:T(8,128)}, f32[3,128,256]{2,1,0:T(8,128)}, u32[]{:S(2)}, u32[]{:S(2)}) collective-permute-start(f32[3,128,256]{2,1,0:T(8,128)} %slice.108), channel_id=1, source_target_pairs={{0,96},{32,0},{64,32},{96,64},{1,97},{33,1},{65,33},{97,65},{2,98}... | collective-permute-start | bytes 1179656 | tf_op jit(solution)/shard_map/ppermute | solution.py:15
  85.2 1.2 copy-start.3
  86.4 7.8 %copy-start.5 = (f32[2,256,256]{2,1,0:T(8,128)S(1)}, f32[2,256,256]{2,1,0:T(8,128)}, u32[]{:S(2)}) copy-start(f32[2,256,256]{2,1,0:T(8,128)} %copy-done.4) | copy-start | bytes 1572868
  86.4 7.8 %copy-start.8 = (f32[4,256,256]{2,1,0:T(8,128)S(1)}, f32[4,256,256]{2,1,0:T(8,128)}, u32[]{:S(2)}) copy-start(f32[4,256,256]{2,1,0:T(8,128)} %copy-done.7) | copy-start | bytes 3145732
  86.4 7.8 %copy-start.11 = (f32[4,256,256]{2,1,0:T(8,128)S(1)}, f32[4,256,256]{2,1,0:T(8,128)}, u32[]{:S(2)}) copy-start(f32[4,256,256]{2,1,0:T(8,128)} %copy-done.10) | copy-start | bytes 3145732
  86.4 7.8 %copy-start.14 = (f32[2,256,256]{2,1,0:T(8,128)S(1)}, f32[2,256,256]{2,1,0:T(8,128)}, u32[]{:S(2)}) copy-start(f32[2,256,256]{2,1,0:T(8,128)} %copy-done.13) | copy-start | bytes 1572868
  86.4 7.8 %copy-start.17 = (f32[2,256,256]{2,1,0:T(8,128)S(1)}, f32[2,256,256]{2,1,0:T(8,128)}, u32[]{:S(2)}) copy-start(f32[2,256,256]{2,1,0:T(8,128)} %copy-done.16) | copy-start | bytes 1572868
  88.8 10.9 %copy-start = (bf16[4,4,256,768]{3,2,1,0:T(8,128)(2,1)}, bf16[4,4,256,768]{3,2,1,0:T(8,128)(2,1)S(1)}, u32[]{:S(2)}) copy-start(bf16[4,4,256,768]{3,2,1,0:T(8,128)(2,1)S(1)} %split_amp.1.a_ref) | copy-start | bytes 18874372
  99.7 10.6 %collective-permute-start.17 = (f32[4,2,256,256]{3,2,1,0:T(8,128)S(1)}, f32[4,2,256,256]{3,2,1,0:T(8,128)S(1)}, u32[]{:S(2)}, u32[]{:S(2)}) collective-permute-start(f32[4,2,256,256]{3,2,1,0:T(8,128)S(1)} %get-tuple-element.37), channel_id=1, source_target_pairs={{0,16},{16,0},{1,17},{17,1},{2,18},{18,2},{3,19},{19,3},{4,20},{20... | collective-permute-start | bytes 6291464 | tf_op jit(solution)/shard_map/ppermute | solution.py:15
  105.9 12.2 %collective-permute-start.18 = (f32[3,128,256]{2,1,0:T(8,128)}, f32[3,128,256]{2,1,0:T(8,128)S(1)}, u32[]{:S(2)}, u32[]{:S(2)}) collective-permute-start(f32[3,128,256]{2,1,0:T(8,128)} %slice.113), channel_id=1, source_target_pairs={{0,32},{32,64},{64,96},{96,0},{1,33},{33,65},{65,97},{97,1},{2,34}... | collective-permute-start | bytes 1179656 | tf_op jit(solution)/shard_map/ppermute | solution.py:15
  107.6 11.2 %collective-permute-start.19 = (f32[3,128,256]{2,1,0:T(8,128)}, f32[3,128,256]{2,1,0:T(8,128)S(1)}, u32[]{:S(2)}, u32[]{:S(2)}) collective-permute-start(f32[3,128,256]{2,1,0:T(8,128)} %slice.114), channel_id=1, source_target_pairs={{0,96},{32,0},{64,32},{96,64},{1,97},{33,1},{65,33},{97,65},{2,98}... | collective-permute-start | bytes 1179656 | tf_op jit(solution)/shard_map/ppermute | solution.py:15
  112.0 7.6 %copy-start.6 = (f32[2,256,256]{2,1,0:T(8,128)S(1)}, f32[2,256,256]{2,1,0:T(8,128)}, u32[]{:S(2)}) copy-start(f32[2,256,256]{2,1,0:T(8,128)} %copy-done.4) | copy-start | bytes 1572868
  112.0 7.6 %copy-start.15 = (f32[2,256,256]{2,1,0:T(8,128)S(1)}, f32[2,256,256]{2,1,0:T(8,128)}, u32[]{:S(2)}) copy-start(f32[2,256,256]{2,1,0:T(8,128)} %copy-done.13) | copy-start | bytes 1572868
  112.0 31.2 %all-to-all-start = ((f32[4,2,256,256]{3,2,1,0:T(8,128)}), f32[4,2,256,256]{3,2,1,0:T(8,128)}, u32[]{:S(2)}, u32[]{:S(2)}) async-start(f32[4,2,256,256]{3,2,1,0:T(8,128)} %add.233), calls=%async_computation | async-start | bytes 4194304 | tf_op jit(solution)/shard_map/all_to_all | solution.py:177
  118.8 0.8 copy-start.20
  119.6 2.8 %copy-start.1 = (bf16[4,4,256,768]{3,2,1,0:T(8,128)(2,1)S(1)}, bf16[4,4,256,768]{3,2,1,0:T(8,128)(2,1)}, u32[]{:S(2)}) copy-start(bf16[4,4,256,768]{3,2,1,0:T(8,128)(2,1)} %copy-done) | copy-start | bytes 18874372
  122.4 1.2 copy-start.9
  123.6 1.2 copy-start.12
  124.8 1.0 copy-start.18
  125.9 1.0 copy-start.21
  133.9 1.4 copy-start.19
  143.2 5.5 %collective-permute-start.20 = (f32[4,2,256,256]{3,2,1,0:T(8,128)}, f32[4,2,256,256]{3,2,1,0:T(8,128)S(1)}, u32[]{:S(2)}, u32[]{:S(2)}) collective-permute-start(f32[4,2,256,256]{3,2,1,0:T(8,128)} %copy-done.19), channel_id=1, source_target_pairs={{0,16},{16,0},{1,17},{17,1},{2,18},{18,2},{3,19},{19,3},{4,20},{20... | collective-permute-start | bytes 6291464 | tf_op jit(solution)/shard_map/ppermute | solution.py:15
  150.3 29.7 %all-to-all-start.1 = ((f32[4,2,256,256]{3,2,1,0:T(8,128)}), f32[4,2,256,256]{3,2,1,0:T(8,128)S(1)}, u32[]{:S(2)}, u32[]{:S(2)}) async-start(f32[4,2,256,256]{3,2,1,0:T(8,128)} %add.238), calls=%async_computation.1 | async-start | bytes 4194304 | tf_op jit(solution)/shard_map/all_to_all | solution.py:182
  180.0 1.2 copy-start.22

commit v13 on v11

--- a/solution.py
+++ b/solution.py
@@ -168,6 +168,7 @@
     two_r, two_l, rest[1] = lax.optimization_barrier((two_r, two_l, rest[1]))
     far0 = shift(two_r[:3, :h], "z", 1), shift(two_l[:3, h:], "z", -1)
     rest1_r, rest1_l = shift(rest[1], "z", 1), shift(rest[1], "z", -1)
+    a3, rest1_r, rest1_l = lax.optimization_barrier((a3, rest1_r, rest1_l))
     far1 = shift(rest1_r[:, :h], "z", 1), shift(rest1_l[:, h:], "z", -1)
 
     pieces = own, own_r, own_l

time: 187 us -> 183 us (0.979)
  starting transfers between devices: 38 us -> 34.1 us
  Pallas kernels: 21.4 us -> 18.5 us
    pallas_call x2, Pallas kernels: 19.1 us -> 16.1 us  [contract(): pl.pallas_call(make_contract_kernel(kp), in_specs=[pl.BlockSpec(memory_sp...]
    ppermute x21, starting transfers between devices: 27.8 us -> 25.4 us  [shift(): return lax.ppermute(t, axis, [(i, (i + s) % n) for i in range(n)])]
    slice x2, local copies, waits for them, and re-layouts: 0.05 us -> 2.04 us  [on_device(): far1 = (shift(rest1_r[:, :h], 'z', 1), shift(rest1_l[:, h:], 'z', -1))]
    unnamed x44 -> x46, local copies, waits for them, and re-layouts: 12.6 us -> 12.5 us
  transfers between devices with their start and end apart: 23 -> 23, of which waited for: 11 -> 13; matrix products, arithmetic and copies ran while one was open for 8% -> 8% of each run, Pallas kernels for 5% -> 6%
where the time goes in v13:
time: 183 us; the launch traced here: 182 us
  waiting for transfers between devices  95 us (52%)
  starting transfers between devices  34.1 us (19%)
  local copies, waits for them, and re-layouts  25.9 us (14%)
  Pallas kernels  18.5 us (10%)
  other arithmetic  7.81 us (4%)
    ppermute x21, waiting for transfers between devices, shift(): return lax.ppermute(t, axis, [(i, (i + s) % n) for i in range(n)])  70.9 us
    ppermute x21, starting transfers between devices, shift(): return lax.ppermute(t, axis, [(i, (i + s) % n) for i in range(n)])  25.4 us
    all_to_all x1, waiting for transfers between devices, on_device(): part = lax.all_to_all(held + shift(away, 'c', 1), 'y', 0, 0, tiled=True)  24.1 us
    pallas_call x2, Pallas kernels, contract(): pl.pallas_call(make_contract_kernel(kp), in_specs=[pl.BlockSpec(memory_sp...  16.1 us
    unnamed x46, local copies, waits for them, and re-layouts  12.5 us
    all_to_all x1, starting transfers between devices, on_device(): part = lax.all_to_all(part, 'y', 0, 0, tiled=True)  4.84 us
    all_to_all x1, starting transfers between devices, on_device(): part = lax.all_to_all(held + shift(away, 'c', 1), 'y', 0, 0, tiled=True)  3.88 us
  transfers between devices with their start and end apart: 23, of which 13 were waited for; matrix products, arithmetic and copies ran while one was open for 8% of the time, Pallas kernels for 6%

profile of v13, /device:TPU:1, one launch (start us, length us, event | category | flops | bytes accessed | tf_op | source)
XLA Modules:
  0.0 181.6 jit_solution(3590602638326674216)
XLA Ops:
  0.0 2.8 %constant_dynamic-slice_fusion = (f32[1,4,256,256]{3,2,1,0:T(8,128)S(1)}, f32[4,256,256]{2,1,0:T(8,128)}) fusion(f32[2,4,256,256]{3,2,1,0:T(8,128)} %param.5, s32[]{:T(128)S(6)} %select_n.122, s32[]{:T(128)S(6)} %select_n.132), kind=kLoop, calls=%fused_computation.35 | loop fusion | bytes 4194312 | tf_op jit(solution)/shard_map/jit(dynamic_index_in_dim)/dynamic_slice | solution.py:138
  2.8 1.4 collective-permute-start.1
  4.5 0.9 fusion
  5.3 1.4 collective-permute-done.1
  6.7 0.2 maximum_select_fusion
  7.1 2.6 %collective-permute-start.4 = (f32[2,256,256]{2,1,0:T(8,128)S(1)}, f32[2,256,256]{2,1,0:T(8,128)S(1)}, u32[]{:S(2)}, u32[]{:S(2)}) collective-permute-start(f32[2,256,256]{2,1,0:T(8,128)S(1)} %get-tuple-element.43), channel_id=1, source_target_pairs={{0,3},{1,0},{2,1},{3,2},{4,7},{5,4},{6,5},{7,6},{8,11},{9,8},{10,9... | collective-permute-start | bytes 1572872 | tf_op jit(solution)/shard_map/ppermute | solution.py:15
  9.8 0.5 collective-permute-start.5
  10.3 0.6 collective-permute-start.6
  11.0 1.7 collective-permute-start.2
  12.7 2.2 %collective-permute-start.3 = (f32[2,256,256]{2,1,0:T(8,128)S(1)}, f32[2,256,256]{2,1,0:T(8,128)S(1)}, u32[]{:S(2)}, u32[]{:S(2)}) collective-permute-start(f32[2,256,256]{2,1,0:T(8,128)S(1)} %dynamic-slice_bitcast_fusion.4.own), channel_id=1, source_target_pairs={{0,96},{32,0},{64,32},{96,64},{1,97},{33,1},{65,33},{97,65},{2,98}... | collective-permute-start | bytes 1572872 | tf_op jit(solution)/shard_map/ppermute | solution.py:15
  14.9 16.9 %collective-permute-done.4 = f32[2,256,256]{2,1,0:T(8,128)S(1)} collective-permute-done((f32[2,256,256]{2,1,0:T(8,128)S(1)}, f32[2,256,256]{2,1,0:T(8,128)S(1)}, u32[]{:S(2)}, u32[]{:S(2)}) %collective-permute-start.4) | collective-permute-done | bytes 524320 | tf_op jit(solution)/shard_map/ppermute | solution.py:15
  31.9 4.5 %collective-permute-done.6 = f32[2,256,256]{2,1,0:T(8,128)S(1)} collective-permute-done((f32[2,256,256]{2,1,0:T(8,128)S(1)}, f32[2,256,256]{2,1,0:T(8,128)S(1)}, u32[]{:S(2)}, u32[]{:S(2)}) %collective-permute-start.6) | collective-permute-done | bytes 524320 | tf_op jit(solution)/shard_map/ppermute | solution.py:15
  36.4 1.0 pad_maximum_fusion.2
  37.5 0.7 copy-done.16
  38.2 0.8 copy-done.13
  39.0 0.2 pad_maximum_fusion
  39.2 1.7 collective-permute-start.11
  40.9 2.2 %collective-permute-start.12 = (f32[4,256,256]{2,1,0:T(8,128)S(1)}, f32[4,256,256]{2,1,0:T(8,128)S(1)}, u32[]{:S(2)}, u32[]{:S(2)}) collective-permute-start(f32[4,256,256]{2,1,0:T(8,128)S(1)} %get-tuple-element.50), channel_id=1, source_target_pairs={{0,96},{32,0},{64,32},{96,64},{1,97},{33,1},{65,33},{97,65},{2,98}... | collective-permute-start | bytes 3145736 | tf_op jit(solution)/shard_map/ppermute | solution.py:15
  43.1 0.8 collective-permute-start.9
  43.9 18.2 %collective-permute-done.7.r_ref = f32[2,520,256]{2,1,0:T(8,128)S(1)} collective-permute-done((f32[2,520,256]{2,1,0:T(8,128)S(1)}, f32[2,520,256]{2,1,0:T(8,128)S(1)}, u32[]{:S(2)}, u32[]{:S(2)}) %collective-permute-start.7) | collective-permute-done | bytes 1064992 | tf_op jit(solution)/shard_map/ppermute | solution.py:15
  62.1 0.8 slice.126
  62.9 0.8 collective-permute-start.8
  63.7 2.4 %collective-permute-done.11.two_r.own_fa = f32[4,256,256]{2,1,0:T(8,128)S(1)} collective-permute-done((f32[4,256,256]{2,1,0:T(8,128)S(1)}, f32[4,256,256]{2,1,0:T(8,128)S(1)}, u32[]{:S(2)}, u32[]{:S(2)}) %collective-permute-start.11) | collective-permute-done | bytes 1048608 | tf_op jit(solution)/shard_map/ppermute | solution.py:15
  66.2 0.3 collective-permute-start.13
  66.5 2.4 %collective-permute-start.14 = (f32[3,256,256]{2,1,0:T(8,128)}, f32[3,256,256]{2,1,0:T(8,128)}, u32[]{:S(2)}, u32[]{:S(2)}) collective-permute-start(f32[3,256,256]{2,1,0:T(8,128)} %get-tuple-element.32.rest), channel_id=1, source_target_pairs={{0,96},{32,0},{64,32},{96,64},{1,97},{33,1},{65,33},{97,65},{2,98}... | collective-permute-start | bytes 2359304 | tf_op jit(solution)/shard_map/ppermute | solution.py:15
  68.9 1.0 copy-done.2
  69.9 0.8 slice.128
  70.7 0.4 collective-permute-start.10
  71.3 1.8 slice.107
  73.1 1.8 slice.108
  74.9 0.6 collective-permute-done.8.fa_ref
  75.5 3.8 %collective-permute-start.16 = (f32[3,128,256]{2,1,0:T(8,128)}, f32[3,128,256]{2,1,0:T(8,128)}, u32[]{:S(2)}, u32[]{:S(2)}) collective-permute-start(f32[3,128,256]{2,1,0:T(8,128)} %slice.108), channel_id=1, source_target_pairs={{0,96},{32,0},{64,32},{96,64},{1,97},{33,1},{65,33},{97,65},{2,98}... | collective-permute-start | bytes 1179656 | tf_op jit(solution)/shard_map/ppermute | solution.py:15
  79.2 0.7 slice_reduce_fusion
  80.2 4.1 %collective-permute-done.10.fb_ref = f32[1,520,256]{2,1,0:T(8,128)} collective-permute-done((f32[1,520,256]{2,1,0:T(8,128)}, f32[1,520,256]{2,1,0:T(8,128)}, u32[]{:S(2)}, u32[]{:S(2)}) %collective-permute-start.10) | collective-permute-done | bytes 532512 | tf_op jit(solution)/shard_map/ppermute | solution.py:15
  84.3 0.7 slice_reduce_fusion.3
  85.2 1.2 copy-done.3
  86.4 2.4 %split_amp.1.a_ref = bf16[4,4,256,768]{3,2,1,0:T(8,128)(2,1)S(1)} custom-call(f32[2,520,256]{2,1,0:T(8,128)S(1)} %maximum_select_fusion.1.a_ref, f32[2,520,256]{2,1,0:T(8,128)S(1)} %collective-permute-done.7.r_ref, f32[2,520,256]{2,1,0:T(8,128)S(1)} %copy-done.3, f32[1,520,256]{2,1,0:T(8,128)S(1)} %collective-permute-done.8.fa_ref, ...), custom_call_target="tpu_custom_call" | custom-call | bytes 10485760 | tf_op jit(solution)/shard_map/split_amp/pallas_call | solution.py:50
  88.9 5.3 %collective-permute-done.15.fa = f32[3,128,256]{2,1,0:T(8,128)} collective-permute-done((f32[3,128,256]{2,1,0:T(8,128)}, f32[3,128,256]{2,1,0:T(8,128)}, u32[]{:S(2)}, u32[]{:S(2)}) %collective-permute-start.15) | collective-permute-done | bytes 393248 | tf_op jit(solution)/shard_map/ppermute | solution.py:15
  94.2 7.3 %contract.2 = (f32[4,2,256,256]{3,2,1,0:T(8,128)S(1)}, f32[4,2,256,256]{3,2,1,0:T(8,128)S(1)}) custom-call(s32[130]{0:T(256)S(1)} %pad_add_fusion.flag_ref, bf16[4,4,256,768]{3,2,1,0:T(8,128)(2,1)S(1)} %split_amp.1.a_ref, f32[2,256,256]{2,1,0:T(8,128)S(1)} %copy-done.5, f32[2,256,256]{2,1,0:T(8,128)S(1)} %copy-done.14, f32[2,256,256]{2,1,0:T(8,128)S(1)} %copy-done.17, ...), custom_call_target="tpu_custom_call" | custom-call | flops 8000000000 | bytes 8388608 | tf_op jit(solution)/shard_map/contract/pallas_call | solution.py:113
  101.5 0.4 collective-permute-start.17
  102.0 3.8 %collective-permute-done.17 = f32[4,2,256,256]{3,2,1,0:T(8,128)S(1)} collective-permute-done((f32[4,2,256,256]{3,2,1,0:T(8,128)S(1)}, f32[4,2,256,256]{3,2,1,0:T(8,128)S(1)}, u32[]{:S(2)}, u32[]{:S(2)}) %collective-permute-start.17) | collective-permute-done | bytes 2097184 | tf_op jit(solution)/shard_map/ppermute | solution.py:15
  105.8 1.7 add.233
  107.4 4.8 %all-to-all-start = ((f32[4,2,256,256]{3,2,1,0:T(8,128)}), f32[4,2,256,256]{3,2,1,0:T(8,128)}, u32[]{:S(2)}, u32[]{:S(2)}) async-start(f32[4,2,256,256]{3,2,1,0:T(8,128)} %add.233), calls=%async_computation | async-start | bytes 4194304 | tf_op jit(solution)/shard_map/all_to_all | solution.py:177
  112.3 1.0 slice.113
  113.3 1.2 collective-permute-start.18
  114.5 1.0 slice.114
  115.5 2.2 %collective-permute-start.19 = (f32[3,128,256]{2,1,0:T(8,128)S(1)}, f32[3,128,256]{2,1,0:T(8,128)S(1)}, u32[]{:S(2)}, u32[]{:S(2)}) collective-permute-start(f32[3,128,256]{2,1,0:T(8,128)S(1)} %slice.114), channel_id=1, source_target_pairs={{0,96},{32,0},{64,32},{96,64},{1,97},{33,1},{65,33},{97,65},{2,98}... | collective-permute-start | bytes 1179656 | tf_op jit(solution)/shard_map/ppermute | solution.py:15
  117.7 7.9 %collective-permute-done.18.fa = f32[3,128,256]{2,1,0:T(8,128)S(1)} collective-permute-done((f32[3,128,256]{2,1,0:T(8,128)S(1)}, f32[3,128,256]{2,1,0:T(8,128)S(1)}, u32[]{:S(2)}, u32[]{:S(2)}) %collective-permute-start.18) | collective-permute-done | bytes 393248 | tf_op jit(solution)/shard_map/ppermute | solution.py:15
  125.5 1.5 collective-permute-done.19.fb
  127.1 2.8 %copy-done.1 = bf16[4,4,256,768]{3,2,1,0:T(8,128)(2,1)S(1)} copy-done((bf16[4,4,256,768]{3,2,1,0:T(8,128)(2,1)S(1)}, bf16[4,4,256,768]{3,2,1,0:T(8,128)(2,1)}, u32[]{:S(2)}) %copy-start.1) | copy-done | bytes 6291480
  129.9 1.2 copy-done.9
  131.1 1.2 copy-done.12
  132.3 1.0 copy-done.18
  133.3 8.8 %contract.3 = (f32[4,2,256,256]{3,2,1,0:T(8,128)S(1)}, f32[4,2,256,256]{3,2,1,0:T(8,128)S(1)}) custom-call(s32[130]{0:T(256)S(1)} %pad_add_fusion.flag_ref, bf16[4,4,256,768]{3,2,1,0:T(8,128)(2,1)S(1)} %copy-done.1, f32[2,256,256]{2,1,0:T(8,128)S(1)} %copy-done.6, f32[2,256,256]{2,1,0:T(8,128)S(1)} %copy-done.15, f32[2,256,256]{2,1,0:T(8,128)S(1)} %copy-done.18, ...), custom_call_target="tpu_custom_call" | custom-call | flops 8000000000 | bytes 8388608 | tf_op jit(solution)/shard_map/contract/pallas_call | solution.py:113
  142.2 1.4 copy-done.19
  143.5 4.4 %collective-permute-done.20 = f32[4,2,256,256]{3,2,1,0:T(8,128)S(1)} collective-permute-done((f32[4,2,256,256]{3,2,1,0:T(8,128)}, f32[4,2,256,256]{3,2,1,0:T(8,128)S(1)}, u32[]{:S(2)}, u32[]{:S(2)}) %collective-permute-start.20) | collective-permute-done | bytes 2097184 | tf_op jit(solution)/shard_map/ppermute | solution.py:15
  147.9 1.6 add.238
  149.6 3.9 %all-to-all-start.1 = ((f32[4,2,256,256]{3,2,1,0:T(8,128)}), f32[4,2,256,256]{3,2,1,0:T(8,128)S(1)}, u32[]{:S(2)}, u32[]{:S(2)}) async-start(f32[4,2,256,256]{3,2,1,0:T(8,128)} %add.238), calls=%async_computation.1 | async-start | bytes 4194304 | tf_op jit(solution)/shard_map/all_to_all | solution.py:182
  153.4 1.6 fusion.2
  155.1 24.1 %all-to-all-done.1 = f32[4,2,256,256]{3,2,1,0:T(8,128)S(1)} async-done(((f32[4,2,256,256]{3,2,1,0:T(8,128)}), f32[4,2,256,256]{3,2,1,0:T(8,128)S(1)}, u32[]{:S(2)}, u32[]{:S(2)}) %all-to-all-start.1) | async-done | bytes 2097184 | tf_op jit(solution)/shard_map/all_to_all | solution.py:182
  179.2 0.1 fusion.1
  179.3 1.1 copy-done.20
  180.4 0.1 maximum_add_fusion
  180.6 1.0 copy.8
  (73 shorter events, 1.4 us)
Async XLA Ops:
  0.0 4.2 %copy-start.22 = (s32[1,1,3,32]{3,1,2,0:T(1,128)S(1)}, s32[1,1,3,32]{3,1,2,0:T(1,128)}, u32[]{:S(2)}) copy-start(s32[1,1,3,32]{3,1,2,0:T(1,128)} %param.7) | copy-start | bytes 1156
  0.0 4.4 %copy-start.21 = (f32[2,2,256,256]{3,2,1,0:T(8,128)S(1)}, f32[2,2,256,256]{3,2,1,0:T(8,128)}, u32[]{:S(2)}) copy-start(f32[2,2,256,256]{3,2,1,0:T(8,128)} %param.4) | copy-start | bytes 3145732
  2.8 3.9 %collective-permute-start.1 = (f32[4,256,256]{2,1,0:T(8,128)}, f32[4,256,256]{2,1,0:T(8,128)S(1)}, u32[]{:S(2)}, u32[]{:S(2)}) collective-permute-start(f32[4,256,256]{2,1,0:T(8,128)} %get-tuple-element.47), channel_id=1, source_target_pairs={{0,16},{16,0},{1,17},{17,1},{2,18},{18,2},{3,19},{19,3},{4,20},{20... | collective-permute-start | bytes 3145736 | tf_op jit(solution)/shard_map/ppermute | solution.py:15
  5.3 5.6 %collective-permute-start = (f32[520,256]{1,0:T(8,128)}, f32[520,256]{1,0:T(8,128)S(1)}, u32[]{:S(2)}, u32[]{:S(2)}) collective-permute-start(f32[520,256]{1,0:T(8,128)} %get-tuple-element.59), channel_id=1, source_target_pairs={{0,16},{16,0},{1,17},{17,1},{2,18},{18,2},{3,19},{19,3},{4,20},{20... | collective-permute-start | bytes 1597448 | tf_op jit(solution)/shard_map/ppermute | solution.py:15
  7.0 5.7 %copy-start.4 = (f32[2,256,256]{2,1,0:T(8,128)}, f32[2,256,256]{2,1,0:T(8,128)S(1)}, u32[]{:S(2)}) copy-start(f32[2,256,256]{2,1,0:T(8,128)S(1)} %dynamic-slice_bitcast_fusion.4.own) | copy-start | bytes 1572868
  7.1 24.7 %collective-permute-start.4 = (f32[2,256,256]{2,1,0:T(8,128)S(1)}, f32[2,256,256]{2,1,0:T(8,128)S(1)}, u32[]{:S(2)}, u32[]{:S(2)}) collective-permute-start(f32[2,256,256]{2,1,0:T(8,128)S(1)} %get-tuple-element.43), channel_id=1, source_target_pairs={{0,3},{1,0},{2,1},{3,2},{4,7},{5,4},{6,5},{7,6},{8,11},{9,8},{10,9... | collective-permute-start | bytes 1572872 | tf_op jit(solution)/shard_map/ppermute | solution.py:15
  9.8 22.1 %collective-permute-start.5 = (f32[2,256,256]{2,1,0:T(8,128)S(1)}, f32[2,256,256]{2,1,0:T(8,128)S(1)}, u32[]{:S(2)}, u32[]{:S(2)}) collective-permute-start(f32[2,256,256]{2,1,0:T(8,128)S(1)} %get-tuple-element.45), channel_id=1, source_target_pairs={{0,2},{1,3},{2,0},{3,1},{4,6},{5,7},{6,4},{7,5},{8,10},{9,11},{10,... | collective-permute-start | bytes 1572872 | tf_op jit(solution)/shard_map/ppermute | solution.py:15
  10.3 26.1 %collective-permute-start.6 = (f32[2,256,256]{2,1,0:T(8,128)S(1)}, f32[2,256,256]{2,1,0:T(8,128)S(1)}, u32[]{:S(2)}, u32[]{:S(2)}) collective-permute-start(f32[2,256,256]{2,1,0:T(8,128)S(1)} %get-tuple-element.44), channel_id=1, source_target_pairs={{0,1},{1,2},{2,3},{3,0},{4,5},{5,6},{6,7},{7,4},{8,9},{9,10},{10,1... | collective-permute-start | bytes 1572872 | tf_op jit(solution)/shard_map/ppermute | solution.py:15
  11.0 26.4 %collective-permute-start.2 = (f32[2,256,256]{2,1,0:T(8,128)S(1)}, f32[2,256,256]{2,1,0:T(8,128)S(1)}, u32[]{:S(2)}, u32[]{:S(2)}) collective-permute-start(f32[2,256,256]{2,1,0:T(8,128)S(1)} %dynamic-slice_bitcast_fusion.4.own), channel_id=1, source_target_pairs={{0,32},{32,64},{64,96},{96,0},{1,33},{33,65},{65,97},{97,1},{2,34}... | collective-permute-start | bytes 1572872 | tf_op jit(solution)/shard_map/ppermute | solution.py:15
  12.7 24.7 %collective-permute-start.3 = (f32[2,256,256]{2,1,0:T(8,128)S(1)}, f32[2,256,256]{2,1,0:T(8,128)S(1)}, u32[]{:S(2)}, u32[]{:S(2)}) collective-permute-start(f32[2,256,256]{2,1,0:T(8,128)S(1)} %dynamic-slice_bitcast_fusion.4.own), channel_id=1, source_target_pairs={{0,96},{32,0},{64,32},{96,64},{1,97},{33,1},{65,33},{97,65},{2,98}... | collective-permute-start | bytes 1572872 | tf_op jit(solution)/shard_map/ppermute | solution.py:15
  37.4 0.8 copy-start.16
  37.4 24.7 %collective-permute-start.7 = (f32[2,520,256]{2,1,0:T(8,128)S(1)}, f32[2,520,256]{2,1,0:T(8,128)S(1)}, u32[]{:S(2)}, u32[]{:S(2)}) collective-permute-start(f32[2,520,256]{2,1,0:T(8,128)S(1)} %maximum_select_fusion.1.a_ref), channel_id=1, source_target_pairs={{0,3},{1,0},{2,1},{3,2},{4,7},{5,4},{6,5},{7,6},{8,11},{9,8},{10,9... | collective-permute-start | bytes 3194888 | tf_op jit(solution)/shard_map/ppermute | solution.py:15
  38.2 0.8 copy-start.13
  39.2 26.9 %collective-permute-start.11 = (f32[4,256,256]{2,1,0:T(8,128)S(1)}, f32[4,256,256]{2,1,0:T(8,128)S(1)}, u32[]{:S(2)}, u32[]{:S(2)}) collective-permute-start(f32[4,256,256]{2,1,0:T(8,128)S(1)} %get-tuple-element.51), channel_id=1, source_target_pairs={{0,32},{32,64},{64,96},{96,0},{1,33},{33,65},{65,97},{97,1},{2,34}... | collective-permute-start | bytes 3145736 | tf_op jit(solution)/shard_map/ppermute | solution.py:15
  40.9 25.2 %collective-permute-start.12 = (f32[4,256,256]{2,1,0:T(8,128)S(1)}, f32[4,256,256]{2,1,0:T(8,128)S(1)}, u32[]{:S(2)}, u32[]{:S(2)}) collective-permute-start(f32[4,256,256]{2,1,0:T(8,128)S(1)} %get-tuple-element.50), channel_id=1, source_target_pairs={{0,96},{32,0},{64,32},{96,64},{1,97},{33,1},{65,33},{97,65},{2,98}... | collective-permute-start | bytes 3145736 | tf_op jit(solution)/shard_map/ppermute | solution.py:15
  43.1 25.8 %collective-permute-start.9 = (f32[2,520,256]{2,1,0:T(8,128)S(1)}, f32[2,520,256]{2,1,0:T(8,128)S(1)}, u32[]{:S(2)}, u32[]{:S(2)}) collective-permute-start(f32[2,520,256]{2,1,0:T(8,128)S(1)} %maximum_select_fusion.1.a_ref), channel_id=1, source_target_pairs={{0,1},{1,2},{2,3},{3,0},{4,5},{5,6},{6,7},{7,4},{8,9},{9,10},{10,1... | collective-permute-start | bytes 3194888 | tf_op jit(solution)/shard_map/ppermute | solution.py:15
  62.9 12.6 %collective-permute-start.8 = (f32[1,520,256]{2,1,0:T(8,128)}, f32[1,520,256]{2,1,0:T(8,128)S(1)}, u32[]{:S(2)}, u32[]{:S(2)}) collective-permute-start(f32[1,520,256]{2,1,0:T(8,128)} %slice.126), channel_id=1, source_target_pairs={{0,3},{1,0},{2,1},{3,2},{4,7},{5,4},{6,5},{7,6},{8,11},{9,8},{10,9... | collective-permute-start | bytes 1597448 | tf_op jit(solution)/shard_map/ppermute | solution.py:15
  66.2 4.6 %copy-start.7 = (f32[4,256,256]{2,1,0:T(8,128)}, f32[4,256,256]{2,1,0:T(8,128)S(1)}, u32[]{:S(2)}) copy-start(f32[4,256,256]{2,1,0:T(8,128)S(1)} %collective-permute-done.11.two_r.own_fa) | copy-start | bytes 3145732
  66.2 4.6 %copy-start.10 = (f32[4,256,256]{2,1,0:T(8,128)}, f32[4,256,256]{2,1,0:T(8,128)S(1)}, u32[]{:S(2)}) copy-start(f32[4,256,256]{2,1,0:T(8,128)S(1)} %collective-permute-done.12.two_l.own_fb) | copy-start | bytes 3145732
  66.2 22.8 %collective-permute-start.13 = (f32[3,256,256]{2,1,0:T(8,128)}, f32[3,256,256]{2,1,0:T(8,128)}, u32[]{:S(2)}, u32[]{:S(2)}) collective-permute-start(f32[3,256,256]{2,1,0:T(8,128)} %get-tuple-element.32.rest), channel_id=1, source_target_pairs={{0,32},{32,64},{64,96},{96,0},{1,33},{33,65},{65,97},{97,1},{2,34}... | collective-permute-start | bytes 2359304 | tf_op jit(solution)/shard_map/ppermute | solution.py:15
  66.5 22.4 %collective-permute-start.14 = (f32[3,256,256]{2,1,0:T(8,128)}, f32[3,256,256]{2,1,0:T(8,128)}, u32[]{:S(2)}, u32[]{:S(2)}) collective-permute-start(f32[3,256,256]{2,1,0:T(8,128)} %get-tuple-element.32.rest), channel_id=1, source_target_pairs={{0,96},{32,0},{64,32},{96,64},{1,97},{33,1},{65,33},{97,65},{2,98}... | collective-permute-start | bytes 2359304 | tf_op jit(solution)/shard_map/ppermute | solution.py:15
  68.9 1.0 copy-start.2
  70.7 13.5 %collective-permute-start.10 = (f32[1,520,256]{2,1,0:T(8,128)}, f32[1,520,256]{2,1,0:T(8,128)}, u32[]{:S(2)}, u32[]{:S(2)}) collective-permute-start(f32[1,520,256]{2,1,0:T(8,128)} %slice.128), channel_id=1, source_target_pairs={{0,1},{1,2},{2,3},{3,0},{4,5},{5,6},{6,7},{7,4},{8,9},{9,10},{10,1... | collective-permute-start | bytes 1597448 | tf_op jit(solution)/shard_map/ppermute | solution.py:15
  73.1 21.1 %collective-permute-start.15 = (f32[3,128,256]{2,1,0:T(8,128)}, f32[3,128,256]{2,1,0:T(8,128)}, u32[]{:S(2)}, u32[]{:S(2)}) collective-permute-start(f32[3,128,256]{2,1,0:T(8,128)} %slice.107), channel_id=1, source_target_pairs={{0,32},{32,64},{64,96},{96,0},{1,33},{33,65},{65,97},{97,1},{2,34}... | collective-permute-start | bytes 1179656 | tf_op jit(solution)/shard_map/ppermute | solution.py:15
  75.5 18.7 %collective-permute-start.16 = (f32[3,128,256]{2,1,0:T(8,128)}, f32[3,128,256]{2,1,0:T(8,128)}, u32[]{:S(2)}, u32[]{:S(2)}) collective-permute-start(f32[3,128,256]{2,1,0:T(8,128)} %slice.108), channel_id=1, source_target_pairs={{0,96},{32,0},{64,32},{96,64},{1,97},{33,1},{65,33},{97,65},{2,98}... | collective-permute-start | bytes 1179656 | tf_op jit(solution)/shard_map/ppermute | solution.py:15
  85.2 1.2 copy-start.3
  86.4 7.8 %copy-start.5 = (f32[2,256,256]{2,1,0:T(8,128)S(1)}, f32[2,256,256]{2,1,0:T(8,128)}, u32[]{:S(2)}) copy-start(f32[2,256,256]{2,1,0:T(8,128)} %copy-done.4) | copy-start | bytes 1572868
  86.4 7.8 %copy-start.8 = (f32[4,256,256]{2,1,0:T(8,128)S(1)}, f32[4,256,256]{2,1,0:T(8,128)}, u32[]{:S(2)}) copy-start(f32[4,256,256]{2,1,0:T(8,128)} %copy-done.7) | copy-start | bytes 3145732
  86.4 7.8 %copy-start.11 = (f32[4,256,256]{2,1,0:T(8,128)S(1)}, f32[4,256,256]{2,1,0:T(8,128)}, u32[]{:S(2)}) copy-start(f32[4,256,256]{2,1,0:T(8,128)} %copy-done.10) | copy-start | bytes 3145732
  86.4 7.8 %copy-start.14 = (f32[2,256,256]{2,1,0:T(8,128)S(1)}, f32[2,256,256]{2,1,0:T(8,128)}, u32[]{:S(2)}) copy-start(f32[2,256,256]{2,1,0:T(8,128)} %copy-done.13) | copy-start | bytes 1572868
  86.4 7.8 %copy-start.17 = (f32[2,256,256]{2,1,0:T(8,128)S(1)}, f32[2,256,256]{2,1,0:T(8,128)}, u32[]{:S(2)}) copy-start(f32[2,256,256]{2,1,0:T(8,128)} %copy-done.16) | copy-start | bytes 1572868
  88.8 12.7 %copy-start = (bf16[4,4,256,768]{3,2,1,0:T(8,128)(2,1)}, bf16[4,4,256,768]{3,2,1,0:T(8,128)(2,1)S(1)}, u32[]{:S(2)}) copy-start(bf16[4,4,256,768]{3,2,1,0:T(8,128)(2,1)S(1)} %split_amp.1.a_ref) | copy-start | bytes 18874372
  101.5 4.2 %collective-permute-start.17 = (f32[4,2,256,256]{3,2,1,0:T(8,128)S(1)}, f32[4,2,256,256]{3,2,1,0:T(8,128)S(1)}, u32[]{:S(2)}, u32[]{:S(2)}) collective-permute-start(f32[4,2,256,256]{3,2,1,0:T(8,128)S(1)} %get-tuple-element.37), channel_id=1, source_target_pairs={{0,16},{16,0},{1,17},{17,1},{2,18},{18,2},{3,19},{19,3},{4,20},{20... | collective-permute-start | bytes 6291464 | tf_op jit(solution)/shard_map/ppermute | solution.py:15
  107.4 19.6 %copy-start.6 = (f32[2,256,256]{2,1,0:T(8,128)S(1)}, f32[2,256,256]{2,1,0:T(8,128)}, u32[]{:S(2)}) copy-start(f32[2,256,256]{2,1,0:T(8,128)} %copy-done.4) | copy-start | bytes 1572868
  107.4 19.6 %copy-start.15 = (f32[2,256,256]{2,1,0:T(8,128)S(1)}, f32[2,256,256]{2,1,0:T(8,128)}, u32[]{:S(2)}) copy-start(f32[2,256,256]{2,1,0:T(8,128)} %copy-done.13) | copy-start | bytes 1572868
  107.4 36.1 %all-to-all-start = ((f32[4,2,256,256]{3,2,1,0:T(8,128)}), f32[4,2,256,256]{3,2,1,0:T(8,128)}, u32[]{:S(2)}, u32[]{:S(2)}) async-start(f32[4,2,256,256]{3,2,1,0:T(8,128)} %add.233), calls=%async_computation | async-start | bytes 4194304 | tf_op jit(solution)/shard_map/all_to_all | solution.py:177
  113.3 12.2 %collective-permute-start.18 = (f32[3,128,256]{2,1,0:T(8,128)S(1)}, f32[3,128,256]{2,1,0:T(8,128)S(1)}, u32[]{:S(2)}, u32[]{:S(2)}) collective-permute-start(f32[3,128,256]{2,1,0:T(8,128)S(1)} %slice.113), channel_id=1, source_target_pairs={{0,32},{32,64},{64,96},{96,0},{1,33},{33,65},{65,97},{97,1},{2,34}... | collective-permute-start | bytes 1179656 | tf_op jit(solution)/shard_map/ppermute | solution.py:15
  115.5 11.5 %collective-permute-start.19 = (f32[3,128,256]{2,1,0:T(8,128)S(1)}, f32[3,128,256]{2,1,0:T(8,128)S(1)}, u32[]{:S(2)}, u32[]{:S(2)}) collective-permute-start(f32[3,128,256]{2,1,0:T(8,128)S(1)} %slice.114), channel_id=1, source_target_pairs={{0,96},{32,0},{64,32},{96,64},{1,97},{33,1},{65,33},{97,65},{2,98}... | collective-permute-start | bytes 1179656 | tf_op jit(solution)/shard_map/ppermute | solution.py:15
  127.1 2.8 %copy-start.1 = (bf16[4,4,256,768]{3,2,1,0:T(8,128)(2,1)S(1)}, bf16[4,4,256,768]{3,2,1,0:T(8,128)(2,1)}, u32[]{:S(2)}) copy-start(bf16[4,4,256,768]{3,2,1,0:T(8,128)(2,1)} %copy-done) | copy-start | bytes 18874372
  129.9 1.2 copy-start.9
  131.1 1.2 copy-start.12
  132.3 1.0 copy-start.18
  142.2 1.4 copy-start.19
  143.5 4.4 %collective-permute-start.20 = (f32[4,2,256,256]{3,2,1,0:T(8,128)}, f32[4,2,256,256]{3,2,1,0:T(8,128)S(1)}, u32[]{:S(2)}, u32[]{:S(2)}) collective-permute-start(f32[4,2,256,256]{3,2,1,0:T(8,128)} %copy-done.19), channel_id=1, source_target_pairs={{0,16},{16,0},{1,17},{17,1},{2,18},{18,2},{3,19},{19,3},{4,20},{20... | collective-permute-start | bytes 6291464 | tf_op jit(solution)/shard_map/ppermute | solution.py:15
  149.6 29.6 %all-to-all-start.1 = ((f32[4,2,256,256]{3,2,1,0:T(8,128)}), f32[4,2,256,256]{3,2,1,0:T(8,128)S(1)}, u32[]{:S(2)}, u32[]{:S(2)}) async-start(f32[4,2,256,256]{3,2,1,0:T(8,128)} %add.238), calls=%async_computation.1 | async-start | bytes 4194304 | tf_op jit(solution)/shard_map/all_to_all | solution.py:182
  179.2 1.2 copy-start.20

commit v14 on v12

--- a/solution.py
+++ b/solution.py
@@ -178,8 +178,9 @@
     gate = part
     even = part[0] + part[1] + part[2] + part[3]
     held, away = contract(1, flags, a3, pieces + (rest[1], rest1_r, rest1_l, two_r, two_l) + far1)
-    away, gate = lax.optimization_barrier((away, gate))
-    part = lax.all_to_all(held + shift(away, "c", 1), "y", 0, 0, tiled=True)
+    last, gate = lax.optimization_barrier((away[:, 1:], gate))
+    away = jnp.concatenate([shift(away[:, :1], "c", 1), shift(last, "c", 1)], axis=1)
+    part = lax.all_to_all(held + away, "y", 0, 0, tiled=True)
     return resid + jnp.stack([even, part[0] + part[1] + part[2] + part[3]], axis=1)
 
 

time: 183 us -> 180 us (0.984)
  waiting for transfers between devices: 91.4 us -> 88.2 us
  starting transfers between devices: 38.9 us -> 41.4 us
    ppermute x21 -> x22, starting transfers between devices: 30.1 us -> 33.2 us  [shift(): return lax.ppermute(t, axis, [(i, (i + s) % n) for i in range(n)])]
    all_to_all x1, waiting for transfers between devices: 7.95 us -> 6.02 us  [on_device(): part = lax.all_to_all(part, 'y', 0, 0, tiled=True)]
    unnamed x50 -> x48, local copies, waits for them, and re-layouts: 14.3 us -> 12.9 us
    ppermute x21 -> x22, waiting for transfers between devices: 59.1 us -> 57.8 us  [shift(): return lax.ppermute(t, axis, [(i, (i + s) % n) for i in range(n)])]
  transfers between devices with their start and end apart: 23 -> 24, of which waited for: 13 -> 12; matrix products, arithmetic and copies ran while one was open for 9% -> 9% of each run, Pallas kernels for 5% -> 6%
where the time goes in v14:
time: 180 us
  waiting for transfers between devices  88.2 us (49%)
  starting transfers between devices  41.4 us (23%)
  local copies, waits for them, and re-layouts  27.8 us (15%)
  Pallas kernels  14.3 us (8%)
  other arithmetic  7.75 us (4%)
    ppermute x22, waiting for transfers between devices, shift(): return lax.ppermute(t, axis, [(i, (i + s) % n) for i in range(n)])  57.8 us
    ppermute x22, starting transfers between devices, shift(): return lax.ppermute(t, axis, [(i, (i + s) % n) for i in range(n)])  33.2 us
    all_to_all x1, waiting for transfers between devices, on_device(): part = lax.all_to_all(held + away, 'y', 0, 0, tiled=True)  24.4 us
    unnamed x48, local copies, waits for them, and re-layouts  12.9 us
    pallas_call x2, Pallas kernels, contract(): pl.pallas_call(make_contract_kernel(kp), in_specs=[pl.BlockSpec(memory_sp...  11.9 us
    all_to_all x1, waiting for transfers between devices, on_device(): part = lax.all_to_all(part, 'y', 0, 0, tiled=True)  6.02 us
    all_to_all x1, starting transfers between devices, on_device(): part = lax.all_to_all(part, 'y', 0, 0, tiled=True)  4.58 us
    all_to_all x1, starting transfers between devices, on_device(): part = lax.all_to_all(held + away, 'y', 0, 0, tiled=True)  3.61 us
  transfers between devices with their start and end apart: 24, of which 12 were waited for; matrix products, arithmetic and copies ran while one was open for 9% of the time, Pallas kernels for 6%

profile of v14, /device:TPU:1, one launch (start us, length us, event | category | flops | bytes accessed | tf_op | source)
XLA Modules:
  0.0 179.7 jit_solution(2257274132087665356)
XLA Ops:
  0.0 2.8 %constant_dynamic-slice_fusion = (f32[1,4,256,256]{3,2,1,0:T(8,128)S(1)}, f32[4,256,256]{2,1,0:T(8,128)}) fusion(f32[2,4,256,256]{3,2,1,0:T(8,128)} %param.5, s32[]{:T(128)S(6)} %select_n.122, s32[]{:T(128)S(6)} %select_n.132), kind=kLoop, calls=%fused_computation.36 | loop fusion | bytes 4194312 | tf_op jit(solution)/shard_map/jit(dynamic_index_in_dim)/dynamic_slice | solution.py:138
  2.8 1.4 collective-permute-start.1
  4.5 0.9 fusion
  5.3 1.4 collective-permute-done.1
  6.7 0.2 maximum_select_fusion
  7.1 2.6 %collective-permute-start.4 = (f32[2,256,256]{2,1,0:T(8,128)S(1)}, f32[2,256,256]{2,1,0:T(8,128)S(1)}, u32[]{:S(2)}, u32[]{:S(2)}) collective-permute-start(f32[2,256,256]{2,1,0:T(8,128)S(1)} %get-tuple-element.45), channel_id=1, source_target_pairs={{0,3},{1,0},{2,1},{3,2},{4,7},{5,4},{6,5},{7,6},{8,11},{9,8},{10,9... | collective-permute-start | bytes 1572872 | tf_op jit(solution)/shard_map/ppermute | solution.py:15
  9.8 0.5 collective-permute-start.5
  10.3 0.6 collective-permute-start.6
  11.0 1.7 collective-permute-start.2
  12.7 2.2 %collective-permute-start.3 = (f32[2,256,256]{2,1,0:T(8,128)S(1)}, f32[2,256,256]{2,1,0:T(8,128)S(1)}, u32[]{:S(2)}, u32[]{:S(2)}) collective-permute-start(f32[2,256,256]{2,1,0:T(8,128)S(1)} %dynamic-slice_bitcast_fusion.4.own), channel_id=1, source_target_pairs={{0,96},{32,0},{64,32},{96,64},{1,97},{33,1},{65,33},{97,65},{2,98}... | collective-permute-start | bytes 1572872 | tf_op jit(solution)/shard_map/ppermute | solution.py:15
  14.9 16.9 %collective-permute-done.4 = f32[2,256,256]{2,1,0:T(8,128)S(1)} collective-permute-done((f32[2,256,256]{2,1,0:T(8,128)S(1)}, f32[2,256,256]{2,1,0:T(8,128)S(1)}, u32[]{:S(2)}, u32[]{:S(2)}) %collective-permute-start.4) | collective-permute-done | bytes 524320 | tf_op jit(solution)/shard_map/ppermute | solution.py:15
  31.9 4.5 %collective-permute-done.6 = f32[2,256,256]{2,1,0:T(8,128)S(1)} collective-permute-done((f32[2,256,256]{2,1,0:T(8,128)S(1)}, f32[2,256,256]{2,1,0:T(8,128)S(1)}, u32[]{:S(2)}, u32[]{:S(2)}) %collective-permute-start.6) | collective-permute-done | bytes 524320 | tf_op jit(solution)/shard_map/ppermute | solution.py:15
  36.4 1.0 pad_maximum_fusion.2
  37.5 0.7 copy-done.16
  38.2 0.8 copy-done.13
  39.0 0.2 pad_maximum_fusion
  39.2 1.7 collective-permute-start.11
  40.9 2.2 %collective-permute-start.12 = (f32[4,256,256]{2,1,0:T(8,128)S(1)}, f32[4,256,256]{2,1,0:T(8,128)S(1)}, u32[]{:S(2)}, u32[]{:S(2)}) collective-permute-start(f32[4,256,256]{2,1,0:T(8,128)S(1)} %get-tuple-element.52), channel_id=1, source_target_pairs={{0,96},{32,0},{64,32},{96,64},{1,97},{33,1},{65,33},{97,65},{2,98}... | collective-permute-start | bytes 3145736 | tf_op jit(solution)/shard_map/ppermute | solution.py:15
  43.1 0.8 collective-permute-start.9
  43.9 18.2 %collective-permute-done.7.r_ref = f32[2,520,256]{2,1,0:T(8,128)S(1)} collective-permute-done((f32[2,520,256]{2,1,0:T(8,128)S(1)}, f32[2,520,256]{2,1,0:T(8,128)S(1)}, u32[]{:S(2)}, u32[]{:S(2)}) %collective-permute-start.7) | collective-permute-done | bytes 1064992 | tf_op jit(solution)/shard_map/ppermute | solution.py:15
  62.0 0.8 slice.134
  62.9 0.8 collective-permute-start.8
  63.7 2.4 %collective-permute-done.11.two_r.own_fa = f32[4,256,256]{2,1,0:T(8,128)S(1)} collective-permute-done((f32[4,256,256]{2,1,0:T(8,128)S(1)}, f32[4,256,256]{2,1,0:T(8,128)S(1)}, u32[]{:S(2)}, u32[]{:S(2)}) %collective-permute-start.11) | collective-permute-done | bytes 1048608 | tf_op jit(solution)/shard_map/ppermute | solution.py:15
  66.1 0.3 collective-permute-start.13
  66.5 2.4 %collective-permute-start.14 = (f32[3,256,256]{2,1,0:T(8,128)}, f32[3,256,256]{2,1,0:T(8,128)}, u32[]{:S(2)}, u32[]{:S(2)}) collective-permute-start(f32[3,256,256]{2,1,0:T(8,128)} %get-tuple-element.32.rest), channel_id=1, source_target_pairs={{0,96},{32,0},{64,32},{96,64},{1,97},{33,1},{65,33},{97,65},{2,98}... | collective-permute-start | bytes 2359304 | tf_op jit(solution)/shard_map/ppermute | solution.py:15
  68.9 1.0 copy-done.2
  69.9 0.8 slice.136
  70.7 0.4 collective-permute-start.10
  71.3 1.8 slice.113
  73.1 1.8 slice.114
  74.8 0.6 collective-permute-done.8.fa_ref
  75.5 3.8 %collective-permute-start.16 = (f32[3,128,256]{2,1,0:T(8,128)}, f32[3,128,256]{2,1,0:T(8,128)}, u32[]{:S(2)}, u32[]{:S(2)}) collective-permute-start(f32[3,128,256]{2,1,0:T(8,128)} %slice.114), channel_id=1, source_target_pairs={{0,96},{32,0},{64,32},{96,64},{1,97},{33,1},{65,33},{97,65},{2,98}... | collective-permute-start | bytes 1179656 | tf_op jit(solution)/shard_map/ppermute | solution.py:15
  79.2 0.7 slice_reduce_fusion
  80.2 4.1 %collective-permute-done.10.fb_ref = f32[1,520,256]{2,1,0:T(8,128)} collective-permute-done((f32[1,520,256]{2,1,0:T(8,128)}, f32[1,520,256]{2,1,0:T(8,128)}, u32[]{:S(2)}, u32[]{:S(2)}) %collective-permute-start.10) | collective-permute-done | bytes 532512 | tf_op jit(solution)/shard_map/ppermute | solution.py:15
  84.3 0.7 slice_reduce_fusion.3
  85.2 1.2 copy-done.3
  86.4 2.4 %split_amp.1.a_ref = bf16[4,4,256,768]{3,2,1,0:T(8,128)(2,1)S(1)} custom-call(f32[2,520,256]{2,1,0:T(8,128)S(1)} %maximum_select_fusion.1.a_ref, f32[2,520,256]{2,1,0:T(8,128)S(1)} %collective-permute-done.7.r_ref, f32[2,520,256]{2,1,0:T(8,128)S(1)} %copy-done.3, f32[1,520,256]{2,1,0:T(8,128)S(1)} %collective-permute-done.8.fa_ref, ...), custom_call_target="tpu_custom_call" | custom-call | bytes 10485760 | tf_op jit(solution)/shard_map/split_amp/pallas_call | solution.py:50
  88.9 5.2 %collective-permute-done.15.fa = f32[3,128,256]{2,1,0:T(8,128)} collective-permute-done((f32[3,128,256]{2,1,0:T(8,128)}, f32[3,128,256]{2,1,0:T(8,128)}, u32[]{:S(2)}, u32[]{:S(2)}) %collective-permute-start.15) | collective-permute-done | bytes 393248 | tf_op jit(solution)/shard_map/ppermute | solution.py:15
  94.2 4.1 %contract.2 = (f32[4,2,256,256]{3,2,1,0:T(8,128)S(1)}, f32[4,2,256,256]{3,2,1,0:T(8,128)S(1)}) custom-call(s32[130]{0:T(256)S(1)} %pad_add_fusion.flag_ref, bf16[4,4,256,768]{3,2,1,0:T(8,128)(2,1)S(1)} %split_amp.1.a_ref, f32[2,256,256]{2,1,0:T(8,128)S(1)} %copy-done.5, f32[2,256,256]{2,1,0:T(8,128)S(1)} %copy-done.14, f32[2,256,256]{2,1,0:T(8,128)S(1)} %copy-done.17, ...), custom_call_target="tpu_custom_call" | custom-call | flops 40000000000 | bytes 8388608 | tf_op jit(solution)/shard_map/contract/pallas_call | solution.py:113
  98.4 6.7 %collective-permute-start.17 = (f32[4,2,256,256]{3,2,1,0:T(8,128)S(1)}, f32[4,2,256,256]{3,2,1,0:T(8,128)S(1)}, u32[]{:S(2)}, u32[]{:S(2)}) collective-permute-start(f32[4,2,256,256]{3,2,1,0:T(8,128)S(1)} %get-tuple-element.37), channel_id=1, source_target_pairs={{0,16},{16,0},{1,17},{17,1},{2,18},{18,2},{3,19},{19,3},{4,20},{20... | collective-permute-start | bytes 6291464 | tf_op jit(solution)/shard_map/ppermute | solution.py:15
  105.1 1.0 slice.119
  106.2 1.0 slice.120
  107.2 2.7 %collective-permute-start.19 = (f32[3,128,256]{2,1,0:T(8,128)S(1)}, f32[3,128,256]{2,1,0:T(8,128)S(1)}, u32[]{:S(2)}, u32[]{:S(2)}) collective-permute-start(f32[3,128,256]{2,1,0:T(8,128)S(1)} %slice.120), channel_id=1, source_target_pairs={{0,96},{32,0},{64,32},{96,64},{1,97},{33,1},{65,33},{97,65},{2,98}... | collective-permute-start | bytes 1179656 | tf_op jit(solution)/shard_map/ppermute | solution.py:15
  110.0 1.6 add.233
  111.6 4.6 %all-to-all-start = ((f32[4,2,256,256]{3,2,1,0:T(8,128)}), f32[4,2,256,256]{3,2,1,0:T(8,128)}, u32[]{:S(2)}, u32[]{:S(2)}) async-start(f32[4,2,256,256]{3,2,1,0:T(8,128)} %add.233), calls=%async_computation | async-start | bytes 4194304 | tf_op jit(solution)/shard_map/all_to_all | solution.py:177
  116.2 1.9 %collective-permute-done.18.fa = f32[3,128,256]{2,1,0:T(8,128)S(1)} collective-permute-done((f32[3,128,256]{2,1,0:T(8,128)S(1)}, f32[3,128,256]{2,1,0:T(8,128)S(1)}, u32[]{:S(2)}, u32[]{:S(2)}) %collective-permute-start.18) | collective-permute-done | bytes 393248 | tf_op jit(solution)/shard_map/ppermute | solution.py:15
  118.2 0.8 copy-done.19
  119.0 2.8 %copy-done.1 = bf16[4,4,256,768]{3,2,1,0:T(8,128)(2,1)S(1)} copy-done((bf16[4,4,256,768]{3,2,1,0:T(8,128)(2,1)S(1)}, bf16[4,4,256,768]{3,2,1,0:T(8,128)(2,1)}, u32[]{:S(2)}) %copy-start.1) | copy-done | bytes 6291480
  121.7 1.2 copy-done.9
  123.0 1.2 copy-done.12
  124.2 1.0 copy-done.18
  125.2 1.0 copy-done.20
  126.2 7.8 %contract.3 = (f32[4,2,256,256]{3,2,1,0:T(8,128)S(1)}, f32[4,2,256,256]{3,2,1,0:T(8,128)S(1)}) custom-call(s32[130]{0:T(256)S(1)} %pad_add_fusion.flag_ref, bf16[4,4,256,768]{3,2,1,0:T(8,128)(2,1)S(1)} %copy-done.1, f32[2,256,256]{2,1,0:T(8,128)S(1)} %copy-done.6, f32[2,256,256]{2,1,0:T(8,128)S(1)} %copy-done.15, f32[2,256,256]{2,1,0:T(8,128)S(1)} %copy-done.18, ...), custom_call_target="tpu_custom_call" | custom-call | flops 40000000000 | bytes 8388608 | tf_op jit(solution)/shard_map/contract/pallas_call | solution.py:113
  134.0 1.5 fusion.15
  135.5 0.6 collective-permute-start.20
  136.1 6.0 %all-to-all-done = f32[4,2,256,256]{3,2,1,0:T(8,128)} async-done(((f32[4,2,256,256]{3,2,1,0:T(8,128)}), f32[4,2,256,256]{3,2,1,0:T(8,128)}, u32[]{:S(2)}, u32[]{:S(2)}) %all-to-all-start) | async-done | bytes 2097184 | tf_op jit(solution)/shard_map/all_to_all | solution.py:177
  142.1 1.4 collective-permute-start.21
  143.6 2.5 %collective-permute-done.21 = f32[4,1,256,256]{3,2,1,0:T(8,128)S(1)} collective-permute-done((f32[4,1,256,256]{3,2,1,0:T(8,128)}, f32[4,1,256,256]{3,2,1,0:T(8,128)S(1)}, u32[]{:S(2)}, u32[]{:S(2)}) %collective-permute-start.21) | collective-permute-done | bytes 1048608 | tf_op jit(solution)/shard_map/ppermute | solution.py:15
  146.1 1.6 maximum_add_fusion
  147.7 3.6 %all-to-all-start.1 = ((f32[4,2,256,256]{3,2,1,0:T(8,128)}), f32[4,2,256,256]{3,2,1,0:T(8,128)S(1)}, u32[]{:S(2)}, u32[]{:S(2)}) async-start(f32[4,2,256,256]{3,2,1,0:T(8,128)} %maximum_add_fusion), calls=%async_computation.1 | async-start | bytes 4194304 | tf_op jit(solution)/shard_map/all_to_all | solution.py:183
  151.3 1.7 fusion.2
  152.9 24.4 %all-to-all-done.1 = f32[4,2,256,256]{3,2,1,0:T(8,128)S(1)} async-done(((f32[4,2,256,256]{3,2,1,0:T(8,128)}), f32[4,2,256,256]{3,2,1,0:T(8,128)S(1)}, u32[]{:S(2)}, u32[]{:S(2)}) %all-to-all-start.1) | async-done | bytes 2097184 | tf_op jit(solution)/shard_map/all_to_all | solution.py:183
  177.5 1.1 copy-done.21
  178.7 1.0 copy.8
  (78 shorter events, 1.8 us)
Async XLA Ops:
  0.0 4.2 %copy-start.23 = (s32[1,1,3,32]{3,1,2,0:T(1,128)S(1)}, s32[1,1,3,32]{3,1,2,0:T(1,128)}, u32[]{:S(2)}) copy-start(s32[1,1,3,32]{3,1,2,0:T(1,128)} %param.7) | copy-start | bytes 1156
  0.0 4.4 %copy-start.22 = (f32[2,2,256,256]{3,2,1,0:T(8,128)S(1)}, f32[2,2,256,256]{3,2,1,0:T(8,128)}, u32[]{:S(2)}) copy-start(f32[2,2,256,256]{3,2,1,0:T(8,128)} %param.4) | copy-start | bytes 3145732
  2.8 3.9 %collective-permute-start.1 = (f32[4,256,256]{2,1,0:T(8,128)}, f32[4,256,256]{2,1,0:T(8,128)S(1)}, u32[]{:S(2)}, u32[]{:S(2)}) collective-permute-start(f32[4,256,256]{2,1,0:T(8,128)} %get-tuple-element.49), channel_id=1, source_target_pairs={{0,16},{16,0},{1,17},{17,1},{2,18},{18,2},{3,19},{19,3},{4,20},{20... | collective-permute-start | bytes 3145736 | tf_op jit(solution)/shard_map/ppermute | solution.py:15
  5.3 5.6 %collective-permute-start = (f32[520,256]{1,0:T(8,128)}, f32[520,256]{1,0:T(8,128)S(1)}, u32[]{:S(2)}, u32[]{:S(2)}) collective-permute-start(f32[520,256]{1,0:T(8,128)} %get-tuple-element.61), channel_id=1, source_target_pairs={{0,16},{16,0},{1,17},{17,1},{2,18},{18,2},{3,19},{19,3},{4,20},{20... | collective-permute-start | bytes 1597448 | tf_op jit(solution)/shard_map/ppermute | solution.py:15
  7.0 5.7 %copy-start.4 = (f32[2,256,256]{2,1,0:T(8,128)}, f32[2,256,256]{2,1,0:T(8,128)S(1)}, u32[]{:S(2)}) copy-start(f32[2,256,256]{2,1,0:T(8,128)S(1)} %dynamic-slice_bitcast_fusion.4.own) | copy-start | bytes 1572868
  7.1 24.7 %collective-permute-start.4 = (f32[2,256,256]{2,1,0:T(8,128)S(1)}, f32[2,256,256]{2,1,0:T(8,128)S(1)}, u32[]{:S(2)}, u32[]{:S(2)}) collective-permute-start(f32[2,256,256]{2,1,0:T(8,128)S(1)} %get-tuple-element.45), channel_id=1, source_target_pairs={{0,3},{1,0},{2,1},{3,2},{4,7},{5,4},{6,5},{7,6},{8,11},{9,8},{10,9... | collective-permute-start | bytes 1572872 | tf_op jit(solution)/shard_map/ppermute | solution.py:15
  9.8 22.1 %collective-permute-start.5 = (f32[2,256,256]{2,1,0:T(8,128)S(1)}, f32[2,256,256]{2,1,0:T(8,128)S(1)}, u32[]{:S(2)}, u32[]{:S(2)}) collective-permute-start(f32[2,256,256]{2,1,0:T(8,128)S(1)} %get-tuple-element.47), channel_id=1, source_target_pairs={{0,2},{1,3},{2,0},{3,1},{4,6},{5,7},{6,4},{7,5},{8,10},{9,11},{10,... | collective-permute-start | bytes 1572872 | tf_op jit(solution)/shard_map/ppermute | solution.py:15
  10.3 26.1 %collective-permute-start.6 = (f32[2,256,256]{2,1,0:T(8,128)S(1)}, f32[2,256,256]{2,1,0:T(8,128)S(1)}, u32[]{:S(2)}, u32[]{:S(2)}) collective-permute-start(f32[2,256,256]{2,1,0:T(8,128)S(1)} %get-tuple-element.46), channel_id=1, source_target_pairs={{0,1},{1,2},{2,3},{3,0},{4,5},{5,6},{6,7},{7,4},{8,9},{9,10},{10,1... | collective-permute-start | bytes 1572872 | tf_op jit(solution)/shard_map/ppermute | solution.py:15
  11.0 26.4 %collective-permute-start.2 = (f32[2,256,256]{2,1,0:T(8,128)S(1)}, f32[2,256,256]{2,1,0:T(8,128)S(1)}, u32[]{:S(2)}, u32[]{:S(2)}) collective-permute-start(f32[2,256,256]{2,1,0:T(8,128)S(1)} %dynamic-slice_bitcast_fusion.4.own), channel_id=1, source_target_pairs={{0,32},{32,64},{64,96},{96,0},{1,33},{33,65},{65,97},{97,1},{2,34}... | collective-permute-start | bytes 1572872 | tf_op jit(solution)/shard_map/ppermute | solution.py:15
  12.7 24.7 %collective-permute-start.3 = (f32[2,256,256]{2,1,0:T(8,128)S(1)}, f32[2,256,256]{2,1,0:T(8,128)S(1)}, u32[]{:S(2)}, u32[]{:S(2)}) collective-permute-start(f32[2,256,256]{2,1,0:T(8,128)S(1)} %dynamic-slice_bitcast_fusion.4.own), channel_id=1, source_target_pairs={{0,96},{32,0},{64,32},{96,64},{1,97},{33,1},{65,33},{97,65},{2,98}... | collective-permute-start | bytes 1572872 | tf_op jit(solution)/shard_map/ppermute | solution.py:15
  37.4 0.8 copy-start.16
  37.4 24.7 %collective-permute-start.7 = (f32[2,520,256]{2,1,0:T(8,128)S(1)}, f32[2,520,256]{2,1,0:T(8,128)S(1)}, u32[]{:S(2)}, u32[]{:S(2)}) collective-permute-start(f32[2,520,256]{2,1,0:T(8,128)S(1)} %maximum_select_fusion.1.a_ref), channel_id=1, source_target_pairs={{0,3},{1,0},{2,1},{3,2},{4,7},{5,4},{6,5},{7,6},{8,11},{9,8},{10,9... | collective-permute-start | bytes 3194888 | tf_op jit(solution)/shard_map/ppermute | solution.py:15
  38.2 0.8 copy-start.13
  39.2 26.9 %collective-permute-start.11 = (f32[4,256,256]{2,1,0:T(8,128)S(1)}, f32[4,256,256]{2,1,0:T(8,128)S(1)}, u32[]{:S(2)}, u32[]{:S(2)}) collective-permute-start(f32[4,256,256]{2,1,0:T(8,128)S(1)} %get-tuple-element.53), channel_id=1, source_target_pairs={{0,32},{32,64},{64,96},{96,0},{1,33},{33,65},{65,97},{97,1},{2,34}... | collective-permute-start | bytes 3145736 | tf_op jit(solution)/shard_map/ppermute | solution.py:15
  40.9 25.2 %collective-permute-start.12 = (f32[4,256,256]{2,1,0:T(8,128)S(1)}, f32[4,256,256]{2,1,0:T(8,128)S(1)}, u32[]{:S(2)}, u32[]{:S(2)}) collective-permute-start(f32[4,256,256]{2,1,0:T(8,128)S(1)} %get-tuple-element.52), channel_id=1, source_target_pairs={{0,96},{32,0},{64,32},{96,64},{1,97},{33,1},{65,33},{97,65},{2,98}... | collective-permute-start | bytes 3145736 | tf_op jit(solution)/shard_map/ppermute | solution.py:15
  43.1 25.8 %collective-permute-start.9 = (f32[2,520,256]{2,1,0:T(8,128)S(1)}, f32[2,520,256]{2,1,0:T(8,128)S(1)}, u32[]{:S(2)}, u32[]{:S(2)}) collective-permute-start(f32[2,520,256]{2,1,0:T(8,128)S(1)} %maximum_select_fusion.1.a_ref), channel_id=1, source_target_pairs={{0,1},{1,2},{2,3},{3,0},{4,5},{5,6},{6,7},{7,4},{8,9},{9,10},{10,1... | collective-permute-start | bytes 3194888 | tf_op jit(solution)/shard_map/ppermute | solution.py:15
  62.9 12.6 %collective-permute-start.8 = (f32[1,520,256]{2,1,0:T(8,128)}, f32[1,520,256]{2,1,0:T(8,128)S(1)}, u32[]{:S(2)}, u32[]{:S(2)}) collective-permute-start(f32[1,520,256]{2,1,0:T(8,128)} %slice.134), channel_id=1, source_target_pairs={{0,3},{1,0},{2,1},{3,2},{4,7},{5,4},{6,5},{7,6},{8,11},{9,8},{10,9... | collective-permute-start | bytes 1597448 | tf_op jit(solution)/shard_map/ppermute | solution.py:15
  66.1 4.6 %copy-start.7 = (f32[4,256,256]{2,1,0:T(8,128)}, f32[4,256,256]{2,1,0:T(8,128)S(1)}, u32[]{:S(2)}) copy-start(f32[4,256,256]{2,1,0:T(8,128)S(1)} %collective-permute-done.11.two_r.own_fa) | copy-start | bytes 3145732
  66.1 4.6 %copy-start.10 = (f32[4,256,256]{2,1,0:T(8,128)}, f32[4,256,256]{2,1,0:T(8,128)S(1)}, u32[]{:S(2)}) copy-start(f32[4,256,256]{2,1,0:T(8,128)S(1)} %collective-permute-done.12.two_l.own_fb) | copy-start | bytes 3145732
  66.1 22.8 %collective-permute-start.13 = (f32[3,256,256]{2,1,0:T(8,128)}, f32[3,256,256]{2,1,0:T(8,128)}, u32[]{:S(2)}, u32[]{:S(2)}) collective-permute-start(f32[3,256,256]{2,1,0:T(8,128)} %get-tuple-element.32.rest), channel_id=1, source_target_pairs={{0,32},{32,64},{64,96},{96,0},{1,33},{33,65},{65,97},{97,1},{2,34}... | collective-permute-start | bytes 2359304 | tf_op jit(solution)/shard_map/ppermute | solution.py:15
  66.5 22.5 %collective-permute-start.14 = (f32[3,256,256]{2,1,0:T(8,128)}, f32[3,256,256]{2,1,0:T(8,128)}, u32[]{:S(2)}, u32[]{:S(2)}) collective-permute-start(f32[3,256,256]{2,1,0:T(8,128)} %get-tuple-element.32.rest), channel_id=1, source_target_pairs={{0,96},{32,0},{64,32},{96,64},{1,97},{33,1},{65,33},{97,65},{2,98}... | collective-permute-start | bytes 2359304 | tf_op jit(solution)/shard_map/ppermute | solution.py:15
  68.9 1.0 copy-start.2
  70.7 13.5 %collective-permute-start.10 = (f32[1,520,256]{2,1,0:T(8,128)}, f32[1,520,256]{2,1,0:T(8,128)}, u32[]{:S(2)}, u32[]{:S(2)}) collective-permute-start(f32[1,520,256]{2,1,0:T(8,128)} %slice.136), channel_id=1, source_target_pairs={{0,1},{1,2},{2,3},{3,0},{4,5},{5,6},{6,7},{7,4},{8,9},{9,10},{10,1... | collective-permute-start | bytes 1597448 | tf_op jit(solution)/shard_map/ppermute | solution.py:15
  73.1 21.1 %collective-permute-start.15 = (f32[3,128,256]{2,1,0:T(8,128)}, f32[3,128,256]{2,1,0:T(8,128)}, u32[]{:S(2)}, u32[]{:S(2)}) collective-permute-start(f32[3,128,256]{2,1,0:T(8,128)} %slice.113), channel_id=1, source_target_pairs={{0,32},{32,64},{64,96},{96,0},{1,33},{33,65},{65,97},{97,1},{2,34}... | collective-permute-start | bytes 1179656 | tf_op jit(solution)/shard_map/ppermute | solution.py:15
  75.5 18.7 %collective-permute-start.16 = (f32[3,128,256]{2,1,0:T(8,128)}, f32[3,128,256]{2,1,0:T(8,128)}, u32[]{:S(2)}, u32[]{:S(2)}) collective-permute-start(f32[3,128,256]{2,1,0:T(8,128)} %slice.114), channel_id=1, source_target_pairs={{0,96},{32,0},{64,32},{96,64},{1,97},{33,1},{65,33},{97,65},{2,98}... | collective-permute-start | bytes 1179656 | tf_op jit(solution)/shard_map/ppermute | solution.py:15
  85.2 1.2 copy-start.3
  86.4 7.8 %copy-start.5 = (f32[2,256,256]{2,1,0:T(8,128)S(1)}, f32[2,256,256]{2,1,0:T(8,128)}, u32[]{:S(2)}) copy-start(f32[2,256,256]{2,1,0:T(8,128)} %copy-done.4) | copy-start | bytes 1572868
  86.4 7.8 %copy-start.8 = (f32[4,256,256]{2,1,0:T(8,128)S(1)}, f32[4,256,256]{2,1,0:T(8,128)}, u32[]{:S(2)}) copy-start(f32[4,256,256]{2,1,0:T(8,128)} %copy-done.7) | copy-start | bytes 3145732
  86.4 7.8 %copy-start.11 = (f32[4,256,256]{2,1,0:T(8,128)S(1)}, f32[4,256,256]{2,1,0:T(8,128)}, u32[]{:S(2)}) copy-start(f32[4,256,256]{2,1,0:T(8,128)} %copy-done.10) | copy-start | bytes 3145732
  86.4 7.8 %copy-start.14 = (f32[2,256,256]{2,1,0:T(8,128)S(1)}, f32[2,256,256]{2,1,0:T(8,128)}, u32[]{:S(2)}) copy-start(f32[2,256,256]{2,1,0:T(8,128)} %copy-done.13) | copy-start | bytes 1572868
  86.4 7.8 %copy-start.17 = (f32[2,256,256]{2,1,0:T(8,128)S(1)}, f32[2,256,256]{2,1,0:T(8,128)}, u32[]{:S(2)}) copy-start(f32[2,256,256]{2,1,0:T(8,128)} %copy-done.16) | copy-start | bytes 1572868
  88.8 9.5 %copy-start = (bf16[4,4,256,768]{3,2,1,0:T(8,128)(2,1)}, bf16[4,4,256,768]{3,2,1,0:T(8,128)(2,1)S(1)}, u32[]{:S(2)}) copy-start(bf16[4,4,256,768]{3,2,1,0:T(8,128)(2,1)S(1)} %split_amp.1.a_ref) | copy-start | bytes 18874372
  98.4 11.6 %collective-permute-start.17 = (f32[4,2,256,256]{3,2,1,0:T(8,128)S(1)}, f32[4,2,256,256]{3,2,1,0:T(8,128)S(1)}, u32[]{:S(2)}, u32[]{:S(2)}) collective-permute-start(f32[4,2,256,256]{3,2,1,0:T(8,128)S(1)} %get-tuple-element.37), channel_id=1, source_target_pairs={{0,16},{16,0},{1,17},{17,1},{2,18},{18,2},{3,19},{19,3},{4,20},{20... | collective-permute-start | bytes 6291464 | tf_op jit(solution)/shard_map/ppermute | solution.py:15
  106.1 12.0 %collective-permute-start.18 = (f32[3,128,256]{2,1,0:T(8,128)S(1)}, f32[3,128,256]{2,1,0:T(8,128)S(1)}, u32[]{:S(2)}, u32[]{:S(2)}) collective-permute-start(f32[3,128,256]{2,1,0:T(8,128)S(1)} %slice.119), channel_id=1, source_target_pairs={{0,32},{32,64},{64,96},{96,0},{1,33},{33,65},{65,97},{97,1},{2,34}... | collective-permute-start | bytes 1179656 | tf_op jit(solution)/shard_map/ppermute | solution.py:15
  107.2 10.9 %collective-permute-start.19 = (f32[3,128,256]{2,1,0:T(8,128)S(1)}, f32[3,128,256]{2,1,0:T(8,128)S(1)}, u32[]{:S(2)}, u32[]{:S(2)}) collective-permute-start(f32[3,128,256]{2,1,0:T(8,128)S(1)} %slice.120), channel_id=1, source_target_pairs={{0,96},{32,0},{64,32},{96,64},{1,97},{33,1},{65,33},{97,65},{2,98}... | collective-permute-start | bytes 1179656 | tf_op jit(solution)/shard_map/ppermute | solution.py:15
  111.6 7.3 %copy-start.6 = (f32[2,256,256]{2,1,0:T(8,128)S(1)}, f32[2,256,256]{2,1,0:T(8,128)}, u32[]{:S(2)}) copy-start(f32[2,256,256]{2,1,0:T(8,128)} %copy-done.4) | copy-start | bytes 1572868
  111.6 7.3 %copy-start.15 = (f32[2,256,256]{2,1,0:T(8,128)S(1)}, f32[2,256,256]{2,1,0:T(8,128)}, u32[]{:S(2)}) copy-start(f32[2,256,256]{2,1,0:T(8,128)} %copy-done.13) | copy-start | bytes 1572868
  111.6 30.5 %all-to-all-start = ((f32[4,2,256,256]{3,2,1,0:T(8,128)}), f32[4,2,256,256]{3,2,1,0:T(8,128)}, u32[]{:S(2)}, u32[]{:S(2)}) async-start(f32[4,2,256,256]{3,2,1,0:T(8,128)} %add.233), calls=%async_computation | async-start | bytes 4194304 | tf_op jit(solution)/shard_map/all_to_all | solution.py:177
  118.2 0.8 copy-start.19
  119.0 2.8 %copy-start.1 = (bf16[4,4,256,768]{3,2,1,0:T(8,128)(2,1)S(1)}, bf16[4,4,256,768]{3,2,1,0:T(8,128)(2,1)}, u32[]{:S(2)}) copy-start(bf16[4,4,256,768]{3,2,1,0:T(8,128)(2,1)} %copy-done) | copy-start | bytes 18874372
  121.7 1.2 copy-start.9
  123.0 1.2 copy-start.12
  124.2 1.0 copy-start.18
  125.2 1.0 copy-start.20
  135.5 8.1 %collective-permute-start.20 = (f32[4,1,256,256]{3,2,1,0:T(8,128)}, f32[4,1,256,256]{3,2,1,0:T(8,128)S(1)}, u32[]{:S(2)}, u32[]{:S(2)}) collective-permute-start(f32[4,1,256,256]{3,2,1,0:T(8,128)} %get-tuple-element.43), channel_id=1, source_target_pairs={{0,16},{16,0},{1,17},{17,1},{2,18},{18,2},{3,19},{19,3},{4,20},{20... | collective-permute-start | bytes 3145736 | tf_op jit(solution)/shard_map/ppermute | solution.py:15
  142.1 3.9 %collective-permute-start.21 = (f32[4,1,256,256]{3,2,1,0:T(8,128)}, f32[4,1,256,256]{3,2,1,0:T(8,128)S(1)}, u32[]{:S(2)}, u32[]{:S(2)}) collective-permute-start(f32[4,1,256,256]{3,2,1,0:T(8,128)} %get-tuple-element.42), channel_id=1, source_target_pairs={{0,16},{16,0},{1,17},{17,1},{2,18},{18,2},{3,19},{19,3},{4,20},{20... | collective-permute-start | bytes 3145736 | tf_op jit(solution)/shard_map/ppermute | solution.py:15
  147.7 29.7 %all-to-all-start.1 = ((f32[4,2,256,256]{3,2,1,0:T(8,128)}), f32[4,2,256,256]{3,2,1,0:T(8,128)S(1)}, u32[]{:S(2)}, u32[]{:S(2)}) async-start(f32[4,2,256,256]{3,2,1,0:T(8,128)} %maximum_add_fusion), calls=%async_computation.1 | async-start | bytes 4194304 | tf_op jit(solution)/shard_map/all_to_all | solution.py:183
  177.3 1.2 copy-start.21
